TPU v7x, 32 devices: a whole 2x2x4 slice. The times are simulated.
32 devices in a mesh: groups: 1, ctx: 32 (over z, y, x, core), kv: 1.
Axes of the slice: x: 2, y: 2, z: 4, core: 2. Of those that a mesh axis runs over, the one named last changes fastest.
Arguments:
- queries: bfloat16 [128, 64, 128], P('groups', 'kv'), may hold values from -10 to 10
- cache_keys: bfloat16 [32768, 4, 128], P(('groups', 'ctx'), 'kv'), may hold values from -5 to 5
- cache_values: bfloat16 [32768, 4, 128], P(('groups', 'ctx'), 'kv'), may hold values from -5 to 5
- block_mask: int32 [1, 256], P('groups', 'ctx'), may hold values from 0 to 1
- key_counts: int32 [256], P(('groups', 'ctx')), may hold values from 1 to 128, as said below
- out_weight: bfloat16 [8192, 16384], P('kv', 'ctx'), may hold values from -0.25 to 0.25
Outputs:
- layer_out: float32 [128, 16384], P(('groups', 'kv'), 'ctx')
Inputs may be any that keep to these rules, and one draw needn't show every extreme that they name: `key_counts`: key block 0 is full.
All inputs are finite; a program needn't handle non-finite values.
Results may differ from a plain program's by a relative error of at most 0.0065.
Values may be sent and summed in bfloat16 or wider, within the bound.
No kernel may reach another device: no remote copies, remote signals or barrier semaphores. Data moves between devices by JAX's collectives and lax.ppermute only.
A program may use at most 64 MiB of HBM per device.

v0:
```python
import math

import jax
import jax.numpy as jnp
from jax import lax
from jax.sharding import PartitionSpec as P

BLK = 128


very_low = -1e30


def partner(value, axis, distance):
    mask = 2**distance
    pairs = [(source, source ^ mask) for source in range(lax.axis_size(axis))]
    return lax.ppermute(value, axis, pairs)


def combine(earlier, later):
    out_one, top_one, sum_one = earlier
    out_two, top_two, sum_two = later
    new_top = jnp.maximum(top_one, top_two)
    factor_one = jnp.exp(top_one - new_top)
    factor_two = jnp.exp(top_two - new_top)
    new_out = out_one * factor_one[..., None] + out_two * factor_two[..., None]
    return (new_out, new_top, sum_one * factor_one + sum_two * factor_two)


def keep_state(key_block, run_state):
    return run_state


def partial_rows(rows_q, row_mask, cache_keys, cache_values, key_counts):
    row_count, head_count, head_size = rows_q.shape
    kv_count = cache_keys.shape[1]
    group_size = head_count // kv_count
    grouped = rows_q.reshape(row_count, kv_count, group_size, head_size)
    block_count = cache_keys.shape[0] // BLK
    score_scale = 1.0 / math.sqrt(head_size)
    offsets = jnp.arange(BLK, dtype=jnp.int32)

    def update(key_block, run_state):
        out_sum, top_score, weight_sum = run_state
        key_part = lax.dynamic_slice_in_dim(cache_keys, key_block * BLK, BLK, 0)
        value_part = lax.dynamic_slice_in_dim(cache_values, key_block * BLK, BLK, 0)
        scores = (
            jnp.einsum("rgqd,kgd->rgqk", grouped, key_part, preferred_element_type=jnp.float32)
            * score_scale
        )
        active_rows = lax.dynamic_slice_in_dim(row_mask, key_block, 1, 1)[:, 0] > 0
        valid_count = lax.dynamic_slice_in_dim(key_counts, key_block, 1, 0)[0]
        valid = active_rows[:, None, None, None] & (offsets < valid_count)[None, None, None, :]
        scores = jnp.where(valid, scores, very_low)
        new_top = jnp.maximum(top_score, jnp.max(scores, axis=-1))
        weights = jnp.where(valid, jnp.exp(scores - new_top[..., None]), 0.0)
        factor = jnp.exp(top_score - new_top)
        new_sum = weight_sum * factor + jnp.sum(weights, axis=-1)
        new_out = out_sum * factor[..., None] + jnp.einsum(
            "rgqk,kgd->rgqd",
            weights.astype(jnp.bfloat16),
            value_part,
            preferred_element_type=jnp.float32,
        )
        return (new_out, new_top, new_sum)

    def visit_block(key_block, run_state):
        active = jnp.any(lax.dynamic_slice_in_dim(row_mask, key_block, 1, 1) > 0)
        return lax.cond(active, update, keep_state, key_block, run_state)

    initial = (
        jnp.zeros((row_count, kv_count, group_size, head_size), jnp.float32),
        jnp.full((row_count, kv_count, group_size), very_low, jnp.float32),
        jnp.zeros((row_count, kv_count, group_size), jnp.float32),
    )
    return lax.fori_loop(0, block_count, visit_block, initial)


def body(queries, cache_keys, cache_values, block_mask, key_counts, out_weight):
    cycle_size = lax.axis_size("ctx")
    cycle_index = lax.axis_index("ctx")
    token_count, head_count, head_size = queries.shape
    segment = token_count // cycle_size
    query_blocks = queries.reshape(block_mask.shape[0], BLK, head_count, head_size)

    def per_block(block_item):
        rows_q, mask_row = block_item
        row_mask = jnp.broadcast_to(mask_row[None, :], (BLK, mask_row.shape[0]))
        return partial_rows(rows_q, row_mask, cache_keys, cache_values, key_counts)

    stacked = lax.map(per_block, (query_blocks, block_mask))
    local_state = tuple((part.reshape((token_count,) + part.shape[2:]) for part in stacked))
    run_state = local_state
    bit_total = cycle_size.bit_length() - 1
    for bit_number in range(bit_total - 1, -1, -1):
        half_rows = run_state[1].shape[0] // 2
        upper_half = jnp.bitwise_and(jnp.right_shift(cycle_index, bit_number), 1)
        kept = tuple(
            (
                lax.dynamic_slice_in_dim(part, upper_half * half_rows, half_rows, 0)
                for part in run_state
            )
        )
        outgoing = tuple(
            (
                lax.dynamic_slice_in_dim(part, (1 - upper_half) * half_rows, half_rows, 0)
                for part in run_state
            )
        )
        received = partner((outgoing[0], outgoing[1], outgoing[2]), "ctx", bit_number)
        run_state = combine(kept, received)
    out_sum, top_score, weight_sum = run_state
    attended = (
        (out_sum / weight_sum[..., None])
        .astype(jnp.bfloat16)
        .reshape(segment, head_count * head_size)
    )
    partial_value = jnp.dot(
        lax.all_gather(attended, "ctx", axis=0, tiled=True),
        out_weight,
        preferred_element_type=jnp.float32,
    )
    summed = lax.psum_scatter(partial_value, "kv", scatter_dimension=0, tiled=True)
    return summed


def solution(mesh):
    placed = (
        P("groups", "kv", None),
        P(("groups", "ctx"), "kv", None),
        P(("groups", "ctx"), "kv", None),
        P("groups", "ctx"),
        P(("groups", "ctx")),
        P("kv", "ctx"),
    )
    return jax.shard_map(
        body, mesh=mesh, in_specs=placed, out_specs=P(("groups", "kv"), "ctx"), check_vma=False
    )
```

profile of v0, /device:TPU:0, one launch (start us, length us, event | category | flops | bytes accessed | tf_op | source)
XLA Modules:
  0.0 292.5 jit_solution(160802962384505553)
XLA Ops:
  6.5 2.4 copy.35
  8.9 2.9 %copy.34 = bf16[128,64,128]{2,0,1:T(8,128)(2,1)S(1)} copy(bf16[128,64,128]{2,1,0:T(8,128)(2,1)} %param.10) | data formatting | bytes 4194304 | tf_op args[0]
  13.6 2.5 broadcast.65
  16.1 72.0 %while.29 = (s32[]{:T(128)}, f32[128,4,16,128]{0,3,2,1:T(8,128)}, f32[128,4,16]{0,2,1:T(8,128)S(1)}, f32[128,4,16]{0,2,1:T(8,128)S(1)}, s32[128,8]{0,1:T(8,128)S...) while((s32[]{:T(128)}, f32[128,4,16,128]{0,3,2,1:T(8,128)}, ...), condition=%wide.region_6.0_spmd.clone, body=%wide.region_0.6_spmd.clone.sunk | while | flops 552632832 | bytes 57478048 | solution.py:76
  17.5 8.8 %conditional.3 = ((f32[128,4,16,128]{0,3,2,1:T(8,128)}, f32[128,4,16]{0,2,1:T(8,128)S(1)}, f32[128,4,16]{0,2,1:T(8,128)S(1)})) conditional(s32[]{:T(128)} %convert_element_type.19, (f32[128,4,16,128]{0,3,2,1:T(8,128)}, f32[128,4,16]{0,2,1:T(8,128)S(1)}, f32[128,4,16]{0,2,1:T(8,128)S(1)}) %tuple.65, (s32[]{:T(128)}, s32[128,8]{0,1:T(8,128)S(1)}, ...), branch_computations={%region_2.2_spmd, %region_3.5_spmd} | conditional | flops 552632576 | bytes 57476800 | solution.py:69
  22.1 2.2 bitcast_add_fusion
  24.2 2.0 copy-done.1
  28.9 8.8 %conditional.3 = ((f32[128,4,16,128]{0,3,2,1:T(8,128)}, f32[128,4,16]{0,2,1:T(8,128)S(1)}, f32[128,4,16]{0,2,1:T(8,128)S(1)})) conditional(s32[]{:T(128)} %convert_element_type.19, (f32[128,4,16,128]{0,3,2,1:T(8,128)}, f32[128,4,16]{0,2,1:T(8,128)S(1)}, f32[128,4,16]{0,2,1:T(8,128)S(1)}) %tuple.65, (s32[]{:T(128)}, s32[128,8]{0,1:T(8,128)S(1)}, ...), branch_computations={%region_2.2_spmd, %region_3.5_spmd} | conditional | flops 552632576 | bytes 57476800 | solution.py:69
  33.5 2.2 bitcast_add_fusion
  39.0 8.8 %conditional.3 = ((f32[128,4,16,128]{0,3,2,1:T(8,128)}, f32[128,4,16]{0,2,1:T(8,128)S(1)}, f32[128,4,16]{0,2,1:T(8,128)S(1)})) conditional(s32[]{:T(128)} %convert_element_type.19, (f32[128,4,16,128]{0,3,2,1:T(8,128)}, f32[128,4,16]{0,2,1:T(8,128)S(1)}, f32[128,4,16]{0,2,1:T(8,128)S(1)}) %tuple.65, (s32[]{:T(128)}, s32[128,8]{0,1:T(8,128)S(1)}, ...), branch_computations={%region_2.2_spmd, %region_3.5_spmd} | conditional | flops 552632576 | bytes 57476800 | solution.py:69
  43.6 2.1 bitcast_add_fusion
  49.1 8.8 %conditional.3 = ((f32[128,4,16,128]{0,3,2,1:T(8,128)}, f32[128,4,16]{0,2,1:T(8,128)S(1)}, f32[128,4,16]{0,2,1:T(8,128)S(1)})) conditional(s32[]{:T(128)} %convert_element_type.19, (f32[128,4,16,128]{0,3,2,1:T(8,128)}, f32[128,4,16]{0,2,1:T(8,128)S(1)}, f32[128,4,16]{0,2,1:T(8,128)S(1)}) %tuple.65, (s32[]{:T(128)}, s32[128,8]{0,1:T(8,128)S(1)}, ...), branch_computations={%region_2.2_spmd, %region_3.5_spmd} | conditional | flops 552632576 | bytes 57476800 | solution.py:69
  53.7 2.1 bitcast_add_fusion
  59.2 8.8 %conditional.3 = ((f32[128,4,16,128]{0,3,2,1:T(8,128)}, f32[128,4,16]{0,2,1:T(8,128)S(1)}, f32[128,4,16]{0,2,1:T(8,128)S(1)})) conditional(s32[]{:T(128)} %convert_element_type.19, (f32[128,4,16,128]{0,3,2,1:T(8,128)}, f32[128,4,16]{0,2,1:T(8,128)S(1)}, f32[128,4,16]{0,2,1:T(8,128)S(1)}) %tuple.65, (s32[]{:T(128)}, s32[128,8]{0,1:T(8,128)S(1)}, ...), branch_computations={%region_2.2_spmd, %region_3.5_spmd} | conditional | flops 552632576 | bytes 57476800 | solution.py:69
  63.8 2.1 bitcast_add_fusion
  69.3 8.8 %conditional.3 = ((f32[128,4,16,128]{0,3,2,1:T(8,128)}, f32[128,4,16]{0,2,1:T(8,128)S(1)}, f32[128,4,16]{0,2,1:T(8,128)S(1)})) conditional(s32[]{:T(128)} %convert_element_type.19, (f32[128,4,16,128]{0,3,2,1:T(8,128)}, f32[128,4,16]{0,2,1:T(8,128)S(1)}, f32[128,4,16]{0,2,1:T(8,128)S(1)}) %tuple.65, (s32[]{:T(128)}, s32[128,8]{0,1:T(8,128)S(1)}, ...), branch_computations={%region_2.2_spmd, %region_3.5_spmd} | conditional | flops 552632576 | bytes 57476800 | solution.py:69
  73.9 2.2 bitcast_add_fusion
  79.4 8.8 %conditional.3 = ((f32[128,4,16,128]{0,3,2,1:T(8,128)}, f32[128,4,16]{0,2,1:T(8,128)S(1)}, f32[128,4,16]{0,2,1:T(8,128)S(1)})) conditional(s32[]{:T(128)} %convert_element_type.19, (f32[128,4,16,128]{0,3,2,1:T(8,128)}, f32[128,4,16]{0,2,1:T(8,128)S(1)}, f32[128,4,16]{0,2,1:T(8,128)S(1)}) %tuple.65, (s32[]{:T(128)}, s32[128,8]{0,1:T(8,128)S(1)}, ...), branch_computations={%region_2.2_spmd, %region_3.5_spmd} | conditional | flops 552632576 | bytes 57476800 | solution.py:69
  84.0 2.2 bitcast_add_fusion
  88.2 5.5 %copy.37 = f32[128,4,16,128]{3,2,1,0:T(8,128)} copy(f32[128,4,16,128]{0,3,2,1:T(8,128)} %get-tuple-element.260) | data formatting | bytes 8388608 | tf_op jit(solution)/shard_map/while/body/eval_jaxpr/while | solution.py:76
  93.6 3.2 %constant_dynamic-slice_fusion.15 = f32[64,4,16,128]{3,2,1,0:T(8,128)} fusion(f32[128,4,16,128]{3,2,1,0:T(8,128)} %copy.37, s32[]{:T(128)S(6)} %select_n.41), kind=kLoop, calls=%fused_computation.69 | loop fusion | bytes 4194308 | tf_op jit(solution)/shard_map/dynamic_slice | solution.py:106
  97.0 3.0 %collective-permute-start.10 = (f32[64,4,16]{2,1,0:T(4,128)S(1)}, f32[64,4,16]{2,1,0:T(4,128)S(1)}, u32[]{:S(2)}, u32[]{:S(2)}) collective-permute-start(f32[64,4,16]{2,1,0:T(4,128)S(1)} %constant_dynamic-slice_fusion.5), channel_id=1, source_target_pairs={{0,16},{1,17},{2,18},{3,19},{4,20},{5,21},{6,22},{7,23},{8,24},{9,... | collective-permute-start | bytes 49160 | tf_op jit(solution)/shard_map/ppermute | solution.py:17
  100.3 40.1 %collective-permute-done.10 = f32[64,4,16]{2,1,0:T(4,128)S(1)} collective-permute-done((f32[64,4,16]{2,1,0:T(4,128)S(1)}, f32[64,4,16]{2,1,0:T(4,128)S(1)}, u32[]{:S(2)}, u32[]{:S(2)}) %collective-permute-start.10) | collective-permute-done | bytes 16416 | tf_op jit(solution)/shard_map/ppermute | solution.py:17
  143.3 3.6 %multiply_add_fusion.1 = f32[64,4,16,128]{3,2,1,0:T(8,128)S(1)} fusion(f32[64,4,16,128]{3,2,1,0:T(8,128)} %copy-done.2, f32[128,4,16,128]{3,2,1,0:T(8,128)} %copy.37, s32[]{:T(128)S(6)} %select_n.40, f32[64,4,16]{2,1,0:T(4,128)S(1)} %get-tuple-element.359, f32[64,4,16]{2,1,0:T(4,128)S(1)} %get-tuple-element.358), kind=kLoop, calls=%fused_computation.29 | loop fusion | flops 1572864 | bytes 6324228 | tf_op jit(solution)/shard_map/add | solution.py:26
  150.4 22.8 %collective-permute-done.11 = f32[32,4,16]{2,1,0:T(4,128)S(1)} collective-permute-done((f32[32,4,16]{2,1,0:T(4,128)S(1)}, f32[32,4,16]{2,1,0:T(4,128)S(1)}, u32[]{:S(2)}, u32[]{:S(2)}) %collective-permute-start.11) | collective-permute-done | bytes 8224 | tf_op jit(solution)/shard_map/ppermute | solution.py:17
  175.0 19.4 %collective-permute-start.12 = (f32[16,4,16]{2,1,0:T(4,128)S(1)}, f32[16,4,16]{2,1,0:T(4,128)S(1)}, u32[]{:S(2)}, u32[]{:S(2)}) collective-permute-start(f32[16,4,16]{2,1,0:T(4,128)S(1)} %constant_dynamic-slice_fusion.3), channel_id=1, source_target_pairs={{0,4},{1,5},{2,6},{3,7},{4,0},{5,1},{6,2},{7,3},{8,12},{9,13},{10,... | collective-permute-start | bytes 12296 | tf_op jit(solution)/shard_map/ppermute | solution.py:17
  198.5 10.7 %collective-permute-done.4 = f32[16,4,16]{2,1,0:T(4,128)S(1)} collective-permute-done((f32[16,4,16]{2,1,0:T(4,128)S(1)}, f32[16,4,16]{2,1,0:T(4,128)S(1)}, u32[]{:S(2)}, u32[]{:S(2)}) %collective-permute-start.4) | collective-permute-done | bytes 4128 | tf_op jit(solution)/shard_map/ppermute | solution.py:17
  209.2 3.8 %collective-permute-start.13 = (f32[8,4,16]{2,1,0:T(4,128)S(1)}, f32[8,4,16]{2,1,0:T(4,128)S(1)}, u32[]{:S(2)}, u32[]{:S(2)}) collective-permute-start(f32[8,4,16]{2,1,0:T(4,128)S(1)} %constant_dynamic-slice_fusion.2), channel_id=1, source_target_pairs={{0,2},{1,3},{2,0},{3,1},{4,6},{5,7},{6,4},{7,5},{8,10},{9,11},{10,... | collective-permute-start | bytes 6152 | tf_op jit(solution)/shard_map/ppermute | solution.py:17
  217.6 3.0 %collective-permute-done.7 = f32[8,4,16,128]{3,2,1,0:T(8,128)S(1)} collective-permute-done((f32[8,4,16,128]{3,2,1,0:T(8,128)S(1)}, f32[8,4,16,128]{3,2,1,0:T(8,128)S(1)}, u32[]{:S(2)}, u32[]{:S(2)}) %collective-permute-start.7) | collective-permute-done | bytes 262176 | tf_op jit(solution)/shard_map/ppermute | solution.py:17
  223.1 54.6 %all-gather.3.cloned.1.call-done = bf16[32,4,8192]{2,1,0:T(4,128)(2,1)} async-done(((bf16[1,4,8192]{2,1,0:T(4,128)(2,1)}), bf16[32,4,8192]{2,1,0:T(4,128)(2,1)}) %all-gather.3.cloned.1.call-update) | async-done | bytes 2097168 | tf_op jit(solution)/shard_map/all_gather | solution.py:119
  277.7 2.5 reshape.72
  280.3 5.3 %fusion.25 = f32[128,512]{1,0:T(8,128)} fusion(bf16[128,8192]{1,0:T(8,128)(2,1)S(1)} %reshape.72, bf16[8192,512]{1,0:T(8,128)(2,1)} %param.15), kind=kOutput, calls=%fused_computation.71 | convolution fusion | flops 1073741824 | bytes 10747904 | tf_op jit(solution)/shard_map/dot_general | solution.py:118
  (170 shorter events, 70.2 us)
Async XLA Ops:
  6.5 271.2 %all-gather.3.cloned.1.call-start = ((), (), s32[]{:S(2)}) async-start(), calls=%async_computation | async-start | bytes 2162688 | tf_op jit(solution)/shard_map/all_gather | solution.py:119
  6.5 7.0 %copy-start.4 = (s32[1,8]{1,0:T(1,128)S(1)}, s32[1,8]{1,0:T(1,128)}, u32[]{:S(2)}) copy-start(s32[1,8]{1,0:T(1,128)} %param.13) | copy-start | bytes 100
  11.9 4.3 %copy-start.5 = (s32[8]{0:T(128)S(1)}, s32[8]{0:T(128)}, u32[]{:S(2)}) copy-start(s32[8]{0:T(128)} %param.14) | copy-start | bytes 100
  18.9 3.2 %copy-start = (f32[128,4,16,128]{0,3,2,1:T(8,128)S(1)}, f32[128,4,16,128]{0,3,2,1:T(8,128)}, u32[]{:S(2)}) copy-start(f32[128,4,16,128]{0,3,2,1:T(8,128)} %get-tuple-element.233) | copy-start | bytes 12582916 | tf_op jit(solution)/shard_map/while/body/eval_jaxpr/while/body/eval_jaxpr/cond
  24.2 2.0 copy-start.1
  30.3 3.2 %copy-start = (f32[128,4,16,128]{0,3,2,1:T(8,128)S(1)}, f32[128,4,16,128]{0,3,2,1:T(8,128)}, u32[]{:S(2)}) copy-start(f32[128,4,16,128]{0,3,2,1:T(8,128)} %get-tuple-element.233) | copy-start | bytes 12582916 | tf_op jit(solution)/shard_map/while/body/eval_jaxpr/while/body/eval_jaxpr/cond
  35.7 2.0 copy-start.1
  40.4 3.2 %copy-start = (f32[128,4,16,128]{0,3,2,1:T(8,128)S(1)}, f32[128,4,16,128]{0,3,2,1:T(8,128)}, u32[]{:S(2)}) copy-start(f32[128,4,16,128]{0,3,2,1:T(8,128)} %get-tuple-element.233) | copy-start | bytes 12582916 | tf_op jit(solution)/shard_map/while/body/eval_jaxpr/while/body/eval_jaxpr/cond
  45.8 2.0 copy-start.1
  50.5 3.2 %copy-start = (f32[128,4,16,128]{0,3,2,1:T(8,128)S(1)}, f32[128,4,16,128]{0,3,2,1:T(8,128)}, u32[]{:S(2)}) copy-start(f32[128,4,16,128]{0,3,2,1:T(8,128)} %get-tuple-element.233) | copy-start | bytes 12582916 | tf_op jit(solution)/shard_map/while/body/eval_jaxpr/while/body/eval_jaxpr/cond
  55.9 2.0 copy-start.1
  60.6 3.2 %copy-start = (f32[128,4,16,128]{0,3,2,1:T(8,128)S(1)}, f32[128,4,16,128]{0,3,2,1:T(8,128)}, u32[]{:S(2)}) copy-start(f32[128,4,16,128]{0,3,2,1:T(8,128)} %get-tuple-element.233) | copy-start | bytes 12582916 | tf_op jit(solution)/shard_map/while/body/eval_jaxpr/while/body/eval_jaxpr/cond
  65.9 2.0 copy-start.1
  70.7 3.2 %copy-start = (f32[128,4,16,128]{0,3,2,1:T(8,128)S(1)}, f32[128,4,16,128]{0,3,2,1:T(8,128)}, u32[]{:S(2)}) copy-start(f32[128,4,16,128]{0,3,2,1:T(8,128)} %get-tuple-element.233) | copy-start | bytes 12582916 | tf_op jit(solution)/shard_map/while/body/eval_jaxpr/while/body/eval_jaxpr/cond
  76.0 2.0 copy-start.1
  80.8 3.2 %copy-start = (f32[128,4,16,128]{0,3,2,1:T(8,128)S(1)}, f32[128,4,16,128]{0,3,2,1:T(8,128)}, u32[]{:S(2)}) copy-start(f32[128,4,16,128]{0,3,2,1:T(8,128)} %get-tuple-element.233) | copy-start | bytes 12582916 | tf_op jit(solution)/shard_map/while/body/eval_jaxpr/while/body/eval_jaxpr/cond
  86.1 2.0 copy-start.1
  96.8 45.1 %collective-permute-start.1 = (f32[64,4,16,128]{3,2,1,0:T(8,128)}, f32[64,4,16,128]{3,2,1,0:T(8,128)S(1)}, u32[]{:S(2)}, u32[]{:S(2)}) collective-permute-start(f32[64,4,16,128]{3,2,1,0:T(8,128)} %constant_dynamic-slice_fusion.15), channel_id=1, source_target_pairs={{0,16},{1,17},{2,18},{3,19},{4,20},{5,21},{6,22},{7,23},{8,24},{9,... | collective-permute-start | bytes 6291464 | tf_op jit(solution)/shard_map/ppermute | solution.py:17
  97.0 43.4 %collective-permute-start.10 = (f32[64,4,16]{2,1,0:T(4,128)S(1)}, f32[64,4,16]{2,1,0:T(4,128)S(1)}, u32[]{:S(2)}, u32[]{:S(2)}) collective-permute-start(f32[64,4,16]{2,1,0:T(4,128)S(1)} %constant_dynamic-slice_fusion.5), channel_id=1, source_target_pairs={{0,16},{1,17},{2,18},{3,19},{4,20},{5,21},{6,22},{7,23},{8,24},{9,... | collective-permute-start | bytes 49160 | tf_op jit(solution)/shard_map/ppermute | solution.py:17
  100.2 41.6 %collective-permute-start = (f32[64,4,16]{2,1,0:T(4,128)S(1)}, f32[64,4,16]{2,1,0:T(4,128)S(1)}, u32[]{:S(2)}, u32[]{:S(2)}) collective-permute-start(f32[64,4,16]{2,1,0:T(4,128)S(1)} %constant_dynamic-slice_fusion.16), channel_id=1, source_target_pairs={{0,16},{1,17},{2,18},{3,19},{4,20},{5,21},{6,22},{7,23},{8,24},{9,... | collective-permute-start | bytes 49160 | tf_op jit(solution)/shard_map/ppermute | solution.py:17
  147.0 47.5 %collective-permute-start.3 = (f32[32,4,16,128]{3,2,1,0:T(8,128)S(1)}, f32[32,4,16,128]{3,2,1,0:T(8,128)}, u32[]{:S(2)}, u32[]{:S(2)}) collective-permute-start(f32[32,4,16,128]{3,2,1,0:T(8,128)S(1)} %constant_dynamic-slice_fusion.13), channel_id=1, source_target_pairs={{0,8},{1,9},{2,10},{3,11},{4,12},{5,13},{6,14},{7,15},{8,0},{9,1},... | collective-permute-start | bytes 3145736 | tf_op jit(solution)/shard_map/ppermute | solution.py:17
  147.8 25.4 %collective-permute-start.11 = (f32[32,4,16]{2,1,0:T(4,128)S(1)}, f32[32,4,16]{2,1,0:T(4,128)S(1)}, u32[]{:S(2)}, u32[]{:S(2)}) collective-permute-start(f32[32,4,16]{2,1,0:T(4,128)S(1)} %constant_dynamic-slice_fusion.4), channel_id=1, source_target_pairs={{0,8},{1,9},{2,10},{3,11},{4,12},{5,13},{6,14},{7,15},{8,0},{9,1},... | collective-permute-start | bytes 24584 | tf_op jit(solution)/shard_map/ppermute | solution.py:17
  149.7 24.3 %collective-permute-start.2 = (f32[32,4,16]{2,1,0:T(4,128)}, f32[32,4,16]{2,1,0:T(4,128)}, u32[]{:S(2)}, u32[]{:S(2)}) collective-permute-start(f32[32,4,16]{2,1,0:T(4,128)} %constant_dynamic-slice_fusion.14), channel_id=1, source_target_pairs={{0,8},{1,9},{2,10},{3,11},{4,12},{5,13},{6,14},{7,15},{8,0},{9,1},... | collective-permute-start | bytes 24584 | tf_op jit(solution)/shard_map/ppermute | solution.py:17
  175.0 23.5 %collective-permute-start.12 = (f32[16,4,16]{2,1,0:T(4,128)S(1)}, f32[16,4,16]{2,1,0:T(4,128)S(1)}, u32[]{:S(2)}, u32[]{:S(2)}) collective-permute-start(f32[16,4,16]{2,1,0:T(4,128)S(1)} %constant_dynamic-slice_fusion.3), channel_id=1, source_target_pairs={{0,4},{1,5},{2,6},{3,7},{4,0},{5,1},{6,2},{7,3},{8,12},{9,13},{10,... | collective-permute-start | bytes 12296 | tf_op jit(solution)/shard_map/ppermute | solution.py:17
  196.4 16.7 %collective-permute-start.5 = (f32[16,4,16,128]{3,2,1,0:T(8,128)S(1)}, f32[16,4,16,128]{3,2,1,0:T(8,128)S(1)}, u32[]{:S(2)}, u32[]{:S(2)}) collective-permute-start(f32[16,4,16,128]{3,2,1,0:T(8,128)S(1)} %constant_dynamic-slice_fusion.11), channel_id=1, source_target_pairs={{0,4},{1,5},{2,6},{3,7},{4,0},{5,1},{6,2},{7,3},{8,12},{9,13},{10,... | collective-permute-start | bytes 1572872 | tf_op jit(solution)/shard_map/ppermute | solution.py:17
  196.5 12.7 %collective-permute-start.4 = (f32[16,4,16]{2,1,0:T(4,128)S(1)}, f32[16,4,16]{2,1,0:T(4,128)S(1)}, u32[]{:S(2)}, u32[]{:S(2)}) collective-permute-start(f32[16,4,16]{2,1,0:T(4,128)S(1)} %constant_dynamic-slice_fusion.12), channel_id=1, source_target_pairs={{0,4},{1,5},{2,6},{3,7},{4,0},{5,1},{6,2},{7,3},{8,12},{9,13},{10,... | collective-permute-start | bytes 12296 | tf_op jit(solution)/shard_map/ppermute | solution.py:17
  209.2 6.3 %collective-permute-start.13 = (f32[8,4,16]{2,1,0:T(4,128)S(1)}, f32[8,4,16]{2,1,0:T(4,128)S(1)}, u32[]{:S(2)}, u32[]{:S(2)}) collective-permute-start(f32[8,4,16]{2,1,0:T(4,128)S(1)} %constant_dynamic-slice_fusion.2), channel_id=1, source_target_pairs={{0,2},{1,3},{2,0},{3,1},{4,6},{5,7},{6,4},{7,5},{8,10},{9,11},{10,... | collective-permute-start | bytes 6152 | tf_op jit(solution)/shard_map/ppermute | solution.py:17
  213.0 4.0 %collective-permute-start.6 = (f32[8,4,16]{2,1,0:T(4,128)S(1)}, f32[8,4,16]{2,1,0:T(4,128)S(1)}, u32[]{:S(2)}, u32[]{:S(2)}) collective-permute-start(f32[8,4,16]{2,1,0:T(4,128)S(1)} %constant_dynamic-slice_fusion.10), channel_id=1, source_target_pairs={{0,2},{1,3},{2,0},{3,1},{4,6},{5,7},{6,4},{7,5},{8,10},{9,11},{10,... | collective-permute-start | bytes 6152 | tf_op jit(solution)/shard_map/ppermute | solution.py:17
  213.5 7.1 %collective-permute-start.7 = (f32[8,4,16,128]{3,2,1,0:T(8,128)S(1)}, f32[8,4,16,128]{3,2,1,0:T(8,128)S(1)}, u32[]{:S(2)}, u32[]{:S(2)}) collective-permute-start(f32[8,4,16,128]{3,2,1,0:T(8,128)S(1)} %constant_dynamic-slice_fusion.9), channel_id=1, source_target_pairs={{0,2},{1,3},{2,0},{3,1},{4,6},{5,7},{6,4},{7,5},{8,10},{9,11},{10,... | collective-permute-start | bytes 786440 | tf_op jit(solution)/shard_map/ppermute | solution.py:17
  217.0 3.9 %collective-permute-start.14 = (f32[4,4,16]{2,1,0:T(4,128)S(1)}, f32[4,4,16]{2,1,0:T(4,128)S(1)}, u32[]{:S(2)}, u32[]{:S(2)}) collective-permute-start(f32[4,4,16]{2,1,0:T(4,128)S(1)} %constant_dynamic-slice_fusion.1), channel_id=1, source_target_pairs={{0,1},{1,0},{2,3},{3,2},{4,5},{5,4},{6,7},{7,6},{8,9},{9,8},{10,11... | collective-permute-start | bytes 3080 | tf_op jit(solution)/shard_map/ppermute | solution.py:17
  217.1 3.8 %collective-permute-start.8 = (f32[4,4,16]{2,1,0:T(4,128)S(1)}, f32[4,4,16]{2,1,0:T(4,128)S(1)}, u32[]{:S(2)}, u32[]{:S(2)}) collective-permute-start(f32[4,4,16]{2,1,0:T(4,128)S(1)} %constant_dynamic-slice_fusion.7), channel_id=1, source_target_pairs={{0,1},{1,0},{2,3},{3,2},{4,5},{5,4},{6,7},{7,6},{8,9},{9,8},{10,11... | collective-permute-start | bytes 3080 | tf_op jit(solution)/shard_map/ppermute | solution.py:17
  220.8 1.4 collective-permute-start.9
  (2 other events, 2.0 us)
Sparse Core Ops, SparseCore 0:
  223.2 54.4 all-gather.2
where the time goes:
time: 292 us
  waiting for transfers between devices  136 us (47%)
  local copies, waits for them, and re-layouts  43.2 us (15%)
  starting transfers between devices  34 us (12%)
  matrix products  33.4 us (11%)
  other arithmetic  26.7 us (9%)
  between operations  13.6 us (5%)
  loops' own time  6.06 us (2%)
    ppermute x15, waiting for transfers between devices, partner(): return lax.ppermute(value, axis, pairs)  80.9 us
    all_gather x1, waiting for transfers between devices, body(): lax.all_gather(attended, 'ctx', axis=0, tiled=True)  54.6 us
    ppermute x15, starting transfers between devices, partner(): return lax.ppermute(value, axis, pairs)  34 us
    dot_general x7, matrix products, update(): jnp.einsum('rgqk,kgd->rgqd', weights.astype(jnp.bfloat16), value_part, pr...  15.1 us
    cond x35, local copies, waits for them, and re-layouts  14.2 us
    dot_general x7, matrix products, update(): jnp.einsum('rgqd,kgd->rgqk', grouped, key_part, preferred_element_type=jn...  13 us
    unnamed x13, local copies, waits for them, and re-layouts  12.1 us
    reduce_sum x7, other arithmetic, update(): new_sum = weight_sum * factor + jnp.sum(weights, axis=-1)  8.72 us
  transfers between devices with their start and end apart: 16, of which 9 were waited for; matrix products, arithmetic and copies ran while one was open for 2% of the time, Pallas kernels for 0%

commit v1 on v0

--- a/solution.py
+++ b/solution.py
@@ -1,17 +1,312 @@
+import functools
 import math
 
 import jax
 import jax.numpy as jnp
 from jax import lax
+from jax.experimental import pallas as pl
+from jax.experimental.pallas import tpu as pltpu
 from jax.sharding import PartitionSpec as P
 
 BLK = 128
-
-
+LANES = 128
+STAT = 16
 very_low = -1e30
-
-
-def partner(value, axis, distance):
+lowest_top = -(2.0**99)
+bf16 = jnp.bfloat16
+f32 = jnp.float32
+
+
+def pack_state(out, top, total):
+    high = total.astype(bf16).astype(f32)
+    low = total - high
+    row = lax.broadcasted_iota(jnp.int32, (STAT, LANES), 0)
+    stats = jnp.where(row == 0, top, jnp.where(row == 1, high, jnp.where(row == 2, low, 0.0)))
+    return out.astype(bf16), stats.astype(bf16)
+
+
+def attention_kernel(with_start, scale2, meta, mask_ref, counts_ref, q_ref, k_ref, v_ref, *rest):
+    if with_start:
+        starts, rest = rest[:4], rest[4:]
+    outs, (listed, kept_counts, kd, vt, spread, acc, top, total) = rest[:4], rest[4:]
+    group, my_xy = meta[0], meta[1]
+    rows = acc.shape[1]
+    d = acc.shape[0]
+    kv_count = spread.shape[0] // BLK
+    block_count = counts_ref.shape[0]
+    z_size = outs[0].shape[0]
+
+    def note(block, found):
+        listed[found] = block
+        kept_counts[found] = counts_ref[block]
+        return found + (mask_ref[0, block] > 0).astype(jnp.int32)
+
+    active = lax.fori_loop(0, block_count, note, jnp.int32(0))
+    kept_counts[active] = 0
+
+    def take(source, block):
+        start = pl.multiple_of(block * (BLK * kv_count), BLK * kv_count)
+        spread[...] = source[pl.ds(start, BLK * kv_count), :].astype(f32)
+        return spread[pl.ds(group, BLK, stride=kv_count), :]
+
+    def fetch(position, _):
+        block = listed[position]
+        offset = pl.multiple_of(position * BLK, BLK)
+        kd[pl.ds(offset, BLK), :] = take(k_ref, block).astype(bf16)
+        vt[:, pl.ds(offset, BLK)] = take(v_ref, block).T.astype(bf16)
+        return _
+
+    lax.fori_loop(0, active, fetch, 0)
+
+    @pl.when(active < block_count)
+    def _():
+        offset = pl.multiple_of(active * BLK, BLK)
+        vt[:, pl.ds(offset, BLK)] = jnp.zeros((d, BLK), bf16)
+
+    if with_start:
+        for j in range(4):
+            for z in range(z_size):
+                piece = ((my_xy ^ j) * z_size + z) * LANES
+                at = pl.ds(pl.multiple_of(piece, LANES), LANES)
+                stats = starts[j][z, d : d + STAT, :].astype(f32)
+                acc[:, at] = starts[j][z, 0:d, :].astype(f32)
+                top[:, at] = stats[0:1]
+                total[:, at] = stats[1:2] + stats[2:3]
+    else:
+        acc[...] = jnp.zeros_like(acc)
+        top[...] = jnp.full_like(top, lowest_top)
+        total[...] = jnp.zeros_like(total)
+
+    tile = min(512, rows)
+
+    def visit(step, _):
+        offset = pl.multiple_of(step * (2 * BLK), 2 * BLK)
+        keys = kd[pl.ds(offset, 2 * BLK), :]
+        values = vt[:, pl.ds(offset, 2 * BLK)]
+        place = lax.broadcasted_iota(jnp.int32, (2 * BLK, LANES), 0)
+        limit = jnp.where(place < BLK, kept_counts[2 * step], kept_counts[2 * step + 1] + BLK)
+        valid = jnp.concatenate([place < limit] * (tile // LANES), axis=1)
+        for part in range(rows // tile):
+            at = slice(part * tile, (part + 1) * tile)
+            q = q_ref[part * (tile // 16) : (part + 1) * (tile // 16)].reshape(tile, d)
+            scores = lax.dot_general(
+                keys, q, (((1,), (1,)), ((), ())), preferred_element_type=f32
+            )
+            scores = jnp.where(valid, scores, very_low)
+            old_top = top[:, at]
+            new_top = jnp.maximum(old_top, jnp.max(scores, axis=0, keepdims=True) * scale2)
+            weights = jnp.exp2(scores * scale2 - new_top)
+            factor = jnp.exp2(old_top - new_top)
+            total[:, at] = total[:, at] * factor + jnp.sum(weights, axis=0, keepdims=True)
+            acc[:, at] = acc[:, at] * factor + jnp.dot(
+                values, weights.astype(bf16), preferred_element_type=f32
+            )
+            top[:, at] = new_top
+        return _
+
+    lax.fori_loop(0, (active + 1) // 2, visit, 0)
+
+    for j in range(4):
+        for z in range(z_size):
+            piece = ((my_xy ^ j) * z_size + z) * LANES
+            at = pl.ds(pl.multiple_of(piece, LANES), LANES)
+            old_top = top[:, at]
+            sent_top = old_top.astype(bf16).astype(f32)
+            factor = jnp.exp2(old_top - sent_top)
+            out, stats = pack_state(acc[:, at] * factor, sent_top, total[:, at] * factor)
+            outs[j][z, 0:d, :] = out
+            outs[j][z, d : d + STAT, :] = stats
+
+
+def merged(parts, d):
+    stats = [part[d : d + STAT, :].astype(f32) for part in parts]
+    tops = [stat[0:1] for stat in stats]
+    top = functools.reduce(jnp.maximum, tops)
+    out, total = 0.0, 0.0
+    for part, stat, one in zip(parts, stats, tops):
+        factor = jnp.exp2(one - top)
+        out = out + part[0:d, :].astype(f32) * factor
+        total = total + (stat[1:2] + stat[2:3]) * factor
+    return out, top, total
+
+
+def plane_kernel(meta, *refs):
+    ins, outs = refs[:4], refs[4:]
+    my_z = meta[2]
+    d = outs[0].shape[0] - STAT
+    for k in range(len(outs)):
+        z = my_z ^ k
+        out, stats = pack_state(*merged([ref[z] for ref in ins], d))
+        outs[k][0:d, :] = out
+        outs[k][d : d + STAT, :] = stats
+
+
+def line_kernel(*refs):
+    ins, out_ref, turned = refs[:-2], refs[-2], refs[-1]
+    d = ins[0].shape[0] - STAT
+    out, _, total = merged([ref[...] for ref in ins], d)
+    turned[...] = (out / total).T
+    tokens = out_ref.shape[0]
+    heads = LANES // tokens
+    for h in range(heads):
+        out_ref[:, h * d : (h + 1) * d] = turned[pl.ds(h, tokens, stride=heads), :].astype(bf16)
+
+
+def project_kernel(last, meta, w_own, w_other, *refs):
+    own, other, refs = refs[:4], refs[4:8], refs[8:]
+    z_size, tokens, depth = own[0].shape
+    total = None
+    for parts, weight in ((own, w_own), (other, w_other)):
+        left = jnp.concatenate(
+            [part[...].reshape(z_size * tokens, depth) for part in parts], axis=0
+        )
+        product = jnp.dot(left, weight[...], preferred_element_type=f32)
+        total = product if total is None else total + product
+    if not last:
+        refs[0][...] = total
+        return
+    earlier, out_ref = refs
+    total = total + earlier[...]
+    my_xy, my_z = meta[1], meta[2]
+    for j in range(4):
+        for k in range(z_size):
+            row = (j * z_size + k) * tokens
+            to = ((my_xy ^ j) * z_size + (my_z ^ k)) * tokens
+            out_ref[pl.ds(pl.multiple_of(to, tokens), tokens), :] = total[row : row + tokens]
+
+
+def hop(value, mask):
+    pairs = [(source, source ^ mask) for source in range(lax.axis_size("ctx"))]
+    return lax.ppermute(value, "ctx", pairs)
+
+
+VMEM = pl.BlockSpec(memory_space=pltpu.VMEM)
+SMEM = pl.BlockSpec(memory_space=pltpu.SMEM)
+
+
+def fast_body(queries, cache_keys, cache_values, block_mask, key_counts, out_weight):
+    index = lax.axis_index("ctx")
+    z_size = lax.axis_size("ctx") // 8
+    token_count, head_count, d = queries.shape
+    kv_count = cache_keys.shape[1]
+    group_size = head_count // kv_count
+    rows = token_count * group_size
+    positions = cache_keys.shape[0]
+    features = out_weight.shape[1]
+    core = index & 1
+    my_xy = (index >> 1) & 3
+    my_z = index >> 3
+    tall = d + STAT
+    scale2 = math.log2(math.e) / math.sqrt(d)
+    keys = cache_keys.reshape(positions * kv_count, d)
+    values = cache_values.reshape(positions * kv_count, d)
+
+    def meta(group):
+        return jnp.stack([group, my_xy, my_z]).astype(jnp.int32)
+
+    def attend(group, starts):
+        ins = [
+            SMEM,
+            SMEM,
+            pl.BlockSpec((token_count, group_size, d), lambda i, m: (0, m[0], 0)),
+            VMEM,
+            VMEM,
+        ] + [VMEM] * len(starts)
+        blocks = positions // BLK
+        return pl.pallas_call(
+            functools.partial(attention_kernel, bool(starts), scale2),
+            grid_spec=pltpu.PrefetchScalarGridSpec(
+                num_scalar_prefetch=1,
+                grid=(1,),
+                in_specs=ins,
+                out_specs=[VMEM] * 4,
+                scratch_shapes=[
+                    pltpu.SMEM((blocks + 1,), jnp.int32),
+                    pltpu.SMEM((blocks + 1,), jnp.int32),
+                    pltpu.VMEM((positions, d), bf16),
+                    pltpu.VMEM((d, positions), bf16),
+                    pltpu.VMEM((BLK * kv_count, d), f32),
+                    pltpu.VMEM((d, rows), f32),
+                    pltpu.VMEM((1, rows), f32),
+                    pltpu.VMEM((1, rows), f32),
+                ],
+            ),
+            out_shape=[jax.ShapeDtypeStruct((z_size, tall, LANES), bf16)] * 4,
+            compiler_params=pltpu.CompilerParams(vmem_limit_bytes=32 << 20),
+            cost_estimate=pl.CostEstimate(
+                flops=4 * rows * positions * d,
+                transcendentals=rows * positions,
+                bytes_accessed=4 * positions * d * kv_count,
+            ),
+            name="attention",
+        )(meta(group), block_mask, key_counts, queries, keys, values, *starts)
+
+    def merge_plane(parts):
+        return pl.pallas_call(
+            plane_kernel,
+            in_specs=[SMEM] + [VMEM] * 4,
+            out_specs=[VMEM] * z_size,
+            out_shape=[jax.ShapeDtypeStruct((tall, LANES), bf16)] * z_size,
+            name="merge_plane",
+        )(meta(core), *parts)
+
+    def merge_line(parts):
+        tokens = LANES // group_size
+        return pl.pallas_call(
+            line_kernel,
+            in_specs=[VMEM] * len(parts),
+            out_specs=VMEM,
+            out_shape=jax.ShapeDtypeStruct((tokens, group_size * d), bf16),
+            scratch_shapes=[pltpu.VMEM((LANES, d), f32)],
+            name="merge_line",
+        )(*parts)
+
+    def project(chunk, own, other, earlier):
+        depth = group_size * d
+        whole = [pl.BlockSpec(a.shape, lambda i, m: (0, 0, 0)) for a in own + other]
+        more = [] if earlier is None else [earlier]
+        return pl.pallas_call(
+            functools.partial(project_kernel, earlier is not None),
+            grid_spec=pltpu.PrefetchScalarGridSpec(
+                num_scalar_prefetch=1,
+                grid=(1,),
+                in_specs=[
+                    pl.BlockSpec((depth, features), lambda i, m: (m[0], 0)),
+                    pl.BlockSpec((depth, features), lambda i, m: (m[0] ^ 1, 0)),
+                ]
+                + whole
+                + [VMEM] * len(more),
+                out_specs=VMEM,
+            ),
+            out_shape=jax.ShapeDtypeStruct((token_count, features), f32),
+            compiler_params=pltpu.CompilerParams(vmem_limit_bytes=32 << 20),
+            cost_estimate=pl.CostEstimate(
+                flops=4 * token_count * depth * features,
+                transcendentals=0,
+                bytes_accessed=4 * depth * features,
+            ),
+            name="project",
+        )(meta(2 * chunk + core), out_weight, out_weight, *own, *other, *more)
+
+    chunks = kv_count // 2
+    sent = [attend(2 * c + 1 - core, []) for c in range(chunks)]
+    partner = [[hop(part, 1) for part in one] for one in sent]
+    total = None
+    for c in range(chunks):
+        state = attend(2 * c + core, partner[c])
+        state = [state[0]] + [hop(state[j], 2 * j) for j in (1, 2, 3)]
+        state = merge_plane(state)
+        state = [state[0]] + [hop(state[k], 8 * k) for k in range(1, z_size)]
+        attended = merge_line(state)
+        line = [attended] + [hop(attended, 8 * k) for k in range(1, z_size)]
+        line = jnp.stack(line)
+        own = [line] + [hop(line, 2 * j) for j in (1, 2, 3)]
+        other = [hop(part, 1) for part in own]
+        total = project(c, own, other, total)
+    return total
+
+
+def partner_of(value, axis, distance):
     mask = 2**distance
     pairs = [(source, source ^ mask) for source in range(lax.axis_size(axis))]
     return lax.ppermute(value, axis, pairs)
@@ -76,7 +371,7 @@
     return lax.fori_loop(0, block_count, visit_block, initial)
 
 
-def body(queries, cache_keys, cache_values, block_mask, key_counts, out_weight):
+def general_body(queries, cache_keys, cache_values, block_mask, key_counts, out_weight):
     cycle_size = lax.axis_size("ctx")
     cycle_index = lax.axis_index("ctx")
     token_count, head_count, head_size = queries.shape
@@ -89,8 +384,7 @@
         return partial_rows(rows_q, row_mask, cache_keys, cache_values, key_counts)
 
     stacked = lax.map(per_block, (query_blocks, block_mask))
-    local_state = tuple((part.reshape((token_count,) + part.shape[2:]) for part in stacked))
-    run_state = local_state
+    run_state = tuple((part.reshape((token_count,) + part.shape[2:]) for part in stacked))
     bit_total = cycle_size.bit_length() - 1
     for bit_number in range(bit_total - 1, -1, -1):
         half_rows = run_state[1].shape[0] // 2
@@ -107,7 +401,7 @@
                 for part in run_state
             )
         )
-        received = partner((outgoing[0], outgoing[1], outgoing[2]), "ctx", bit_number)
+        received = partner_of((outgoing[0], outgoing[1], outgoing[2]), "ctx", bit_number)
         run_state = combine(kept, received)
     out_sum, top_score, weight_sum = run_state
     attended = (
@@ -120,8 +414,26 @@
         out_weight,
         preferred_element_type=jnp.float32,
     )
-    summed = lax.psum_scatter(partial_value, "kv", scatter_dimension=0, tiled=True)
-    return summed
+    return lax.psum_scatter(partial_value, "kv", scatter_dimension=0, tiled=True)
+
+
+def body(queries, cache_keys, cache_values, block_mask, key_counts, out_weight):
+    devices = lax.axis_size("ctx")
+    token_count, head_count, d = queries.shape
+    kv_count = cache_keys.shape[1]
+    group_size = head_count // kv_count
+    suits = (
+        lax.axis_size("kv") == 1
+        and devices == 32
+        and token_count == BLK
+        and block_mask.shape[0] == 1
+        and kv_count % 2 == 0
+        and d == LANES
+        and group_size == 16
+        and token_count * group_size == LANES * (devices // 2)
+    )
+    run = fast_body if suits else general_body
+    return run(queries, cache_keys, cache_values, block_mask, key_counts, out_weight)
 
 
 def solution(mesh):

time: 292 us -> 108 us (0.37)
  waiting for transfers between devices: 136 us -> 4.24 us
  matrix products: 33.4 us -> 0 us
  Pallas kernels: 0 us -> 26.4 us
  other arithmetic: 26.7 us -> 1.78 us
  local copies, waits for them, and re-layouts: 43.2 us -> 22.5 us
  starting transfers between devices: 34 us -> 52.5 us
  between operations: 13.6 us -> 0.24 us
  loops' own time: 6.06 us -> 0 us
    ppermute x15 -> x40, waiting for transfers between devices: 80.9 us -> 4.24 us  [hop(): return lax.ppermute(value, 'ctx', pairs)]
    all_gather x1 -> x0, waiting for transfers between devices: 54.6 us -> none  [body(): lax.all_gather(attended, 'ctx', axis=0, tiled=True)]
    dot_general x15 -> x0, matrix products: 33.4 us -> none  [the longest x7 15.1 us: update(): jnp.einsum('rgqk,kgd->rgqd', weights.astype(jnp.bfloat16), value_part, pr...]
    pallas_call x0 -> x10, Pallas kernels: none -> 26.4 us  [the longest x4 16.3 us: attend(): pl.pallas_call(functools.partial(attention_kernel, bool(starts), scale2),...]
    ppermute x15 -> x40, starting transfers between devices: 34 us -> 52.5 us  [hop(): return lax.ppermute(value, 'ctx', pairs)]
    cond x35 -> x0, local copies, waits for them, and re-layouts: 14.2 us -> none
    unnamed x13 -> x70, local copies, waits for them, and re-layouts: 12.1 us -> 22.5 us
    reduce_sum x7 -> x0, other arithmetic: 8.72 us -> none  [update(): new_sum = weight_sum * factor + jnp.sum(weights, axis=-1)]
  transfers between devices with their start and end apart: 16 -> 40, of which waited for: 9 -> 3; matrix products, arithmetic and copies ran while one was open for 2% -> 2% of each run, Pallas kernels for 0% -> 19%
where the time goes in v1:
time: 108 us
  starting transfers between devices  52.5 us (49%)
  Pallas kernels  26.4 us (24%)
  local copies, waits for them, and re-layouts  22.5 us (21%)
  waiting for transfers between devices  4.24 us (4%)
  other arithmetic  1.78 us (2%)
    ppermute x40, starting transfers between devices, hop(): return lax.ppermute(value, 'ctx', pairs)  52.5 us
    unnamed x70, local copies, waits for them, and re-layouts  22.5 us
    pallas_call x4, Pallas kernels, attend(): pl.pallas_call(functools.partial(attention_kernel, bool(starts), scale2),...  16.3 us
    ppermute x40, waiting for transfers between devices, hop(): return lax.ppermute(value, 'ctx', pairs)  4.24 us
    pallas_call x2, Pallas kernels, merge_plane(): pl.pallas_call(plane_kernel, in_specs=[SMEM] + [VMEM] * 4, out_specs=[VME...  3.84 us
    pallas_call x2, Pallas kernels, project(): pl.pallas_call(functools.partial(project_kernel, earlier is not None), gr...  3.23 us
    pallas_call x2, Pallas kernels, merge_line(): pl.pallas_call(line_kernel, in_specs=[VMEM] * len(parts), out_specs=VMEM,...  3.13 us
  transfers between devices with their start and end apart: 40, of which 3 were waited for; matrix products, arithmetic and copies ran while one was open for 2% of the time, Pallas kernels for 19%

profile of v1, /device:TPU:0, one launch (start us, length us, event | category | flops | bytes accessed | tf_op | source)
XLA Modules:
  0.0 107.7 jit_solution(1260616251759949832)
XLA Ops:
  0.1 1.6 %copy-done.1 = bf16[128,64,128]{2,1,0:T(8,128)(2,1)S(1)} copy-done((bf16[128,64,128]{2,1,0:T(8,128)(2,1)S(1)}, bf16[128,64,128]{2,1,0:T(8,128)(2,1)}, u32[]{:S(2)}) %copy-start.1) | copy-done | bytes 2097176
  5.4 4.2 %attention.6 = (bf16[4,144,128]{2,1,0:T(8,128)(2,1)}, bf16[4,144,128]{2,1,0:T(8,128)(2,1)}, bf16[4,144,128]{2,1,0:T(8,128)(2,1)}, bf16[4,144,128]{2,1,0:T(8,128)(2,1)}) custom-call(s32[3]{0:T(128)S(1)} %get-tuple-element.54.meta, s32[1,8]{1,0:T(1,128)S(1)} %copy-done.14, s32[8]{0:T(128)S(1)} %copy-done.17, bf16[128,64,128]{2,1,0:T(8,128)(2,1)S(1)} %copy-done.1, ...), custom_call_target="tpu_custom_call" | custom-call | flops 1073741824 | bytes 2097152 | tf_op jit(solution)/shard_map/attention/pallas_call | solution.py:216
  10.6 1.6 %copy-done.2 = bf16[128,64,128]{2,1,0:T(8,128)(2,1)S(1)} copy-done((bf16[128,64,128]{2,1,0:T(8,128)(2,1)S(1)}, bf16[128,64,128]{2,1,0:T(8,128)(2,1)}, u32[]{:S(2)}) %copy-start.2) | copy-done | bytes 2097176
  12.2 1.2 %copy-done.5 = bf16[1024,4,128]{2,1,0:T(4,128)(2,1)S(1)} copy-done((bf16[1024,4,128]{2,1,0:T(4,128)(2,1)S(1)}, bf16[1024,4,128]{2,1,0:T(4,128)(2,1)}, u32[]{:S(2)}) %copy-start.5) | copy-done | bytes 1048600
  16.0 3.9 %attention.4 = (bf16[4,144,128]{2,1,0:T(8,128)(2,1)}, bf16[4,144,128]{2,1,0:T(8,128)(2,1)S(1)}, bf16[4,144,128]{2,1,0:T(8,128)(2,1)S(1)}, bf16[4,144,128]{2,1,0:T(8,128)(2,1)S(1)}) custom-call(s32[3]{0:T(128)S(1)} %get-tuple-element.53.meta, s32[1,8]{1,0:T(1,128)S(1)} %copy-done.15, s32[8]{0:T(128)S(1)} %copy-done.18, bf16[128,64,128]{2,1,0:T(8,128)(2,1)S(1)} %copy-done.2, ...), custom_call_target="tpu_custom_call" | custom-call | flops 1073741824 | bytes 2097152 | tf_op jit(solution)/shard_map/attention/pallas_call | solution.py:216
  24.3 3.9 %attention.7 = (bf16[4,144,128]{2,1,0:T(8,128)(2,1)S(1)}, bf16[4,144,128]{2,1,0:T(8,128)(2,1)S(1)}, bf16[4,144,128]{2,1,0:T(8,128)(2,1)S(1)}, bf16[4,144,128]{2,1,0:T(8,128)(2,1)S(1)}) custom-call(s32[3]{0:T(128)S(1)} %add_add_fusion.1.meta, s32[1,8]{1,0:T(1,128)S(1)} %copy-done.16, s32[8]{0:T(128)S(1)} %copy-done.19, bf16[128,64,128]{2,1,0:T(8,128)(2,1)S(1)} %copy-done.3, ...), custom_call_target="tpu_custom_call" | custom-call | flops 1073741824 | bytes 2097152 | tf_op jit(solution)/shard_map/attention/pallas_call | solution.py:216
  28.9 5.9 %collective-permute-start.24 = (bf16[4,144,128]{2,1,0:T(8,128)(2,1)S(1)}, bf16[4,144,128]{2,1,0:T(8,128)(2,1)S(1)}, u32[]{:S(2)}, u32[]{:S(2)}) collective-permute-start(bf16[4,144,128]{2,1,0:T(8,128)(2,1)S(1)} %get-tuple-element.46), channel_id=1, source_target_pairs={{0,2},{1,3},{2,0},{3,1},{4,6},{5,7},{6,4},{7,5},{8,10},{9,11},{10,... | collective-permute-start | bytes 442376 | tf_op jit(solution)/shard_map/ppermute | solution.py:180
  34.8 3.0 %collective-permute-start.25 = (bf16[4,144,128]{2,1,0:T(8,128)(2,1)S(1)}, bf16[4,144,128]{2,1,0:T(8,128)(2,1)S(1)}, u32[]{:S(2)}, u32[]{:S(2)}) collective-permute-start(bf16[4,144,128]{2,1,0:T(8,128)(2,1)S(1)} %get-tuple-element.47), channel_id=1, source_target_pairs={{0,4},{1,5},{2,6},{3,7},{4,0},{5,1},{6,2},{7,3},{8,12},{9,13},{10,... | collective-permute-start | bytes 442376 | tf_op jit(solution)/shard_map/ppermute | solution.py:180
  37.9 1.5 %collective-permute-start.26 = (bf16[4,144,128]{2,1,0:T(8,128)(2,1)S(1)}, bf16[4,144,128]{2,1,0:T(8,128)(2,1)S(1)}, u32[]{:S(2)}, u32[]{:S(2)}) collective-permute-start(bf16[4,144,128]{2,1,0:T(8,128)(2,1)S(1)} %get-tuple-element.48), channel_id=1, source_target_pairs={{0,6},{1,7},{2,4},{3,5},{4,2},{5,3},{6,0},{7,1},{8,14},{9,15},{10,... | collective-permute-start | bytes 442376 | tf_op jit(solution)/shard_map/ppermute | solution.py:180
  39.4 4.2 %attention.5 = (bf16[4,144,128]{2,1,0:T(8,128)(2,1)S(1)}, bf16[4,144,128]{2,1,0:T(8,128)(2,1)}, bf16[4,144,128]{2,1,0:T(8,128)(2,1)}, bf16[4,144,128]{2,1,0:T(8,128)(2,1)S(1)}) custom-call(s32[3]{0:T(128)S(1)} %add_add_fusion.meta, s32[1,8]{1,0:T(1,128)S(1)} %copy-done.16, s32[8]{0:T(128)S(1)} %copy-done.19, bf16[128,64,128]{2,1,0:T(8,128)(2,1)S(1)} %copy-done.3, ...), custom_call_target="tpu_custom_call" | custom-call | flops 1073741824 | bytes 2097152 | tf_op jit(solution)/shard_map/attention/pallas_call | solution.py:216
  44.6 3.6 %collective-permute-start.5 = (bf16[4,144,128]{2,1,0:T(8,128)(2,1)}, bf16[4,144,128]{2,1,0:T(8,128)(2,1)S(1)}, u32[]{:S(2)}, u32[]{:S(2)}) collective-permute-start(bf16[4,144,128]{2,1,0:T(8,128)(2,1)} %get-tuple-element.35), channel_id=1, source_target_pairs={{0,4},{1,5},{2,6},{3,7},{4,0},{5,1},{6,2},{7,3},{8,12},{9,13},{10,... | collective-permute-start | bytes 442376 | tf_op jit(solution)/shard_map/ppermute | solution.py:180
  48.2 1.5 %collective-permute-start.6 = (bf16[4,144,128]{2,1,0:T(8,128)(2,1)S(1)}, bf16[4,144,128]{2,1,0:T(8,128)(2,1)S(1)}, u32[]{:S(2)}, u32[]{:S(2)}) collective-permute-start(bf16[4,144,128]{2,1,0:T(8,128)(2,1)S(1)} %get-tuple-element.36), channel_id=1, source_target_pairs={{0,6},{1,7},{2,4},{3,5},{4,2},{5,3},{6,0},{7,1},{8,14},{9,15},{10,... | collective-permute-start | bytes 442376 | tf_op jit(solution)/shard_map/ppermute | solution.py:180
  51.1 1.9 %merge_plane.3 = (bf16[144,128]{1,0:T(8,128)(2,1)}, bf16[144,128]{1,0:T(8,128)(2,1)}, bf16[144,128]{1,0:T(8,128)(2,1)}, bf16[144,128]{1,0:T(8,128)(2,1)}) custom-call(s32[3]{0:T(128)} %copy-done.12, bf16[4,144,128]{2,1,0:T(8,128)(2,1)} %copy-done.10, bf16[4,144,128]{2,1,0:T(8,128)(2,1)} %copy-done.23, bf16[4,144,128]{2,1,0:T(8,128)(2,1)} %copy-done.26, ...), custom_call_target="tpu_custom_call" | custom-call | tf_op jit(solution)/shard_map/merge_plane/pallas_call | solution.py:245
  53.0 8.9 %collective-permute-start.27 = (bf16[144,128]{1,0:T(8,128)(2,1)}, bf16[144,128]{1,0:T(8,128)(2,1)S(1)}, u32[]{:S(2)}, u32[]{:S(2)}) collective-permute-start(bf16[144,128]{1,0:T(8,128)(2,1)} %get-tuple-element.50), channel_id=1, source_target_pairs={{0,8},{1,9},{2,10},{3,11},{4,12},{5,13},{6,14},{7,15},{8,0},{9,1},... | collective-permute-start | bytes 110600 | tf_op jit(solution)/shard_map/ppermute | solution.py:180
  61.9 2.4 %collective-permute-start.29 = (bf16[144,128]{1,0:T(8,128)(2,1)}, bf16[144,128]{1,0:T(8,128)(2,1)S(1)}, u32[]{:S(2)}, u32[]{:S(2)}) collective-permute-start(bf16[144,128]{1,0:T(8,128)(2,1)} %get-tuple-element.52), channel_id=1, source_target_pairs={{0,24},{1,25},{2,26},{3,27},{4,28},{5,29},{6,30},{7,31},{8,16},{9,... | collective-permute-start | bytes 110600 | tf_op jit(solution)/shard_map/ppermute | solution.py:180
  65.0 1.9 %merge_plane.2 = (bf16[144,128]{1,0:T(8,128)(2,1)}, bf16[144,128]{1,0:T(8,128)(2,1)}, bf16[144,128]{1,0:T(8,128)(2,1)}, bf16[144,128]{1,0:T(8,128)(2,1)}) custom-call(s32[3]{0:T(128)} %copy-done.12, bf16[4,144,128]{2,1,0:T(8,128)(2,1)} %copy-done.11, bf16[4,144,128]{2,1,0:T(8,128)(2,1)} %copy-done.24, bf16[4,144,128]{2,1,0:T(8,128)(2,1)} %copy-done.25, ...), custom_call_target="tpu_custom_call" | custom-call | tf_op jit(solution)/shard_map/merge_plane/pallas_call | solution.py:245
  69.0 2.3 %collective-permute-start.9 = (bf16[144,128]{1,0:T(8,128)(2,1)}, bf16[144,128]{1,0:T(8,128)(2,1)S(1)}, u32[]{:S(2)}, u32[]{:S(2)}) collective-permute-start(bf16[144,128]{1,0:T(8,128)(2,1)} %get-tuple-element.40), channel_id=1, source_target_pairs={{0,24},{1,25},{2,26},{3,27},{4,28},{5,29},{6,30},{7,31},{8,16},{9,... | collective-permute-start | bytes 110600 | tf_op jit(solution)/shard_map/ppermute | solution.py:180
  72.0 1.6 %merge_line.3 = bf16[8,2048]{1,0:T(8,128)(2,1)} custom-call(bf16[144,128]{1,0:T(8,128)(2,1)} %get-tuple-element.49.refs_0_, bf16[144,128]{1,0:T(8,128)(2,1)} %copy-done.29, bf16[144,128]{1,0:T(8,128)(2,1)} %copy-done.30, bf16[144,128]{1,0:T(8,128)(2,1)} %copy-done.33), custom_call_target="tpu_custom_call" | custom-call | tf_op jit(solution)/shard_map/merge_line/pallas_call | solution.py:255
  73.8 1.9 %collective-permute-start.31 = (bf16[8,2048]{1,0:T(8,128)(2,1)}, bf16[8,2048]{1,0:T(8,128)(2,1)S(1)}, u32[]{:S(2)}, u32[]{:S(2)}) collective-permute-start(bf16[8,2048]{1,0:T(8,128)(2,1)} %merge_line.3), channel_id=1, source_target_pairs={{0,16},{1,17},{2,18},{3,19},{4,20},{5,21},{6,22},{7,23},{8,24},{9,... | collective-permute-start | bytes 98312 | tf_op jit(solution)/shard_map/ppermute | solution.py:180
  75.6 2.3 %collective-permute-start.32 = (bf16[8,2048]{1,0:T(8,128)(2,1)}, bf16[8,2048]{1,0:T(8,128)(2,1)S(1)}, u32[]{:S(2)}, u32[]{:S(2)}) collective-permute-start(bf16[8,2048]{1,0:T(8,128)(2,1)} %merge_line.3), channel_id=1, source_target_pairs={{0,24},{1,25},{2,26},{3,27},{4,28},{5,29},{6,30},{7,31},{8,16},{9,... | collective-permute-start | bytes 98312 | tf_op jit(solution)/shard_map/ppermute | solution.py:180
  78.6 1.6 %merge_line.2 = bf16[8,2048]{1,0:T(8,128)(2,1)} custom-call(bf16[144,128]{1,0:T(8,128)(2,1)} %get-tuple-element.37.refs_0_, bf16[144,128]{1,0:T(8,128)(2,1)} %copy-done.31, bf16[144,128]{1,0:T(8,128)(2,1)} %copy-done.32, bf16[144,128]{1,0:T(8,128)(2,1)} %copy-done.34), custom_call_target="tpu_custom_call" | custom-call | tf_op jit(solution)/shard_map/merge_line/pallas_call | solution.py:255
  80.1 1.5 %collective-permute-start.12 = (bf16[8,2048]{1,0:T(8,128)(2,1)}, bf16[8,2048]{1,0:T(8,128)(2,1)S(1)}, u32[]{:S(2)}, u32[]{:S(2)}) collective-permute-start(bf16[8,2048]{1,0:T(8,128)(2,1)} %merge_line.2), channel_id=1, source_target_pairs={{0,24},{1,25},{2,26},{3,27},{4,28},{5,29},{6,30},{7,31},{8,16},{9,... | collective-permute-start | bytes 98312 | tf_op jit(solution)/shard_map/ppermute | solution.py:180
  81.7 2.9 %collective-permute-start.11 = (bf16[8,2048]{1,0:T(8,128)(2,1)}, bf16[8,2048]{1,0:T(8,128)(2,1)S(1)}, u32[]{:S(2)}, u32[]{:S(2)}) collective-permute-start(bf16[8,2048]{1,0:T(8,128)(2,1)} %merge_line.2), channel_id=1, source_target_pairs={{0,16},{1,17},{2,18},{3,19},{4,20},{5,21},{6,22},{7,23},{8,24},{9,... | collective-permute-start | bytes 98312 | tf_op jit(solution)/shard_map/ppermute | solution.py:180
  85.9 1.5 %collective-permute-start.34 = (bf16[4,8,2048]{2,1,0:T(8,128)(2,1)S(1)}, bf16[4,8,2048]{2,1,0:T(8,128)(2,1)S(1)}, u32[]{:S(2)}, u32[]{:S(2)}) collective-permute-start(bf16[4,8,2048]{2,1,0:T(8,128)(2,1)S(1)} %pad_maximum_fusion.1.refs_0_), channel_id=1, source_target_pairs={{0,4},{1,5},{2,6},{3,7},{4,0},{5,1},{6,2},{7,3},{8,12},{9,13},{10,... | collective-permute-start | bytes 393224 | tf_op jit(solution)/shard_map/ppermute | solution.py:180
  87.4 1.5 %collective-permute-start.35 = (bf16[4,8,2048]{2,1,0:T(8,128)(2,1)S(1)}, bf16[4,8,2048]{2,1,0:T(8,128)(2,1)S(1)}, u32[]{:S(2)}, u32[]{:S(2)}) collective-permute-start(bf16[4,8,2048]{2,1,0:T(8,128)(2,1)S(1)} %pad_maximum_fusion.1.refs_0_), channel_id=1, source_target_pairs={{0,6},{1,7},{2,4},{3,5},{4,2},{5,3},{6,0},{7,1},{8,14},{9,15},{10,... | collective-permute-start | bytes 393224 | tf_op jit(solution)/shard_map/ppermute | solution.py:180
  90.4 1.9 %collective-permute-start.14 = (bf16[4,8,2048]{2,1,0:T(8,128)(2,1)S(1)}, bf16[4,8,2048]{2,1,0:T(8,128)(2,1)S(1)}, u32[]{:S(2)}, u32[]{:S(2)}) collective-permute-start(bf16[4,8,2048]{2,1,0:T(8,128)(2,1)S(1)} %pad_maximum_fusion.refs_0_), channel_id=1, source_target_pairs={{0,4},{1,5},{2,6},{3,7},{4,0},{5,1},{6,2},{7,3},{8,12},{9,13},{10,... | collective-permute-start | bytes 393224 | tf_op jit(solution)/shard_map/ppermute | solution.py:180
  92.3 2.9 %collective-permute-start.15 = (bf16[4,8,2048]{2,1,0:T(8,128)(2,1)S(1)}, bf16[4,8,2048]{2,1,0:T(8,128)(2,1)S(1)}, u32[]{:S(2)}, u32[]{:S(2)}) collective-permute-start(bf16[4,8,2048]{2,1,0:T(8,128)(2,1)S(1)} %pad_maximum_fusion.refs_0_), channel_id=1, source_target_pairs={{0,6},{1,7},{2,4},{3,5},{4,2},{5,3},{6,0},{7,1},{8,14},{9,15},{10,... | collective-permute-start | bytes 393224 | tf_op jit(solution)/shard_map/ppermute | solution.py:180
  96.0 2.0 %collective-permute-done.14.refs_2_ = bf16[4,8,2048]{2,1,0:T(8,128)(2,1)S(1)} collective-permute-done((bf16[4,8,2048]{2,1,0:T(8,128)(2,1)S(1)}, bf16[4,8,2048]{2,1,0:T(8,128)(2,1)S(1)}, u32[]{:S(2)}, u32[]{:S(2)}) %collective-permute-start.14) | collective-permute-done | bytes 131104 | tf_op jit(solution)/shard_map/ppermute | solution.py:180
  98.0 1.8 %collective-permute-done.15.refs_3_ = bf16[4,8,2048]{2,1,0:T(8,128)(2,1)S(1)} collective-permute-done((bf16[4,8,2048]{2,1,0:T(8,128)(2,1)S(1)}, bf16[4,8,2048]{2,1,0:T(8,128)(2,1)S(1)}, u32[]{:S(2)}, u32[]{:S(2)}) %collective-permute-start.15) | collective-permute-done | bytes 131104 | tf_op jit(solution)/shard_map/ppermute | solution.py:180
  100.4 3.4 %copy-done = bf16[8192,512]{1,0:T(8,128)(2,1)S(1)} copy-done((bf16[8192,512]{1,0:T(8,128)(2,1)S(1)}, bf16[8192,512]{1,0:T(8,128)(2,1)}, u32[]{:S(2)}) %copy-start) | copy-done | bytes 8388632
  104.4 1.3 %project.2.refs_8_ = f32[128,512]{1,0:T(8,128)S(1)} custom-call(s32[3]{0:T(128)S(1)} %copy-done.13, bf16[8192,512]{1,0:T(8,128)(2,1)S(1)} %copy-done, bf16[8192,512]{1,0:T(8,128)(2,1)S(1)} %copy-done, bf16[4,8,2048]{2,1,0:T(8,128)(2,1)S(1)} %pad_maximum_fusion.1.refs_0_, bf16[4,8,2048]{2,1,0:T(8,128)(2,1)S(1)} %collective-permute-done.33.refs_1_, ...), custom_call_target="tpu_custom_call" | custom-call | flops 536870912 | bytes 4194304 | tf_op jit(solution)/shard_map/project/pallas_call | solution.py:268
  105.8 2.0 %project.3 = f32[128,512]{1,0:T(8,128)} custom-call(s32[3]{0:T(128)S(1)} %add_add_fusion.meta, bf16[8192,512]{1,0:T(8,128)(2,1)S(1)} %copy-done, bf16[8192,512]{1,0:T(8,128)(2,1)S(1)} %copy-done, bf16[4,8,2048]{2,1,0:T(8,128)(2,1)S(1)} %pad_maximum_fusion.refs_0_, bf16[4,8,2048]{2,1,0:T(8,128)(2,1)S(1)} %collective-permute-done.13.refs_1_, ...), custom_call_target="tpu_custom_call" | custom-call | flops 536870912 | bytes 4194304 | tf_op jit(solution)/shard_map/project/pallas_call | solution.py:268
  (133 shorter events, 24.1 us)
Async XLA Ops:
  9.6 12.5 %collective-permute-start.20 = (bf16[4,144,128]{2,1,0:T(8,128)(2,1)}, bf16[4,144,128]{2,1,0:T(8,128)(2,1)S(1)}, u32[]{:S(2)}, u32[]{:S(2)}) collective-permute-start(bf16[4,144,128]{2,1,0:T(8,128)(2,1)} %get-tuple-element.41), channel_id=1, source_target_pairs={{0,1},{1,0},{2,3},{3,2},{4,5},{5,4},{6,7},{7,6},{8,9},{9,8},{10,11... | collective-permute-start | bytes 442376 | tf_op jit(solution)/shard_map/ppermute | solution.py:180
  9.9 12.6 %collective-permute-start.21 = (bf16[4,144,128]{2,1,0:T(8,128)(2,1)}, bf16[4,144,128]{2,1,0:T(8,128)(2,1)}, u32[]{:S(2)}, u32[]{:S(2)}) collective-permute-start(bf16[4,144,128]{2,1,0:T(8,128)(2,1)} %get-tuple-element.42), channel_id=1, source_target_pairs={{0,1},{1,0},{2,3},{3,2},{4,5},{5,4},{6,7},{7,6},{8,9},{9,8},{10,11... | collective-permute-start | bytes 442376 | tf_op jit(solution)/shard_map/ppermute | solution.py:180
  10.1 12.6 %collective-permute-start.22 = (bf16[4,144,128]{2,1,0:T(8,128)(2,1)}, bf16[4,144,128]{2,1,0:T(8,128)(2,1)}, u32[]{:S(2)}, u32[]{:S(2)}) collective-permute-start(bf16[4,144,128]{2,1,0:T(8,128)(2,1)} %get-tuple-element.43), channel_id=1, source_target_pairs={{0,1},{1,0},{2,3},{3,2},{4,5},{5,4},{6,7},{7,6},{8,9},{9,8},{10,11... | collective-permute-start | bytes 442376 | tf_op jit(solution)/shard_map/ppermute | solution.py:180
  10.4 12.6 %collective-permute-start.23 = (bf16[4,144,128]{2,1,0:T(8,128)(2,1)}, bf16[4,144,128]{2,1,0:T(8,128)(2,1)}, u32[]{:S(2)}, u32[]{:S(2)}) collective-permute-start(bf16[4,144,128]{2,1,0:T(8,128)(2,1)} %get-tuple-element.44), channel_id=1, source_target_pairs={{0,1},{1,0},{2,3},{3,2},{4,5},{5,4},{6,7},{7,6},{8,9},{9,8},{10,11... | collective-permute-start | bytes 442376 | tf_op jit(solution)/shard_map/ppermute | solution.py:180
  21.9 13.0 %collective-permute-start = (bf16[4,144,128]{2,1,0:T(8,128)(2,1)}, bf16[4,144,128]{2,1,0:T(8,128)(2,1)S(1)}, u32[]{:S(2)}, u32[]{:S(2)}) collective-permute-start(bf16[4,144,128]{2,1,0:T(8,128)(2,1)} %get-tuple-element.29), channel_id=1, source_target_pairs={{0,1},{1,0},{2,3},{3,2},{4,5},{5,4},{6,7},{7,6},{8,9},{9,8},{10,11... | collective-permute-start | bytes 442376 | tf_op jit(solution)/shard_map/ppermute | solution.py:180
  22.1 15.7 %collective-permute-start.1 = (bf16[4,144,128]{2,1,0:T(8,128)(2,1)}, bf16[4,144,128]{2,1,0:T(8,128)(2,1)S(1)}, u32[]{:S(2)}, u32[]{:S(2)}) collective-permute-start(bf16[4,144,128]{2,1,0:T(8,128)(2,1)} %copy-done.22), channel_id=1, source_target_pairs={{0,1},{1,0},{2,3},{3,2},{4,5},{5,4},{6,7},{7,6},{8,9},{9,8},{10,11... | collective-permute-start | bytes 442376 | tf_op jit(solution)/shard_map/ppermute | solution.py:180
  22.5 16.9 %collective-permute-start.2 = (bf16[4,144,128]{2,1,0:T(8,128)(2,1)}, bf16[4,144,128]{2,1,0:T(8,128)(2,1)S(1)}, u32[]{:S(2)}, u32[]{:S(2)}) collective-permute-start(bf16[4,144,128]{2,1,0:T(8,128)(2,1)} %copy-done.21), channel_id=1, source_target_pairs={{0,1},{1,0},{2,3},{3,2},{4,5},{5,4},{6,7},{7,6},{8,9},{9,8},{10,11... | collective-permute-start | bytes 442376 | tf_op jit(solution)/shard_map/ppermute | solution.py:180
  22.7 16.8 %collective-permute-start.3 = (bf16[4,144,128]{2,1,0:T(8,128)(2,1)}, bf16[4,144,128]{2,1,0:T(8,128)(2,1)S(1)}, u32[]{:S(2)}, u32[]{:S(2)}) collective-permute-start(bf16[4,144,128]{2,1,0:T(8,128)(2,1)} %copy-done.20), channel_id=1, source_target_pairs={{0,1},{1,0},{2,3},{3,2},{4,5},{5,4},{6,7},{7,6},{8,9},{9,8},{10,11... | collective-permute-start | bytes 442376 | tf_op jit(solution)/shard_map/ppermute | solution.py:180
  28.9 19.3 %collective-permute-start.24 = (bf16[4,144,128]{2,1,0:T(8,128)(2,1)S(1)}, bf16[4,144,128]{2,1,0:T(8,128)(2,1)S(1)}, u32[]{:S(2)}, u32[]{:S(2)}) collective-permute-start(bf16[4,144,128]{2,1,0:T(8,128)(2,1)S(1)} %get-tuple-element.46), channel_id=1, source_target_pairs={{0,2},{1,3},{2,0},{3,1},{4,6},{5,7},{6,4},{7,5},{8,10},{9,11},{10,... | collective-permute-start | bytes 442376 | tf_op jit(solution)/shard_map/ppermute | solution.py:180
  34.8 14.9 %collective-permute-start.25 = (bf16[4,144,128]{2,1,0:T(8,128)(2,1)S(1)}, bf16[4,144,128]{2,1,0:T(8,128)(2,1)S(1)}, u32[]{:S(2)}, u32[]{:S(2)}) collective-permute-start(bf16[4,144,128]{2,1,0:T(8,128)(2,1)S(1)} %get-tuple-element.47), channel_id=1, source_target_pairs={{0,4},{1,5},{2,6},{3,7},{4,0},{5,1},{6,2},{7,3},{8,12},{9,13},{10,... | collective-permute-start | bytes 442376 | tf_op jit(solution)/shard_map/ppermute | solution.py:180
  37.9 11.9 %collective-permute-start.26 = (bf16[4,144,128]{2,1,0:T(8,128)(2,1)S(1)}, bf16[4,144,128]{2,1,0:T(8,128)(2,1)S(1)}, u32[]{:S(2)}, u32[]{:S(2)}) collective-permute-start(bf16[4,144,128]{2,1,0:T(8,128)(2,1)S(1)} %get-tuple-element.48), channel_id=1, source_target_pairs={{0,6},{1,7},{2,4},{3,5},{4,2},{5,3},{6,0},{7,1},{8,14},{9,15},{10,... | collective-permute-start | bytes 442376 | tf_op jit(solution)/shard_map/ppermute | solution.py:180
  44.3 17.6 %collective-permute-start.4 = (bf16[4,144,128]{2,1,0:T(8,128)(2,1)}, bf16[4,144,128]{2,1,0:T(8,128)(2,1)S(1)}, u32[]{:S(2)}, u32[]{:S(2)}) collective-permute-start(bf16[4,144,128]{2,1,0:T(8,128)(2,1)} %get-tuple-element.34), channel_id=1, source_target_pairs={{0,2},{1,3},{2,0},{3,1},{4,6},{5,7},{6,4},{7,5},{8,10},{9,11},{10,... | collective-permute-start | bytes 442376 | tf_op jit(solution)/shard_map/ppermute | solution.py:180
  44.6 19.7 %collective-permute-start.5 = (bf16[4,144,128]{2,1,0:T(8,128)(2,1)}, bf16[4,144,128]{2,1,0:T(8,128)(2,1)S(1)}, u32[]{:S(2)}, u32[]{:S(2)}) collective-permute-start(bf16[4,144,128]{2,1,0:T(8,128)(2,1)} %get-tuple-element.35), channel_id=1, source_target_pairs={{0,4},{1,5},{2,6},{3,7},{4,0},{5,1},{6,2},{7,3},{8,12},{9,13},{10,... | collective-permute-start | bytes 442376 | tf_op jit(solution)/shard_map/ppermute | solution.py:180
  48.2 16.1 %collective-permute-start.6 = (bf16[4,144,128]{2,1,0:T(8,128)(2,1)S(1)}, bf16[4,144,128]{2,1,0:T(8,128)(2,1)S(1)}, u32[]{:S(2)}, u32[]{:S(2)}) collective-permute-start(bf16[4,144,128]{2,1,0:T(8,128)(2,1)S(1)} %get-tuple-element.36), channel_id=1, source_target_pairs={{0,6},{1,7},{2,4},{3,5},{4,2},{5,3},{6,0},{7,1},{8,14},{9,15},{10,... | collective-permute-start | bytes 442376 | tf_op jit(solution)/shard_map/ppermute | solution.py:180
  53.0 16.0 %collective-permute-start.27 = (bf16[144,128]{1,0:T(8,128)(2,1)}, bf16[144,128]{1,0:T(8,128)(2,1)S(1)}, u32[]{:S(2)}, u32[]{:S(2)}) collective-permute-start(bf16[144,128]{1,0:T(8,128)(2,1)} %get-tuple-element.50), channel_id=1, source_target_pairs={{0,8},{1,9},{2,10},{3,11},{4,12},{5,13},{6,14},{7,15},{8,0},{9,1},... | collective-permute-start | bytes 110600 | tf_op jit(solution)/shard_map/ppermute | solution.py:180
  61.9 9.4 %collective-permute-start.28 = (bf16[144,128]{1,0:T(8,128)(2,1)}, bf16[144,128]{1,0:T(8,128)(2,1)S(1)}, u32[]{:S(2)}, u32[]{:S(2)}) collective-permute-start(bf16[144,128]{1,0:T(8,128)(2,1)} %get-tuple-element.51), channel_id=1, source_target_pairs={{0,16},{1,17},{2,18},{3,19},{4,20},{5,21},{6,22},{7,23},{8,24},{9,... | collective-permute-start | bytes 110600 | tf_op jit(solution)/shard_map/ppermute | solution.py:180
  61.9 9.4 %collective-permute-start.29 = (bf16[144,128]{1,0:T(8,128)(2,1)}, bf16[144,128]{1,0:T(8,128)(2,1)S(1)}, u32[]{:S(2)}, u32[]{:S(2)}) collective-permute-start(bf16[144,128]{1,0:T(8,128)(2,1)} %get-tuple-element.52), channel_id=1, source_target_pairs={{0,24},{1,25},{2,26},{3,27},{4,28},{5,29},{6,30},{7,31},{8,16},{9,... | collective-permute-start | bytes 110600 | tf_op jit(solution)/shard_map/ppermute | solution.py:180
  66.9 8.7 %collective-permute-start.7 = (bf16[144,128]{1,0:T(8,128)(2,1)}, bf16[144,128]{1,0:T(8,128)(2,1)S(1)}, u32[]{:S(2)}, u32[]{:S(2)}) collective-permute-start(bf16[144,128]{1,0:T(8,128)(2,1)} %get-tuple-element.38), channel_id=1, source_target_pairs={{0,8},{1,9},{2,10},{3,11},{4,12},{5,13},{6,14},{7,15},{8,0},{9,1},... | collective-permute-start | bytes 110600 | tf_op jit(solution)/shard_map/ppermute | solution.py:180
  68.1 9.9 %collective-permute-start.8 = (bf16[144,128]{1,0:T(8,128)(2,1)}, bf16[144,128]{1,0:T(8,128)(2,1)S(1)}, u32[]{:S(2)}, u32[]{:S(2)}) collective-permute-start(bf16[144,128]{1,0:T(8,128)(2,1)} %get-tuple-element.39), channel_id=1, source_target_pairs={{0,16},{1,17},{2,18},{3,19},{4,20},{5,21},{6,22},{7,23},{8,24},{9,... | collective-permute-start | bytes 110600 | tf_op jit(solution)/shard_map/ppermute | solution.py:180
  69.0 8.9 %collective-permute-start.9 = (bf16[144,128]{1,0:T(8,128)(2,1)}, bf16[144,128]{1,0:T(8,128)(2,1)S(1)}, u32[]{:S(2)}, u32[]{:S(2)}) collective-permute-start(bf16[144,128]{1,0:T(8,128)(2,1)} %get-tuple-element.40), channel_id=1, source_target_pairs={{0,24},{1,25},{2,26},{3,27},{4,28},{5,29},{6,30},{7,31},{8,16},{9,... | collective-permute-start | bytes 110600 | tf_op jit(solution)/shard_map/ppermute | solution.py:180
  73.5 8.1 %collective-permute-start.30 = (bf16[8,2048]{1,0:T(8,128)(2,1)}, bf16[8,2048]{1,0:T(8,128)(2,1)S(1)}, u32[]{:S(2)}, u32[]{:S(2)}) collective-permute-start(bf16[8,2048]{1,0:T(8,128)(2,1)} %merge_line.3), channel_id=1, source_target_pairs={{0,8},{1,9},{2,10},{3,11},{4,12},{5,13},{6,14},{7,15},{8,0},{9,1},... | collective-permute-start | bytes 98312 | tf_op jit(solution)/shard_map/ppermute | solution.py:180
  73.8 10.8 %collective-permute-start.31 = (bf16[8,2048]{1,0:T(8,128)(2,1)}, bf16[8,2048]{1,0:T(8,128)(2,1)S(1)}, u32[]{:S(2)}, u32[]{:S(2)}) collective-permute-start(bf16[8,2048]{1,0:T(8,128)(2,1)} %merge_line.3), channel_id=1, source_target_pairs={{0,16},{1,17},{2,18},{3,19},{4,20},{5,21},{6,22},{7,23},{8,24},{9,... | collective-permute-start | bytes 98312 | tf_op jit(solution)/shard_map/ppermute | solution.py:180
  75.6 8.9 %collective-permute-start.32 = (bf16[8,2048]{1,0:T(8,128)(2,1)}, bf16[8,2048]{1,0:T(8,128)(2,1)S(1)}, u32[]{:S(2)}, u32[]{:S(2)}) collective-permute-start(bf16[8,2048]{1,0:T(8,128)(2,1)} %merge_line.3), channel_id=1, source_target_pairs={{0,24},{1,25},{2,26},{3,27},{4,28},{5,29},{6,30},{7,31},{8,16},{9,... | collective-permute-start | bytes 98312 | tf_op jit(solution)/shard_map/ppermute | solution.py:180
  80.1 7.3 %collective-permute-start.12 = (bf16[8,2048]{1,0:T(8,128)(2,1)}, bf16[8,2048]{1,0:T(8,128)(2,1)S(1)}, u32[]{:S(2)}, u32[]{:S(2)}) collective-permute-start(bf16[8,2048]{1,0:T(8,128)(2,1)} %merge_line.2), channel_id=1, source_target_pairs={{0,24},{1,25},{2,26},{3,27},{4,28},{5,29},{6,30},{7,31},{8,16},{9,... | collective-permute-start | bytes 98312 | tf_op jit(solution)/shard_map/ppermute | solution.py:180
  81.7 7.2 %collective-permute-start.10 = (bf16[8,2048]{1,0:T(8,128)(2,1)}, bf16[8,2048]{1,0:T(8,128)(2,1)S(1)}, u32[]{:S(2)}, u32[]{:S(2)}) collective-permute-start(bf16[8,2048]{1,0:T(8,128)(2,1)} %merge_line.2), channel_id=1, source_target_pairs={{0,8},{1,9},{2,10},{3,11},{4,12},{5,13},{6,14},{7,15},{8,0},{9,1},... | collective-permute-start | bytes 98312 | tf_op jit(solution)/shard_map/ppermute | solution.py:180
  81.7 7.2 %collective-permute-start.11 = (bf16[8,2048]{1,0:T(8,128)(2,1)}, bf16[8,2048]{1,0:T(8,128)(2,1)S(1)}, u32[]{:S(2)}, u32[]{:S(2)}) collective-permute-start(bf16[8,2048]{1,0:T(8,128)(2,1)} %merge_line.2), channel_id=1, source_target_pairs={{0,16},{1,17},{2,18},{3,19},{4,20},{5,21},{6,22},{7,23},{8,24},{9,... | collective-permute-start | bytes 98312 | tf_op jit(solution)/shard_map/ppermute | solution.py:180
  85.9 6.4 %collective-permute-start.34 = (bf16[4,8,2048]{2,1,0:T(8,128)(2,1)S(1)}, bf16[4,8,2048]{2,1,0:T(8,128)(2,1)S(1)}, u32[]{:S(2)}, u32[]{:S(2)}) collective-permute-start(bf16[4,8,2048]{2,1,0:T(8,128)(2,1)S(1)} %pad_maximum_fusion.1.refs_0_), channel_id=1, source_target_pairs={{0,4},{1,5},{2,6},{3,7},{4,0},{5,1},{6,2},{7,3},{8,12},{9,13},{10,... | collective-permute-start | bytes 393224 | tf_op jit(solution)/shard_map/ppermute | solution.py:180
  87.4 7.8 %collective-permute-start.35 = (bf16[4,8,2048]{2,1,0:T(8,128)(2,1)S(1)}, bf16[4,8,2048]{2,1,0:T(8,128)(2,1)S(1)}, u32[]{:S(2)}, u32[]{:S(2)}) collective-permute-start(bf16[4,8,2048]{2,1,0:T(8,128)(2,1)S(1)} %pad_maximum_fusion.1.refs_0_), channel_id=1, source_target_pairs={{0,6},{1,7},{2,4},{3,5},{4,2},{5,3},{6,0},{7,1},{8,14},{9,15},{10,... | collective-permute-start | bytes 393224 | tf_op jit(solution)/shard_map/ppermute | solution.py:180
  89.7 6.4 %collective-permute-start.13 = (bf16[4,8,2048]{2,1,0:T(8,128)(2,1)S(1)}, bf16[4,8,2048]{2,1,0:T(8,128)(2,1)S(1)}, u32[]{:S(2)}, u32[]{:S(2)}) collective-permute-start(bf16[4,8,2048]{2,1,0:T(8,128)(2,1)S(1)} %pad_maximum_fusion.refs_0_), channel_id=1, source_target_pairs={{0,2},{1,3},{2,0},{3,1},{4,6},{5,7},{6,4},{7,5},{8,10},{9,11},{10,... | collective-permute-start | bytes 393224 | tf_op jit(solution)/shard_map/ppermute | solution.py:180
  90.4 7.6 %collective-permute-start.14 = (bf16[4,8,2048]{2,1,0:T(8,128)(2,1)S(1)}, bf16[4,8,2048]{2,1,0:T(8,128)(2,1)S(1)}, u32[]{:S(2)}, u32[]{:S(2)}) collective-permute-start(bf16[4,8,2048]{2,1,0:T(8,128)(2,1)S(1)} %pad_maximum_fusion.refs_0_), channel_id=1, source_target_pairs={{0,4},{1,5},{2,6},{3,7},{4,0},{5,1},{6,2},{7,3},{8,12},{9,13},{10,... | collective-permute-start | bytes 393224 | tf_op jit(solution)/shard_map/ppermute | solution.py:180
  92.3 7.5 %collective-permute-start.15 = (bf16[4,8,2048]{2,1,0:T(8,128)(2,1)S(1)}, bf16[4,8,2048]{2,1,0:T(8,128)(2,1)S(1)}, u32[]{:S(2)}, u32[]{:S(2)}) collective-permute-start(bf16[4,8,2048]{2,1,0:T(8,128)(2,1)S(1)} %pad_maximum_fusion.refs_0_), channel_id=1, source_target_pairs={{0,6},{1,7},{2,4},{3,5},{4,2},{5,3},{6,0},{7,1},{8,14},{9,15},{10,... | collective-permute-start | bytes 393224 | tf_op jit(solution)/shard_map/ppermute | solution.py:180
  98.0 7.7 %collective-permute-start.16 = (bf16[4,8,2048]{2,1,0:T(8,128)(2,1)S(1)}, bf16[4,8,2048]{2,1,0:T(8,128)(2,1)S(1)}, u32[]{:S(2)}, u32[]{:S(2)}) collective-permute-start(bf16[4,8,2048]{2,1,0:T(8,128)(2,1)S(1)} %pad_maximum_fusion.refs_0_), channel_id=1, source_target_pairs={{0,1},{1,0},{2,3},{3,2},{4,5},{5,4},{6,7},{7,6},{8,9},{9,8},{10,11... | collective-permute-start | bytes 393224 | tf_op jit(solution)/shard_map/ppermute | solution.py:180
  (43 other events, 186.0 us)

commit v2 on v0

--- a/solution.py
+++ b/solution.py
@@ -1,17 +1,340 @@
+import functools
 import math
 
 import jax
 import jax.numpy as jnp
 from jax import lax
+from jax.experimental import pallas as pl
+from jax.experimental.pallas import tpu as pltpu
 from jax.sharding import PartitionSpec as P
 
 BLK = 128
-
-
+LANES = 128
+STAT = 16
 very_low = -1e30
-
-
-def partner(value, axis, distance):
+lowest_top = -(2.0**99)
+bf16 = jnp.bfloat16
+f32 = jnp.float32
+
+
+def pack_state(out, top, total):
+    high = total.astype(bf16).astype(f32)
+    low = total - high
+    row = lax.broadcasted_iota(jnp.int32, (STAT, LANES), 0)
+    stats = jnp.where(row == 0, top, jnp.where(row == 1, high, jnp.where(row == 2, low, 0.0)))
+    return out.astype(bf16), stats.astype(bf16)
+
+
+def attention_kernel(
+    chunk, scale2, meta, mask_ref, counts_ref, q_hbm, k_hbm, v_hbm, send_ref, keep_ref, *scratch
+):
+    listed, kept_counts, q_ref, k_ref, v_ref, kd, vt, spread, sems = scratch
+    core = meta[0]
+    d = k_hbm.shape[1]
+    kv_count = spread.shape[0] // BLK
+    rows = send_ref.shape[0] * LANES
+    group_size = q_ref.shape[2]
+    block_count = counts_ref.shape[0]
+
+    copies = [
+        pltpu.make_async_copy(k_hbm, k_ref, sems.at[0]),
+        pltpu.make_async_copy(v_hbm, v_ref, sems.at[1]),
+    ]
+    for g in range(2):
+        heads = pl.ds((2 * chunk + g) * group_size, group_size)
+        copies.append(pltpu.make_async_copy(q_hbm.at[:, heads, :], q_ref.at[g], sems.at[2 + g]))
+    for copy in copies:
+        copy.start()
+
+    def note(block, found):
+        listed[found] = block
+        kept_counts[found] = counts_ref[block]
+        return found + (mask_ref[0, block] > 0).astype(jnp.int32)
+
+    active = lax.fori_loop(0, block_count, note, jnp.int32(0))
+    place = lax.broadcasted_iota(jnp.int32, (BLK, LANES), 0)
+    across = lax.broadcasted_iota(jnp.int32, (STAT, LANES), 1)
+
+    def split(source, position):
+        start = pl.multiple_of(listed[position] * (BLK * kv_count), BLK * kv_count)
+        spread[...] = source[pl.ds(start, BLK * kv_count), :].astype(f32)
+        return [spread[pl.ds(2 * chunk + g, BLK, stride=kv_count), :] for g in range(2)]
+
+    def fetch_keys(position, carry):
+        at = pl.ds(pl.multiple_of(position * BLK, BLK), BLK)
+        valid = place < kept_counts[position]
+        for g, key in enumerate(split(k_ref, position)):
+            kd[g, at, :] = jnp.where(valid, key, key[0:1]).astype(bf16)
+        return carry
+
+    def fetch_values(position, carry):
+        at = pl.ds(pl.multiple_of(position * BLK, BLK), BLK)
+        count = kept_counts[position]
+        for g, value in enumerate(split(v_ref, position)):
+            vt[g, 0:d, at] = jnp.where(place < count, value, 0.0).T.astype(bf16)
+            vt[g, d:, at] = (across < count).astype(f32).astype(bf16)
+        return carry
+
+    copies[0].wait()
+    lax.fori_loop(0, active, fetch_keys, 0)
+    copies[1].wait()
+    lax.fori_loop(0, active, fetch_values, 0)
+
+    @pl.when(active % 2 == 1)
+    def _():
+        at = pl.ds(pl.multiple_of(active * BLK, BLK), BLK)
+        before = pl.ds(pl.multiple_of((active - 1) * BLK, BLK), BLK)
+        for g in range(2):
+            kd[g, at, :] = kd[g, before, :]
+            vt[g, :, at] = jnp.zeros((d + STAT, BLK), bf16)
+
+    copies[2].wait()
+    copies[3].wait()
+    pairs = (active + 1) // 2
+    row = lax.broadcasted_iota(jnp.int32, (STAT, rows), 0)
+
+    def attend(width, role, carry):
+        group = jnp.where(role == 0, 1 - core, core)
+        q = q_ref[group].reshape(rows, d)
+        scores = lax.dot_general(
+            kd[group, 0:width, :], q, (((1,), (1,)), ((), ())), preferred_element_type=f32
+        )
+        top = (jnp.max(scores, axis=0, keepdims=True) * scale2).astype(bf16).astype(f32)
+        weights = jnp.exp2(scores * scale2 - top).astype(bf16)
+        sums = jnp.dot(vt[group, :, 0:width], weights, preferred_element_type=f32)
+        total = sums[d:]
+        high = total.astype(bf16).astype(f32)
+        stats = jnp.where(row == 0, top, jnp.where(row == 1, high, total - high)).astype(bf16)
+        out = sums[:d].astype(bf16)
+        for ref, its_role in ((send_ref, 0), (keep_ref, 1)):
+
+            @pl.when(role == its_role)
+            def _():
+                for piece in range(rows // LANES):
+                    at = slice(piece * LANES, (piece + 1) * LANES)
+                    ref[piece, 0:d] = out[:, at]
+                    ref[piece, d:] = stats[:, at]
+
+        return carry
+
+    for n in range(1, block_count // 2 + 1):
+
+        @pl.when(pairs == n)
+        def _(n=n):
+            lax.fori_loop(0, 2, functools.partial(attend, 2 * BLK * n), 0)
+
+    @pl.when(pairs == 0)
+    def _():
+        row = lax.broadcasted_iota(jnp.int32, (d + STAT, LANES), 0)
+        empty = jnp.where(row == d, lowest_top, 0.0).astype(bf16)
+        for ref in (send_ref, keep_ref):
+            for piece in range(rows // LANES):
+                ref[piece] = empty
+
+
+def merged(parts, d):
+    stats = [part[d : d + STAT, :].astype(f32) for part in parts]
+    tops = [stat[0:1] for stat in stats]
+    top = functools.reduce(jnp.maximum, tops)
+    out, total = 0.0, 0.0
+    for part, stat, one in zip(parts, stats, tops):
+        factor = jnp.exp2(one - top)
+        out = out + part[0:d, :].astype(f32) * factor
+        total = total + (stat[1:2] + stat[2:3]) * factor
+    return out, top, total
+
+
+def store_merged(ref, z, parts):
+    d = ref.shape[1] - STAT
+    out, stats = pack_state(*merged(parts, d))
+    ref[z, 0:d, :] = out
+    ref[z, d : d + STAT, :] = stats
+
+
+def core_kernel(meta, kept, received, *outs):
+    my_xy = meta[1]
+    z_size = outs[0].shape[0]
+    for j, out in enumerate(outs):
+        for z in range(z_size):
+            piece = (my_xy ^ j) * z_size + z
+            store_merged(out, z, [kept[piece], received[piece]])
+
+
+def plane_kernel(*refs):
+    ins, out = refs[:-1], refs[-1]
+    for z in range(out.shape[0]):
+        store_merged(out, z, [ref[z] for ref in ins])
+
+
+def last_kernel(*refs):
+    ins, out_ref, turned = refs[:-2], refs[-2], refs[-1]
+    d = ins[0].shape[1] - STAT
+    tokens = out_ref.shape[1]
+    heads = LANES // tokens
+    for z in range(out_ref.shape[0]):
+        out, _, total = merged([ref[z] for ref in ins], d)
+        turned[z] = (out / total).T
+        for h in range(heads):
+            picked = turned[z, pl.ds(h, tokens, stride=heads), :]
+            out_ref[z, :, h * d : (h + 1) * d] = picked.astype(bf16)
+
+
+def project_kernel(last, meta, w_own, w_other, *refs):
+    own, other, refs = refs[:4], refs[4:8], refs[8:]
+    z_size, tokens, depth = own[0].shape
+    total = None
+    for parts, weight in ((own, w_own), (other, w_other)):
+        left = jnp.concatenate(
+            [part[...].reshape(z_size * tokens, depth) for part in parts], axis=0
+        )
+        product = jnp.dot(left, weight[...], preferred_element_type=f32)
+        total = product if total is None else total + product
+    if not last:
+        refs[0][...] = total
+        return
+    earlier, out_ref = refs
+    total = total + earlier[...]
+    my_xy = meta[1]
+    size = z_size * tokens
+    for j in range(4):
+        to = pl.ds(pl.multiple_of((my_xy ^ j) * size, size), size)
+        out_ref[to, :] = total[j * size : (j + 1) * size]
+
+
+def hop(value, mask):
+    pairs = [(source, source ^ mask) for source in range(lax.axis_size("ctx"))]
+    return lax.ppermute(value, "ctx", pairs)
+
+
+VMEM = pl.BlockSpec(memory_space=pltpu.VMEM)
+SMEM = pl.BlockSpec(memory_space=pltpu.SMEM)
+HBM = pl.BlockSpec(memory_space=pltpu.HBM)
+
+
+def fast_body(queries, cache_keys, cache_values, block_mask, key_counts, out_weight):
+    index = lax.axis_index("ctx")
+    z_size = lax.axis_size("ctx") // 8
+    token_count, head_count, d = queries.shape
+    kv_count = cache_keys.shape[1]
+    group_size = head_count // kv_count
+    rows = token_count * group_size
+    pieces = rows // LANES
+    positions = cache_keys.shape[0]
+    features = out_weight.shape[1]
+    core = index & 1
+    my_xy = (index >> 1) & 3
+    tall = d + STAT
+    scale2 = math.log2(math.e) / math.sqrt(d)
+    keys = cache_keys.reshape(positions * kv_count, d)
+    values = cache_values.reshape(positions * kv_count, d)
+    place = jnp.stack([core, my_xy]).astype(jnp.int32)
+    state = jax.ShapeDtypeStruct((z_size, tall, LANES), bf16)
+
+    def attend(chunk):
+        blocks = positions // BLK
+        return pl.pallas_call(
+            functools.partial(attention_kernel, chunk, scale2),
+            in_specs=[SMEM] * 3 + [HBM] * 3,
+            out_specs=[VMEM] * 2,
+            scratch_shapes=[
+                pltpu.SMEM((blocks + 1,), jnp.int32),
+                pltpu.SMEM((blocks + 1,), jnp.int32),
+                pltpu.VMEM((2, token_count, group_size, d), bf16),
+                pltpu.VMEM((positions * kv_count, d), bf16),
+                pltpu.VMEM((positions * kv_count, d), bf16),
+                pltpu.VMEM((2, positions, d), bf16),
+                pltpu.VMEM((2, tall, positions), bf16),
+                pltpu.VMEM((BLK * kv_count, d), f32),
+                pltpu.SemaphoreType.DMA((4,)),
+            ],
+            out_shape=[jax.ShapeDtypeStruct((pieces, tall, LANES), bf16)] * 2,
+            compiler_params=pltpu.CompilerParams(vmem_limit_bytes=40 << 20),
+            cost_estimate=pl.CostEstimate(
+                flops=8 * rows * positions * d,
+                transcendentals=2 * rows * positions,
+                bytes_accessed=4 * positions * d * kv_count,
+            ),
+            name="attention",
+        )(place, block_mask, key_counts, queries, keys, values)
+
+    def merge_cores(kept, received):
+        return pl.pallas_call(
+            core_kernel,
+            in_specs=[SMEM] + [VMEM] * 2,
+            out_specs=[VMEM] * 4,
+            out_shape=[state] * 4,
+            name="merge_cores",
+        )(place, kept, received)
+
+    def merge_chips(parts):
+        return pl.pallas_call(
+            plane_kernel,
+            in_specs=[VMEM] * len(parts),
+            out_specs=VMEM,
+            out_shape=state,
+            name="merge_chips",
+        )(*parts)
+
+    def finish(parts):
+        tokens = LANES // group_size
+        return pl.pallas_call(
+            last_kernel,
+            in_specs=[VMEM] * len(parts),
+            out_specs=VMEM,
+            out_shape=jax.ShapeDtypeStruct((z_size, tokens, group_size * d), bf16),
+            scratch_shapes=[pltpu.VMEM((z_size, LANES, d), f32)],
+            name="finish",
+        )(*parts)
+
+    def project(chunk, own, other, earlier):
+        depth = group_size * d
+        whole = [pl.BlockSpec(a.shape, lambda i, m: (0, 0, 0)) for a in own + other]
+        more = [] if earlier is None else [earlier]
+        return pl.pallas_call(
+            functools.partial(project_kernel, earlier is not None),
+            grid_spec=pltpu.PrefetchScalarGridSpec(
+                num_scalar_prefetch=1,
+                grid=(1,),
+                in_specs=[
+                    pl.BlockSpec((depth, features), lambda i, m: (2 * chunk + m[0], 0)),
+                    pl.BlockSpec((depth, features), lambda i, m: (2 * chunk + 1 - m[0], 0)),
+                ]
+                + whole
+                + [VMEM] * len(more),
+                out_specs=VMEM,
+            ),
+            out_shape=jax.ShapeDtypeStruct((token_count, features), f32),
+            compiler_params=pltpu.CompilerParams(vmem_limit_bytes=32 << 20),
+            cost_estimate=pl.CostEstimate(
+                flops=4 * token_count * depth * features,
+                transcendentals=0,
+                bytes_accessed=4 * depth * features,
+            ),
+            name="project",
+        )(place, out_weight, out_weight, *own, *other, *more)
+
+    chunks = kv_count // 2
+    partials = []
+    for c in range(chunks):
+        sent, kept = attend(c)
+        partials.append((kept, hop(sent, 1)))
+    total = None
+    for c in range(chunks):
+        parts = merge_cores(*partials[c])
+        parts = [parts[0]] + [hop(parts[j], 2 * j) for j in (1, 2, 3)]
+        part = merge_chips(parts)
+        reach = 1
+        while 2 * reach < z_size:
+            part = merge_chips([part, hop(part, 8 * reach)])
+            reach *= 2
+        attended = finish([part, hop(part, 8 * reach)])
+        own = [attended] + [hop(attended, 2 * j) for j in (1, 2, 3)]
+        other = [hop(part, 1) for part in own]
+        total = project(c, own, other, total)
+    return total
+
+
+def partner_of(value, axis, distance):
     mask = 2**distance
     pairs = [(source, source ^ mask) for source in range(lax.axis_size(axis))]
     return lax.ppermute(value, axis, pairs)
@@ -76,7 +399,7 @@
     return lax.fori_loop(0, block_count, visit_block, initial)
 
 
-def body(queries, cache_keys, cache_values, block_mask, key_counts, out_weight):
+def general_body(queries, cache_keys, cache_values, block_mask, key_counts, out_weight):
     cycle_size = lax.axis_size("ctx")
     cycle_index = lax.axis_index("ctx")
     token_count, head_count, head_size = queries.shape
@@ -89,8 +412,7 @@
         return partial_rows(rows_q, row_mask, cache_keys, cache_values, key_counts)
 
     stacked = lax.map(per_block, (query_blocks, block_mask))
-    local_state = tuple((part.reshape((token_count,) + part.shape[2:]) for part in stacked))
-    run_state = local_state
+    run_state = tuple((part.reshape((token_count,) + part.shape[2:]) for part in stacked))
     bit_total = cycle_size.bit_length() - 1
     for bit_number in range(bit_total - 1, -1, -1):
         half_rows = run_state[1].shape[0] // 2
@@ -107,7 +429,7 @@
                 for part in run_state
             )
         )
-        received = partner((outgoing[0], outgoing[1], outgoing[2]), "ctx", bit_number)
+        received = partner_of((outgoing[0], outgoing[1], outgoing[2]), "ctx", bit_number)
         run_state = combine(kept, received)
     out_sum, top_score, weight_sum = run_state
     attended = (
@@ -120,8 +442,26 @@
         out_weight,
         preferred_element_type=jnp.float32,
     )
-    summed = lax.psum_scatter(partial_value, "kv", scatter_dimension=0, tiled=True)
-    return summed
+    return lax.psum_scatter(partial_value, "kv", scatter_dimension=0, tiled=True)
+
+
+def body(queries, cache_keys, cache_values, block_mask, key_counts, out_weight):
+    devices = lax.axis_size("ctx")
+    token_count, head_count, d = queries.shape
+    kv_count = cache_keys.shape[1]
+    group_size = head_count // kv_count
+    suits = (
+        lax.axis_size("kv") == 1
+        and devices == 32
+        and token_count == BLK
+        and block_mask.shape[0] == 1
+        and kv_count % 2 == 0
+        and d == LANES
+        and group_size == 16
+        and token_count * group_size == LANES * (devices // 2)
+    )
+    run = fast_body if suits else general_body
+    return run(queries, cache_keys, cache_values, block_mask, key_counts, out_weight)
 
 
 def solution(mesh):

time: 292 us -> 89.8 us (0.31)
  waiting for transfers between devices: 136 us -> 14.6 us
  matrix products: 33.4 us -> 0 us
  other arithmetic: 26.7 us -> 0.07 us
  local copies, waits for them, and re-layouts: 43.2 us -> 17.6 us
  Pallas kernels: 0 us -> 25 us
  between operations: 13.6 us -> 0.14 us
  loops' own time: 6.06 us -> 0 us
    ppermute x15 -> x26, waiting for transfers between devices: 80.9 us -> 14.6 us  [hop(): return lax.ppermute(value, 'ctx', pairs)]
    all_gather x1 -> x0, waiting for transfers between devices: 54.6 us -> none  [body(): lax.all_gather(attended, 'ctx', axis=0, tiled=True)]
    dot_general x15 -> x0, matrix products: 33.4 us -> none  [the longest x7 15.1 us: update(): jnp.einsum('rgqk,kgd->rgqd', weights.astype(jnp.bfloat16), value_part, pr...]
    pallas_call x0 -> x12, Pallas kernels: none -> 25 us  [the longest x4 7.32 us: merge_chips(): pl.pallas_call(plane_kernel, in_specs=[VMEM] * len(parts), out_specs=VMEM...]
    cond x35 -> x0, local copies, waits for them, and re-layouts: 14.2 us -> none
    reduce_sum x7 -> x0, other arithmetic: 8.72 us -> none  [update(): new_sum = weight_sum * factor + jnp.sum(weights, axis=-1)]
    dynamic_slice x22 -> x0, local copies, waits for them, and re-layouts: 8.45 us -> none  [the longest x7 4.32 us: update(): valid_count = lax.dynamic_slice_in_dim(key_counts, key_block, 1, 0)[0]]
    add x16 -> x0, other arithmetic: 7.25 us -> none  [the longest x4 5.97 us: combine(): new_out = out_one * factor_one[..., None] + out_two * factor_two[..., None]]
  transfers between devices with their start and end apart: 16 -> 26, of which waited for: 9 -> 8; matrix products, arithmetic and copies ran while one was open for 2% -> 0% of each run, Pallas kernels for 0% -> 22%
where the time goes in v2:
time: 89.8 us; the launch traced here: 90.7 us
  starting transfers between devices  33.3 us (37%)
  Pallas kernels  25 us (28%)
  local copies, waits for them, and re-layouts  17.6 us (20%)
  waiting for transfers between devices  14.6 us (16%)
    ppermute x26, starting transfers between devices, hop(): return lax.ppermute(value, 'ctx', pairs)  33.3 us
    unnamed x48, local copies, waits for them, and re-layouts  17.6 us
    ppermute x26, waiting for transfers between devices, hop(): return lax.ppermute(value, 'ctx', pairs)  14.6 us
    pallas_call x4, Pallas kernels, merge_chips(): pl.pallas_call(plane_kernel, in_specs=[VMEM] * len(parts), out_specs=VMEM...  7.32 us
    pallas_call x2, Pallas kernels, attend(): pl.pallas_call(functools.partial(attention_kernel, chunk, scale2), in_spe...  6.38 us
    pallas_call x2, Pallas kernels, merge_cores(): pl.pallas_call(core_kernel, in_specs=[SMEM] + [VMEM] * 2, out_specs=[VMEM...  4.4 us
    pallas_call x2, Pallas kernels, finish(): pl.pallas_call(last_kernel, in_specs=[VMEM] * len(parts), out_specs=VMEM,...  3.69 us
    pallas_call x2, Pallas kernels, project(): pl.pallas_call(functools.partial(project_kernel, earlier is not None), gr...  3.24 us
  transfers between devices with their start and end apart: 26, of which 8 were waited for; matrix products, arithmetic and copies ran while one was open for 0% of the time, Pallas kernels for 22%

profile of v2, /device:TPU:0, one launch (start us, length us, event | category | flops | bytes accessed | tf_op | source)
XLA Modules:
  0.0 90.7 jit_solution(16525895191064617806)
XLA Ops:
  0.1 1.6 %copy-done.7 = bf16[128,64,128]{2,1,0:T(8,128)(2,1)S(1)} copy-done((bf16[128,64,128]{2,1,0:T(8,128)(2,1)S(1)}, bf16[128,64,128]{2,1,0:T(8,128)(2,1)}, u32[]{:S(2)}) %copy-start.7) | copy-done | bytes 2097176
  1.7 1.2 %copy-done.8 = bf16[1024,4,128]{2,1,0:T(4,128)(2,1)S(1)} copy-done((bf16[1024,4,128]{2,1,0:T(4,128)(2,1)S(1)}, bf16[1024,4,128]{2,1,0:T(4,128)(2,1)}, u32[]{:S(2)}) %copy-start.8) | copy-done | bytes 1048600
  2.9 1.2 %copy-done.9 = bf16[1024,4,128]{2,1,0:T(4,128)(2,1)S(1)} copy-done((bf16[1024,4,128]{2,1,0:T(4,128)(2,1)S(1)}, bf16[1024,4,128]{2,1,0:T(4,128)(2,1)}, u32[]{:S(2)}) %copy-start.9) | copy-done | bytes 1048600
  5.4 3.1 %attention.3 = (bf16[16,144,128]{2,1,0:T(8,128)(2,1)S(1)}, bf16[16,144,128]{2,1,0:T(8,128)(2,1)S(1)}) custom-call(s32[2]{0:T(128)S(1)} %pad_add_fusion.meta, s32[1,8]{1,0:T(1,128)S(1)} %copy-done.10, s32[8]{0:T(128)S(1)} %copy-done.11, bf16[128,64,128]{2,1,0:T(8,128)(2,1)S(1)} %copy-done.7, bf16[4096,128]{1,0:T(8,128)(2,1)S(1)} %bitcast.4, ...), custom_call_target="tpu_custom_call" | custom-call | flops 2147483648 | bytes 2097152 | tf_op jit(solution)/shard_map/attention/pallas_call | solution.py:235
  9.7 3.3 %attention.2 = (bf16[16,144,128]{2,1,0:T(8,128)(2,1)S(1)}, bf16[16,144,128]{2,1,0:T(8,128)(2,1)S(1)}) custom-call(s32[2]{0:T(128)S(1)} %pad_add_fusion.meta, s32[1,8]{1,0:T(1,128)S(1)} %copy-done.10, s32[8]{0:T(128)S(1)} %copy-done.11, bf16[128,64,128]{2,1,0:T(8,128)(2,1)S(1)} %copy-done.7, bf16[4096,128]{1,0:T(8,128)(2,1)S(1)} %bitcast.5, ...), custom_call_target="tpu_custom_call" | custom-call | flops 2147483648 | bytes 2097152 | tf_op jit(solution)/shard_map/attention/pallas_call | solution.py:235
  14.7 2.2 %merge_cores.3 = (bf16[4,144,128]{2,1,0:T(8,128)(2,1)}, bf16[4,144,128]{2,1,0:T(8,128)(2,1)}, bf16[4,144,128]{2,1,0:T(8,128)(2,1)}, bf16[4,144,128]{2,1,0:T(8,128)(2,1)}) custom-call(s32[2]{0:T(128)} %copy-done.5, bf16[16,144,128]{2,1,0:T(8,128)(2,1)} %copy-done.2, bf16[16,144,128]{2,1,0:T(8,128)(2,1)} %copy-done.13), custom_call_target="tpu_custom_call" | custom-call | tf_op jit(solution)/shard_map/merge_cores/pallas_call | solution.py:261
  16.9 2.9 %collective-permute-start.14 = (bf16[4,144,128]{2,1,0:T(8,128)(2,1)}, bf16[4,144,128]{2,1,0:T(8,128)(2,1)S(1)}, u32[]{:S(2)}, u32[]{:S(2)}) collective-permute-start(bf16[4,144,128]{2,1,0:T(8,128)(2,1)} %get-tuple-element.26), channel_id=1, source_target_pairs={{0,2},{1,3},{2,0},{3,1},{4,6},{5,7},{6,4},{7,5},{8,10},{9,11},{10,... | collective-permute-start | bytes 442376 | tf_op jit(solution)/shard_map/ppermute | solution.py:206
  19.8 2.4 %collective-permute-start.15 = (bf16[4,144,128]{2,1,0:T(8,128)(2,1)}, bf16[4,144,128]{2,1,0:T(8,128)(2,1)S(1)}, u32[]{:S(2)}, u32[]{:S(2)}) collective-permute-start(bf16[4,144,128]{2,1,0:T(8,128)(2,1)} %get-tuple-element.27), channel_id=1, source_target_pairs={{0,4},{1,5},{2,6},{3,7},{4,0},{5,1},{6,2},{7,3},{8,12},{9,13},{10,... | collective-permute-start | bytes 442376 | tf_op jit(solution)/shard_map/ppermute | solution.py:206
  22.2 1.5 %collective-permute-start.16 = (bf16[4,144,128]{2,1,0:T(8,128)(2,1)}, bf16[4,144,128]{2,1,0:T(8,128)(2,1)S(1)}, u32[]{:S(2)}, u32[]{:S(2)}) collective-permute-start(bf16[4,144,128]{2,1,0:T(8,128)(2,1)} %get-tuple-element.28), channel_id=1, source_target_pairs={{0,6},{1,7},{2,4},{3,5},{4,2},{5,3},{6,0},{7,1},{8,14},{9,15},{10,... | collective-permute-start | bytes 442376 | tf_op jit(solution)/shard_map/ppermute | solution.py:206
  24.5 2.2 %merge_cores.2 = (bf16[4,144,128]{2,1,0:T(8,128)(2,1)}, bf16[4,144,128]{2,1,0:T(8,128)(2,1)}, bf16[4,144,128]{2,1,0:T(8,128)(2,1)}, bf16[4,144,128]{2,1,0:T(8,128)(2,1)}) custom-call(s32[2]{0:T(128)} %copy-done.5, bf16[16,144,128]{2,1,0:T(8,128)(2,1)} %copy-done.1, bf16[16,144,128]{2,1,0:T(8,128)(2,1)} %copy-done.12), custom_call_target="tpu_custom_call" | custom-call | tf_op jit(solution)/shard_map/merge_cores/pallas_call | solution.py:261
  27.3 1.5 %collective-permute-start.2 = (bf16[4,144,128]{2,1,0:T(8,128)(2,1)}, bf16[4,144,128]{2,1,0:T(8,128)(2,1)S(1)}, u32[]{:S(2)}, u32[]{:S(2)}) collective-permute-start(bf16[4,144,128]{2,1,0:T(8,128)(2,1)} %get-tuple-element.21), channel_id=1, source_target_pairs={{0,4},{1,5},{2,6},{3,7},{4,0},{5,1},{6,2},{7,3},{8,12},{9,13},{10,... | collective-permute-start | bytes 442376 | tf_op jit(solution)/shard_map/ppermute | solution.py:206
  28.7 1.5 %collective-permute-start.3 = (bf16[4,144,128]{2,1,0:T(8,128)(2,1)}, bf16[4,144,128]{2,1,0:T(8,128)(2,1)S(1)}, u32[]{:S(2)}, u32[]{:S(2)}) collective-permute-start(bf16[4,144,128]{2,1,0:T(8,128)(2,1)} %get-tuple-element.22), channel_id=1, source_target_pairs={{0,6},{1,7},{2,4},{3,5},{4,2},{5,3},{6,0},{7,1},{8,14},{9,15},{10,... | collective-permute-start | bytes 442376 | tf_op jit(solution)/shard_map/ppermute | solution.py:206
  32.0 1.9 %merge_chips.6.refs_0_ = bf16[4,144,128]{2,1,0:T(8,128)(2,1)} custom-call(bf16[4,144,128]{2,1,0:T(8,128)(2,1)} %get-tuple-element.25.refs_0_, bf16[4,144,128]{2,1,0:T(8,128)(2,1)} %copy-done.18, bf16[4,144,128]{2,1,0:T(8,128)(2,1)} %copy-done.20, bf16[4,144,128]{2,1,0:T(8,128)(2,1)} %copy-done.22), custom_call_target="tpu_custom_call" | custom-call | tf_op jit(solution)/shard_map/merge_chips/pallas_call | solution.py:270
  33.9 2.1 %collective-permute-start.17 = (bf16[4,144,128]{2,1,0:T(8,128)(2,1)}, bf16[4,144,128]{2,1,0:T(8,128)(2,1)S(1)}, u32[]{:S(2)}, u32[]{:S(2)}) collective-permute-start(bf16[4,144,128]{2,1,0:T(8,128)(2,1)} %merge_chips.6.refs_0_), channel_id=1, source_target_pairs={{0,8},{1,9},{2,10},{3,11},{4,12},{5,13},{6,14},{7,15},{8,0},{9,1},... | collective-permute-start | bytes 442376 | tf_op jit(solution)/shard_map/ppermute | solution.py:206
  37.7 1.9 %merge_chips.4.refs_0_ = bf16[4,144,128]{2,1,0:T(8,128)(2,1)} custom-call(bf16[4,144,128]{2,1,0:T(8,128)(2,1)} %get-tuple-element.19.refs_0_, bf16[4,144,128]{2,1,0:T(8,128)(2,1)} %copy-done.19, bf16[4,144,128]{2,1,0:T(8,128)(2,1)} %copy-done.21, bf16[4,144,128]{2,1,0:T(8,128)(2,1)} %copy-done.23), custom_call_target="tpu_custom_call" | custom-call | tf_op jit(solution)/shard_map/merge_chips/pallas_call | solution.py:270
  39.7 2.3 %collective-permute-start.4 = (bf16[4,144,128]{2,1,0:T(8,128)(2,1)}, bf16[4,144,128]{2,1,0:T(8,128)(2,1)S(1)}, u32[]{:S(2)}, u32[]{:S(2)}) collective-permute-start(bf16[4,144,128]{2,1,0:T(8,128)(2,1)} %merge_chips.4.refs_0_), channel_id=1, source_target_pairs={{0,8},{1,9},{2,10},{3,11},{4,12},{5,13},{6,14},{7,15},{8,0},{9,1},... | collective-permute-start | bytes 442376 | tf_op jit(solution)/shard_map/ppermute | solution.py:206
  42.7 1.7 %merge_chips.7.refs_0_ = bf16[4,144,128]{2,1,0:T(8,128)(2,1)} custom-call(bf16[4,144,128]{2,1,0:T(8,128)(2,1)} %merge_chips.6.refs_0_, bf16[4,144,128]{2,1,0:T(8,128)(2,1)} %copy-done.14), custom_call_target="tpu_custom_call" | custom-call | tf_op jit(solution)/shard_map/merge_chips/pallas_call | solution.py:270
  44.4 8.8 %collective-permute-start.18 = (bf16[4,144,128]{2,1,0:T(8,128)(2,1)}, bf16[4,144,128]{2,1,0:T(8,128)(2,1)S(1)}, u32[]{:S(2)}, u32[]{:S(2)}) collective-permute-start(bf16[4,144,128]{2,1,0:T(8,128)(2,1)} %merge_chips.7.refs_0_), channel_id=1, source_target_pairs={{0,16},{1,17},{2,18},{3,19},{4,20},{5,21},{6,22},{7,23},{8,24},{9,... | collective-permute-start | bytes 442376 | tf_op jit(solution)/shard_map/ppermute | solution.py:206
  53.9 1.7 %merge_chips.5.refs_0_ = bf16[4,144,128]{2,1,0:T(8,128)(2,1)} custom-call(bf16[4,144,128]{2,1,0:T(8,128)(2,1)} %merge_chips.4.refs_0_, bf16[4,144,128]{2,1,0:T(8,128)(2,1)} %copy-done.15), custom_call_target="tpu_custom_call" | custom-call | tf_op jit(solution)/shard_map/merge_chips/pallas_call | solution.py:270
  55.6 1.7 %collective-permute-start.5 = (bf16[4,144,128]{2,1,0:T(8,128)(2,1)}, bf16[4,144,128]{2,1,0:T(8,128)(2,1)S(1)}, u32[]{:S(2)}, u32[]{:S(2)}) collective-permute-start(bf16[4,144,128]{2,1,0:T(8,128)(2,1)} %merge_chips.5.refs_0_), channel_id=1, source_target_pairs={{0,16},{1,17},{2,18},{3,19},{4,20},{5,21},{6,22},{7,23},{8,24},{9,... | collective-permute-start | bytes 442376 | tf_op jit(solution)/shard_map/ppermute | solution.py:206
  57.4 5.9 %collective-permute-done.18.refs_1_ = bf16[4,144,128]{2,1,0:T(8,128)(2,1)S(1)} collective-permute-done((bf16[4,144,128]{2,1,0:T(8,128)(2,1)}, bf16[4,144,128]{2,1,0:T(8,128)(2,1)S(1)}, u32[]{:S(2)}, u32[]{:S(2)}) %collective-permute-start.18) | collective-permute-done | bytes 147488 | tf_op jit(solution)/shard_map/ppermute | solution.py:206
  63.9 1.8 %finish.3.refs_0_ = bf16[4,8,2048]{2,1,0:T(8,128)(2,1)} custom-call(bf16[4,144,128]{2,1,0:T(8,128)(2,1)} %merge_chips.7.refs_0_, bf16[4,144,128]{2,1,0:T(8,128)(2,1)} %copy-done.17), custom_call_target="tpu_custom_call" | custom-call | tf_op jit(solution)/shard_map/finish/pallas_call | solution.py:280
  65.8 1.7 %collective-permute-start.21 = (bf16[4,8,2048]{2,1,0:T(8,128)(2,1)}, bf16[4,8,2048]{2,1,0:T(8,128)(2,1)S(1)}, u32[]{:S(2)}, u32[]{:S(2)}) collective-permute-start(bf16[4,8,2048]{2,1,0:T(8,128)(2,1)} %finish.3.refs_0_), channel_id=1, source_target_pairs={{0,6},{1,7},{2,4},{3,5},{4,2},{5,3},{6,0},{7,1},{8,14},{9,15},{10,... | collective-permute-start | bytes 393224 | tf_op jit(solution)/shard_map/ppermute | solution.py:206
  67.5 1.4 %collective-permute-start.20 = (bf16[4,8,2048]{2,1,0:T(8,128)(2,1)}, bf16[4,8,2048]{2,1,0:T(8,128)(2,1)S(1)}, u32[]{:S(2)}, u32[]{:S(2)}) collective-permute-start(bf16[4,8,2048]{2,1,0:T(8,128)(2,1)} %finish.3.refs_0_), channel_id=1, source_target_pairs={{0,4},{1,5},{2,6},{3,7},{4,0},{5,1},{6,2},{7,3},{8,12},{9,13},{10,... | collective-permute-start | bytes 393224 | tf_op jit(solution)/shard_map/ppermute | solution.py:206
  69.9 1.8 %finish.2.refs_0_ = bf16[4,8,2048]{2,1,0:T(8,128)(2,1)} custom-call(bf16[4,144,128]{2,1,0:T(8,128)(2,1)} %merge_chips.5.refs_0_, bf16[4,144,128]{2,1,0:T(8,128)(2,1)} %copy-done.16), custom_call_target="tpu_custom_call" | custom-call | tf_op jit(solution)/shard_map/finish/pallas_call | solution.py:280
  71.8 1.7 %collective-permute-start.8 = (bf16[4,8,2048]{2,1,0:T(8,128)(2,1)}, bf16[4,8,2048]{2,1,0:T(8,128)(2,1)S(1)}, u32[]{:S(2)}, u32[]{:S(2)}) collective-permute-start(bf16[4,8,2048]{2,1,0:T(8,128)(2,1)} %finish.2.refs_0_), channel_id=1, source_target_pairs={{0,6},{1,7},{2,4},{3,5},{4,2},{5,3},{6,0},{7,1},{8,14},{9,15},{10,... | collective-permute-start | bytes 393224 | tf_op jit(solution)/shard_map/ppermute | solution.py:206
  73.5 1.4 %collective-permute-start.7 = (bf16[4,8,2048]{2,1,0:T(8,128)(2,1)}, bf16[4,8,2048]{2,1,0:T(8,128)(2,1)S(1)}, u32[]{:S(2)}, u32[]{:S(2)}) collective-permute-start(bf16[4,8,2048]{2,1,0:T(8,128)(2,1)} %finish.2.refs_0_), channel_id=1, source_target_pairs={{0,4},{1,5},{2,6},{3,7},{4,0},{5,1},{6,2},{7,3},{8,12},{9,13},{10,... | collective-permute-start | bytes 393224 | tf_op jit(solution)/shard_map/ppermute | solution.py:206
  76.6 2.7 %collective-permute-done.8.refs_3_ = bf16[4,8,2048]{2,1,0:T(8,128)(2,1)S(1)} collective-permute-done((bf16[4,8,2048]{2,1,0:T(8,128)(2,1)}, bf16[4,8,2048]{2,1,0:T(8,128)(2,1)S(1)}, u32[]{:S(2)}, u32[]{:S(2)}) %collective-permute-start.8) | collective-permute-done | bytes 131104 | tf_op jit(solution)/shard_map/ppermute | solution.py:206
  79.3 1.9 %collective-permute-done.7.refs_2_ = bf16[4,8,2048]{2,1,0:T(8,128)(2,1)S(1)} collective-permute-done((bf16[4,8,2048]{2,1,0:T(8,128)(2,1)}, bf16[4,8,2048]{2,1,0:T(8,128)(2,1)S(1)}, u32[]{:S(2)}, u32[]{:S(2)}) %collective-permute-start.7) | collective-permute-done | bytes 131104 | tf_op jit(solution)/shard_map/ppermute | solution.py:206
  82.5 3.4 %copy-done = bf16[8192,512]{1,0:T(8,128)(2,1)S(1)} copy-done((bf16[8192,512]{1,0:T(8,128)(2,1)S(1)}, bf16[8192,512]{1,0:T(8,128)(2,1)}, u32[]{:S(2)}) %copy-start) | copy-done | bytes 8388632
  87.4 1.3 %project.2.refs_8_ = f32[128,512]{1,0:T(8,128)S(1)} custom-call(s32[2]{0:T(128)S(1)} %copy-done.6, bf16[8192,512]{1,0:T(8,128)(2,1)S(1)} %copy-done, bf16[8192,512]{1,0:T(8,128)(2,1)S(1)} %copy-done, bf16[4,8,2048]{2,1,0:T(8,128)(2,1)S(1)} %copy-done.3, bf16[4,8,2048]{2,1,0:T(8,128)(2,1)S(1)} %collective-permute-done.19.refs_1_, ...), custom_call_target="tpu_custom_call" | custom-call | flops 536870912 | bytes 4194304 | tf_op jit(solution)/shard_map/project/pallas_call | solution.py:293
  88.7 2.0 %project.3 = f32[128,512]{1,0:T(8,128)} custom-call(s32[2]{0:T(128)S(1)} %copy-done.6, bf16[8192,512]{1,0:T(8,128)(2,1)S(1)} %copy-done, bf16[8192,512]{1,0:T(8,128)(2,1)S(1)} %copy-done, bf16[4,8,2048]{2,1,0:T(8,128)(2,1)S(1)} %copy-done.4, bf16[4,8,2048]{2,1,0:T(8,128)(2,1)S(1)} %collective-permute-done.6.refs_1_, ...), custom_call_target="tpu_custom_call" | custom-call | flops 536870912 | bytes 4194304 | tf_op jit(solution)/shard_map/project/pallas_call | solution.py:293
  (81 shorter events, 16.6 us)
Async XLA Ops:
  0.1 13.8 %copy-start.5 = (s32[2]{0:T(128)}, s32[2]{0:T(128)S(1)}, u32[]{:S(2)}) copy-start(s32[2]{0:T(128)S(1)} %pad_add_fusion.meta) | copy-start | bytes 28
  0.1 1.6 %copy-start.7 = (bf16[128,64,128]{2,1,0:T(8,128)(2,1)S(1)}, bf16[128,64,128]{2,1,0:T(8,128)(2,1)}, u32[]{:S(2)}) copy-start(bf16[128,64,128]{2,1,0:T(8,128)(2,1)} %q_hbm.3) | copy-start | bytes 6291460
  1.7 1.2 %copy-start.8 = (bf16[1024,4,128]{2,1,0:T(4,128)(2,1)S(1)}, bf16[1024,4,128]{2,1,0:T(4,128)(2,1)}, u32[]{:S(2)}) copy-start(bf16[1024,4,128]{2,1,0:T(4,128)(2,1)} %param.7) | copy-start | bytes 3145732
  9.4 4.5 %collective-permute-start.13 = (bf16[16,144,128]{2,1,0:T(8,128)(2,1)S(1)}, bf16[16,144,128]{2,1,0:T(8,128)(2,1)S(1)}, u32[]{:S(2)}, u32[]{:S(2)}) collective-permute-start(bf16[16,144,128]{2,1,0:T(8,128)(2,1)S(1)} %get-tuple-element.24), channel_id=1, source_target_pairs={{0,1},{1,0},{2,3},{3,2},{4,5},{5,4},{6,7},{7,6},{8,9},{9,8},{10,11... | collective-permute-start | bytes 1769480 | tf_op jit(solution)/shard_map/ppermute | solution.py:206
  13.8 9.9 %collective-permute-start = (bf16[16,144,128]{2,1,0:T(8,128)(2,1)S(1)}, bf16[16,144,128]{2,1,0:T(8,128)(2,1)S(1)}, u32[]{:S(2)}, u32[]{:S(2)}) collective-permute-start(bf16[16,144,128]{2,1,0:T(8,128)(2,1)S(1)} %get-tuple-element.18), channel_id=1, source_target_pairs={{0,1},{1,0},{2,3},{3,2},{4,5},{5,4},{6,7},{7,6},{8,9},{9,8},{10,11... | collective-permute-start | bytes 1769480 | tf_op jit(solution)/shard_map/ppermute | solution.py:206
  16.9 11.9 %collective-permute-start.14 = (bf16[4,144,128]{2,1,0:T(8,128)(2,1)}, bf16[4,144,128]{2,1,0:T(8,128)(2,1)S(1)}, u32[]{:S(2)}, u32[]{:S(2)}) collective-permute-start(bf16[4,144,128]{2,1,0:T(8,128)(2,1)} %get-tuple-element.26), channel_id=1, source_target_pairs={{0,2},{1,3},{2,0},{3,1},{4,6},{5,7},{6,4},{7,5},{8,10},{9,11},{10,... | collective-permute-start | bytes 442376 | tf_op jit(solution)/shard_map/ppermute | solution.py:206
  19.8 10.5 %collective-permute-start.15 = (bf16[4,144,128]{2,1,0:T(8,128)(2,1)}, bf16[4,144,128]{2,1,0:T(8,128)(2,1)S(1)}, u32[]{:S(2)}, u32[]{:S(2)}) collective-permute-start(bf16[4,144,128]{2,1,0:T(8,128)(2,1)} %get-tuple-element.27), channel_id=1, source_target_pairs={{0,4},{1,5},{2,6},{3,7},{4,0},{5,1},{6,2},{7,3},{8,12},{9,13},{10,... | collective-permute-start | bytes 442376 | tf_op jit(solution)/shard_map/ppermute | solution.py:206
  22.2 9.1 %collective-permute-start.16 = (bf16[4,144,128]{2,1,0:T(8,128)(2,1)}, bf16[4,144,128]{2,1,0:T(8,128)(2,1)S(1)}, u32[]{:S(2)}, u32[]{:S(2)}) collective-permute-start(bf16[4,144,128]{2,1,0:T(8,128)(2,1)} %get-tuple-element.28), channel_id=1, source_target_pairs={{0,6},{1,7},{2,4},{3,5},{4,2},{5,3},{6,0},{7,1},{8,14},{9,15},{10,... | collective-permute-start | bytes 442376 | tf_op jit(solution)/shard_map/ppermute | solution.py:206
  26.7 9.3 %collective-permute-start.1 = (bf16[4,144,128]{2,1,0:T(8,128)(2,1)}, bf16[4,144,128]{2,1,0:T(8,128)(2,1)S(1)}, u32[]{:S(2)}, u32[]{:S(2)}) collective-permute-start(bf16[4,144,128]{2,1,0:T(8,128)(2,1)} %get-tuple-element.20), channel_id=1, source_target_pairs={{0,2},{1,3},{2,0},{3,1},{4,6},{5,7},{6,4},{7,5},{8,10},{9,11},{10,... | collective-permute-start | bytes 442376 | tf_op jit(solution)/shard_map/ppermute | solution.py:206
  27.3 8.8 %collective-permute-start.2 = (bf16[4,144,128]{2,1,0:T(8,128)(2,1)}, bf16[4,144,128]{2,1,0:T(8,128)(2,1)S(1)}, u32[]{:S(2)}, u32[]{:S(2)}) collective-permute-start(bf16[4,144,128]{2,1,0:T(8,128)(2,1)} %get-tuple-element.21), channel_id=1, source_target_pairs={{0,4},{1,5},{2,6},{3,7},{4,0},{5,1},{6,2},{7,3},{8,12},{9,13},{10,... | collective-permute-start | bytes 442376 | tf_op jit(solution)/shard_map/ppermute | solution.py:206
  28.7 2.6 %copy-start.18 = (bf16[4,144,128]{2,1,0:T(8,128)(2,1)}, bf16[4,144,128]{2,1,0:T(8,128)(2,1)S(1)}, u32[]{:S(2)}) copy-start(bf16[4,144,128]{2,1,0:T(8,128)(2,1)S(1)} %collective-permute-done.14.refs_1_) | copy-start | bytes 442372
  28.7 8.3 %collective-permute-start.3 = (bf16[4,144,128]{2,1,0:T(8,128)(2,1)}, bf16[4,144,128]{2,1,0:T(8,128)(2,1)S(1)}, u32[]{:S(2)}, u32[]{:S(2)}) collective-permute-start(bf16[4,144,128]{2,1,0:T(8,128)(2,1)} %get-tuple-element.22), channel_id=1, source_target_pairs={{0,6},{1,7},{2,4},{3,5},{4,2},{5,3},{6,0},{7,1},{8,14},{9,15},{10,... | collective-permute-start | bytes 442376 | tf_op jit(solution)/shard_map/ppermute | solution.py:206
  33.9 8.1 %collective-permute-start.17 = (bf16[4,144,128]{2,1,0:T(8,128)(2,1)}, bf16[4,144,128]{2,1,0:T(8,128)(2,1)S(1)}, u32[]{:S(2)}, u32[]{:S(2)}) collective-permute-start(bf16[4,144,128]{2,1,0:T(8,128)(2,1)} %merge_chips.6.refs_0_), channel_id=1, source_target_pairs={{0,8},{1,9},{2,10},{3,11},{4,12},{5,13},{6,14},{7,15},{8,0},{9,1},... | collective-permute-start | bytes 442376 | tf_op jit(solution)/shard_map/ppermute | solution.py:206
  39.7 13.6 %collective-permute-start.4 = (bf16[4,144,128]{2,1,0:T(8,128)(2,1)}, bf16[4,144,128]{2,1,0:T(8,128)(2,1)S(1)}, u32[]{:S(2)}, u32[]{:S(2)}) collective-permute-start(bf16[4,144,128]{2,1,0:T(8,128)(2,1)} %merge_chips.4.refs_0_), channel_id=1, source_target_pairs={{0,8},{1,9},{2,10},{3,11},{4,12},{5,13},{6,14},{7,15},{8,0},{9,1},... | collective-permute-start | bytes 442376 | tf_op jit(solution)/shard_map/ppermute | solution.py:206
  44.4 18.9 %collective-permute-start.18 = (bf16[4,144,128]{2,1,0:T(8,128)(2,1)}, bf16[4,144,128]{2,1,0:T(8,128)(2,1)S(1)}, u32[]{:S(2)}, u32[]{:S(2)}) collective-permute-start(bf16[4,144,128]{2,1,0:T(8,128)(2,1)} %merge_chips.7.refs_0_), channel_id=1, source_target_pairs={{0,16},{1,17},{2,18},{3,19},{4,20},{5,21},{6,22},{7,23},{8,24},{9,... | collective-permute-start | bytes 442376 | tf_op jit(solution)/shard_map/ppermute | solution.py:206
  55.6 13.7 %collective-permute-start.5 = (bf16[4,144,128]{2,1,0:T(8,128)(2,1)}, bf16[4,144,128]{2,1,0:T(8,128)(2,1)S(1)}, u32[]{:S(2)}, u32[]{:S(2)}) collective-permute-start(bf16[4,144,128]{2,1,0:T(8,128)(2,1)} %merge_chips.5.refs_0_), channel_id=1, source_target_pairs={{0,16},{1,17},{2,18},{3,19},{4,20},{5,21},{6,22},{7,23},{8,24},{9,... | collective-permute-start | bytes 442376 | tf_op jit(solution)/shard_map/ppermute | solution.py:206
  65.8 7.7 %collective-permute-start.22 = (bf16[4,8,2048]{2,1,0:T(8,128)(2,1)}, bf16[4,8,2048]{2,1,0:T(8,128)(2,1)S(1)}, u32[]{:S(2)}, u32[]{:S(2)}) collective-permute-start(bf16[4,8,2048]{2,1,0:T(8,128)(2,1)} %finish.3.refs_0_), channel_id=1, source_target_pairs={{0,1},{1,0},{2,3},{3,2},{4,5},{5,4},{6,7},{7,6},{8,9},{9,8},{10,11... | collective-permute-start | bytes 393224 | tf_op jit(solution)/shard_map/ppermute | solution.py:206
  65.8 9.1 %collective-permute-start.21 = (bf16[4,8,2048]{2,1,0:T(8,128)(2,1)}, bf16[4,8,2048]{2,1,0:T(8,128)(2,1)S(1)}, u32[]{:S(2)}, u32[]{:S(2)}) collective-permute-start(bf16[4,8,2048]{2,1,0:T(8,128)(2,1)} %finish.3.refs_0_), channel_id=1, source_target_pairs={{0,6},{1,7},{2,4},{3,5},{4,2},{5,3},{6,0},{7,1},{8,14},{9,15},{10,... | collective-permute-start | bytes 393224 | tf_op jit(solution)/shard_map/ppermute | solution.py:206
  67.5 8.2 %collective-permute-start.20 = (bf16[4,8,2048]{2,1,0:T(8,128)(2,1)}, bf16[4,8,2048]{2,1,0:T(8,128)(2,1)S(1)}, u32[]{:S(2)}, u32[]{:S(2)}) collective-permute-start(bf16[4,8,2048]{2,1,0:T(8,128)(2,1)} %finish.3.refs_0_), channel_id=1, source_target_pairs={{0,4},{1,5},{2,6},{3,7},{4,0},{5,1},{6,2},{7,3},{8,12},{9,13},{10,... | collective-permute-start | bytes 393224 | tf_op jit(solution)/shard_map/ppermute | solution.py:206
  68.9 7.7 %collective-permute-start.19 = (bf16[4,8,2048]{2,1,0:T(8,128)(2,1)}, bf16[4,8,2048]{2,1,0:T(8,128)(2,1)S(1)}, u32[]{:S(2)}, u32[]{:S(2)}) collective-permute-start(bf16[4,8,2048]{2,1,0:T(8,128)(2,1)} %finish.3.refs_0_), channel_id=1, source_target_pairs={{0,2},{1,3},{2,0},{3,1},{4,6},{5,7},{6,4},{7,5},{8,10},{9,11},{10,... | collective-permute-start | bytes 393224 | tf_op jit(solution)/shard_map/ppermute | solution.py:206
  71.8 7.5 %collective-permute-start.8 = (bf16[4,8,2048]{2,1,0:T(8,128)(2,1)}, bf16[4,8,2048]{2,1,0:T(8,128)(2,1)S(1)}, u32[]{:S(2)}, u32[]{:S(2)}) collective-permute-start(bf16[4,8,2048]{2,1,0:T(8,128)(2,1)} %finish.2.refs_0_), channel_id=1, source_target_pairs={{0,6},{1,7},{2,4},{3,5},{4,2},{5,3},{6,0},{7,1},{8,14},{9,15},{10,... | collective-permute-start | bytes 393224 | tf_op jit(solution)/shard_map/ppermute | solution.py:206
  73.5 7.7 %collective-permute-start.7 = (bf16[4,8,2048]{2,1,0:T(8,128)(2,1)}, bf16[4,8,2048]{2,1,0:T(8,128)(2,1)S(1)}, u32[]{:S(2)}, u32[]{:S(2)}) collective-permute-start(bf16[4,8,2048]{2,1,0:T(8,128)(2,1)} %finish.2.refs_0_), channel_id=1, source_target_pairs={{0,4},{1,5},{2,6},{3,7},{4,0},{5,1},{6,2},{7,3},{8,12},{9,13},{10,... | collective-permute-start | bytes 393224 | tf_op jit(solution)/shard_map/ppermute | solution.py:206
  74.9 6.9 %collective-permute-start.6 = (bf16[4,8,2048]{2,1,0:T(8,128)(2,1)}, bf16[4,8,2048]{2,1,0:T(8,128)(2,1)S(1)}, u32[]{:S(2)}, u32[]{:S(2)}) collective-permute-start(bf16[4,8,2048]{2,1,0:T(8,128)(2,1)} %finish.2.refs_0_), channel_id=1, source_target_pairs={{0,2},{1,3},{2,0},{3,1},{4,6},{5,7},{6,4},{7,5},{8,10},{9,11},{10,... | collective-permute-start | bytes 393224 | tf_op jit(solution)/shard_map/ppermute | solution.py:206
  75.8 6.1 %collective-permute-start.25 = (bf16[4,8,2048]{2,1,0:T(8,128)(2,1)S(1)}, bf16[4,8,2048]{2,1,0:T(8,128)(2,1)S(1)}, u32[]{:S(2)}, u32[]{:S(2)}) collective-permute-start(bf16[4,8,2048]{2,1,0:T(8,128)(2,1)S(1)} %collective-permute-done.21.refs_3_), channel_id=1, source_target_pairs={{0,1},{1,0},{2,3},{3,2},{4,5},{5,4},{6,7},{7,6},{8,9},{9,8},{10,11... | collective-permute-start | bytes 393224 | tf_op jit(solution)/shard_map/ppermute | solution.py:206
  76.6 5.8 %collective-permute-start.24 = (bf16[4,8,2048]{2,1,0:T(8,128)(2,1)S(1)}, bf16[4,8,2048]{2,1,0:T(8,128)(2,1)S(1)}, u32[]{:S(2)}, u32[]{:S(2)}) collective-permute-start(bf16[4,8,2048]{2,1,0:T(8,128)(2,1)S(1)} %collective-permute-done.20.refs_2_), channel_id=1, source_target_pairs={{0,1},{1,0},{2,3},{3,2},{4,5},{5,4},{6,7},{7,6},{8,9},{9,8},{10,11... | collective-permute-start | bytes 393224 | tf_op jit(solution)/shard_map/ppermute | solution.py:206
  79.3 3.1 %collective-permute-start.23 = (bf16[4,8,2048]{2,1,0:T(8,128)(2,1)S(1)}, bf16[4,8,2048]{2,1,0:T(8,128)(2,1)S(1)}, u32[]{:S(2)}, u32[]{:S(2)}) collective-permute-start(bf16[4,8,2048]{2,1,0:T(8,128)(2,1)S(1)} %collective-permute-done.19.refs_1_), channel_id=1, source_target_pairs={{0,1},{1,0},{2,3},{3,2},{4,5},{5,4},{6,7},{7,6},{8,9},{9,8},{10,11... | collective-permute-start | bytes 393224 | tf_op jit(solution)/shard_map/ppermute | solution.py:206
  81.2 7.5 %collective-permute-start.9 = (bf16[4,8,2048]{2,1,0:T(8,128)(2,1)}, bf16[4,8,2048]{2,1,0:T(8,128)(2,1)S(1)}, u32[]{:S(2)}, u32[]{:S(2)}) collective-permute-start(bf16[4,8,2048]{2,1,0:T(8,128)(2,1)} %finish.2.refs_0_), channel_id=1, source_target_pairs={{0,1},{1,0},{2,3},{3,2},{4,5},{5,4},{6,7},{7,6},{8,9},{9,8},{10,11... | collective-permute-start | bytes 393224 | tf_op jit(solution)/shard_map/ppermute | solution.py:206
  81.9 6.8 %collective-permute-start.12 = (bf16[4,8,2048]{2,1,0:T(8,128)(2,1)S(1)}, bf16[4,8,2048]{2,1,0:T(8,128)(2,1)S(1)}, u32[]{:S(2)}, u32[]{:S(2)}) collective-permute-start(bf16[4,8,2048]{2,1,0:T(8,128)(2,1)S(1)} %collective-permute-done.8.refs_3_), channel_id=1, source_target_pairs={{0,1},{1,0},{2,3},{3,2},{4,5},{5,4},{6,7},{7,6},{8,9},{9,8},{10,11... | collective-permute-start | bytes 393224 | tf_op jit(solution)/shard_map/ppermute | solution.py:206
  81.9 6.8 %collective-permute-start.11 = (bf16[4,8,2048]{2,1,0:T(8,128)(2,1)S(1)}, bf16[4,8,2048]{2,1,0:T(8,128)(2,1)S(1)}, u32[]{:S(2)}, u32[]{:S(2)}) collective-permute-start(bf16[4,8,2048]{2,1,0:T(8,128)(2,1)S(1)} %collective-permute-done.7.refs_2_), channel_id=1, source_target_pairs={{0,1},{1,0},{2,3},{3,2},{4,5},{5,4},{6,7},{7,6},{8,9},{9,8},{10,11... | collective-permute-start | bytes 393224 | tf_op jit(solution)/shard_map/ppermute | solution.py:206
  82.4 6.3 %collective-permute-start.10 = (bf16[4,8,2048]{2,1,0:T(8,128)(2,1)S(1)}, bf16[4,8,2048]{2,1,0:T(8,128)(2,1)S(1)}, u32[]{:S(2)}, u32[]{:S(2)}) collective-permute-start(bf16[4,8,2048]{2,1,0:T(8,128)(2,1)S(1)} %collective-permute-done.6.refs_1_), channel_id=1, source_target_pairs={{0,1},{1,0},{2,3},{3,2},{4,5},{5,4},{6,7},{7,6},{8,9},{9,8},{10,11... | collective-permute-start | bytes 393224 | tf_op jit(solution)/shard_map/ppermute | solution.py:206
  82.5 3.4 %copy-start = (bf16[8192,512]{1,0:T(8,128)(2,1)S(1)}, bf16[8192,512]{1,0:T(8,128)(2,1)}, u32[]{:S(2)}) copy-start(bf16[8192,512]{1,0:T(8,128)(2,1)} %w_other.3) | copy-start | bytes 25165828
  87.4 1.3 %copy-start.4 = (bf16[4,8,2048]{2,1,0:T(8,128)(2,1)S(1)}, bf16[4,8,2048]{2,1,0:T(8,128)(2,1)}, u32[]{:S(2)}) copy-start(bf16[4,8,2048]{2,1,0:T(8,128)(2,1)} %finish.2.refs_0_) | copy-start | bytes 393220
  (18 other events, 14.6 us)

commit v3 on v2

--- a/solution.py
+++ b/solution.py
@@ -26,7 +26,7 @@
 
 
 def attention_kernel(
-    chunk, scale2, meta, mask_ref, counts_ref, q_hbm, k_hbm, v_hbm, send_ref, keep_ref, *scratch
+    chunk, scale2, meta, q_hbm, k_hbm, v_hbm, send_ref, keep_ref, *scratch
 ):
     listed, kept_counts, q_ref, k_ref, v_ref, kd, vt, spread, sems = scratch
     core = meta[0]
@@ -34,7 +34,7 @@
     kv_count = spread.shape[0] // BLK
     rows = send_ref.shape[0] * LANES
     group_size = q_ref.shape[2]
-    block_count = counts_ref.shape[0]
+    block_count = (meta.shape[0] - 2) // 2
 
     copies = [
         pltpu.make_async_copy(k_hbm, k_ref, sems.at[0]),
@@ -48,8 +48,8 @@
 
     def note(block, found):
         listed[found] = block
-        kept_counts[found] = counts_ref[block]
-        return found + (mask_ref[0, block] > 0).astype(jnp.int32)
+        kept_counts[found] = meta[2 + block_count + block]
+        return found + (meta[2 + block] > 0).astype(jnp.int32)
 
     active = lax.fori_loop(0, block_count, note, jnp.int32(0))
     place = lax.broadcasted_iota(jnp.int32, (BLK, LANES), 0)
@@ -179,15 +179,16 @@
             out_ref[z, :, h * d : (h + 1) * d] = picked.astype(bf16)
 
 
-def project_kernel(last, meta, w_own, w_other, *refs):
+def project_kernel(chunk, last, meta, weight, *refs):
     own, other, refs = refs[:4], refs[4:8], refs[8:]
     z_size, tokens, depth = own[0].shape
     total = None
-    for parts, weight in ((own, w_own), (other, w_other)):
+    for parts, core in ((own, meta[0]), (other, 1 - meta[0])):
         left = jnp.concatenate(
             [part[...].reshape(z_size * tokens, depth) for part in parts], axis=0
         )
-        product = jnp.dot(left, weight[...], preferred_element_type=f32)
+        at = pl.ds(pl.multiple_of((2 * chunk + core) * depth, depth), depth)
+        product = jnp.dot(left, weight[at, :], preferred_element_type=f32)
         total = product if total is None else total + product
     if not last:
         refs[0][...] = total
@@ -209,6 +210,7 @@
 VMEM = pl.BlockSpec(memory_space=pltpu.VMEM)
 SMEM = pl.BlockSpec(memory_space=pltpu.SMEM)
 HBM = pl.BlockSpec(memory_space=pltpu.HBM)
+SMALL = pltpu.CompilerParams(vmem_limit_bytes=4 << 20)
 
 
 def fast_body(queries, cache_keys, cache_values, block_mask, key_counts, out_weight):
@@ -227,14 +229,18 @@
     scale2 = math.log2(math.e) / math.sqrt(d)
     keys = cache_keys.reshape(positions * kv_count, d)
     values = cache_values.reshape(positions * kv_count, d)
-    place = jnp.stack([core, my_xy]).astype(jnp.int32)
+    place = jnp.concatenate(
+        [jnp.stack([core, my_xy]).astype(jnp.int32), block_mask[0], key_counts]
+    )
+    kept_in_hbm = functools.partial(pltpu.with_memory_space_constraint, memory_space=pltpu.HBM)
+    queries, keys, values = kept_in_hbm(queries), kept_in_hbm(keys), kept_in_hbm(values)
     state = jax.ShapeDtypeStruct((z_size, tall, LANES), bf16)
 
     def attend(chunk):
         blocks = positions // BLK
         return pl.pallas_call(
             functools.partial(attention_kernel, chunk, scale2),
-            in_specs=[SMEM] * 3 + [HBM] * 3,
+            in_specs=[SMEM] + [HBM] * 3,
             out_specs=[VMEM] * 2,
             scratch_shapes=[
                 pltpu.SMEM((blocks + 1,), jnp.int32),
@@ -255,7 +261,7 @@
                 bytes_accessed=4 * positions * d * kv_count,
             ),
             name="attention",
-        )(place, block_mask, key_counts, queries, keys, values)
+        )(place, queries, keys, values)
 
     def merge_cores(kept, received):
         return pl.pallas_call(
@@ -263,6 +269,7 @@
             in_specs=[SMEM] + [VMEM] * 2,
             out_specs=[VMEM] * 4,
             out_shape=[state] * 4,
+            compiler_params=SMALL,
             name="merge_cores",
         )(place, kept, received)
 
@@ -272,6 +279,7 @@
             in_specs=[VMEM] * len(parts),
             out_specs=VMEM,
             out_shape=state,
+            compiler_params=SMALL,
             name="merge_chips",
         )(*parts)
 
@@ -283,35 +291,26 @@
             out_specs=VMEM,
             out_shape=jax.ShapeDtypeStruct((z_size, tokens, group_size * d), bf16),
             scratch_shapes=[pltpu.VMEM((z_size, LANES, d), f32)],
+            compiler_params=SMALL,
             name="finish",
         )(*parts)
 
     def project(chunk, own, other, earlier):
         depth = group_size * d
-        whole = [pl.BlockSpec(a.shape, lambda i, m: (0, 0, 0)) for a in own + other]
         more = [] if earlier is None else [earlier]
         return pl.pallas_call(
-            functools.partial(project_kernel, earlier is not None),
-            grid_spec=pltpu.PrefetchScalarGridSpec(
-                num_scalar_prefetch=1,
-                grid=(1,),
-                in_specs=[
-                    pl.BlockSpec((depth, features), lambda i, m: (2 * chunk + m[0], 0)),
-                    pl.BlockSpec((depth, features), lambda i, m: (2 * chunk + 1 - m[0], 0)),
-                ]
-                + whole
-                + [VMEM] * len(more),
-                out_specs=VMEM,
-            ),
+            functools.partial(project_kernel, chunk, earlier is not None),
+            in_specs=[SMEM] + [VMEM] * (1 + len(own + other + more)),
+            out_specs=VMEM,
             out_shape=jax.ShapeDtypeStruct((token_count, features), f32),
-            compiler_params=pltpu.CompilerParams(vmem_limit_bytes=32 << 20),
+            compiler_params=pltpu.CompilerParams(vmem_limit_bytes=8 << 20),
             cost_estimate=pl.CostEstimate(
                 flops=4 * token_count * depth * features,
                 transcendentals=0,
                 bytes_accessed=4 * depth * features,
             ),
             name="project",
-        )(place, out_weight, out_weight, *own, *other, *more)
+        )(place, out_weight, *own, *other, *more)
 
     chunks = kv_count // 2
     partials = []

time: 89.8 us -> 69.9 us (0.78)
  local copies, waits for them, and re-layouts: 17.6 us -> 0.01 us
  waiting for transfers between devices: 14.6 us -> 24.2 us
  Pallas kernels: 25 us -> 17.5 us
  starting transfers between devices: 33.3 us -> 28.6 us
    unnamed x48 -> x4, local copies, waits for them, and re-layouts: 17.6 us -> 0.01 us
    ppermute x26, waiting for transfers between devices: 14.6 us -> 24.2 us  [hop(): return lax.ppermute(value, 'ctx', pairs)]
    pallas_call x4, Pallas kernels: 7.32 us -> 0.47 us  [merge_chips(): pl.pallas_call(plane_kernel, in_specs=[VMEM] * len(parts), out_specs=VMEM...]
    pallas_call x2, Pallas kernels: 6.38 us -> 11.7 us  [attend(): pl.pallas_call(functools.partial(attention_kernel, chunk, scale2), in_spe...]
    ppermute x26, starting transfers between devices: 33.3 us -> 28.6 us  [hop(): return lax.ppermute(value, 'ctx', pairs)]
    pallas_call x2, Pallas kernels: 3.69 us -> 0.41 us  [finish(): pl.pallas_call(last_kernel, in_specs=[VMEM] * len(parts), out_specs=VMEM,...]
    pallas_call x2, Pallas kernels: 4.4 us -> 1.64 us  [merge_cores(): pl.pallas_call(core_kernel, in_specs=[SMEM] + [VMEM] * 2, out_specs=[VMEM...]
  transfers between devices with their start and end apart: 26 -> 26, of which waited for: 8 -> 11; matrix products, arithmetic and copies ran while one was open for 0% -> 0% of each run, Pallas kernels for 22% -> 14%
where the time goes in v3:
time: 69.9 us; the launch traced here: 71.2 us
  starting transfers between devices  28.6 us (41%)
  waiting for transfers between devices  24.2 us (35%)
  Pallas kernels  17.5 us (25%)
  other arithmetic  0.75 us (1%)
    ppermute x26, starting transfers between devices, hop(): return lax.ppermute(value, 'ctx', pairs)  28.6 us
    ppermute x26, waiting for transfers between devices, hop(): return lax.ppermute(value, 'ctx', pairs)  24.2 us
    pallas_call x2, Pallas kernels, attend(): pl.pallas_call(functools.partial(attention_kernel, chunk, scale2), in_spe...  11.7 us
    pallas_call x2, Pallas kernels, project(): pl.pallas_call(functools.partial(project_kernel, chunk, earlier is not No...  3.23 us
    pallas_call x2, Pallas kernels, merge_cores(): pl.pallas_call(core_kernel, in_specs=[SMEM] + [VMEM] * 2, out_specs=[VMEM...  1.64 us
  transfers between devices with their start and end apart: 26, of which 11 were waited for; matrix products, arithmetic and copies ran while one was open for 0% of the time, Pallas kernels for 14%

profile of v3, /device:TPU:0, one launch (start us, length us, event | category | flops | bytes accessed | tf_op | source)
XLA Modules:
  0.0 71.2 jit_solution(4414456627363853692)
XLA Ops:
  0.0 0.7 %pad_add_fusion.meta = s32[18]{0:T(128)S(1)} fusion(s32[8]{0:T(128)} %param.10, s32[8]{0:T(128)} %bitcast.7, s32[1]{0:T(128)} %bitcast.1, s32[1]{0:T(128)} %bitcast), kind=kLoop, calls=%fused_computation | loop fusion | flops 54 | bytes 144 | tf_op jit(solution)/shard_map/concatenate | solution.py:232
  0.8 5.8 %attention.3 = (bf16[16,144,128]{2,1,0:T(8,128)(2,1)S(1)}, bf16[16,144,128]{2,1,0:T(8,128)(2,1)S(1)}) custom-call(s32[18]{0:T(128)S(1)} %pad_add_fusion.meta, bf16[128,64,128]{2,1,0:T(8,128)(2,1)} %q_hbm.3, bf16[4096,128]{1,0:T(8,128)(2,1)} %bitcast.8, bf16[4096,128]{1,0:T(8,128)(2,1)} %bitcast.10), custom_call_target="tpu_custom_call" | custom-call | flops 2147483648 | bytes 2097152 | tf_op jit(solution)/shard_map/attention/pallas_call | solution.py:241
  6.6 6.0 %attention.2 = (bf16[16,144,128]{2,1,0:T(8,128)(2,1)S(1)}, bf16[16,144,128]{2,1,0:T(8,128)(2,1)S(1)}) custom-call(s32[18]{0:T(128)S(1)} %pad_add_fusion.meta, bf16[128,64,128]{2,1,0:T(8,128)(2,1)} %q_hbm.3, bf16[4096,128]{1,0:T(8,128)(2,1)} %bitcast.9, bf16[4096,128]{1,0:T(8,128)(2,1)} %bitcast.11), custom_call_target="tpu_custom_call" | custom-call | flops 2147483648 | bytes 2097152 | tf_op jit(solution)/shard_map/attention/pallas_call | solution.py:241
  12.7 0.8 %merge_cores.3 = (bf16[4,144,128]{2,1,0:T(8,128)(2,1)S(1)}, bf16[4,144,128]{2,1,0:T(8,128)(2,1)S(1)}, bf16[4,144,128]{2,1,0:T(8,128)(2,1)S(1)}, bf16[4,144,128]{2,1,0:T(8,128)(2,1)S(1)}) custom-call(s32[18]{0:T(128)S(1)} %pad_add_fusion.meta, bf16[16,144,128]{2,1,0:T(8,128)(2,1)S(1)} %get-tuple-element.23.kept, ...), custom_call_target="tpu_custom_call" | custom-call | tf_op jit(solution)/shard_map/merge_cores/pallas_call | solution.py:267
  13.5 3.0 %collective-permute-start.14 = (bf16[4,144,128]{2,1,0:T(8,128)(2,1)S(1)}, bf16[4,144,128]{2,1,0:T(8,128)(2,1)S(1)}, u32[]{:S(2)}, u32[]{:S(2)}) collective-permute-start(bf16[4,144,128]{2,1,0:T(8,128)(2,1)S(1)} %get-tuple-element.26), channel_id=1, source_target_pairs={{0,2},{1,3},{2,0},{3,1},{4,6},{5,7},{6,4},{7,5},{8,10},{9,11},{10,... | collective-permute-start | bytes 442376 | tf_op jit(solution)/shard_map/ppermute | solution.py:207
  16.5 1.5 %collective-permute-start.16 = (bf16[4,144,128]{2,1,0:T(8,128)(2,1)S(1)}, bf16[4,144,128]{2,1,0:T(8,128)(2,1)S(1)}, u32[]{:S(2)}, u32[]{:S(2)}) collective-permute-start(bf16[4,144,128]{2,1,0:T(8,128)(2,1)S(1)} %get-tuple-element.28), channel_id=1, source_target_pairs={{0,6},{1,7},{2,4},{3,5},{4,2},{5,3},{6,0},{7,1},{8,14},{9,15},{10,... | collective-permute-start | bytes 442376 | tf_op jit(solution)/shard_map/ppermute | solution.py:207
  18.1 0.8 %merge_cores.2 = (bf16[4,144,128]{2,1,0:T(8,128)(2,1)S(1)}, bf16[4,144,128]{2,1,0:T(8,128)(2,1)S(1)}, bf16[4,144,128]{2,1,0:T(8,128)(2,1)S(1)}, bf16[4,144,128]{2,1,0:T(8,128)(2,1)S(1)}) custom-call(s32[18]{0:T(128)S(1)} %pad_add_fusion.meta, bf16[16,144,128]{2,1,0:T(8,128)(2,1)S(1)} %get-tuple-element.17.kept, ...), custom_call_target="tpu_custom_call" | custom-call | tf_op jit(solution)/shard_map/merge_cores/pallas_call | solution.py:267
  18.9 2.0 %collective-permute-start.1 = (bf16[4,144,128]{2,1,0:T(8,128)(2,1)S(1)}, bf16[4,144,128]{2,1,0:T(8,128)(2,1)S(1)}, u32[]{:S(2)}, u32[]{:S(2)}) collective-permute-start(bf16[4,144,128]{2,1,0:T(8,128)(2,1)S(1)} %get-tuple-element.20), channel_id=1, source_target_pairs={{0,2},{1,3},{2,0},{3,1},{4,6},{5,7},{6,4},{7,5},{8,10},{9,11},{10,... | collective-permute-start | bytes 442376 | tf_op jit(solution)/shard_map/ppermute | solution.py:207
  21.0 1.4 %collective-permute-start.3 = (bf16[4,144,128]{2,1,0:T(8,128)(2,1)S(1)}, bf16[4,144,128]{2,1,0:T(8,128)(2,1)S(1)}, u32[]{:S(2)}, u32[]{:S(2)}) collective-permute-start(bf16[4,144,128]{2,1,0:T(8,128)(2,1)S(1)} %get-tuple-element.22), channel_id=1, source_target_pairs={{0,6},{1,7},{2,4},{3,5},{4,2},{5,3},{6,0},{7,1},{8,14},{9,15},{10,... | collective-permute-start | bytes 442376 | tf_op jit(solution)/shard_map/ppermute | solution.py:207
  22.5 5.0 %collective-permute-done.15.refs_2_ = bf16[4,144,128]{2,1,0:T(8,128)(2,1)S(1)} collective-permute-done((bf16[4,144,128]{2,1,0:T(8,128)(2,1)S(1)}, bf16[4,144,128]{2,1,0:T(8,128)(2,1)S(1)}, u32[]{:S(2)}, u32[]{:S(2)}) %collective-permute-start.15) | collective-permute-done | bytes 147488 | tf_op jit(solution)/shard_map/ppermute | solution.py:207
  27.6 7.6 %collective-permute-start.17 = (bf16[4,144,128]{2,1,0:T(8,128)(2,1)S(1)}, bf16[4,144,128]{2,1,0:T(8,128)(2,1)S(1)}, u32[]{:S(2)}, u32[]{:S(2)}) collective-permute-start(bf16[4,144,128]{2,1,0:T(8,128)(2,1)S(1)} %merge_chips.6.refs_0_), channel_id=1, source_target_pairs={{0,8},{1,9},{2,10},{3,11},{4,12},{5,13},{6,14},{7,15},{8,0},{9,1},... | collective-permute-start | bytes 442376 | tf_op jit(solution)/shard_map/ppermute | solution.py:207
  35.3 4.9 %collective-permute-start.4 = (bf16[4,144,128]{2,1,0:T(8,128)(2,1)S(1)}, bf16[4,144,128]{2,1,0:T(8,128)(2,1)S(1)}, u32[]{:S(2)}, u32[]{:S(2)}) collective-permute-start(bf16[4,144,128]{2,1,0:T(8,128)(2,1)S(1)} %merge_chips.4.refs_0_), channel_id=1, source_target_pairs={{0,8},{1,9},{2,10},{3,11},{4,12},{5,13},{6,14},{7,15},{8,0},{9,1},... | collective-permute-start | bytes 442376 | tf_op jit(solution)/shard_map/ppermute | solution.py:207
  40.4 4.1 %collective-permute-done.4.refs_1_ = bf16[4,144,128]{2,1,0:T(8,128)(2,1)S(1)} collective-permute-done((bf16[4,144,128]{2,1,0:T(8,128)(2,1)S(1)}, bf16[4,144,128]{2,1,0:T(8,128)(2,1)S(1)}, u32[]{:S(2)}, u32[]{:S(2)}) %collective-permute-start.4) | collective-permute-done | bytes 147488 | tf_op jit(solution)/shard_map/ppermute | solution.py:207
  44.7 6.0 %collective-permute-done.18.refs_1_ = bf16[4,144,128]{2,1,0:T(8,128)(2,1)S(1)} collective-permute-done((bf16[4,144,128]{2,1,0:T(8,128)(2,1)S(1)}, bf16[4,144,128]{2,1,0:T(8,128)(2,1)S(1)}, u32[]{:S(2)}, u32[]{:S(2)}) %collective-permute-start.18) | collective-permute-done | bytes 147488 | tf_op jit(solution)/shard_map/ppermute | solution.py:207
  50.7 0.2 finish.3.refs_0_
  51.0 1.6 %collective-permute-start.21 = (bf16[4,8,2048]{2,1,0:T(8,128)(2,1)S(1)}, bf16[4,8,2048]{2,1,0:T(8,128)(2,1)S(1)}, u32[]{:S(2)}, u32[]{:S(2)}) collective-permute-start(bf16[4,8,2048]{2,1,0:T(8,128)(2,1)S(1)} %finish.3.refs_0_), channel_id=1, source_target_pairs={{0,6},{1,7},{2,4},{3,5},{4,2},{5,3},{6,0},{7,1},{8,14},{9,15},{10,... | collective-permute-start | bytes 393224 | tf_op jit(solution)/shard_map/ppermute | solution.py:207
  52.6 1.0 %collective-permute-start.20 = (bf16[4,8,2048]{2,1,0:T(8,128)(2,1)S(1)}, bf16[4,8,2048]{2,1,0:T(8,128)(2,1)S(1)}, u32[]{:S(2)}, u32[]{:S(2)}) collective-permute-start(bf16[4,8,2048]{2,1,0:T(8,128)(2,1)S(1)} %finish.3.refs_0_), channel_id=1, source_target_pairs={{0,4},{1,5},{2,6},{3,7},{4,0},{5,1},{6,2},{7,3},{8,12},{9,13},{10,... | collective-permute-start | bytes 393224 | tf_op jit(solution)/shard_map/ppermute | solution.py:207
  53.6 1.4 %collective-permute-start.19 = (bf16[4,8,2048]{2,1,0:T(8,128)(2,1)S(1)}, bf16[4,8,2048]{2,1,0:T(8,128)(2,1)S(1)}, u32[]{:S(2)}, u32[]{:S(2)}) collective-permute-start(bf16[4,8,2048]{2,1,0:T(8,128)(2,1)S(1)} %finish.3.refs_0_), channel_id=1, source_target_pairs={{0,2},{1,3},{2,0},{3,1},{4,6},{5,7},{6,4},{7,5},{8,10},{9,11},{10,... | collective-permute-start | bytes 393224 | tf_op jit(solution)/shard_map/ppermute | solution.py:207
  55.0 0.3 collective-permute-done.5.refs_1_
  55.4 0.2 finish.2.refs_0_
  55.6 1.6 %collective-permute-start.8 = (bf16[4,8,2048]{2,1,0:T(8,128)(2,1)S(1)}, bf16[4,8,2048]{2,1,0:T(8,128)(2,1)S(1)}, u32[]{:S(2)}, u32[]{:S(2)}) collective-permute-start(bf16[4,8,2048]{2,1,0:T(8,128)(2,1)S(1)} %finish.2.refs_0_), channel_id=1, source_target_pairs={{0,6},{1,7},{2,4},{3,5},{4,2},{5,3},{6,0},{7,1},{8,14},{9,15},{10,... | collective-permute-start | bytes 393224 | tf_op jit(solution)/shard_map/ppermute | solution.py:207
  57.2 0.6 collective-permute-start.7
  57.8 0.5 collective-permute-done.21.refs_3_
  58.3 0.9 %collective-permute-start.6 = (bf16[4,8,2048]{2,1,0:T(8,128)(2,1)S(1)}, bf16[4,8,2048]{2,1,0:T(8,128)(2,1)S(1)}, u32[]{:S(2)}, u32[]{:S(2)}) collective-permute-start(bf16[4,8,2048]{2,1,0:T(8,128)(2,1)S(1)} %finish.2.refs_0_), channel_id=1, source_target_pairs={{0,2},{1,3},{2,0},{3,1},{4,6},{5,7},{6,4},{7,5},{8,10},{9,11},{10,... | collective-permute-start | bytes 393224 | tf_op jit(solution)/shard_map/ppermute | solution.py:207
  59.2 2.0 %collective-permute-done.20.refs_2_ = bf16[4,8,2048]{2,1,0:T(8,128)(2,1)S(1)} collective-permute-done((bf16[4,8,2048]{2,1,0:T(8,128)(2,1)S(1)}, bf16[4,8,2048]{2,1,0:T(8,128)(2,1)S(1)}, u32[]{:S(2)}, u32[]{:S(2)}) %collective-permute-start.20) | collective-permute-done | bytes 131104 | tf_op jit(solution)/shard_map/ppermute | solution.py:207
  61.2 1.0 %collective-permute-done.19.refs_1_ = bf16[4,8,2048]{2,1,0:T(8,128)(2,1)S(1)} collective-permute-done((bf16[4,8,2048]{2,1,0:T(8,128)(2,1)S(1)}, bf16[4,8,2048]{2,1,0:T(8,128)(2,1)S(1)}, u32[]{:S(2)}, u32[]{:S(2)}) %collective-permute-start.19) | collective-permute-done | bytes 131104 | tf_op jit(solution)/shard_map/ppermute | solution.py:207
  62.1 1.8 %collective-permute-done.8.refs_3_ = bf16[4,8,2048]{2,1,0:T(8,128)(2,1)S(1)} collective-permute-done((bf16[4,8,2048]{2,1,0:T(8,128)(2,1)S(1)}, bf16[4,8,2048]{2,1,0:T(8,128)(2,1)S(1)}, u32[]{:S(2)}, u32[]{:S(2)}) %collective-permute-start.8) | collective-permute-done | bytes 131104 | tf_op jit(solution)/shard_map/ppermute | solution.py:207
  64.0 2.3 %collective-permute-done.7.refs_2_ = bf16[4,8,2048]{2,1,0:T(8,128)(2,1)S(1)} collective-permute-done((bf16[4,8,2048]{2,1,0:T(8,128)(2,1)S(1)}, bf16[4,8,2048]{2,1,0:T(8,128)(2,1)S(1)}, u32[]{:S(2)}, u32[]{:S(2)}) %collective-permute-start.7) | collective-permute-done | bytes 131104 | tf_op jit(solution)/shard_map/ppermute | solution.py:207
  66.3 1.1 %collective-permute-done.6.refs_1_ = bf16[4,8,2048]{2,1,0:T(8,128)(2,1)S(1)} collective-permute-done((bf16[4,8,2048]{2,1,0:T(8,128)(2,1)S(1)}, bf16[4,8,2048]{2,1,0:T(8,128)(2,1)S(1)}, u32[]{:S(2)}, u32[]{:S(2)}) %collective-permute-start.6) | collective-permute-done | bytes 131104 | tf_op jit(solution)/shard_map/ppermute | solution.py:207
  67.3 0.5 collective-permute-start.11
  68.0 1.3 %project.2.refs_8_ = f32[128,512]{1,0:T(8,128)S(1)} custom-call(s32[18]{0:T(128)S(1)} %pad_add_fusion.meta, bf16[8192,512]{1,0:T(8,128)(2,1)S(1)} %bitcast.6, bf16[4,8,2048]{2,1,0:T(8,128)(2,1)S(1)} %finish.3.refs_0_, bf16[4,8,2048]{2,1,0:T(8,128)(2,1)S(1)} %collective-permute-done.19.refs_1_, bf16[4,8,2048]{2,1,0:T(8,128)(2,1)S(1)} %collective-permute-done.20.refs_2_, ...), custom_call_target="tpu_custom_call" | custom-call | flops 536870912 | bytes 4194304 | tf_op jit(solution)/shard_map/project/pallas_call | solution.py:301
  69.3 2.0 %project.3 = f32[128,512]{1,0:T(8,128)} custom-call(s32[18]{0:T(128)S(1)} %pad_add_fusion.meta, bf16[8192,512]{1,0:T(8,128)(2,1)S(1)} %bitcast.6, bf16[4,8,2048]{2,1,0:T(8,128)(2,1)S(1)} %finish.2.refs_0_, bf16[4,8,2048]{2,1,0:T(8,128)(2,1)S(1)} %collective-permute-done.6.refs_1_, bf16[4,8,2048]{2,1,0:T(8,128)(2,1)S(1)} %collective-permute-done.7.refs_2_, ...), custom_call_target="tpu_custom_call" | custom-call | flops 536870912 | bytes 4194304 | tf_op jit(solution)/shard_map/project/pallas_call | solution.py:301
  (38 shorter events, 1.1 us)
Async XLA Ops:
  0.7 67.2 %slice-start = ((s8[8388608]{0:T(1024)(128)(4,1)}), s8[4194304]{0:T(1024)(128)(4,1)S(1)}, s32[]{:S(2)}) async-start(s8[8388608]{0:T(1024)(128)(4,1)} %bitcast.5), calls=%async_computation | async-start | bytes 8388608
  6.5 61.4 %slice-start.1 = ((s8[8388608]{0:T(1024)(128)(4,1)}), s8[4194304]{0:T(1024)(128)(4,1)S(1)}, s32[]{:S(2)}) async-start(s8[8388608]{0:T(1024)(128)(4,1)} %bitcast.5), calls=%async_computation.1 | async-start | bytes 8388608
  6.5 6.2 %collective-permute-start.13 = (bf16[16,144,128]{2,1,0:T(8,128)(2,1)S(1)}, bf16[16,144,128]{2,1,0:T(8,128)(2,1)S(1)}, u32[]{:S(2)}, u32[]{:S(2)}) collective-permute-start(bf16[16,144,128]{2,1,0:T(8,128)(2,1)S(1)} %get-tuple-element.24), channel_id=1, source_target_pairs={{0,1},{1,0},{2,3},{3,2},{4,5},{5,4},{6,7},{7,6},{8,9},{9,8},{10,11... | collective-permute-start | bytes 1769480 | tf_op jit(solution)/shard_map/ppermute | solution.py:207
  12.6 5.5 %collective-permute-start = (bf16[16,144,128]{2,1,0:T(8,128)(2,1)S(1)}, bf16[16,144,128]{2,1,0:T(8,128)(2,1)S(1)}, u32[]{:S(2)}, u32[]{:S(2)}) collective-permute-start(bf16[16,144,128]{2,1,0:T(8,128)(2,1)S(1)} %get-tuple-element.18), channel_id=1, source_target_pairs={{0,1},{1,0},{2,3},{3,2},{4,5},{5,4},{6,7},{7,6},{8,9},{9,8},{10,11... | collective-permute-start | bytes 1769480 | tf_op jit(solution)/shard_map/ppermute | solution.py:207
  13.5 7.5 %collective-permute-start.14 = (bf16[4,144,128]{2,1,0:T(8,128)(2,1)S(1)}, bf16[4,144,128]{2,1,0:T(8,128)(2,1)S(1)}, u32[]{:S(2)}, u32[]{:S(2)}) collective-permute-start(bf16[4,144,128]{2,1,0:T(8,128)(2,1)S(1)} %get-tuple-element.26), channel_id=1, source_target_pairs={{0,2},{1,3},{2,0},{3,1},{4,6},{5,7},{6,4},{7,5},{8,10},{9,11},{10,... | collective-permute-start | bytes 442376 | tf_op jit(solution)/shard_map/ppermute | solution.py:207
  16.5 10.9 %collective-permute-start.15 = (bf16[4,144,128]{2,1,0:T(8,128)(2,1)S(1)}, bf16[4,144,128]{2,1,0:T(8,128)(2,1)S(1)}, u32[]{:S(2)}, u32[]{:S(2)}) collective-permute-start(bf16[4,144,128]{2,1,0:T(8,128)(2,1)S(1)} %get-tuple-element.27), channel_id=1, source_target_pairs={{0,4},{1,5},{2,6},{3,7},{4,0},{5,1},{6,2},{7,3},{8,12},{9,13},{10,... | collective-permute-start | bytes 442376 | tf_op jit(solution)/shard_map/ppermute | solution.py:207
  16.5 10.9 %collective-permute-start.16 = (bf16[4,144,128]{2,1,0:T(8,128)(2,1)S(1)}, bf16[4,144,128]{2,1,0:T(8,128)(2,1)S(1)}, u32[]{:S(2)}, u32[]{:S(2)}) collective-permute-start(bf16[4,144,128]{2,1,0:T(8,128)(2,1)S(1)} %get-tuple-element.28), channel_id=1, source_target_pairs={{0,6},{1,7},{2,4},{3,5},{4,2},{5,3},{6,0},{7,1},{8,14},{9,15},{10,... | collective-permute-start | bytes 442376 | tf_op jit(solution)/shard_map/ppermute | solution.py:207
  18.9 16.3 %collective-permute-start.1 = (bf16[4,144,128]{2,1,0:T(8,128)(2,1)S(1)}, bf16[4,144,128]{2,1,0:T(8,128)(2,1)S(1)}, u32[]{:S(2)}, u32[]{:S(2)}) collective-permute-start(bf16[4,144,128]{2,1,0:T(8,128)(2,1)S(1)} %get-tuple-element.20), channel_id=1, source_target_pairs={{0,2},{1,3},{2,0},{3,1},{4,6},{5,7},{6,4},{7,5},{8,10},{9,11},{10,... | collective-permute-start | bytes 442376 | tf_op jit(solution)/shard_map/ppermute | solution.py:207
  20.9 14.2 %collective-permute-start.2 = (bf16[4,144,128]{2,1,0:T(8,128)(2,1)S(1)}, bf16[4,144,128]{2,1,0:T(8,128)(2,1)S(1)}, u32[]{:S(2)}, u32[]{:S(2)}) collective-permute-start(bf16[4,144,128]{2,1,0:T(8,128)(2,1)S(1)} %get-tuple-element.21), channel_id=1, source_target_pairs={{0,4},{1,5},{2,6},{3,7},{4,0},{5,1},{6,2},{7,3},{8,12},{9,13},{10,... | collective-permute-start | bytes 442376 | tf_op jit(solution)/shard_map/ppermute | solution.py:207
  21.0 14.1 %collective-permute-start.3 = (bf16[4,144,128]{2,1,0:T(8,128)(2,1)S(1)}, bf16[4,144,128]{2,1,0:T(8,128)(2,1)S(1)}, u32[]{:S(2)}, u32[]{:S(2)}) collective-permute-start(bf16[4,144,128]{2,1,0:T(8,128)(2,1)S(1)} %get-tuple-element.22), channel_id=1, source_target_pairs={{0,6},{1,7},{2,4},{3,5},{4,2},{5,3},{6,0},{7,1},{8,14},{9,15},{10,... | collective-permute-start | bytes 442376 | tf_op jit(solution)/shard_map/ppermute | solution.py:207
  27.6 12.6 %collective-permute-start.17 = (bf16[4,144,128]{2,1,0:T(8,128)(2,1)S(1)}, bf16[4,144,128]{2,1,0:T(8,128)(2,1)S(1)}, u32[]{:S(2)}, u32[]{:S(2)}) collective-permute-start(bf16[4,144,128]{2,1,0:T(8,128)(2,1)S(1)} %merge_chips.6.refs_0_), channel_id=1, source_target_pairs={{0,8},{1,9},{2,10},{3,11},{4,12},{5,13},{6,14},{7,15},{8,0},{9,1},... | collective-permute-start | bytes 442376 | tf_op jit(solution)/shard_map/ppermute | solution.py:207
  35.3 9.2 %collective-permute-start.4 = (bf16[4,144,128]{2,1,0:T(8,128)(2,1)S(1)}, bf16[4,144,128]{2,1,0:T(8,128)(2,1)S(1)}, u32[]{:S(2)}, u32[]{:S(2)}) collective-permute-start(bf16[4,144,128]{2,1,0:T(8,128)(2,1)S(1)} %merge_chips.4.refs_0_), channel_id=1, source_target_pairs={{0,8},{1,9},{2,10},{3,11},{4,12},{5,13},{6,14},{7,15},{8,0},{9,1},... | collective-permute-start | bytes 442376 | tf_op jit(solution)/shard_map/ppermute | solution.py:207
  40.3 10.4 %collective-permute-start.18 = (bf16[4,144,128]{2,1,0:T(8,128)(2,1)S(1)}, bf16[4,144,128]{2,1,0:T(8,128)(2,1)S(1)}, u32[]{:S(2)}, u32[]{:S(2)}) collective-permute-start(bf16[4,144,128]{2,1,0:T(8,128)(2,1)S(1)} %merge_chips.7.refs_0_), channel_id=1, source_target_pairs={{0,16},{1,17},{2,18},{3,19},{4,20},{5,21},{6,22},{7,23},{8,24},{9,... | collective-permute-start | bytes 442376 | tf_op jit(solution)/shard_map/ppermute | solution.py:207
  44.6 10.7 %collective-permute-start.5 = (bf16[4,144,128]{2,1,0:T(8,128)(2,1)S(1)}, bf16[4,144,128]{2,1,0:T(8,128)(2,1)S(1)}, u32[]{:S(2)}, u32[]{:S(2)}) collective-permute-start(bf16[4,144,128]{2,1,0:T(8,128)(2,1)S(1)} %merge_chips.5.refs_0_), channel_id=1, source_target_pairs={{0,16},{1,17},{2,18},{3,19},{4,20},{5,21},{6,22},{7,23},{8,24},{9,... | collective-permute-start | bytes 442376 | tf_op jit(solution)/shard_map/ppermute | solution.py:207
  50.9 6.3 %collective-permute-start.22 = (bf16[4,8,2048]{2,1,0:T(8,128)(2,1)S(1)}, bf16[4,8,2048]{2,1,0:T(8,128)(2,1)S(1)}, u32[]{:S(2)}, u32[]{:S(2)}) collective-permute-start(bf16[4,8,2048]{2,1,0:T(8,128)(2,1)S(1)} %finish.3.refs_0_), channel_id=1, source_target_pairs={{0,1},{1,0},{2,3},{3,2},{4,5},{5,4},{6,7},{7,6},{8,9},{9,8},{10,11... | collective-permute-start | bytes 393224 | tf_op jit(solution)/shard_map/ppermute | solution.py:207
  51.0 7.3 %collective-permute-start.21 = (bf16[4,8,2048]{2,1,0:T(8,128)(2,1)S(1)}, bf16[4,8,2048]{2,1,0:T(8,128)(2,1)S(1)}, u32[]{:S(2)}, u32[]{:S(2)}) collective-permute-start(bf16[4,8,2048]{2,1,0:T(8,128)(2,1)S(1)} %finish.3.refs_0_), channel_id=1, source_target_pairs={{0,6},{1,7},{2,4},{3,5},{4,2},{5,3},{6,0},{7,1},{8,14},{9,15},{10,... | collective-permute-start | bytes 393224 | tf_op jit(solution)/shard_map/ppermute | solution.py:207
  52.6 8.5 %collective-permute-start.20 = (bf16[4,8,2048]{2,1,0:T(8,128)(2,1)S(1)}, bf16[4,8,2048]{2,1,0:T(8,128)(2,1)S(1)}, u32[]{:S(2)}, u32[]{:S(2)}) collective-permute-start(bf16[4,8,2048]{2,1,0:T(8,128)(2,1)S(1)} %finish.3.refs_0_), channel_id=1, source_target_pairs={{0,4},{1,5},{2,6},{3,7},{4,0},{5,1},{6,2},{7,3},{8,12},{9,13},{10,... | collective-permute-start | bytes 393224 | tf_op jit(solution)/shard_map/ppermute | solution.py:207
  53.6 8.5 %collective-permute-start.19 = (bf16[4,8,2048]{2,1,0:T(8,128)(2,1)S(1)}, bf16[4,8,2048]{2,1,0:T(8,128)(2,1)S(1)}, u32[]{:S(2)}, u32[]{:S(2)}) collective-permute-start(bf16[4,8,2048]{2,1,0:T(8,128)(2,1)S(1)} %finish.3.refs_0_), channel_id=1, source_target_pairs={{0,2},{1,3},{2,0},{3,1},{4,6},{5,7},{6,4},{7,5},{8,10},{9,11},{10,... | collective-permute-start | bytes 393224 | tf_op jit(solution)/shard_map/ppermute | solution.py:207
  55.6 8.4 %collective-permute-start.8 = (bf16[4,8,2048]{2,1,0:T(8,128)(2,1)S(1)}, bf16[4,8,2048]{2,1,0:T(8,128)(2,1)S(1)}, u32[]{:S(2)}, u32[]{:S(2)}) collective-permute-start(bf16[4,8,2048]{2,1,0:T(8,128)(2,1)S(1)} %finish.2.refs_0_), channel_id=1, source_target_pairs={{0,6},{1,7},{2,4},{3,5},{4,2},{5,3},{6,0},{7,1},{8,14},{9,15},{10,... | collective-permute-start | bytes 393224 | tf_op jit(solution)/shard_map/ppermute | solution.py:207
  57.2 9.1 %collective-permute-start.7 = (bf16[4,8,2048]{2,1,0:T(8,128)(2,1)S(1)}, bf16[4,8,2048]{2,1,0:T(8,128)(2,1)S(1)}, u32[]{:S(2)}, u32[]{:S(2)}) collective-permute-start(bf16[4,8,2048]{2,1,0:T(8,128)(2,1)S(1)} %finish.2.refs_0_), channel_id=1, source_target_pairs={{0,4},{1,5},{2,6},{3,7},{4,0},{5,1},{6,2},{7,3},{8,12},{9,13},{10,... | collective-permute-start | bytes 393224 | tf_op jit(solution)/shard_map/ppermute | solution.py:207
  58.3 9.0 %collective-permute-start.6 = (bf16[4,8,2048]{2,1,0:T(8,128)(2,1)S(1)}, bf16[4,8,2048]{2,1,0:T(8,128)(2,1)S(1)}, u32[]{:S(2)}, u32[]{:S(2)}) collective-permute-start(bf16[4,8,2048]{2,1,0:T(8,128)(2,1)S(1)} %finish.2.refs_0_), channel_id=1, source_target_pairs={{0,2},{1,3},{2,0},{3,1},{4,6},{5,7},{6,4},{7,5},{8,10},{9,11},{10,... | collective-permute-start | bytes 393224 | tf_op jit(solution)/shard_map/ppermute | solution.py:207
  61.2 6.2 %collective-permute-start.25 = (bf16[4,8,2048]{2,1,0:T(8,128)(2,1)S(1)}, bf16[4,8,2048]{2,1,0:T(8,128)(2,1)S(1)}, u32[]{:S(2)}, u32[]{:S(2)}) collective-permute-start(bf16[4,8,2048]{2,1,0:T(8,128)(2,1)S(1)} %collective-permute-done.21.refs_3_), channel_id=1, source_target_pairs={{0,1},{1,0},{2,3},{3,2},{4,5},{5,4},{6,7},{7,6},{8,9},{9,8},{10,11... | collective-permute-start | bytes 393224 | tf_op jit(solution)/shard_map/ppermute | solution.py:207
  62.1 5.7 %collective-permute-start.24 = (bf16[4,8,2048]{2,1,0:T(8,128)(2,1)S(1)}, bf16[4,8,2048]{2,1,0:T(8,128)(2,1)S(1)}, u32[]{:S(2)}, u32[]{:S(2)}) collective-permute-start(bf16[4,8,2048]{2,1,0:T(8,128)(2,1)S(1)} %collective-permute-done.20.refs_2_), channel_id=1, source_target_pairs={{0,1},{1,0},{2,3},{3,2},{4,5},{5,4},{6,7},{7,6},{8,9},{9,8},{10,11... | collective-permute-start | bytes 393224 | tf_op jit(solution)/shard_map/ppermute | solution.py:207
  64.0 4.0 %collective-permute-start.23 = (bf16[4,8,2048]{2,1,0:T(8,128)(2,1)S(1)}, bf16[4,8,2048]{2,1,0:T(8,128)(2,1)S(1)}, u32[]{:S(2)}, u32[]{:S(2)}) collective-permute-start(bf16[4,8,2048]{2,1,0:T(8,128)(2,1)S(1)} %collective-permute-done.19.refs_1_), channel_id=1, source_target_pairs={{0,1},{1,0},{2,3},{3,2},{4,5},{5,4},{6,7},{7,6},{8,9},{9,8},{10,11... | collective-permute-start | bytes 393224 | tf_op jit(solution)/shard_map/ppermute | solution.py:207
  66.2 3.0 %collective-permute-start.9 = (bf16[4,8,2048]{2,1,0:T(8,128)(2,1)S(1)}, bf16[4,8,2048]{2,1,0:T(8,128)(2,1)S(1)}, u32[]{:S(2)}, u32[]{:S(2)}) collective-permute-start(bf16[4,8,2048]{2,1,0:T(8,128)(2,1)S(1)} %finish.2.refs_0_), channel_id=1, source_target_pairs={{0,1},{1,0},{2,3},{3,2},{4,5},{5,4},{6,7},{7,6},{8,9},{9,8},{10,11... | collective-permute-start | bytes 393224 | tf_op jit(solution)/shard_map/ppermute | solution.py:207
  67.3 1.9 %collective-permute-start.12 = (bf16[4,8,2048]{2,1,0:T(8,128)(2,1)S(1)}, bf16[4,8,2048]{2,1,0:T(8,128)(2,1)S(1)}, u32[]{:S(2)}, u32[]{:S(2)}) collective-permute-start(bf16[4,8,2048]{2,1,0:T(8,128)(2,1)S(1)} %collective-permute-done.8.refs_3_), channel_id=1, source_target_pairs={{0,1},{1,0},{2,3},{3,2},{4,5},{5,4},{6,7},{7,6},{8,9},{9,8},{10,11... | collective-permute-start | bytes 393224 | tf_op jit(solution)/shard_map/ppermute | solution.py:207
  67.3 1.9 %collective-permute-start.11 = (bf16[4,8,2048]{2,1,0:T(8,128)(2,1)S(1)}, bf16[4,8,2048]{2,1,0:T(8,128)(2,1)S(1)}, u32[]{:S(2)}, u32[]{:S(2)}) collective-permute-start(bf16[4,8,2048]{2,1,0:T(8,128)(2,1)S(1)} %collective-permute-done.7.refs_2_), channel_id=1, source_target_pairs={{0,1},{1,0},{2,3},{3,2},{4,5},{5,4},{6,7},{7,6},{8,9},{9,8},{10,11... | collective-permute-start | bytes 393224 | tf_op jit(solution)/shard_map/ppermute | solution.py:207
  67.9 1.4 %collective-permute-start.10 = (bf16[4,8,2048]{2,1,0:T(8,128)(2,1)S(1)}, bf16[4,8,2048]{2,1,0:T(8,128)(2,1)S(1)}, u32[]{:S(2)}, u32[]{:S(2)}) collective-permute-start(bf16[4,8,2048]{2,1,0:T(8,128)(2,1)S(1)} %collective-permute-done.6.refs_1_), channel_id=1, source_target_pairs={{0,1},{1,0},{2,3},{3,2},{4,5},{5,4},{6,7},{7,6},{8,9},{9,8},{10,11... | collective-permute-start | bytes 393224 | tf_op jit(solution)/shard_map/ppermute | solution.py:207

commit v4 on v3

--- a/solution.py
+++ b/solution.py
@@ -25,24 +25,25 @@
     return out.astype(bf16), stats.astype(bf16)
 
 
-def attention_kernel(
-    chunk, scale2, meta, q_hbm, k_hbm, v_hbm, send_ref, keep_ref, *scratch
-):
-    listed, kept_counts, q_ref, k_ref, v_ref, kd, vt, spread, sems = scratch
-    core = meta[0]
+def active_count(meta):
+    block_count = (meta.shape[0] - 2) // 2
+    return sum((meta[2 + block] > 0).astype(jnp.int32) for block in range(block_count))
+
+
+def split_kernel(meta, k_hbm, v_hbm, q_hbm, kd, vt, sent_ref, *scratch):
+    listed, kept_counts, q_ref, k_ref, v_ref, spread, sems = scratch
     d = k_hbm.shape[1]
-    kv_count = spread.shape[0] // BLK
-    rows = send_ref.shape[0] * LANES
-    group_size = q_ref.shape[2]
+    kv_count = kd.shape[0]
+    group_size = q_ref.shape[1]
     block_count = (meta.shape[0] - 2) // 2
-
+    group = 1 - meta[0]
+
+    heads = pl.ds(pl.multiple_of(group * group_size, group_size), group_size)
     copies = [
         pltpu.make_async_copy(k_hbm, k_ref, sems.at[0]),
         pltpu.make_async_copy(v_hbm, v_ref, sems.at[1]),
+        pltpu.make_async_copy(q_hbm.at[:, heads, :], q_ref, sems.at[2]),
     ]
-    for g in range(2):
-        heads = pl.ds((2 * chunk + g) * group_size, group_size)
-        copies.append(pltpu.make_async_copy(q_hbm.at[:, heads, :], q_ref.at[g], sems.at[2 + g]))
     for copy in copies:
         copy.start()
 
@@ -58,7 +59,7 @@
     def split(source, position):
         start = pl.multiple_of(listed[position] * (BLK * kv_count), BLK * kv_count)
         spread[...] = source[pl.ds(start, BLK * kv_count), :].astype(f32)
-        return [spread[pl.ds(2 * chunk + g, BLK, stride=kv_count), :] for g in range(2)]
+        return [spread[pl.ds(g, BLK, stride=kv_count), :] for g in range(kv_count)]
 
     def fetch_keys(position, carry):
         at = pl.ds(pl.multiple_of(position * BLK, BLK), BLK)
@@ -84,18 +85,36 @@
     def _():
         at = pl.ds(pl.multiple_of(active * BLK, BLK), BLK)
         before = pl.ds(pl.multiple_of((active - 1) * BLK, BLK), BLK)
-        for g in range(2):
+        for g in range(kv_count):
             kd[g, at, :] = kd[g, before, :]
             vt[g, :, at] = jnp.zeros((d + STAT, BLK), bf16)
 
     copies[2].wait()
-    copies[3].wait()
+    attend_all(active, [(sent_ref, group, lambda: q_ref[...])], kd, vt)
+
+
+def attention_kernel(chunk_roles, meta, kd, vt, q_ref, *outs):
+    group_size = q_ref.shape[1] // kd.shape[0]
+    todo = []
+    for out, (chunk, is_other) in zip(outs, chunk_roles):
+        group = 2 * chunk + (1 - meta[0] if is_other else meta[0])
+
+        def read(group=group):
+            heads = pl.ds(pl.multiple_of(group * group_size, group_size), group_size)
+            return q_ref[:, heads, :]
+
+        todo.append((out, group, read))
+    attend_all(active_count(meta), todo, kd, vt)
+
+
+def attend_all(active, todo, kd, vt):
+    d = kd.shape[2]
+    scale2 = math.log2(math.e) / math.sqrt(d)
+    rows = todo[0][0].shape[0] * LANES
     pairs = (active + 1) // 2
-    row = lax.broadcasted_iota(jnp.int32, (STAT, rows), 0)
-
-    def attend(width, role, carry):
-        group = jnp.where(role == 0, 1 - core, core)
-        q = q_ref[group].reshape(rows, d)
+
+    def attend(width, out, group, read):
+        q = read().reshape(rows, d)
         scores = lax.dot_general(
             kd[group, 0:width, :], q, (((1,), (1,)), ((), ())), preferred_element_type=f32
         )
@@ -104,32 +123,28 @@
         sums = jnp.dot(vt[group, :, 0:width], weights, preferred_element_type=f32)
         total = sums[d:]
         high = total.astype(bf16).astype(f32)
+        row = lax.broadcasted_iota(jnp.int32, (STAT, rows), 0)
         stats = jnp.where(row == 0, top, jnp.where(row == 1, high, total - high)).astype(bf16)
-        out = sums[:d].astype(bf16)
-        for ref, its_role in ((send_ref, 0), (keep_ref, 1)):
-
-            @pl.when(role == its_role)
-            def _():
-                for piece in range(rows // LANES):
-                    at = slice(piece * LANES, (piece + 1) * LANES)
-                    ref[piece, 0:d] = out[:, at]
-                    ref[piece, d:] = stats[:, at]
-
-        return carry
-
-    for n in range(1, block_count // 2 + 1):
+        value = sums[:d].astype(bf16)
+        for piece in range(rows // LANES):
+            at = slice(piece * LANES, (piece + 1) * LANES)
+            out[piece, 0:d] = value[:, at]
+            out[piece, d:] = stats[:, at]
+
+    for n in range(1, kd.shape[1] // (2 * BLK) + 1):
 
         @pl.when(pairs == n)
         def _(n=n):
-            lax.fori_loop(0, 2, functools.partial(attend, 2 * BLK * n), 0)
+            for out, group, read in todo:
+                attend(2 * BLK * n, out, group, read)
 
     @pl.when(pairs == 0)
     def _():
         row = lax.broadcasted_iota(jnp.int32, (d + STAT, LANES), 0)
         empty = jnp.where(row == d, lowest_top, 0.0).astype(bf16)
-        for ref in (send_ref, keep_ref):
+        for out, _, _ in todo:
             for piece in range(rows // LANES):
-                ref[piece] = empty
+                out[piece] = empty
 
 
 def merged(parts, d):
@@ -179,22 +194,21 @@
             out_ref[z, :, h * d : (h + 1) * d] = picked.astype(bf16)
 
 
-def project_kernel(chunk, last, meta, weight, *refs):
-    own, other, refs = refs[:4], refs[4:8], refs[8:]
-    z_size, tokens, depth = own[0].shape
-    total = None
-    for parts, core in ((own, meta[0]), (other, 1 - meta[0])):
+def project_kernel(terms, has_earlier, last, meta, weight, *refs):
+    z_size, tokens, depth = refs[0].shape
+    total = refs[4 * len(terms)][...] if has_earlier else None
+    out_ref = refs[-1]
+    for i, (chunk, is_other) in enumerate(terms):
         left = jnp.concatenate(
-            [part[...].reshape(z_size * tokens, depth) for part in parts], axis=0
+            [part[...].reshape(z_size * tokens, depth) for part in refs[4 * i : 4 * i + 4]], axis=0
         )
-        at = pl.ds(pl.multiple_of((2 * chunk + core) * depth, depth), depth)
+        group = 2 * chunk + (1 - meta[0] if is_other else meta[0])
+        at = pl.ds(pl.multiple_of(group * depth, depth), depth)
         product = jnp.dot(left, weight[at, :], preferred_element_type=f32)
         total = product if total is None else total + product
     if not last:
-        refs[0][...] = total
+        out_ref[...] = total
         return
-    earlier, out_ref = refs
-    total = total + earlier[...]
     my_xy = meta[1]
     size = z_size * tokens
     for j in range(4):
@@ -226,42 +240,60 @@
     core = index & 1
     my_xy = (index >> 1) & 3
     tall = d + STAT
-    scale2 = math.log2(math.e) / math.sqrt(d)
     keys = cache_keys.reshape(positions * kv_count, d)
     values = cache_values.reshape(positions * kv_count, d)
     place = jnp.concatenate(
         [jnp.stack([core, my_xy]).astype(jnp.int32), block_mask[0], key_counts]
     )
     kept_in_hbm = functools.partial(pltpu.with_memory_space_constraint, memory_space=pltpu.HBM)
-    queries, keys, values = kept_in_hbm(queries), kept_in_hbm(keys), kept_in_hbm(values)
     state = jax.ShapeDtypeStruct((z_size, tall, LANES), bf16)
 
-    def attend(chunk):
-        blocks = positions // BLK
+    partial = jax.ShapeDtypeStruct((pieces, tall, LANES), bf16)
+    blocks = positions // BLK
+
+    def split_and_attend():
         return pl.pallas_call(
-            functools.partial(attention_kernel, chunk, scale2),
+            split_kernel,
             in_specs=[SMEM] + [HBM] * 3,
-            out_specs=[VMEM] * 2,
+            out_specs=[VMEM] * 3,
             scratch_shapes=[
                 pltpu.SMEM((blocks + 1,), jnp.int32),
                 pltpu.SMEM((blocks + 1,), jnp.int32),
-                pltpu.VMEM((2, token_count, group_size, d), bf16),
+                pltpu.VMEM((token_count, group_size, d), bf16),
                 pltpu.VMEM((positions * kv_count, d), bf16),
                 pltpu.VMEM((positions * kv_count, d), bf16),
-                pltpu.VMEM((2, positions, d), bf16),
-                pltpu.VMEM((2, tall, positions), bf16),
                 pltpu.VMEM((BLK * kv_count, d), f32),
-                pltpu.SemaphoreType.DMA((4,)),
+                pltpu.SemaphoreType.DMA((3,)),
             ],
-            out_shape=[jax.ShapeDtypeStruct((pieces, tall, LANES), bf16)] * 2,
-            compiler_params=pltpu.CompilerParams(vmem_limit_bytes=40 << 20),
+            out_shape=[
+                jax.ShapeDtypeStruct((kv_count, positions, d), bf16),
+                jax.ShapeDtypeStruct((kv_count, tall, positions), bf16),
+                partial,
+            ],
+            compiler_params=pltpu.CompilerParams(vmem_limit_bytes=32 << 20),
             cost_estimate=pl.CostEstimate(
-                flops=8 * rows * positions * d,
-                transcendentals=2 * rows * positions,
+                flops=4 * rows * positions * d,
+                transcendentals=rows * positions,
                 bytes_accessed=4 * positions * d * kv_count,
             ),
-            name="attention",
-        )(place, queries, keys, values)
+            name="split_and_attend",
+        )(place, kept_in_hbm(keys), kept_in_hbm(values), kept_in_hbm(queries))
+
+    def attend(chunk_roles, kd, vt):
+        count = len(chunk_roles)
+        return pl.pallas_call(
+            functools.partial(attention_kernel, chunk_roles),
+            in_specs=[SMEM] + [VMEM] * 3,
+            out_specs=[VMEM] * count,
+            out_shape=[partial] * count,
+            compiler_params=pltpu.CompilerParams(vmem_limit_bytes=32 << 20),
+            cost_estimate=pl.CostEstimate(
+                flops=4 * count * rows * positions * d,
+                transcendentals=count * rows * positions,
+                bytes_accessed=4 * positions * d * count,
+            ),
+            name="attend",
+        )(place, kd, vt, queries)
 
     def merge_cores(kept, received):
         return pl.pallas_call(
@@ -295,42 +327,55 @@
             name="finish",
         )(*parts)
 
-    def project(chunk, own, other, earlier):
+    def project(terms, parts, earlier, last=False):
         depth = group_size * d
         more = [] if earlier is None else [earlier]
         return pl.pallas_call(
-            functools.partial(project_kernel, chunk, earlier is not None),
-            in_specs=[SMEM] + [VMEM] * (1 + len(own + other + more)),
+            functools.partial(project_kernel, terms, bool(more), last),
+            in_specs=[SMEM] + [VMEM] * (1 + len(parts) + len(more)),
             out_specs=VMEM,
             out_shape=jax.ShapeDtypeStruct((token_count, features), f32),
             compiler_params=pltpu.CompilerParams(vmem_limit_bytes=8 << 20),
             cost_estimate=pl.CostEstimate(
-                flops=4 * token_count * depth * features,
+                flops=2 * len(terms) * token_count * depth * features,
                 transcendentals=0,
-                bytes_accessed=4 * depth * features,
+                bytes_accessed=2 * len(terms) * depth * features,
             ),
             name="project",
-        )(place, out_weight, *own, *other, *more)
-
-    chunks = kv_count // 2
-    partials = []
-    for c in range(chunks):
-        sent, kept = attend(c)
-        partials.append((kept, hop(sent, 1)))
-    total = None
-    for c in range(chunks):
-        parts = merge_cores(*partials[c])
-        parts = [parts[0]] + [hop(parts[j], 2 * j) for j in (1, 2, 3)]
+        )(place, out_weight, *parts, *more)
+
+    def exchange_plane(kept, received):
+        parts = merge_cores(kept, received)
+        return [parts[0]] + [hop(parts[j], 2 * j) for j in (1, 2, 3)]
+
+    def exchange_line(parts):
         part = merge_chips(parts)
         reach = 1
         while 2 * reach < z_size:
             part = merge_chips([part, hop(part, 8 * reach)])
             reach *= 2
-        attended = finish([part, hop(part, 8 * reach)])
-        own = [attended] + [hop(attended, 2 * j) for j in (1, 2, 3)]
-        other = [hop(part, 1) for part in own]
-        total = project(c, own, other, total)
-    return total
+        return finish([part, hop(part, 8 * reach)])
+
+    def gather_plane(attended):
+        return [attended] + [hop(attended, 2 * j) for j in (1, 2, 3)]
+
+    kd, vt, sent = split_and_attend()
+    received = hop(sent, 1)
+    kept, sent = attend([(0, False), (1, True)], kd, vt)
+    next_received = hop(sent, 1)
+    parts = merge_cores(kept, received)
+    parts, kd = lax.optimization_barrier((parts, kd))
+    first = [parts[0]] + [hop(parts[j], 2 * j) for j in (1, 2, 3)]
+    (kept,) = attend([(1, False)], kd, vt)
+    second = exchange_plane(kept, next_received)
+    own = gather_plane(exchange_line(first))
+    other = [hop(part, 1) for part in own]
+    next_own = gather_plane(exchange_line(second))
+    total = project([(0, False), (0, True)], own + other, None)
+    next_own[3], total = lax.optimization_barrier((next_own[3], total))
+    next_other = [hop(part, 1) for part in next_own]
+    total = project([(1, False)], next_own, total)
+    return project([(1, True)], next_other, total, last=True)
 
 
 def partner_of(value, axis, distance):
@@ -454,7 +499,7 @@
         and devices == 32
         and token_count == BLK
         and block_mask.shape[0] == 1
-        and kv_count % 2 == 0
+        and kv_count == 4
         and d == LANES
         and group_size == 16
         and token_count * group_size == LANES * (devices // 2)

time: 69.9 us -> 63.8 us (0.913); the launches traced: 71.2 us -> 63.9 us
  Pallas kernels: 17.5 us -> 13.8 us
  starting transfers between devices: 28.6 us -> 25 us
    pallas_call x4 -> x6, Pallas kernels: 15 us -> 11.3 us  [the longest x2 4.01 us: attend(): pl.pallas_call(functools.partial(attention_kernel, chunk_roles), in_specs...]
    ppermute x26, starting transfers between devices: 28.6 us -> 25 us  [hop(): return lax.ppermute(value, 'ctx', pairs)]
  transfers between devices with their start and end apart: 26 -> 26, of which waited for: 11 -> 10; matrix products, arithmetic and copies ran while one was open for 0% -> 0% of each run, Pallas kernels for 14% -> 14%
where the time goes in v4:
time: 63.8 us; the launch traced here: 63.9 us
  starting transfers between devices  25 us (39%)
  waiting for transfers between devices  24.1 us (38%)
  Pallas kernels  13.8 us (22%)
  other arithmetic  0.75 us (1%)
    ppermute x26, starting transfers between devices, hop(): return lax.ppermute(value, 'ctx', pairs)  25 us
    ppermute x26, waiting for transfers between devices, hop(): return lax.ppermute(value, 'ctx', pairs)  24.1 us
    pallas_call x2, Pallas kernels, attend(): pl.pallas_call(functools.partial(attention_kernel, chunk_roles), in_specs...  4.01 us
    pallas_call x3, Pallas kernels, project(): pl.pallas_call(functools.partial(project_kernel, terms, bool(more), last)...  3.95 us
    pallas_call x1, Pallas kernels, split_and_attend(): pl.pallas_call(split_kernel, in_specs=[SMEM] + [HBM] * 3, out_specs=[VMEM...  3.33 us
    pallas_call x2, Pallas kernels, merge_cores(): pl.pallas_call(core_kernel, in_specs=[SMEM] + [VMEM] * 2, out_specs=[VMEM...  1.64 us
  transfers between devices with their start and end apart: 26, of which 10 were waited for; matrix products, arithmetic and copies ran while one was open for 0% of the time, Pallas kernels for 14%

profile of v4, /device:TPU:0, one launch (start us, length us, event | category | flops | bytes accessed | tf_op | source)
XLA Modules:
  0.0 63.9 jit_solution(9810108457972420394)
XLA Ops:
  0.0 0.7 %pad_add_fusion.meta = s32[18]{0:T(128)S(1)} fusion(s32[8]{0:T(128)} %param.10, s32[8]{0:T(128)} %bitcast.9, s32[1]{0:T(128)} %bitcast.1, s32[1]{0:T(128)} %bitcast), kind=kLoop, calls=%fused_computation | loop fusion | flops 54 | bytes 144 | tf_op jit(solution)/shard_map/concatenate | solution.py:245
  0.8 3.3 %split_and_attend.1 = (bf16[4,1024,128]{2,1,0:T(8,128)(2,1)S(1)}, bf16[4,144,1024]{2,1,0:T(8,128)(2,1)S(1)}, bf16[16,144,128]{2,1,0:T(8,128)(2,1)S(1)}) custom-call(s32[18]{0:T(128)S(1)} %pad_add_fusion.meta, bf16[4096,128]{1,0:T(8,128)(2,1)} %bitcast.7, bf16[4096,128]{1,0:T(8,128)(2,1)} %bitcast.8, bf16[128,64,128]{2,1,0:T(8,128)(2,1)} %q_ref.3), custom_call_target="tpu_custom_call" | custom-call | flops 1073741824 | bytes 2097152 | tf_op jit(solution)/shard_map/split_and_attend/pallas_call | solution.py:255
  4.1 1.3 %collective-permute-start = (bf16[16,144,128]{2,1,0:T(8,128)(2,1)S(1)}, bf16[16,144,128]{2,1,0:T(8,128)(2,1)S(1)}, u32[]{:S(2)}, u32[]{:S(2)}) collective-permute-start(bf16[16,144,128]{2,1,0:T(8,128)(2,1)S(1)} %get-tuple-element.28), channel_id=1, source_target_pairs={{0,1},{1,0},{2,3},{3,2},{4,5},{5,4},{6,7},{7,6},{8,9},{9,8},{10,11... | collective-permute-start | bytes 1769480 | tf_op jit(solution)/shard_map/ppermute | solution.py:221
  5.4 2.3 %attend.2 = (bf16[16,144,128]{2,1,0:T(8,128)(2,1)S(1)}, bf16[16,144,128]{2,1,0:T(8,128)(2,1)S(1)}) custom-call(s32[18]{0:T(128)S(1)} %pad_add_fusion.meta, bf16[4,1024,128]{2,1,0:T(8,128)(2,1)S(1)} %get-tuple-element.33.kd, bf16[4,144,1024]{2,1,0:T(8,128)(2,1)S(1)} %get-tuple-element.26.vt, bf16[128,64,128]{2,1,0:T(8,128)(2,1)S(1)} %copy-done), custom_call_target="tpu_custom_call" | custom-call | flops 2147483648 | bytes 1048576 | tf_op jit(solution)/shard_map/attend/pallas_call | solution.py:284
  7.8 1.4 %collective-permute-start.1 = (bf16[16,144,128]{2,1,0:T(8,128)(2,1)S(1)}, bf16[16,144,128]{2,1,0:T(8,128)(2,1)S(1)}, u32[]{:S(2)}, u32[]{:S(2)}) collective-permute-start(bf16[16,144,128]{2,1,0:T(8,128)(2,1)S(1)} %get-tuple-element.34), channel_id=1, source_target_pairs={{0,1},{1,0},{2,3},{3,2},{4,5},{5,4},{6,7},{7,6},{8,9},{9,8},{10,11... | collective-permute-start | bytes 1769480 | tf_op jit(solution)/shard_map/ppermute | solution.py:221
  9.2 0.8 %merge_cores.2 = (bf16[4,144,128]{2,1,0:T(8,128)(2,1)S(1)}, bf16[4,144,128]{2,1,0:T(8,128)(2,1)S(1)}, bf16[4,144,128]{2,1,0:T(8,128)(2,1)S(1)}, bf16[4,144,128]{2,1,0:T(8,128)(2,1)S(1)}) custom-call(s32[18]{0:T(128)S(1)} %pad_add_fusion.meta, bf16[16,144,128]{2,1,0:T(8,128)(2,1)S(1)} %get-tuple-element.27.kept, ...), custom_call_target="tpu_custom_call" | custom-call | tf_op jit(solution)/shard_map/merge_cores/pallas_call | solution.py:299
  10.0 2.4 %collective-permute-start.13 = (bf16[4,144,128]{2,1,0:T(8,128)(2,1)S(1)}, bf16[4,144,128]{2,1,0:T(8,128)(2,1)S(1)}, u32[]{:S(2)}, u32[]{:S(2)}) collective-permute-start(bf16[4,144,128]{2,1,0:T(8,128)(2,1)S(1)} %get-tuple-element.40), channel_id=1, source_target_pairs={{0,2},{1,3},{2,0},{3,1},{4,6},{5,7},{6,4},{7,5},{8,10},{9,11},{10,... | collective-permute-start | bytes 442376 | tf_op jit(solution)/shard_map/ppermute | solution.py:221
  12.4 3.8 %collective-permute-start.14 = (bf16[4,144,128]{2,1,0:T(8,128)(2,1)S(1)}, bf16[4,144,128]{2,1,0:T(8,128)(2,1)S(1)}, u32[]{:S(2)}, u32[]{:S(2)}) collective-permute-start(bf16[4,144,128]{2,1,0:T(8,128)(2,1)S(1)} %get-tuple-element.41), channel_id=1, source_target_pairs={{0,4},{1,5},{2,6},{3,7},{4,0},{5,1},{6,2},{7,3},{8,12},{9,13},{10,... | collective-permute-start | bytes 442376 | tf_op jit(solution)/shard_map/ppermute | solution.py:221
  16.1 1.7 %attend.3.kept = bf16[16,144,128]{2,1,0:T(8,128)(2,1)S(1)} custom-call(s32[18]{0:T(128)S(1)} %pad_add_fusion.meta, bf16[4,1024,128]{2,1,0:T(8,128)(2,1)S(1)} %get-tuple-element.33.kd, bf16[4,144,1024]{2,1,0:T(8,128)(2,1)S(1)} %get-tuple-element.26.vt, bf16[128,64,128]{2,1,0:T(8,128)(2,1)S(1)} %copy-done), custom_call_target="tpu_custom_call" | custom-call | flops 1073741824 | bytes 524288 | tf_op jit(solution)/shard_map/attend/pallas_call | solution.py:284
  17.8 0.8 %merge_cores.3 = (bf16[4,144,128]{2,1,0:T(8,128)(2,1)S(1)}, bf16[4,144,128]{2,1,0:T(8,128)(2,1)S(1)}, bf16[4,144,128]{2,1,0:T(8,128)(2,1)S(1)}, bf16[4,144,128]{2,1,0:T(8,128)(2,1)S(1)}) custom-call(s32[18]{0:T(128)S(1)} %pad_add_fusion.meta, bf16[16,144,128]{2,1,0:T(8,128)(2,1)S(1)} %attend.3.kept, bf16[16,144,128]{2,1,0:T(8,128)(2,1)S(1)} %collective-permute-done.1.received), custom_call_target="tpu_custom_call" | custom-call | tf_op jit(solution)/shard_map/merge_cores/pallas_call | solution.py:299
  18.7 1.5 %collective-permute-start.2 = (bf16[4,144,128]{2,1,0:T(8,128)(2,1)S(1)}, bf16[4,144,128]{2,1,0:T(8,128)(2,1)S(1)}, u32[]{:S(2)}, u32[]{:S(2)}) collective-permute-start(bf16[4,144,128]{2,1,0:T(8,128)(2,1)S(1)} %get-tuple-element.36), channel_id=1, source_target_pairs={{0,2},{1,3},{2,0},{3,1},{4,6},{5,7},{6,4},{7,5},{8,10},{9,11},{10,... | collective-permute-start | bytes 442376 | tf_op jit(solution)/shard_map/ppermute | solution.py:221
  20.2 3.3 %collective-permute-start.3 = (bf16[4,144,128]{2,1,0:T(8,128)(2,1)S(1)}, bf16[4,144,128]{2,1,0:T(8,128)(2,1)S(1)}, u32[]{:S(2)}, u32[]{:S(2)}) collective-permute-start(bf16[4,144,128]{2,1,0:T(8,128)(2,1)S(1)} %get-tuple-element.37), channel_id=1, source_target_pairs={{0,4},{1,5},{2,6},{3,7},{4,0},{5,1},{6,2},{7,3},{8,12},{9,13},{10,... | collective-permute-start | bytes 442376 | tf_op jit(solution)/shard_map/ppermute | solution.py:221
  23.5 0.4 collective-permute-done.15.refs_3_
  24.1 1.2 %collective-permute-done.2.refs_1_ = bf16[4,144,128]{2,1,0:T(8,128)(2,1)S(1)} collective-permute-done((bf16[4,144,128]{2,1,0:T(8,128)(2,1)S(1)}, bf16[4,144,128]{2,1,0:T(8,128)(2,1)S(1)}, u32[]{:S(2)}, u32[]{:S(2)}) %collective-permute-start.2) | collective-permute-done | bytes 147488 | tf_op jit(solution)/shard_map/ppermute | solution.py:221
  25.4 4.5 %collective-permute-done.3.refs_2_ = bf16[4,144,128]{2,1,0:T(8,128)(2,1)S(1)} collective-permute-done((bf16[4,144,128]{2,1,0:T(8,128)(2,1)S(1)}, bf16[4,144,128]{2,1,0:T(8,128)(2,1)S(1)}, u32[]{:S(2)}, u32[]{:S(2)}) %collective-permute-start.3) | collective-permute-done | bytes 147488 | tf_op jit(solution)/shard_map/ppermute | solution.py:221
  30.2 2.2 %collective-permute-start.17 = (bf16[4,144,128]{2,1,0:T(8,128)(2,1)S(1)}, bf16[4,144,128]{2,1,0:T(8,128)(2,1)S(1)}, u32[]{:S(2)}, u32[]{:S(2)}) collective-permute-start(bf16[4,144,128]{2,1,0:T(8,128)(2,1)S(1)} %merge_chips.7.refs_0_), channel_id=1, source_target_pairs={{0,16},{1,17},{2,18},{3,19},{4,20},{5,21},{6,22},{7,23},{8,24},{9,... | collective-permute-start | bytes 442376 | tf_op jit(solution)/shard_map/ppermute | solution.py:221
  32.4 4.6 %collective-permute-done.5.refs_1_ = bf16[4,144,128]{2,1,0:T(8,128)(2,1)S(1)} collective-permute-done((bf16[4,144,128]{2,1,0:T(8,128)(2,1)S(1)}, bf16[4,144,128]{2,1,0:T(8,128)(2,1)S(1)}, u32[]{:S(2)}, u32[]{:S(2)}) %collective-permute-start.5) | collective-permute-done | bytes 147488 | tf_op jit(solution)/shard_map/ppermute | solution.py:221
  37.0 2.1 %collective-permute-start.6 = (bf16[4,144,128]{2,1,0:T(8,128)(2,1)S(1)}, bf16[4,144,128]{2,1,0:T(8,128)(2,1)S(1)}, u32[]{:S(2)}, u32[]{:S(2)}) collective-permute-start(bf16[4,144,128]{2,1,0:T(8,128)(2,1)S(1)} %merge_chips.5.refs_0_), channel_id=1, source_target_pairs={{0,16},{1,17},{2,18},{3,19},{4,20},{5,21},{6,22},{7,23},{8,24},{9,... | collective-permute-start | bytes 442376 | tf_op jit(solution)/shard_map/ppermute | solution.py:221
  39.1 4.0 %collective-permute-done.17.refs_1_ = bf16[4,144,128]{2,1,0:T(8,128)(2,1)S(1)} collective-permute-done((bf16[4,144,128]{2,1,0:T(8,128)(2,1)S(1)}, bf16[4,144,128]{2,1,0:T(8,128)(2,1)S(1)}, u32[]{:S(2)}, u32[]{:S(2)}) %collective-permute-start.17) | collective-permute-done | bytes 147488 | tf_op jit(solution)/shard_map/ppermute | solution.py:221
  43.6 3.4 %collective-permute-start.18 = (bf16[4,8,2048]{2,1,0:T(8,128)(2,1)S(1)}, bf16[4,8,2048]{2,1,0:T(8,128)(2,1)S(1)}, u32[]{:S(2)}, u32[]{:S(2)}) collective-permute-start(bf16[4,8,2048]{2,1,0:T(8,128)(2,1)S(1)} %finish.3.refs_0_), channel_id=1, source_target_pairs={{0,2},{1,3},{2,0},{3,1},{4,6},{5,7},{6,4},{7,5},{8,10},{9,11},{10,... | collective-permute-start | bytes 393224 | tf_op jit(solution)/shard_map/ppermute | solution.py:221
  47.2 1.0 %collective-permute-start.10 = (bf16[4,8,2048]{2,1,0:T(8,128)(2,1)S(1)}, bf16[4,8,2048]{2,1,0:T(8,128)(2,1)S(1)}, u32[]{:S(2)}, u32[]{:S(2)}) collective-permute-start(bf16[4,8,2048]{2,1,0:T(8,128)(2,1)S(1)} %finish.2.refs_0_), channel_id=1, source_target_pairs={{0,4},{1,5},{2,6},{3,7},{4,0},{5,1},{6,2},{7,3},{8,12},{9,13},{10,... | collective-permute-start | bytes 393224 | tf_op jit(solution)/shard_map/ppermute | solution.py:221
  48.2 2.5 %collective-permute-done.20.refs_3_ = bf16[4,8,2048]{2,1,0:T(8,128)(2,1)S(1)} collective-permute-done((bf16[4,8,2048]{2,1,0:T(8,128)(2,1)S(1)}, bf16[4,8,2048]{2,1,0:T(8,128)(2,1)S(1)}, u32[]{:S(2)}, u32[]{:S(2)}) %collective-permute-start.20) | collective-permute-done | bytes 131104 | tf_op jit(solution)/shard_map/ppermute | solution.py:221
  50.7 2.0 %collective-permute-done.19.refs_2_ = bf16[4,8,2048]{2,1,0:T(8,128)(2,1)S(1)} collective-permute-done((bf16[4,8,2048]{2,1,0:T(8,128)(2,1)S(1)}, bf16[4,8,2048]{2,1,0:T(8,128)(2,1)S(1)}, u32[]{:S(2)}, u32[]{:S(2)}) %collective-permute-start.19) | collective-permute-done | bytes 131104 | tf_op jit(solution)/shard_map/ppermute | solution.py:221
  52.7 0.5 collective-permute-start.22
  53.2 1.7 %collective-permute-done.10.refs_2_ = bf16[4,8,2048]{2,1,0:T(8,128)(2,1)S(1)} collective-permute-done((bf16[4,8,2048]{2,1,0:T(8,128)(2,1)S(1)}, bf16[4,8,2048]{2,1,0:T(8,128)(2,1)S(1)}, u32[]{:S(2)}, u32[]{:S(2)}) %collective-permute-start.10) | collective-permute-done | bytes 131104 | tf_op jit(solution)/shard_map/ppermute | solution.py:221
  54.9 1.2 %collective-permute-start.12 = (bf16[4,8,2048]{2,1,0:T(8,128)(2,1)S(1)}, bf16[4,8,2048]{2,1,0:T(8,128)(2,1)S(1)}, u32[]{:S(2)}, u32[]{:S(2)}) collective-permute-start(bf16[4,8,2048]{2,1,0:T(8,128)(2,1)S(1)} %finish.2.refs_0_), channel_id=1, source_target_pairs={{0,6},{1,7},{2,4},{3,5},{4,2},{5,3},{6,0},{7,1},{8,14},{9,15},{10,... | collective-permute-start | bytes 393224 | tf_op jit(solution)/shard_map/ppermute | solution.py:221
  56.1 0.5 collective-permute-start.11
  56.7 1.3 %project.3.refs_4_ = f32[128,512]{1,0:T(8,128)S(1)} custom-call(s32[18]{0:T(128)S(1)} %pad_add_fusion.meta, bf16[8192,512]{1,0:T(8,128)(2,1)S(1)} %bitcast.6, bf16[4,8,2048]{2,1,0:T(8,128)(2,1)S(1)} %finish.3.refs_0_, bf16[4,8,2048]{2,1,0:T(8,128)(2,1)S(1)} %collective-permute-done.18.refs_1_, bf16[4,8,2048]{2,1,0:T(8,128)(2,1)S(1)} %collective-permute-done.19.refs_2_, ...), custom_call_target="tpu_custom_call" | custom-call | flops 536870912 | bytes 4194304 | tf_op jit(solution)/shard_map/project/pallas_call | solution.py:333
  58.0 2.8 %collective-permute-done.12.refs_3_ = bf16[4,8,2048]{2,1,0:T(8,128)(2,1)S(1)} collective-permute-done((bf16[4,8,2048]{2,1,0:T(8,128)(2,1)S(1)}, bf16[4,8,2048]{2,1,0:T(8,128)(2,1)S(1)}, u32[]{:S(2)}, u32[]{:S(2)}) %collective-permute-start.12) | collective-permute-done | bytes 131104 | tf_op jit(solution)/shard_map/ppermute | solution.py:221
  60.8 1.0 %project.4.refs_4_ = f32[128,512]{1,0:T(8,128)S(1)} custom-call(s32[18]{0:T(128)S(1)} %pad_add_fusion.meta, bf16[8192,512]{1,0:T(8,128)(2,1)S(1)} %bitcast.6, bf16[4,8,2048]{2,1,0:T(8,128)(2,1)S(1)} %finish.2.refs_0_, bf16[4,8,2048]{2,1,0:T(8,128)(2,1)S(1)} %collective-permute-done.8.refs_1_, bf16[4,8,2048]{2,1,0:T(8,128)(2,1)S(1)} %collective-permute-done.10.refs_2_, ...), custom_call_target="tpu_custom_call" | custom-call | flops 268435456 | bytes 2097152 | tf_op jit(solution)/shard_map/project/pallas_call | solution.py:333
  61.8 0.3 collective-permute-done.25.refs_3_
  62.2 1.7 %project.5 = f32[128,512]{1,0:T(8,128)} custom-call(s32[18]{0:T(128)S(1)} %pad_add_fusion.meta, bf16[8192,512]{1,0:T(8,128)(2,1)S(1)} %bitcast.6, bf16[4,8,2048]{2,1,0:T(8,128)(2,1)S(1)} %collective-permute-done.7.refs_0_, bf16[4,8,2048]{2,1,0:T(8,128)(2,1)S(1)} %collective-permute-done.9.refs_1_, bf16[4,8,2048]{2,1,0:T(8,128)(2,1)S(1)} %collective-permute-done.11.refs_2_, ...), custom_call_target="tpu_custom_call" | custom-call | flops 268435456 | bytes 2097152 | tf_op jit(solution)/shard_map/project/pallas_call | solution.py:333
  (42 shorter events, 1.4 us)
Async XLA Ops:
  0.7 4.7 %copy-start = (bf16[128,64,128]{2,1,0:T(8,128)(2,1)S(1)}, bf16[128,64,128]{2,1,0:T(8,128)(2,1)}, u32[]{:S(2)}) copy-start(bf16[128,64,128]{2,1,0:T(8,128)(2,1)} %q_ref.3) | copy-start | bytes 6291460
  4.1 5.1 %collective-permute-start = (bf16[16,144,128]{2,1,0:T(8,128)(2,1)S(1)}, bf16[16,144,128]{2,1,0:T(8,128)(2,1)S(1)}, u32[]{:S(2)}, u32[]{:S(2)}) collective-permute-start(bf16[16,144,128]{2,1,0:T(8,128)(2,1)S(1)} %get-tuple-element.28), channel_id=1, source_target_pairs={{0,1},{1,0},{2,3},{3,2},{4,5},{5,4},{6,7},{7,6},{8,9},{9,8},{10,11... | collective-permute-start | bytes 1769480 | tf_op jit(solution)/shard_map/ppermute | solution.py:221
  5.4 51.3 %slice-start = ((s8[8388608]{0:T(1024)(128)(4,1)}), s8[4194304]{0:T(1024)(128)(4,1)S(1)}, s32[]{:S(2)}) async-start(s8[8388608]{0:T(1024)(128)(4,1)} %bitcast.5), calls=%async_computation | async-start | bytes 8388608
  7.8 10.0 %collective-permute-start.1 = (bf16[16,144,128]{2,1,0:T(8,128)(2,1)S(1)}, bf16[16,144,128]{2,1,0:T(8,128)(2,1)S(1)}, u32[]{:S(2)}, u32[]{:S(2)}) collective-permute-start(bf16[16,144,128]{2,1,0:T(8,128)(2,1)S(1)} %get-tuple-element.34), channel_id=1, source_target_pairs={{0,1},{1,0},{2,3},{3,2},{4,5},{5,4},{6,7},{7,6},{8,9},{9,8},{10,11... | collective-permute-start | bytes 1769480 | tf_op jit(solution)/shard_map/ppermute | solution.py:221
  10.0 46.7 %slice-start.1 = ((s8[8388608]{0:T(1024)(128)(4,1)}), s8[4194304]{0:T(1024)(128)(4,1)S(1)}, s32[]{:S(2)}) async-start(s8[8388608]{0:T(1024)(128)(4,1)} %bitcast.5), calls=%async_computation.1 | async-start | bytes 8388608
  10.0 13.5 %collective-permute-start.13 = (bf16[4,144,128]{2,1,0:T(8,128)(2,1)S(1)}, bf16[4,144,128]{2,1,0:T(8,128)(2,1)S(1)}, u32[]{:S(2)}, u32[]{:S(2)}) collective-permute-start(bf16[4,144,128]{2,1,0:T(8,128)(2,1)S(1)} %get-tuple-element.40), channel_id=1, source_target_pairs={{0,2},{1,3},{2,0},{3,1},{4,6},{5,7},{6,4},{7,5},{8,10},{9,11},{10,... | collective-permute-start | bytes 442376 | tf_op jit(solution)/shard_map/ppermute | solution.py:221
  12.4 11.1 %collective-permute-start.14 = (bf16[4,144,128]{2,1,0:T(8,128)(2,1)S(1)}, bf16[4,144,128]{2,1,0:T(8,128)(2,1)S(1)}, u32[]{:S(2)}, u32[]{:S(2)}) collective-permute-start(bf16[4,144,128]{2,1,0:T(8,128)(2,1)S(1)} %get-tuple-element.41), channel_id=1, source_target_pairs={{0,4},{1,5},{2,6},{3,7},{4,0},{5,1},{6,2},{7,3},{8,12},{9,13},{10,... | collective-permute-start | bytes 442376 | tf_op jit(solution)/shard_map/ppermute | solution.py:221
  16.1 7.7 %collective-permute-start.15 = (bf16[4,144,128]{2,1,0:T(8,128)(2,1)S(1)}, bf16[4,144,128]{2,1,0:T(8,128)(2,1)S(1)}, u32[]{:S(2)}, u32[]{:S(2)}) collective-permute-start(bf16[4,144,128]{2,1,0:T(8,128)(2,1)S(1)} %get-tuple-element.42), channel_id=1, source_target_pairs={{0,6},{1,7},{2,4},{3,5},{4,2},{5,3},{6,0},{7,1},{8,14},{9,15},{10,... | collective-permute-start | bytes 442376 | tf_op jit(solution)/shard_map/ppermute | solution.py:221
  18.7 6.7 %collective-permute-start.2 = (bf16[4,144,128]{2,1,0:T(8,128)(2,1)S(1)}, bf16[4,144,128]{2,1,0:T(8,128)(2,1)S(1)}, u32[]{:S(2)}, u32[]{:S(2)}) collective-permute-start(bf16[4,144,128]{2,1,0:T(8,128)(2,1)S(1)} %get-tuple-element.36), channel_id=1, source_target_pairs={{0,2},{1,3},{2,0},{3,1},{4,6},{5,7},{6,4},{7,5},{8,10},{9,11},{10,... | collective-permute-start | bytes 442376 | tf_op jit(solution)/shard_map/ppermute | solution.py:221
  20.2 9.7 %collective-permute-start.3 = (bf16[4,144,128]{2,1,0:T(8,128)(2,1)S(1)}, bf16[4,144,128]{2,1,0:T(8,128)(2,1)S(1)}, u32[]{:S(2)}, u32[]{:S(2)}) collective-permute-start(bf16[4,144,128]{2,1,0:T(8,128)(2,1)S(1)} %get-tuple-element.37), channel_id=1, source_target_pairs={{0,4},{1,5},{2,6},{3,7},{4,0},{5,1},{6,2},{7,3},{8,12},{9,13},{10,... | collective-permute-start | bytes 442376 | tf_op jit(solution)/shard_map/ppermute | solution.py:221
  23.5 6.4 %collective-permute-start.4 = (bf16[4,144,128]{2,1,0:T(8,128)(2,1)S(1)}, bf16[4,144,128]{2,1,0:T(8,128)(2,1)S(1)}, u32[]{:S(2)}, u32[]{:S(2)}) collective-permute-start(bf16[4,144,128]{2,1,0:T(8,128)(2,1)S(1)} %get-tuple-element.38), channel_id=1, source_target_pairs={{0,6},{1,7},{2,4},{3,5},{4,2},{5,3},{6,0},{7,1},{8,14},{9,15},{10,... | collective-permute-start | bytes 442376 | tf_op jit(solution)/shard_map/ppermute | solution.py:221
  24.0 6.1 %collective-permute-start.16 = (bf16[4,144,128]{2,1,0:T(8,128)(2,1)S(1)}, bf16[4,144,128]{2,1,0:T(8,128)(2,1)S(1)}, u32[]{:S(2)}, u32[]{:S(2)}) collective-permute-start(bf16[4,144,128]{2,1,0:T(8,128)(2,1)S(1)} %merge_chips.6.refs_0_), channel_id=1, source_target_pairs={{0,8},{1,9},{2,10},{3,11},{4,12},{5,13},{6,14},{7,15},{8,0},{9,1},... | collective-permute-start | bytes 442376 | tf_op jit(solution)/shard_map/ppermute | solution.py:221
  30.0 6.9 %collective-permute-start.5 = (bf16[4,144,128]{2,1,0:T(8,128)(2,1)S(1)}, bf16[4,144,128]{2,1,0:T(8,128)(2,1)S(1)}, u32[]{:S(2)}, u32[]{:S(2)}) collective-permute-start(bf16[4,144,128]{2,1,0:T(8,128)(2,1)S(1)} %merge_chips.4.refs_0_), channel_id=1, source_target_pairs={{0,8},{1,9},{2,10},{3,11},{4,12},{5,13},{6,14},{7,15},{8,0},{9,1},... | collective-permute-start | bytes 442376 | tf_op jit(solution)/shard_map/ppermute | solution.py:221
  30.2 13.0 %collective-permute-start.17 = (bf16[4,144,128]{2,1,0:T(8,128)(2,1)S(1)}, bf16[4,144,128]{2,1,0:T(8,128)(2,1)S(1)}, u32[]{:S(2)}, u32[]{:S(2)}) collective-permute-start(bf16[4,144,128]{2,1,0:T(8,128)(2,1)S(1)} %merge_chips.7.refs_0_), channel_id=1, source_target_pairs={{0,16},{1,17},{2,18},{3,19},{4,20},{5,21},{6,22},{7,23},{8,24},{9,... | collective-permute-start | bytes 442376 | tf_op jit(solution)/shard_map/ppermute | solution.py:221
  37.0 10.0 %collective-permute-start.6 = (bf16[4,144,128]{2,1,0:T(8,128)(2,1)S(1)}, bf16[4,144,128]{2,1,0:T(8,128)(2,1)S(1)}, u32[]{:S(2)}, u32[]{:S(2)}) collective-permute-start(bf16[4,144,128]{2,1,0:T(8,128)(2,1)S(1)} %merge_chips.5.refs_0_), channel_id=1, source_target_pairs={{0,16},{1,17},{2,18},{3,19},{4,20},{5,21},{6,22},{7,23},{8,24},{9,... | collective-permute-start | bytes 442376 | tf_op jit(solution)/shard_map/ppermute | solution.py:221
  43.3 4.9 %collective-permute-start.21 = (bf16[4,8,2048]{2,1,0:T(8,128)(2,1)S(1)}, bf16[4,8,2048]{2,1,0:T(8,128)(2,1)S(1)}, u32[]{:S(2)}, u32[]{:S(2)}) collective-permute-start(bf16[4,8,2048]{2,1,0:T(8,128)(2,1)S(1)} %finish.3.refs_0_), channel_id=1, source_target_pairs={{0,1},{1,0},{2,3},{3,2},{4,5},{5,4},{6,7},{7,6},{8,9},{9,8},{10,11... | collective-permute-start | bytes 393224 | tf_op jit(solution)/shard_map/ppermute | solution.py:221
  43.4 7.3 %collective-permute-start.20 = (bf16[4,8,2048]{2,1,0:T(8,128)(2,1)S(1)}, bf16[4,8,2048]{2,1,0:T(8,128)(2,1)S(1)}, u32[]{:S(2)}, u32[]{:S(2)}) collective-permute-start(bf16[4,8,2048]{2,1,0:T(8,128)(2,1)S(1)} %finish.3.refs_0_), channel_id=1, source_target_pairs={{0,6},{1,7},{2,4},{3,5},{4,2},{5,3},{6,0},{7,1},{8,14},{9,15},{10,... | collective-permute-start | bytes 393224 | tf_op jit(solution)/shard_map/ppermute | solution.py:221
  43.5 9.2 %collective-permute-start.19 = (bf16[4,8,2048]{2,1,0:T(8,128)(2,1)S(1)}, bf16[4,8,2048]{2,1,0:T(8,128)(2,1)S(1)}, u32[]{:S(2)}, u32[]{:S(2)}) collective-permute-start(bf16[4,8,2048]{2,1,0:T(8,128)(2,1)S(1)} %finish.3.refs_0_), channel_id=1, source_target_pairs={{0,4},{1,5},{2,6},{3,7},{4,0},{5,1},{6,2},{7,3},{8,12},{9,13},{10,... | collective-permute-start | bytes 393224 | tf_op jit(solution)/shard_map/ppermute | solution.py:221
  43.6 9.1 %collective-permute-start.18 = (bf16[4,8,2048]{2,1,0:T(8,128)(2,1)S(1)}, bf16[4,8,2048]{2,1,0:T(8,128)(2,1)S(1)}, u32[]{:S(2)}, u32[]{:S(2)}) collective-permute-start(bf16[4,8,2048]{2,1,0:T(8,128)(2,1)S(1)} %finish.3.refs_0_), channel_id=1, source_target_pairs={{0,2},{1,3},{2,0},{3,1},{4,6},{5,7},{6,4},{7,5},{8,10},{9,11},{10,... | collective-permute-start | bytes 393224 | tf_op jit(solution)/shard_map/ppermute | solution.py:221
  47.2 7.7 %collective-permute-start.10 = (bf16[4,8,2048]{2,1,0:T(8,128)(2,1)S(1)}, bf16[4,8,2048]{2,1,0:T(8,128)(2,1)S(1)}, u32[]{:S(2)}, u32[]{:S(2)}) collective-permute-start(bf16[4,8,2048]{2,1,0:T(8,128)(2,1)S(1)} %finish.2.refs_0_), channel_id=1, source_target_pairs={{0,4},{1,5},{2,6},{3,7},{4,0},{5,1},{6,2},{7,3},{8,12},{9,13},{10,... | collective-permute-start | bytes 393224 | tf_op jit(solution)/shard_map/ppermute | solution.py:221
  48.2 7.9 %collective-permute-start.8 = (bf16[4,8,2048]{2,1,0:T(8,128)(2,1)S(1)}, bf16[4,8,2048]{2,1,0:T(8,128)(2,1)S(1)}, u32[]{:S(2)}, u32[]{:S(2)}) collective-permute-start(bf16[4,8,2048]{2,1,0:T(8,128)(2,1)S(1)} %finish.2.refs_0_), channel_id=1, source_target_pairs={{0,2},{1,3},{2,0},{3,1},{4,6},{5,7},{6,4},{7,5},{8,10},{9,11},{10,... | collective-permute-start | bytes 393224 | tf_op jit(solution)/shard_map/ppermute | solution.py:221
  50.7 5.4 %collective-permute-start.24 = (bf16[4,8,2048]{2,1,0:T(8,128)(2,1)S(1)}, bf16[4,8,2048]{2,1,0:T(8,128)(2,1)S(1)}, u32[]{:S(2)}, u32[]{:S(2)}) collective-permute-start(bf16[4,8,2048]{2,1,0:T(8,128)(2,1)S(1)} %collective-permute-done.20.refs_3_), channel_id=1, source_target_pairs={{0,1},{1,0},{2,3},{3,2},{4,5},{5,4},{6,7},{7,6},{8,9},{9,8},{10,11... | collective-permute-start | bytes 393224 | tf_op jit(solution)/shard_map/ppermute | solution.py:221
  52.7 4.0 %collective-permute-start.23 = (bf16[4,8,2048]{2,1,0:T(8,128)(2,1)S(1)}, bf16[4,8,2048]{2,1,0:T(8,128)(2,1)S(1)}, u32[]{:S(2)}, u32[]{:S(2)}) collective-permute-start(bf16[4,8,2048]{2,1,0:T(8,128)(2,1)S(1)} %collective-permute-done.19.refs_2_), channel_id=1, source_target_pairs={{0,1},{1,0},{2,3},{3,2},{4,5},{5,4},{6,7},{7,6},{8,9},{9,8},{10,11... | collective-permute-start | bytes 393224 | tf_op jit(solution)/shard_map/ppermute | solution.py:221
  52.7 4.0 %collective-permute-start.22 = (bf16[4,8,2048]{2,1,0:T(8,128)(2,1)S(1)}, bf16[4,8,2048]{2,1,0:T(8,128)(2,1)S(1)}, u32[]{:S(2)}, u32[]{:S(2)}) collective-permute-start(bf16[4,8,2048]{2,1,0:T(8,128)(2,1)S(1)} %collective-permute-done.18.refs_1_), channel_id=1, source_target_pairs={{0,1},{1,0},{2,3},{3,2},{4,5},{5,4},{6,7},{7,6},{8,9},{9,8},{10,11... | collective-permute-start | bytes 393224 | tf_op jit(solution)/shard_map/ppermute | solution.py:221
  54.9 5.9 %collective-permute-start.12 = (bf16[4,8,2048]{2,1,0:T(8,128)(2,1)S(1)}, bf16[4,8,2048]{2,1,0:T(8,128)(2,1)S(1)}, u32[]{:S(2)}, u32[]{:S(2)}) collective-permute-start(bf16[4,8,2048]{2,1,0:T(8,128)(2,1)S(1)} %finish.2.refs_0_), channel_id=1, source_target_pairs={{0,6},{1,7},{2,4},{3,5},{4,2},{5,3},{6,0},{7,1},{8,14},{9,15},{10,... | collective-permute-start | bytes 393224 | tf_op jit(solution)/shard_map/ppermute | solution.py:221
  56.1 5.7 %collective-permute-start.7 = (bf16[4,8,2048]{2,1,0:T(8,128)(2,1)S(1)}, bf16[4,8,2048]{2,1,0:T(8,128)(2,1)S(1)}, u32[]{:S(2)}, u32[]{:S(2)}) collective-permute-start(bf16[4,8,2048]{2,1,0:T(8,128)(2,1)S(1)} %finish.2.refs_0_), channel_id=1, source_target_pairs={{0,1},{1,0},{2,3},{3,2},{4,5},{5,4},{6,7},{7,6},{8,9},{9,8},{10,11... | collective-permute-start | bytes 393224 | tf_op jit(solution)/shard_map/ppermute | solution.py:221
  56.1 5.7 %collective-permute-start.11 = (bf16[4,8,2048]{2,1,0:T(8,128)(2,1)S(1)}, bf16[4,8,2048]{2,1,0:T(8,128)(2,1)S(1)}, u32[]{:S(2)}, u32[]{:S(2)}) collective-permute-start(bf16[4,8,2048]{2,1,0:T(8,128)(2,1)S(1)} %collective-permute-done.10.refs_2_), channel_id=1, source_target_pairs={{0,1},{1,0},{2,3},{3,2},{4,5},{5,4},{6,7},{7,6},{8,9},{9,8},{10,11... | collective-permute-start | bytes 393224 | tf_op jit(solution)/shard_map/ppermute | solution.py:221
  56.6 5.2 %collective-permute-start.9 = (bf16[4,8,2048]{2,1,0:T(8,128)(2,1)S(1)}, bf16[4,8,2048]{2,1,0:T(8,128)(2,1)S(1)}, u32[]{:S(2)}, u32[]{:S(2)}) collective-permute-start(bf16[4,8,2048]{2,1,0:T(8,128)(2,1)S(1)} %collective-permute-done.8.refs_1_), channel_id=1, source_target_pairs={{0,1},{1,0},{2,3},{3,2},{4,5},{5,4},{6,7},{7,6},{8,9},{9,8},{10,11... | collective-permute-start | bytes 393224 | tf_op jit(solution)/shard_map/ppermute | solution.py:221
  60.8 1.3 %collective-permute-start.25 = (bf16[4,8,2048]{2,1,0:T(8,128)(2,1)S(1)}, bf16[4,8,2048]{2,1,0:T(8,128)(2,1)S(1)}, u32[]{:S(2)}, u32[]{:S(2)}) collective-permute-start(bf16[4,8,2048]{2,1,0:T(8,128)(2,1)S(1)} %collective-permute-done.12.refs_3_), channel_id=1, source_target_pairs={{0,1},{1,0},{2,3},{3,2},{4,5},{5,4},{6,7},{7,6},{8,9},{9,8},{10,11... | collective-permute-start | bytes 393224 | tf_op jit(solution)/shard_map/ppermute | solution.py:221

commit v5 on v4

--- a/solution.py
+++ b/solution.py
@@ -11,6 +11,7 @@
 BLK = 128
 LANES = 128
 STAT = 16
+PLACE = 3
 very_low = -1e30
 lowest_top = -(2.0**99)
 bf16 = jnp.bfloat16
@@ -26,8 +27,8 @@
 
 
 def active_count(meta):
-    block_count = (meta.shape[0] - 2) // 2
-    return sum((meta[2 + block] > 0).astype(jnp.int32) for block in range(block_count))
+    block_count = (meta.shape[0] - PLACE) // 2
+    return sum((meta[PLACE + block] > 0).astype(jnp.int32) for block in range(block_count))
 
 
 def split_kernel(meta, k_hbm, v_hbm, q_hbm, kd, vt, sent_ref, *scratch):
@@ -35,7 +36,7 @@
     d = k_hbm.shape[1]
     kv_count = kd.shape[0]
     group_size = q_ref.shape[1]
-    block_count = (meta.shape[0] - 2) // 2
+    block_count = (meta.shape[0] - PLACE) // 2
     group = 1 - meta[0]
 
     heads = pl.ds(pl.multiple_of(group * group_size, group_size), group_size)
@@ -49,8 +50,8 @@
 
     def note(block, found):
         listed[found] = block
-        kept_counts[found] = meta[2 + block_count + block]
-        return found + (meta[2 + block] > 0).astype(jnp.int32)
+        kept_counts[found] = meta[PLACE + block_count + block]
+        return found + (meta[PLACE + block] > 0).astype(jnp.int32)
 
     active = lax.fori_loop(0, block_count, note, jnp.int32(0))
     place = lax.broadcasted_iota(jnp.int32, (BLK, LANES), 0)
@@ -175,10 +176,25 @@
             store_merged(out, z, [kept[piece], received[piece]])
 
 
-def plane_kernel(*refs):
+def plane_kernel(meta, *refs):
+    ins, kept, sent = refs[:-2], refs[-2], refs[-1]
+    parity = meta[2] & 1
+    for out, first in ((sent, 1 - parity), (kept, parity)):
+        for i in range(out.shape[0]):
+            store_merged(out, i, [ref[first + 2 * i] for ref in ins])
+
+
+def line_kernel(*refs):
     ins, out = refs[:-1], refs[-1]
-    for z in range(out.shape[0]):
-        store_merged(out, z, [ref[z] for ref in ins])
+    for i in range(out.shape[0]):
+        store_merged(out, i, [ref[i] for ref in ins])
+
+
+def join_kernel(meta, own, other, out):
+    parity = meta[2] & 1
+    for ref, first in ((own, parity), (other, 1 - parity)):
+        for i in range(ref.shape[0]):
+            out[first + 2 * i] = ref[i]
 
 
 def last_kernel(*refs):
@@ -239,11 +255,12 @@
     features = out_weight.shape[1]
     core = index & 1
     my_xy = (index >> 1) & 3
+    my_z = index >> 3
     tall = d + STAT
     keys = cache_keys.reshape(positions * kv_count, d)
     values = cache_values.reshape(positions * kv_count, d)
     place = jnp.concatenate(
-        [jnp.stack([core, my_xy]).astype(jnp.int32), block_mask[0], key_counts]
+        [jnp.stack([core, my_xy, my_z]).astype(jnp.int32), block_mask[0], key_counts]
     )
     kept_in_hbm = functools.partial(pltpu.with_memory_space_constraint, memory_space=pltpu.HBM)
     state = jax.ShapeDtypeStruct((z_size, tall, LANES), bf16)
@@ -305,27 +322,49 @@
             name="merge_cores",
         )(place, kept, received)
 
-    def merge_chips(parts):
+    half = jax.ShapeDtypeStruct((z_size // 2, tall, LANES), bf16)
+    tokens = LANES // group_size
+
+    def merge_plane(parts):
         return pl.pallas_call(
             plane_kernel,
+            in_specs=[SMEM] + [VMEM] * len(parts),
+            out_specs=[VMEM] * 2,
+            out_shape=[half] * 2,
+            compiler_params=SMALL,
+            name="merge_plane",
+        )(place, *parts)
+
+    def merge_line(parts):
+        return pl.pallas_call(
+            line_kernel,
             in_specs=[VMEM] * len(parts),
             out_specs=VMEM,
-            out_shape=state,
+            out_shape=half,
             compiler_params=SMALL,
-            name="merge_chips",
+            name="merge_line",
         )(*parts)
 
     def finish(parts):
-        tokens = LANES // group_size
         return pl.pallas_call(
             last_kernel,
             in_specs=[VMEM] * len(parts),
             out_specs=VMEM,
-            out_shape=jax.ShapeDtypeStruct((z_size, tokens, group_size * d), bf16),
-            scratch_shapes=[pltpu.VMEM((z_size, LANES, d), f32)],
+            out_shape=jax.ShapeDtypeStruct((z_size // 2, tokens, group_size * d), bf16),
+            scratch_shapes=[pltpu.VMEM((z_size // 2, LANES, d), f32)],
             compiler_params=SMALL,
             name="finish",
         )(*parts)
+
+    def join(own, other):
+        return pl.pallas_call(
+            join_kernel,
+            in_specs=[SMEM] + [VMEM] * 2,
+            out_specs=VMEM,
+            out_shape=jax.ShapeDtypeStruct((z_size, tokens, group_size * d), bf16),
+            compiler_params=SMALL,
+            name="join",
+        )(place, own, other)
 
     def project(terms, parts, earlier, last=False):
         depth = group_size * d
@@ -349,12 +388,10 @@
         return [parts[0]] + [hop(parts[j], 2 * j) for j in (1, 2, 3)]
 
     def exchange_line(parts):
-        part = merge_chips(parts)
-        reach = 1
-        while 2 * reach < z_size:
-            part = merge_chips([part, hop(part, 8 * reach)])
-            reach *= 2
-        return finish([part, hop(part, 8 * reach)])
+        kept, sent = merge_plane(parts)
+        part = merge_line([kept, hop(sent, 8)])
+        attended = finish([part, hop(part, 16)])
+        return join(attended, hop(attended, 8))
 
     def gather_plane(attended):
         return [attended] + [hop(attended, 2 * j) for j in (1, 2, 3)]

time: 63.8 us -> 66.4 us (1.041)
  Pallas kernels: 13.8 us -> 18.5 us
  waiting for transfers between devices: 24.1 us -> 21.9 us
  local copies, waits for them, and re-layouts: 0.01 us -> 0.76 us
  other arithmetic: 0.75 us -> 0.01 us
    ppermute x26 -> x28, waiting for transfers between devices: 24.1 us -> 21.9 us  [hop(): return lax.ppermute(value, 'ctx', pairs)]
    pallas_call x4 -> x6, Pallas kernels: 0.47 us -> 2.58 us  [the longest x2 1.39 us: merge_plane(): pl.pallas_call(plane_kernel, in_specs=[SMEM] + [VMEM] * len(parts), out_s...]
    pallas_call x2, Pallas kernels: 4.01 us -> 5.92 us  [attend(): pl.pallas_call(functools.partial(attention_kernel, chunk_roles), in_specs...]
    pallas_call x1, Pallas kernels: 3.33 us -> 4.17 us  [split_and_attend(): pl.pallas_call(split_kernel, in_specs=[SMEM] + [HBM] * 3, out_specs=[VMEM...]
    concatenate x1 -> x0, other arithmetic: 0.75 us -> none  [fast_body(): jnp.concatenate([jnp.stack([core, my_xy]).astype(jnp.int32), block_mask[0...]
    concatenate x0 -> x1, local copies, waits for them, and re-layouts: none -> 0.74 us  [fast_body(): jnp.concatenate([jnp.stack([core, my_xy, my_z]).astype(jnp.int32), block_...]
    ppermute x26 -> x28, starting transfers between devices: 25 us -> 25.6 us  [hop(): return lax.ppermute(value, 'ctx', pairs)]
  transfers between devices with their start and end apart: 26 -> 28, of which waited for: 10 -> 12; matrix products, arithmetic and copies ran while one was open for 0% -> 0% of each run, Pallas kernels for 14% -> 19%
where the time goes in v5:
time: 66.4 us; the launch traced here: 67 us
  starting transfers between devices  25.6 us (39%)
  waiting for transfers between devices  21.9 us (33%)
  Pallas kernels  18.5 us (28%)
  local copies, waits for them, and re-layouts  0.76 us (1%)
    ppermute x28, starting transfers between devices, hop(): return lax.ppermute(value, 'ctx', pairs)  25.6 us
    ppermute x28, waiting for transfers between devices, hop(): return lax.ppermute(value, 'ctx', pairs)  21.9 us
    pallas_call x2, Pallas kernels, attend(): pl.pallas_call(functools.partial(attention_kernel, chunk_roles), in_specs...  5.92 us
    pallas_call x1, Pallas kernels, split_and_attend(): pl.pallas_call(split_kernel, in_specs=[SMEM] + [HBM] * 3, out_specs=[VMEM...  4.17 us
    pallas_call x3, Pallas kernels, project(): pl.pallas_call(functools.partial(project_kernel, terms, bool(more), last)...  3.94 us
    pallas_call x2, Pallas kernels, merge_cores(): pl.pallas_call(core_kernel, in_specs=[SMEM] + [VMEM] * 2, out_specs=[VMEM...  1.64 us
    pallas_call x2, Pallas kernels, merge_plane(): pl.pallas_call(plane_kernel, in_specs=[SMEM] + [VMEM] * len(parts), out_s...  1.39 us
  transfers between devices with their start and end apart: 28, of which 12 were waited for; matrix products, arithmetic and copies ran while one was open for 0% of the time, Pallas kernels for 19%

profile of v5, /device:TPU:0, one launch (start us, length us, event | category | flops | bytes accessed | tf_op | source)
XLA Modules:
  0.0 67.0 jit_solution(2231652433082036688)
XLA Ops:
  0.0 0.7 %concatenate.3.meta = s32[19]{0:T(128)S(1)} concatenate(s32[1]{0:T(128)} %bitcast, s32[1]{0:T(128)} %bitcast.1, s32[1]{0:T(128)} %bitcast.2, s32[8]{0:T(128)} %bitcast.10, s32[8]{0:T(128)} %param.10), dimensions={0} | concatenate | bytes 152 | tf_op jit(solution)/shard_map/concatenate | solution.py:262
  0.7 4.2 %split_and_attend.1 = (bf16[4,1024,128]{2,1,0:T(8,128)(2,1)S(1)}, bf16[4,144,1024]{2,1,0:T(8,128)(2,1)S(1)}, bf16[16,144,128]{2,1,0:T(8,128)(2,1)S(1)}) custom-call(s32[19]{0:T(128)S(1)} %concatenate.3.meta, bf16[4096,128]{1,0:T(8,128)(2,1)} %bitcast.8, bf16[4096,128]{1,0:T(8,128)(2,1)} %bitcast.9, bf16[128,64,128]{2,1,0:T(8,128)(2,1)} %q_ref.3), custom_call_target="tpu_custom_call" | custom-call | flops 1073741824 | bytes 2097152 | tf_op jit(solution)/shard_map/split_and_attend/pallas_call | solution.py:272
  5.0 3.6 %attend.2 = (bf16[16,144,128]{2,1,0:T(8,128)(2,1)S(1)}, bf16[16,144,128]{2,1,0:T(8,128)(2,1)S(1)}) custom-call(s32[19]{0:T(128)S(1)} %concatenate.3.meta, bf16[4,1024,128]{2,1,0:T(8,128)(2,1)S(1)} %get-tuple-element.37.kd, bf16[4,144,1024]{2,1,0:T(8,128)(2,1)S(1)} %get-tuple-element.30.vt, bf16[128,64,128]{2,1,0:T(8,128)(2,1)S(1)} %copy-done), custom_call_target="tpu_custom_call" | custom-call | flops 2147483648 | bytes 1048576 | tf_op jit(solution)/shard_map/attend/pallas_call | solution.py:301
  8.7 0.8 %merge_cores.2 = (bf16[4,144,128]{2,1,0:T(8,128)(2,1)S(1)}, bf16[4,144,128]{2,1,0:T(8,128)(2,1)S(1)}, bf16[4,144,128]{2,1,0:T(8,128)(2,1)S(1)}, bf16[4,144,128]{2,1,0:T(8,128)(2,1)S(1)}) custom-call(s32[19]{0:T(128)S(1)} %concatenate.3.meta, bf16[16,144,128]{2,1,0:T(8,128)(2,1)S(1)} %get-tuple-element.31.kept, ...), custom_call_target="tpu_custom_call" | custom-call | tf_op jit(solution)/shard_map/merge_cores/pallas_call | solution.py:316
  9.6 7.2 %collective-permute-start.14 = (bf16[4,144,128]{2,1,0:T(8,128)(2,1)S(1)}, bf16[4,144,128]{2,1,0:T(8,128)(2,1)S(1)}, u32[]{:S(2)}, u32[]{:S(2)}) collective-permute-start(bf16[4,144,128]{2,1,0:T(8,128)(2,1)S(1)} %get-tuple-element.46), channel_id=1, source_target_pairs={{0,2},{1,3},{2,0},{3,1},{4,6},{5,7},{6,4},{7,5},{8,10},{9,11},{10,... | collective-permute-start | bytes 442376 | tf_op jit(solution)/shard_map/ppermute | solution.py:237
  16.8 1.5 %collective-permute-start.16 = (bf16[4,144,128]{2,1,0:T(8,128)(2,1)S(1)}, bf16[4,144,128]{2,1,0:T(8,128)(2,1)S(1)}, u32[]{:S(2)}, u32[]{:S(2)}) collective-permute-start(bf16[4,144,128]{2,1,0:T(8,128)(2,1)S(1)} %get-tuple-element.48), channel_id=1, source_target_pairs={{0,6},{1,7},{2,4},{3,5},{4,2},{5,3},{6,0},{7,1},{8,14},{9,15},{10,... | collective-permute-start | bytes 442376 | tf_op jit(solution)/shard_map/ppermute | solution.py:237
  18.3 2.3 %attend.3.kept = bf16[16,144,128]{2,1,0:T(8,128)(2,1)S(1)} custom-call(s32[19]{0:T(128)S(1)} %concatenate.3.meta, bf16[4,1024,128]{2,1,0:T(8,128)(2,1)S(1)} %get-tuple-element.37.kd, bf16[4,144,1024]{2,1,0:T(8,128)(2,1)S(1)} %get-tuple-element.30.vt, bf16[128,64,128]{2,1,0:T(8,128)(2,1)S(1)} %copy-done), custom_call_target="tpu_custom_call" | custom-call | flops 1073741824 | bytes 524288 | tf_op jit(solution)/shard_map/attend/pallas_call | solution.py:301
  20.7 0.8 %merge_cores.3 = (bf16[4,144,128]{2,1,0:T(8,128)(2,1)S(1)}, bf16[4,144,128]{2,1,0:T(8,128)(2,1)S(1)}, bf16[4,144,128]{2,1,0:T(8,128)(2,1)S(1)}, bf16[4,144,128]{2,1,0:T(8,128)(2,1)S(1)}) custom-call(s32[19]{0:T(128)S(1)} %concatenate.3.meta, bf16[16,144,128]{2,1,0:T(8,128)(2,1)S(1)} %attend.3.kept, bf16[16,144,128]{2,1,0:T(8,128)(2,1)S(1)} %collective-permute-done.1.received), custom_call_target="tpu_custom_call" | custom-call | tf_op jit(solution)/shard_map/merge_cores/pallas_call | solution.py:316
  21.5 3.3 %collective-permute-start.2 = (bf16[4,144,128]{2,1,0:T(8,128)(2,1)S(1)}, bf16[4,144,128]{2,1,0:T(8,128)(2,1)S(1)}, u32[]{:S(2)}, u32[]{:S(2)}) collective-permute-start(bf16[4,144,128]{2,1,0:T(8,128)(2,1)S(1)} %get-tuple-element.40), channel_id=1, source_target_pairs={{0,2},{1,3},{2,0},{3,1},{4,6},{5,7},{6,4},{7,5},{8,10},{9,11},{10,... | collective-permute-start | bytes 442376 | tf_op jit(solution)/shard_map/ppermute | solution.py:237
  24.8 1.5 %collective-permute-start.4 = (bf16[4,144,128]{2,1,0:T(8,128)(2,1)S(1)}, bf16[4,144,128]{2,1,0:T(8,128)(2,1)S(1)}, u32[]{:S(2)}, u32[]{:S(2)}) collective-permute-start(bf16[4,144,128]{2,1,0:T(8,128)(2,1)S(1)} %get-tuple-element.42), channel_id=1, source_target_pairs={{0,6},{1,7},{2,4},{3,5},{4,2},{5,3},{6,0},{7,1},{8,14},{9,15},{10,... | collective-permute-start | bytes 442376 | tf_op jit(solution)/shard_map/ppermute | solution.py:237
  26.6 0.7 %merge_plane.3 = (bf16[2,144,128]{2,1,0:T(8,128)(2,1)S(1)}, bf16[2,144,128]{2,1,0:T(8,128)(2,1)S(1)}) custom-call(s32[19]{0:T(128)S(1)} %concatenate.3.meta, bf16[4,144,128]{2,1,0:T(8,128)(2,1)S(1)} %get-tuple-element.45.refs_0_, bf16[4,144,128]{2,1,0:T(8,128)(2,1)S(1)} %collective-permute-done.14.refs_1_, ...), custom_call_target="tpu_custom_call" | custom-call | tf_op jit(solution)/shard_map/merge_plane/pallas_call | solution.py:329
  27.4 1.8 %collective-permute-done.2.refs_1_ = bf16[4,144,128]{2,1,0:T(8,128)(2,1)S(1)} collective-permute-done((bf16[4,144,128]{2,1,0:T(8,128)(2,1)S(1)}, bf16[4,144,128]{2,1,0:T(8,128)(2,1)S(1)}, u32[]{:S(2)}, u32[]{:S(2)}) %collective-permute-start.2) | collective-permute-done | bytes 147488 | tf_op jit(solution)/shard_map/ppermute | solution.py:237
  29.2 3.0 %collective-permute-done.3.refs_2_ = bf16[4,144,128]{2,1,0:T(8,128)(2,1)S(1)} collective-permute-done((bf16[4,144,128]{2,1,0:T(8,128)(2,1)S(1)}, bf16[4,144,128]{2,1,0:T(8,128)(2,1)S(1)}, u32[]{:S(2)}, u32[]{:S(2)}) %collective-permute-start.3) | collective-permute-done | bytes 147488 | tf_op jit(solution)/shard_map/ppermute | solution.py:237
  32.2 0.7 %merge_plane.2 = (bf16[2,144,128]{2,1,0:T(8,128)(2,1)S(1)}, bf16[2,144,128]{2,1,0:T(8,128)(2,1)S(1)}) custom-call(s32[19]{0:T(128)S(1)} %concatenate.3.meta, bf16[4,144,128]{2,1,0:T(8,128)(2,1)S(1)} %get-tuple-element.39.refs_0_, bf16[4,144,128]{2,1,0:T(8,128)(2,1)S(1)} %collective-permute-done.2.refs_1_, ...), custom_call_target="tpu_custom_call" | custom-call | tf_op jit(solution)/shard_map/merge_plane/pallas_call | solution.py:329
  33.0 2.6 %collective-permute-start.18 = (bf16[2,144,128]{2,1,0:T(8,128)(2,1)S(1)}, bf16[2,144,128]{2,1,0:T(8,128)(2,1)S(1)}, u32[]{:S(2)}, u32[]{:S(2)}) collective-permute-start(bf16[2,144,128]{2,1,0:T(8,128)(2,1)S(1)} %merge_line.3.refs_0_), channel_id=1, source_target_pairs={{0,16},{1,17},{2,18},{3,19},{4,20},{5,21},{6,22},{7,23},{8,24},{9,... | collective-permute-start | bytes 221192 | tf_op jit(solution)/shard_map/ppermute | solution.py:237
  35.6 2.1 %collective-permute-done.5.refs_1_ = bf16[2,144,128]{2,1,0:T(8,128)(2,1)S(1)} collective-permute-done((bf16[2,144,128]{2,1,0:T(8,128)(2,1)S(1)}, bf16[2,144,128]{2,1,0:T(8,128)(2,1)S(1)}, u32[]{:S(2)}, u32[]{:S(2)}) %collective-permute-start.5) | collective-permute-done | bytes 73760 | tf_op jit(solution)/shard_map/ppermute | solution.py:237
  38.2 1.9 %collective-permute-done.18.refs_1_ = bf16[2,144,128]{2,1,0:T(8,128)(2,1)S(1)} collective-permute-done((bf16[2,144,128]{2,1,0:T(8,128)(2,1)S(1)}, bf16[2,144,128]{2,1,0:T(8,128)(2,1)S(1)}, u32[]{:S(2)}, u32[]{:S(2)}) %collective-permute-start.18) | collective-permute-done | bytes 73760 | tf_op jit(solution)/shard_map/ppermute | solution.py:237
  40.7 2.5 %collective-permute-done.6.refs_1_ = bf16[2,144,128]{2,1,0:T(8,128)(2,1)S(1)} collective-permute-done((bf16[2,144,128]{2,1,0:T(8,128)(2,1)S(1)}, bf16[2,144,128]{2,1,0:T(8,128)(2,1)S(1)}, u32[]{:S(2)}, u32[]{:S(2)}) %collective-permute-start.6) | collective-permute-done | bytes 73760 | tf_op jit(solution)/shard_map/ppermute | solution.py:237
  43.5 1.1 %collective-permute-done.19.other = bf16[2,8,2048]{2,1,0:T(8,128)(2,1)S(1)} collective-permute-done((bf16[2,8,2048]{2,1,0:T(8,128)(2,1)S(1)}, bf16[2,8,2048]{2,1,0:T(8,128)(2,1)S(1)}, u32[]{:S(2)}, u32[]{:S(2)}) %collective-permute-start.19) | collective-permute-done | bytes 65568 | tf_op jit(solution)/shard_map/ppermute | solution.py:237
  44.5 0.6 join.3.refs_0_
  45.2 1.5 %collective-permute-start.22 = (bf16[4,8,2048]{2,1,0:T(8,128)(2,1)S(1)}, bf16[4,8,2048]{2,1,0:T(8,128)(2,1)S(1)}, u32[]{:S(2)}, u32[]{:S(2)}) collective-permute-start(bf16[4,8,2048]{2,1,0:T(8,128)(2,1)S(1)} %join.3.refs_0_), channel_id=1, source_target_pairs={{0,6},{1,7},{2,4},{3,5},{4,2},{5,3},{6,0},{7,1},{8,14},{9,15},{10,... | collective-permute-start | bytes 393224 | tf_op jit(solution)/shard_map/ppermute | solution.py:237
  46.7 1.8 %collective-permute-start.21 = (bf16[4,8,2048]{2,1,0:T(8,128)(2,1)S(1)}, bf16[4,8,2048]{2,1,0:T(8,128)(2,1)S(1)}, u32[]{:S(2)}, u32[]{:S(2)}) collective-permute-start(bf16[4,8,2048]{2,1,0:T(8,128)(2,1)S(1)} %join.3.refs_0_), channel_id=1, source_target_pairs={{0,4},{1,5},{2,6},{3,7},{4,0},{5,1},{6,2},{7,3},{8,12},{9,13},{10,... | collective-permute-start | bytes 393224 | tf_op jit(solution)/shard_map/ppermute | solution.py:237
  48.7 0.6 join.2.refs_0_
  49.7 1.6 %collective-permute-start.9 = (bf16[4,8,2048]{2,1,0:T(8,128)(2,1)S(1)}, bf16[4,8,2048]{2,1,0:T(8,128)(2,1)S(1)}, u32[]{:S(2)}, u32[]{:S(2)}) collective-permute-start(bf16[4,8,2048]{2,1,0:T(8,128)(2,1)S(1)} %join.2.refs_0_), channel_id=1, source_target_pairs={{0,2},{1,3},{2,0},{3,1},{4,6},{5,7},{6,4},{7,5},{8,10},{9,11},{10,... | collective-permute-start | bytes 393224 | tf_op jit(solution)/shard_map/ppermute | solution.py:237
  51.3 1.1 %collective-permute-done.22.refs_3_ = bf16[4,8,2048]{2,1,0:T(8,128)(2,1)S(1)} collective-permute-done((bf16[4,8,2048]{2,1,0:T(8,128)(2,1)S(1)}, bf16[4,8,2048]{2,1,0:T(8,128)(2,1)S(1)}, u32[]{:S(2)}, u32[]{:S(2)}) %collective-permute-start.22) | collective-permute-done | bytes 131104 | tf_op jit(solution)/shard_map/ppermute | solution.py:237
  52.5 2.4 %collective-permute-done.21.refs_2_ = bf16[4,8,2048]{2,1,0:T(8,128)(2,1)S(1)} collective-permute-done((bf16[4,8,2048]{2,1,0:T(8,128)(2,1)S(1)}, bf16[4,8,2048]{2,1,0:T(8,128)(2,1)S(1)}, u32[]{:S(2)}, u32[]{:S(2)}) %collective-permute-start.21) | collective-permute-done | bytes 131104 | tf_op jit(solution)/shard_map/ppermute | solution.py:237
  55.4 2.2 %collective-permute-done.11.refs_2_ = bf16[4,8,2048]{2,1,0:T(8,128)(2,1)S(1)} collective-permute-done((bf16[4,8,2048]{2,1,0:T(8,128)(2,1)S(1)}, bf16[4,8,2048]{2,1,0:T(8,128)(2,1)S(1)}, u32[]{:S(2)}, u32[]{:S(2)}) %collective-permute-start.11) | collective-permute-done | bytes 131104 | tf_op jit(solution)/shard_map/ppermute | solution.py:237
  57.6 1.4 %collective-permute-start.13 = (bf16[4,8,2048]{2,1,0:T(8,128)(2,1)S(1)}, bf16[4,8,2048]{2,1,0:T(8,128)(2,1)S(1)}, u32[]{:S(2)}, u32[]{:S(2)}) collective-permute-start(bf16[4,8,2048]{2,1,0:T(8,128)(2,1)S(1)} %join.2.refs_0_), channel_id=1, source_target_pairs={{0,6},{1,7},{2,4},{3,5},{4,2},{5,3},{6,0},{7,1},{8,14},{9,15},{10,... | collective-permute-start | bytes 393224 | tf_op jit(solution)/shard_map/ppermute | solution.py:237
  59.6 1.3 %project.3.refs_4_ = f32[128,512]{1,0:T(8,128)S(1)} custom-call(s32[19]{0:T(128)S(1)} %concatenate.3.meta, bf16[8192,512]{1,0:T(8,128)(2,1)S(1)} %bitcast.7, bf16[4,8,2048]{2,1,0:T(8,128)(2,1)S(1)} %join.3.refs_0_, bf16[4,8,2048]{2,1,0:T(8,128)(2,1)S(1)} %collective-permute-done.20.refs_1_, bf16[4,8,2048]{2,1,0:T(8,128)(2,1)S(1)} %collective-permute-done.21.refs_2_, ...), custom_call_target="tpu_custom_call" | custom-call | flops 536870912 | bytes 4194304 | tf_op jit(solution)/shard_map/project/pallas_call | solution.py:372
  60.9 3.1 %collective-permute-done.13.refs_3_ = bf16[4,8,2048]{2,1,0:T(8,128)(2,1)S(1)} collective-permute-done((bf16[4,8,2048]{2,1,0:T(8,128)(2,1)S(1)}, bf16[4,8,2048]{2,1,0:T(8,128)(2,1)S(1)}, u32[]{:S(2)}, u32[]{:S(2)}) %collective-permute-start.13) | collective-permute-done | bytes 131104 | tf_op jit(solution)/shard_map/ppermute | solution.py:237
  64.0 1.0 %project.4.refs_4_ = f32[128,512]{1,0:T(8,128)S(1)} custom-call(s32[19]{0:T(128)S(1)} %concatenate.3.meta, bf16[8192,512]{1,0:T(8,128)(2,1)S(1)} %bitcast.7, bf16[4,8,2048]{2,1,0:T(8,128)(2,1)S(1)} %join.2.refs_0_, bf16[4,8,2048]{2,1,0:T(8,128)(2,1)S(1)} %collective-permute-done.9.refs_1_, bf16[4,8,2048]{2,1,0:T(8,128)(2,1)S(1)} %collective-permute-done.11.refs_2_, ...), custom_call_target="tpu_custom_call" | custom-call | flops 268435456 | bytes 2097152 | tf_op jit(solution)/shard_map/project/pallas_call | solution.py:372
  65.3 1.7 %project.5 = f32[128,512]{1,0:T(8,128)} custom-call(s32[19]{0:T(128)S(1)} %concatenate.3.meta, bf16[8192,512]{1,0:T(8,128)(2,1)S(1)} %bitcast.7, bf16[4,8,2048]{2,1,0:T(8,128)(2,1)S(1)} %collective-permute-done.8.refs_0_, bf16[4,8,2048]{2,1,0:T(8,128)(2,1)S(1)} %collective-permute-done.10.refs_1_, bf16[4,8,2048]{2,1,0:T(8,128)(2,1)S(1)} %collective-permute-done.12.refs_2_, ...), custom_call_target="tpu_custom_call" | custom-call | flops 268435456 | bytes 2097152 | tf_op jit(solution)/shard_map/project/pallas_call | solution.py:372
  (48 shorter events, 4.2 us)
Async XLA Ops:
  0.7 4.3 %copy-start = (bf16[128,64,128]{2,1,0:T(8,128)(2,1)S(1)}, bf16[128,64,128]{2,1,0:T(8,128)(2,1)}, u32[]{:S(2)}) copy-start(bf16[128,64,128]{2,1,0:T(8,128)(2,1)} %q_ref.3) | copy-start | bytes 6291460
  4.9 3.8 %collective-permute-start = (bf16[16,144,128]{2,1,0:T(8,128)(2,1)S(1)}, bf16[16,144,128]{2,1,0:T(8,128)(2,1)S(1)}, u32[]{:S(2)}, u32[]{:S(2)}) collective-permute-start(bf16[16,144,128]{2,1,0:T(8,128)(2,1)S(1)} %get-tuple-element.32), channel_id=1, source_target_pairs={{0,1},{1,0},{2,3},{3,2},{4,5},{5,4},{6,7},{7,6},{8,9},{9,8},{10,11... | collective-permute-start | bytes 1769480 | tf_op jit(solution)/shard_map/ppermute | solution.py:237
  5.0 54.6 %slice-start = ((s8[8388608]{0:T(1024)(128)(4,1)}), s8[4194304]{0:T(1024)(128)(4,1)S(1)}, s32[]{:S(2)}) async-start(s8[8388608]{0:T(1024)(128)(4,1)} %bitcast.6), calls=%async_computation | async-start | bytes 8388608
  8.6 12.0 %collective-permute-start.1 = (bf16[16,144,128]{2,1,0:T(8,128)(2,1)S(1)}, bf16[16,144,128]{2,1,0:T(8,128)(2,1)S(1)}, u32[]{:S(2)}, u32[]{:S(2)}) collective-permute-start(bf16[16,144,128]{2,1,0:T(8,128)(2,1)S(1)} %get-tuple-element.38), channel_id=1, source_target_pairs={{0,1},{1,0},{2,3},{3,2},{4,5},{5,4},{6,7},{7,6},{8,9},{9,8},{10,11... | collective-permute-start | bytes 1769480 | tf_op jit(solution)/shard_map/ppermute | solution.py:237
  8.7 50.9 %slice-start.1 = ((s8[8388608]{0:T(1024)(128)(4,1)}), s8[4194304]{0:T(1024)(128)(4,1)S(1)}, s32[]{:S(2)}) async-start(s8[8388608]{0:T(1024)(128)(4,1)} %bitcast.6), calls=%async_computation.1 | async-start | bytes 8388608
  9.6 15.2 %collective-permute-start.14 = (bf16[4,144,128]{2,1,0:T(8,128)(2,1)S(1)}, bf16[4,144,128]{2,1,0:T(8,128)(2,1)S(1)}, u32[]{:S(2)}, u32[]{:S(2)}) collective-permute-start(bf16[4,144,128]{2,1,0:T(8,128)(2,1)S(1)} %get-tuple-element.46), channel_id=1, source_target_pairs={{0,2},{1,3},{2,0},{3,1},{4,6},{5,7},{6,4},{7,5},{8,10},{9,11},{10,... | collective-permute-start | bytes 442376 | tf_op jit(solution)/shard_map/ppermute | solution.py:237
  16.8 9.8 %collective-permute-start.15 = (bf16[4,144,128]{2,1,0:T(8,128)(2,1)S(1)}, bf16[4,144,128]{2,1,0:T(8,128)(2,1)S(1)}, u32[]{:S(2)}, u32[]{:S(2)}) collective-permute-start(bf16[4,144,128]{2,1,0:T(8,128)(2,1)S(1)} %get-tuple-element.47), channel_id=1, source_target_pairs={{0,4},{1,5},{2,6},{3,7},{4,0},{5,1},{6,2},{7,3},{8,12},{9,13},{10,... | collective-permute-start | bytes 442376 | tf_op jit(solution)/shard_map/ppermute | solution.py:237
  16.8 9.8 %collective-permute-start.16 = (bf16[4,144,128]{2,1,0:T(8,128)(2,1)S(1)}, bf16[4,144,128]{2,1,0:T(8,128)(2,1)S(1)}, u32[]{:S(2)}, u32[]{:S(2)}) collective-permute-start(bf16[4,144,128]{2,1,0:T(8,128)(2,1)S(1)} %get-tuple-element.48), channel_id=1, source_target_pairs={{0,6},{1,7},{2,4},{3,5},{4,2},{5,3},{6,0},{7,1},{8,14},{9,15},{10,... | collective-permute-start | bytes 442376 | tf_op jit(solution)/shard_map/ppermute | solution.py:237
  21.5 7.7 %collective-permute-start.2 = (bf16[4,144,128]{2,1,0:T(8,128)(2,1)S(1)}, bf16[4,144,128]{2,1,0:T(8,128)(2,1)S(1)}, u32[]{:S(2)}, u32[]{:S(2)}) collective-permute-start(bf16[4,144,128]{2,1,0:T(8,128)(2,1)S(1)} %get-tuple-element.40), channel_id=1, source_target_pairs={{0,2},{1,3},{2,0},{3,1},{4,6},{5,7},{6,4},{7,5},{8,10},{9,11},{10,... | collective-permute-start | bytes 442376 | tf_op jit(solution)/shard_map/ppermute | solution.py:237
  24.8 7.4 %collective-permute-start.3 = (bf16[4,144,128]{2,1,0:T(8,128)(2,1)S(1)}, bf16[4,144,128]{2,1,0:T(8,128)(2,1)S(1)}, u32[]{:S(2)}, u32[]{:S(2)}) collective-permute-start(bf16[4,144,128]{2,1,0:T(8,128)(2,1)S(1)} %get-tuple-element.41), channel_id=1, source_target_pairs={{0,4},{1,5},{2,6},{3,7},{4,0},{5,1},{6,2},{7,3},{8,12},{9,13},{10,... | collective-permute-start | bytes 442376 | tf_op jit(solution)/shard_map/ppermute | solution.py:237
  24.8 7.4 %collective-permute-start.4 = (bf16[4,144,128]{2,1,0:T(8,128)(2,1)S(1)}, bf16[4,144,128]{2,1,0:T(8,128)(2,1)S(1)}, u32[]{:S(2)}, u32[]{:S(2)}) collective-permute-start(bf16[4,144,128]{2,1,0:T(8,128)(2,1)S(1)} %get-tuple-element.42), channel_id=1, source_target_pairs={{0,6},{1,7},{2,4},{3,5},{4,2},{5,3},{6,0},{7,1},{8,14},{9,15},{10,... | collective-permute-start | bytes 442376 | tf_op jit(solution)/shard_map/ppermute | solution.py:237
  27.3 5.7 %collective-permute-start.17 = (bf16[2,144,128]{2,1,0:T(8,128)(2,1)S(1)}, bf16[2,144,128]{2,1,0:T(8,128)(2,1)S(1)}, u32[]{:S(2)}, u32[]{:S(2)}) collective-permute-start(bf16[2,144,128]{2,1,0:T(8,128)(2,1)S(1)} %get-tuple-element.50), channel_id=1, source_target_pairs={{0,8},{1,9},{2,10},{3,11},{4,12},{5,13},{6,14},{7,15},{8,0},{9,1},... | collective-permute-start | bytes 221192 | tf_op jit(solution)/shard_map/ppermute | solution.py:237
  32.9 4.8 %collective-permute-start.5 = (bf16[2,144,128]{2,1,0:T(8,128)(2,1)S(1)}, bf16[2,144,128]{2,1,0:T(8,128)(2,1)S(1)}, u32[]{:S(2)}, u32[]{:S(2)}) collective-permute-start(bf16[2,144,128]{2,1,0:T(8,128)(2,1)S(1)} %get-tuple-element.44), channel_id=1, source_target_pairs={{0,8},{1,9},{2,10},{3,11},{4,12},{5,13},{6,14},{7,15},{8,0},{9,1},... | collective-permute-start | bytes 221192 | tf_op jit(solution)/shard_map/ppermute | solution.py:237
  33.0 7.0 %collective-permute-start.18 = (bf16[2,144,128]{2,1,0:T(8,128)(2,1)S(1)}, bf16[2,144,128]{2,1,0:T(8,128)(2,1)S(1)}, u32[]{:S(2)}, u32[]{:S(2)}) collective-permute-start(bf16[2,144,128]{2,1,0:T(8,128)(2,1)S(1)} %merge_line.3.refs_0_), channel_id=1, source_target_pairs={{0,16},{1,17},{2,18},{3,19},{4,20},{5,21},{6,22},{7,23},{8,24},{9,... | collective-permute-start | bytes 221192 | tf_op jit(solution)/shard_map/ppermute | solution.py:237
  37.8 5.5 %collective-permute-start.6 = (bf16[2,144,128]{2,1,0:T(8,128)(2,1)S(1)}, bf16[2,144,128]{2,1,0:T(8,128)(2,1)S(1)}, u32[]{:S(2)}, u32[]{:S(2)}) collective-permute-start(bf16[2,144,128]{2,1,0:T(8,128)(2,1)S(1)} %merge_line.2.refs_0_), channel_id=1, source_target_pairs={{0,16},{1,17},{2,18},{3,19},{4,20},{5,21},{6,22},{7,23},{8,24},{9,... | collective-permute-start | bytes 221192 | tf_op jit(solution)/shard_map/ppermute | solution.py:237
  40.2 4.3 %collective-permute-start.19 = (bf16[2,8,2048]{2,1,0:T(8,128)(2,1)S(1)}, bf16[2,8,2048]{2,1,0:T(8,128)(2,1)S(1)}, u32[]{:S(2)}, u32[]{:S(2)}) collective-permute-start(bf16[2,8,2048]{2,1,0:T(8,128)(2,1)S(1)} %finish.3.own), channel_id=1, source_target_pairs={{0,8},{1,9},{2,10},{3,11},{4,12},{5,13},{6,14},{7,15},{8,0},{9,1},... | collective-permute-start | bytes 196616 | tf_op jit(solution)/shard_map/ppermute | solution.py:237
  43.4 5.4 %collective-permute-start.7 = (bf16[2,8,2048]{2,1,0:T(8,128)(2,1)S(1)}, bf16[2,8,2048]{2,1,0:T(8,128)(2,1)S(1)}, u32[]{:S(2)}, u32[]{:S(2)}) collective-permute-start(bf16[2,8,2048]{2,1,0:T(8,128)(2,1)S(1)} %finish.2.own), channel_id=1, source_target_pairs={{0,8},{1,9},{2,10},{3,11},{4,12},{5,13},{6,14},{7,15},{8,0},{9,1},... | collective-permute-start | bytes 196616 | tf_op jit(solution)/shard_map/ppermute | solution.py:237
  45.1 4.6 %collective-permute-start.23 = (bf16[4,8,2048]{2,1,0:T(8,128)(2,1)S(1)}, bf16[4,8,2048]{2,1,0:T(8,128)(2,1)S(1)}, u32[]{:S(2)}, u32[]{:S(2)}) collective-permute-start(bf16[4,8,2048]{2,1,0:T(8,128)(2,1)S(1)} %join.3.refs_0_), channel_id=1, source_target_pairs={{0,1},{1,0},{2,3},{3,2},{4,5},{5,4},{6,7},{7,6},{8,9},{9,8},{10,11... | collective-permute-start | bytes 393224 | tf_op jit(solution)/shard_map/ppermute | solution.py:237
  45.2 7.3 %collective-permute-start.22 = (bf16[4,8,2048]{2,1,0:T(8,128)(2,1)S(1)}, bf16[4,8,2048]{2,1,0:T(8,128)(2,1)S(1)}, u32[]{:S(2)}, u32[]{:S(2)}) collective-permute-start(bf16[4,8,2048]{2,1,0:T(8,128)(2,1)S(1)} %join.3.refs_0_), channel_id=1, source_target_pairs={{0,6},{1,7},{2,4},{3,5},{4,2},{5,3},{6,0},{7,1},{8,14},{9,15},{10,... | collective-permute-start | bytes 393224 | tf_op jit(solution)/shard_map/ppermute | solution.py:237
  46.7 8.2 %collective-permute-start.21 = (bf16[4,8,2048]{2,1,0:T(8,128)(2,1)S(1)}, bf16[4,8,2048]{2,1,0:T(8,128)(2,1)S(1)}, u32[]{:S(2)}, u32[]{:S(2)}) collective-permute-start(bf16[4,8,2048]{2,1,0:T(8,128)(2,1)S(1)} %join.3.refs_0_), channel_id=1, source_target_pairs={{0,4},{1,5},{2,6},{3,7},{4,0},{5,1},{6,2},{7,3},{8,12},{9,13},{10,... | collective-permute-start | bytes 393224 | tf_op jit(solution)/shard_map/ppermute | solution.py:237
  48.4 6.4 %collective-permute-start.20 = (bf16[4,8,2048]{2,1,0:T(8,128)(2,1)S(1)}, bf16[4,8,2048]{2,1,0:T(8,128)(2,1)S(1)}, u32[]{:S(2)}, u32[]{:S(2)}) collective-permute-start(bf16[4,8,2048]{2,1,0:T(8,128)(2,1)S(1)} %join.3.refs_0_), channel_id=1, source_target_pairs={{0,2},{1,3},{2,0},{3,1},{4,6},{5,7},{6,4},{7,5},{8,10},{9,11},{10,... | collective-permute-start | bytes 393224 | tf_op jit(solution)/shard_map/ppermute | solution.py:237
  49.3 8.3 %collective-permute-start.11 = (bf16[4,8,2048]{2,1,0:T(8,128)(2,1)S(1)}, bf16[4,8,2048]{2,1,0:T(8,128)(2,1)S(1)}, u32[]{:S(2)}, u32[]{:S(2)}) collective-permute-start(bf16[4,8,2048]{2,1,0:T(8,128)(2,1)S(1)} %join.2.refs_0_), channel_id=1, source_target_pairs={{0,4},{1,5},{2,6},{3,7},{4,0},{5,1},{6,2},{7,3},{8,12},{9,13},{10,... | collective-permute-start | bytes 393224 | tf_op jit(solution)/shard_map/ppermute | solution.py:237
  49.7 9.3 %collective-permute-start.9 = (bf16[4,8,2048]{2,1,0:T(8,128)(2,1)S(1)}, bf16[4,8,2048]{2,1,0:T(8,128)(2,1)S(1)}, u32[]{:S(2)}, u32[]{:S(2)}) collective-permute-start(bf16[4,8,2048]{2,1,0:T(8,128)(2,1)S(1)} %join.2.refs_0_), channel_id=1, source_target_pairs={{0,2},{1,3},{2,0},{3,1},{4,6},{5,7},{6,4},{7,5},{8,10},{9,11},{10,... | collective-permute-start | bytes 393224 | tf_op jit(solution)/shard_map/ppermute | solution.py:237
  52.5 6.5 %collective-permute-start.26 = (bf16[4,8,2048]{2,1,0:T(8,128)(2,1)S(1)}, bf16[4,8,2048]{2,1,0:T(8,128)(2,1)S(1)}, u32[]{:S(2)}, u32[]{:S(2)}) collective-permute-start(bf16[4,8,2048]{2,1,0:T(8,128)(2,1)S(1)} %collective-permute-done.22.refs_3_), channel_id=1, source_target_pairs={{0,1},{1,0},{2,3},{3,2},{4,5},{5,4},{6,7},{7,6},{8,9},{9,8},{10,11... | collective-permute-start | bytes 393224 | tf_op jit(solution)/shard_map/ppermute | solution.py:237
  54.9 4.7 %collective-permute-start.25 = (bf16[4,8,2048]{2,1,0:T(8,128)(2,1)S(1)}, bf16[4,8,2048]{2,1,0:T(8,128)(2,1)S(1)}, u32[]{:S(2)}, u32[]{:S(2)}) collective-permute-start(bf16[4,8,2048]{2,1,0:T(8,128)(2,1)S(1)} %collective-permute-done.21.refs_2_), channel_id=1, source_target_pairs={{0,1},{1,0},{2,3},{3,2},{4,5},{5,4},{6,7},{7,6},{8,9},{9,8},{10,11... | collective-permute-start | bytes 393224 | tf_op jit(solution)/shard_map/ppermute | solution.py:237
  54.9 4.7 %collective-permute-start.24 = (bf16[4,8,2048]{2,1,0:T(8,128)(2,1)S(1)}, bf16[4,8,2048]{2,1,0:T(8,128)(2,1)S(1)}, u32[]{:S(2)}, u32[]{:S(2)}) collective-permute-start(bf16[4,8,2048]{2,1,0:T(8,128)(2,1)S(1)} %collective-permute-done.20.refs_1_), channel_id=1, source_target_pairs={{0,1},{1,0},{2,3},{3,2},{4,5},{5,4},{6,7},{7,6},{8,9},{9,8},{10,11... | collective-permute-start | bytes 393224 | tf_op jit(solution)/shard_map/ppermute | solution.py:237
  57.6 6.3 %collective-permute-start.13 = (bf16[4,8,2048]{2,1,0:T(8,128)(2,1)S(1)}, bf16[4,8,2048]{2,1,0:T(8,128)(2,1)S(1)}, u32[]{:S(2)}, u32[]{:S(2)}) collective-permute-start(bf16[4,8,2048]{2,1,0:T(8,128)(2,1)S(1)} %join.2.refs_0_), channel_id=1, source_target_pairs={{0,6},{1,7},{2,4},{3,5},{4,2},{5,3},{6,0},{7,1},{8,14},{9,15},{10,... | collective-permute-start | bytes 393224 | tf_op jit(solution)/shard_map/ppermute | solution.py:237
  59.0 5.9 %collective-permute-start.8 = (bf16[4,8,2048]{2,1,0:T(8,128)(2,1)S(1)}, bf16[4,8,2048]{2,1,0:T(8,128)(2,1)S(1)}, u32[]{:S(2)}, u32[]{:S(2)}) collective-permute-start(bf16[4,8,2048]{2,1,0:T(8,128)(2,1)S(1)} %join.2.refs_0_), channel_id=1, source_target_pairs={{0,1},{1,0},{2,3},{3,2},{4,5},{5,4},{6,7},{7,6},{8,9},{9,8},{10,11... | collective-permute-start | bytes 393224 | tf_op jit(solution)/shard_map/ppermute | solution.py:237
  59.0 5.9 %collective-permute-start.12 = (bf16[4,8,2048]{2,1,0:T(8,128)(2,1)S(1)}, bf16[4,8,2048]{2,1,0:T(8,128)(2,1)S(1)}, u32[]{:S(2)}, u32[]{:S(2)}) collective-permute-start(bf16[4,8,2048]{2,1,0:T(8,128)(2,1)S(1)} %collective-permute-done.11.refs_2_), channel_id=1, source_target_pairs={{0,1},{1,0},{2,3},{3,2},{4,5},{5,4},{6,7},{7,6},{8,9},{9,8},{10,11... | collective-permute-start | bytes 393224 | tf_op jit(solution)/shard_map/ppermute | solution.py:237
  59.5 5.4 %collective-permute-start.10 = (bf16[4,8,2048]{2,1,0:T(8,128)(2,1)S(1)}, bf16[4,8,2048]{2,1,0:T(8,128)(2,1)S(1)}, u32[]{:S(2)}, u32[]{:S(2)}) collective-permute-start(bf16[4,8,2048]{2,1,0:T(8,128)(2,1)S(1)} %collective-permute-done.9.refs_1_), channel_id=1, source_target_pairs={{0,1},{1,0},{2,3},{3,2},{4,5},{5,4},{6,7},{7,6},{8,9},{9,8},{10,11... | collective-permute-start | bytes 393224 | tf_op jit(solution)/shard_map/ppermute | solution.py:237
  64.0 1.3 %collective-permute-start.27 = (bf16[4,8,2048]{2,1,0:T(8,128)(2,1)S(1)}, bf16[4,8,2048]{2,1,0:T(8,128)(2,1)S(1)}, u32[]{:S(2)}, u32[]{:S(2)}) collective-permute-start(bf16[4,8,2048]{2,1,0:T(8,128)(2,1)S(1)} %collective-permute-done.13.refs_3_), channel_id=1, source_target_pairs={{0,1},{1,0},{2,3},{3,2},{4,5},{5,4},{6,7},{7,6},{8,9},{9,8},{10,11... | collective-permute-start | bytes 393224 | tf_op jit(solution)/shard_map/ppermute | solution.py:237

commit v6 on v4

--- a/solution.py
+++ b/solution.py
@@ -166,12 +166,16 @@
     ref[z, d : d + STAT, :] = stats
 
 
+def plane_chips(meta):
+    core, my_xy = meta[0], meta[1]
+    return [my_xy, my_xy ^ (1 + core), my_xy ^ (2 - core), my_xy ^ 3]
+
+
 def core_kernel(meta, kept, received, *outs):
-    my_xy = meta[1]
     z_size = outs[0].shape[0]
-    for j, out in enumerate(outs):
+    for chip, out in zip(plane_chips(meta), outs):
         for z in range(z_size):
-            piece = (my_xy ^ j) * z_size + z
+            piece = chip * z_size + z
             store_merged(out, z, [kept[piece], received[piece]])
 
 
@@ -209,15 +213,20 @@
     if not last:
         out_ref[...] = total
         return
-    my_xy = meta[1]
     size = z_size * tokens
-    for j in range(4):
-        to = pl.ds(pl.multiple_of((my_xy ^ j) * size, size), size)
+    for j, chip in enumerate(plane_chips(meta)):
+        to = pl.ds(pl.multiple_of(chip * size, size), size)
         out_ref[to, :] = total[j * size : (j + 1) * size]
 
 
 def hop(value, mask):
     pairs = [(source, source ^ mask) for source in range(lax.axis_size("ctx"))]
+    return lax.ppermute(value, "ctx", pairs)
+
+
+def plane_hop(value, number):
+    masks = {1: (2, 4), 2: (4, 2), 3: (6, 6)}[number]
+    pairs = [(source, source ^ masks[source % 2]) for source in range(lax.axis_size("ctx"))]
     return lax.ppermute(value, "ctx", pairs)
 
 
@@ -346,7 +355,7 @@
 
     def exchange_plane(kept, received):
         parts = merge_cores(kept, received)
-        return [parts[0]] + [hop(parts[j], 2 * j) for j in (1, 2, 3)]
+        return [parts[0]] + [plane_hop(parts[j], j) for j in (1, 2, 3)]
 
     def exchange_line(parts):
         part = merge_chips(parts)
@@ -357,7 +366,7 @@
         return finish([part, hop(part, 8 * reach)])
 
     def gather_plane(attended):
-        return [attended] + [hop(attended, 2 * j) for j in (1, 2, 3)]
+        return [attended] + [plane_hop(attended, j) for j in (1, 2, 3)]
 
     kd, vt, sent = split_and_attend()
     received = hop(sent, 1)
@@ -365,15 +374,15 @@
     next_received = hop(sent, 1)
     parts = merge_cores(kept, received)
     parts, kd = lax.optimization_barrier((parts, kd))
-    first = [parts[0]] + [hop(parts[j], 2 * j) for j in (1, 2, 3)]
+    first = [parts[0]] + [plane_hop(parts[j], j) for j in (1, 2, 3)]
     (kept,) = attend([(1, False)], kd, vt)
     second = exchange_plane(kept, next_received)
     own = gather_plane(exchange_line(first))
-    other = [hop(part, 1) for part in own]
+    other = [hop(own[j], 1) for j in (0, 2, 1, 3)]
     next_own = gather_plane(exchange_line(second))
     total = project([(0, False), (0, True)], own + other, None)
     next_own[3], total = lax.optimization_barrier((next_own[3], total))
-    next_other = [hop(part, 1) for part in next_own]
+    next_other = [hop(next_own[j], 1) for j in (0, 2, 1, 3)]
     total = project([(1, False)], next_own, total)
     return project([(1, True)], next_other, total, last=True)
 

time: 63.8 us -> 67.7 us (1.061); the launches traced: 63.9 us -> 68.6 us
  starting transfers between devices: 25 us -> 29.8 us
    ppermute x0 -> x12, starting transfers between devices: none -> 17.4 us  [plane_hop(): return lax.ppermute(value, 'ctx', pairs)]
    ppermute x26 -> x14, starting transfers between devices: 25 us -> 12.4 us  [hop(): return lax.ppermute(value, 'ctx', pairs)]
    ppermute x26 -> x14, waiting for transfers between devices: 24.1 us -> 12.8 us  [hop(): return lax.ppermute(value, 'ctx', pairs)]
    ppermute x0 -> x12, waiting for transfers between devices: none -> 11.2 us  [plane_hop(): return lax.ppermute(value, 'ctx', pairs)]
  transfers between devices with their start and end apart: 26 -> 26, of which waited for: 10 -> 9; matrix products, arithmetic and copies ran while one was open for 0% -> 0% of each run, Pallas kernels for 14% -> 13%
where the time goes in v6:
time: 67.7 us; the launch traced here: 68.6 us
  starting transfers between devices  29.8 us (44%)
  waiting for transfers between devices  24.1 us (36%)
  Pallas kernels  13.8 us (20%)
  other arithmetic  0.75 us (1%)
    ppermute x12, starting transfers between devices, plane_hop(): return lax.ppermute(value, 'ctx', pairs)  17.4 us
    ppermute x14, waiting for transfers between devices, hop(): return lax.ppermute(value, 'ctx', pairs)  12.8 us
    ppermute x14, starting transfers between devices, hop(): return lax.ppermute(value, 'ctx', pairs)  12.4 us
    ppermute x12, waiting for transfers between devices, plane_hop(): return lax.ppermute(value, 'ctx', pairs)  11.2 us
    pallas_call x2, Pallas kernels, attend(): pl.pallas_call(functools.partial(attention_kernel, chunk_roles), in_specs...  4.02 us
    pallas_call x3, Pallas kernels, project(): pl.pallas_call(functools.partial(project_kernel, terms, bool(more), last)...  3.94 us
    pallas_call x1, Pallas kernels, split_and_attend(): pl.pallas_call(split_kernel, in_specs=[SMEM] + [HBM] * 3, out_specs=[VMEM...  3.27 us
    pallas_call x2, Pallas kernels, merge_cores(): pl.pallas_call(core_kernel, in_specs=[SMEM] + [VMEM] * 2, out_specs=[VMEM...  1.64 us
  transfers between devices with their start and end apart: 26, of which 9 were waited for; matrix products, arithmetic and copies ran while one was open for 0% of the time, Pallas kernels for 13%

profile of v6, /device:TPU:0, one launch (start us, length us, event | category | flops | bytes accessed | tf_op | source)
XLA Modules:
  0.0 68.6 jit_solution(4881311651364187643)
XLA Ops:
  0.0 0.7 %pad_add_fusion.meta = s32[18]{0:T(128)S(1)} fusion(s32[8]{0:T(128)} %param.10, s32[8]{0:T(128)} %bitcast.9, s32[1]{0:T(128)} %bitcast.1, s32[1]{0:T(128)} %bitcast), kind=kLoop, calls=%fused_computation | loop fusion | flops 54 | bytes 144 | tf_op jit(solution)/shard_map/concatenate | solution.py:254
  0.8 3.3 %split_and_attend.1 = (bf16[4,1024,128]{2,1,0:T(8,128)(2,1)S(1)}, bf16[4,144,1024]{2,1,0:T(8,128)(2,1)S(1)}, bf16[16,144,128]{2,1,0:T(8,128)(2,1)S(1)}) custom-call(s32[18]{0:T(128)S(1)} %pad_add_fusion.meta, bf16[4096,128]{1,0:T(8,128)(2,1)} %bitcast.7, bf16[4096,128]{1,0:T(8,128)(2,1)} %bitcast.8, bf16[128,64,128]{2,1,0:T(8,128)(2,1)} %q_ref.3), custom_call_target="tpu_custom_call" | custom-call | flops 1073741824 | bytes 2097152 | tf_op jit(solution)/shard_map/split_and_attend/pallas_call | solution.py:264
  4.1 2.3 %attend.2 = (bf16[16,144,128]{2,1,0:T(8,128)(2,1)S(1)}, bf16[16,144,128]{2,1,0:T(8,128)(2,1)S(1)}) custom-call(s32[18]{0:T(128)S(1)} %pad_add_fusion.meta, bf16[4,1024,128]{2,1,0:T(8,128)(2,1)S(1)} %get-tuple-element.33.kd, bf16[4,144,1024]{2,1,0:T(8,128)(2,1)S(1)} %get-tuple-element.26.vt, bf16[128,64,128]{2,1,0:T(8,128)(2,1)S(1)} %copy-done), custom_call_target="tpu_custom_call" | custom-call | flops 2147483648 | bytes 1048576 | tf_op jit(solution)/shard_map/attend/pallas_call | solution.py:293
  6.6 0.8 %merge_cores.2 = (bf16[4,144,128]{2,1,0:T(8,128)(2,1)S(1)}, bf16[4,144,128]{2,1,0:T(8,128)(2,1)S(1)}, bf16[4,144,128]{2,1,0:T(8,128)(2,1)S(1)}, bf16[4,144,128]{2,1,0:T(8,128)(2,1)S(1)}) custom-call(s32[18]{0:T(128)S(1)} %pad_add_fusion.meta, bf16[16,144,128]{2,1,0:T(8,128)(2,1)S(1)} %get-tuple-element.27.kept, ...), custom_call_target="tpu_custom_call" | custom-call | tf_op jit(solution)/shard_map/merge_cores/pallas_call | solution.py:308
  7.4 5.7 %collective-permute-start.13 = (bf16[4,144,128]{2,1,0:T(8,128)(2,1)S(1)}, bf16[4,144,128]{2,1,0:T(8,128)(2,1)S(1)}, u32[]{:S(2)}, u32[]{:S(2)}) collective-permute-start(bf16[4,144,128]{2,1,0:T(8,128)(2,1)S(1)} %get-tuple-element.40), channel_id=1, source_target_pairs={{0,2},{1,5},{2,0},{3,7},{4,6},{5,1},{6,4},{7,3},{8,10},{9,13},{10,... | collective-permute-start | bytes 442376 | tf_op jit(solution)/shard_map/ppermute | solution.py:230
  13.1 1.5 %collective-permute-start.15 = (bf16[4,144,128]{2,1,0:T(8,128)(2,1)S(1)}, bf16[4,144,128]{2,1,0:T(8,128)(2,1)S(1)}, u32[]{:S(2)}, u32[]{:S(2)}) collective-permute-start(bf16[4,144,128]{2,1,0:T(8,128)(2,1)S(1)} %get-tuple-element.42), channel_id=1, source_target_pairs={{0,6},{1,7},{2,4},{3,5},{4,2},{5,3},{6,0},{7,1},{8,14},{9,15},{10,... | collective-permute-start | bytes 442376 | tf_op jit(solution)/shard_map/ppermute | solution.py:230
  14.6 1.7 %attend.3.kept = bf16[16,144,128]{2,1,0:T(8,128)(2,1)S(1)} custom-call(s32[18]{0:T(128)S(1)} %pad_add_fusion.meta, bf16[4,1024,128]{2,1,0:T(8,128)(2,1)S(1)} %get-tuple-element.33.kd, bf16[4,144,1024]{2,1,0:T(8,128)(2,1)S(1)} %get-tuple-element.26.vt, bf16[128,64,128]{2,1,0:T(8,128)(2,1)S(1)} %copy-done), custom_call_target="tpu_custom_call" | custom-call | flops 1073741824 | bytes 524288 | tf_op jit(solution)/shard_map/attend/pallas_call | solution.py:293
  16.3 0.8 %merge_cores.3 = (bf16[4,144,128]{2,1,0:T(8,128)(2,1)S(1)}, bf16[4,144,128]{2,1,0:T(8,128)(2,1)S(1)}, bf16[4,144,128]{2,1,0:T(8,128)(2,1)S(1)}, bf16[4,144,128]{2,1,0:T(8,128)(2,1)S(1)}) custom-call(s32[18]{0:T(128)S(1)} %pad_add_fusion.meta, bf16[16,144,128]{2,1,0:T(8,128)(2,1)S(1)} %attend.3.kept, bf16[16,144,128]{2,1,0:T(8,128)(2,1)S(1)} %collective-permute-done.1.received), custom_call_target="tpu_custom_call" | custom-call | tf_op jit(solution)/shard_map/merge_cores/pallas_call | solution.py:308
  17.1 2.7 %collective-permute-start.2 = (bf16[4,144,128]{2,1,0:T(8,128)(2,1)S(1)}, bf16[4,144,128]{2,1,0:T(8,128)(2,1)S(1)}, u32[]{:S(2)}, u32[]{:S(2)}) collective-permute-start(bf16[4,144,128]{2,1,0:T(8,128)(2,1)S(1)} %get-tuple-element.36), channel_id=1, source_target_pairs={{0,2},{1,5},{2,0},{3,7},{4,6},{5,1},{6,4},{7,3},{8,10},{9,13},{10,... | collective-permute-start | bytes 442376 | tf_op jit(solution)/shard_map/ppermute | solution.py:230
  19.8 1.5 %collective-permute-start.4 = (bf16[4,144,128]{2,1,0:T(8,128)(2,1)S(1)}, bf16[4,144,128]{2,1,0:T(8,128)(2,1)S(1)}, u32[]{:S(2)}, u32[]{:S(2)}) collective-permute-start(bf16[4,144,128]{2,1,0:T(8,128)(2,1)S(1)} %get-tuple-element.38), channel_id=1, source_target_pairs={{0,6},{1,7},{2,4},{3,5},{4,2},{5,3},{6,0},{7,1},{8,14},{9,15},{10,... | collective-permute-start | bytes 442376 | tf_op jit(solution)/shard_map/ppermute | solution.py:230
  21.4 0.4 collective-permute-done.15.refs_3_
  21.9 5.0 %collective-permute-start.16 = (bf16[4,144,128]{2,1,0:T(8,128)(2,1)S(1)}, bf16[4,144,128]{2,1,0:T(8,128)(2,1)S(1)}, u32[]{:S(2)}, u32[]{:S(2)}) collective-permute-start(bf16[4,144,128]{2,1,0:T(8,128)(2,1)S(1)} %merge_chips.6.refs_0_), channel_id=1, source_target_pairs={{0,8},{1,9},{2,10},{3,11},{4,12},{5,13},{6,14},{7,15},{8,0},{9,1},... | collective-permute-start | bytes 442376 | tf_op jit(solution)/shard_map/ppermute | solution.py:224
  26.9 1.2 %collective-permute-done.3.refs_2_ = bf16[4,144,128]{2,1,0:T(8,128)(2,1)S(1)} collective-permute-done((bf16[4,144,128]{2,1,0:T(8,128)(2,1)S(1)}, bf16[4,144,128]{2,1,0:T(8,128)(2,1)S(1)}, u32[]{:S(2)}, u32[]{:S(2)}) %collective-permute-start.3) | collective-permute-done | bytes 147488 | tf_op jit(solution)/shard_map/ppermute | solution.py:230
  28.3 5.3 %collective-permute-start.5 = (bf16[4,144,128]{2,1,0:T(8,128)(2,1)S(1)}, bf16[4,144,128]{2,1,0:T(8,128)(2,1)S(1)}, u32[]{:S(2)}, u32[]{:S(2)}) collective-permute-start(bf16[4,144,128]{2,1,0:T(8,128)(2,1)S(1)} %merge_chips.4.refs_0_), channel_id=1, source_target_pairs={{0,8},{1,9},{2,10},{3,11},{4,12},{5,13},{6,14},{7,15},{8,0},{9,1},... | collective-permute-start | bytes 442376 | tf_op jit(solution)/shard_map/ppermute | solution.py:224
  33.8 4.6 %collective-permute-done.5.refs_1_ = bf16[4,144,128]{2,1,0:T(8,128)(2,1)S(1)} collective-permute-done((bf16[4,144,128]{2,1,0:T(8,128)(2,1)S(1)}, bf16[4,144,128]{2,1,0:T(8,128)(2,1)S(1)}, u32[]{:S(2)}, u32[]{:S(2)}) %collective-permute-start.5) | collective-permute-done | bytes 147488 | tf_op jit(solution)/shard_map/ppermute | solution.py:224
  38.4 0.6 collective-permute-start.6
  39.0 8.0 %collective-permute-done.17.refs_1_ = bf16[4,144,128]{2,1,0:T(8,128)(2,1)S(1)} collective-permute-done((bf16[4,144,128]{2,1,0:T(8,128)(2,1)S(1)}, bf16[4,144,128]{2,1,0:T(8,128)(2,1)S(1)}, u32[]{:S(2)}, u32[]{:S(2)}) %collective-permute-start.17) | collective-permute-done | bytes 147488 | tf_op jit(solution)/shard_map/ppermute | solution.py:224
  47.3 0.5 collective-permute-start.20
  47.8 1.2 %collective-permute-start.19 = (bf16[4,8,2048]{2,1,0:T(8,128)(2,1)S(1)}, bf16[4,8,2048]{2,1,0:T(8,128)(2,1)S(1)}, u32[]{:S(2)}, u32[]{:S(2)}) collective-permute-start(bf16[4,8,2048]{2,1,0:T(8,128)(2,1)S(1)} %finish.3.refs_0_), channel_id=1, source_target_pairs={{0,4},{1,3},{2,6},{3,1},{4,0},{5,7},{6,2},{7,5},{8,12},{9,11},{10,... | collective-permute-start | bytes 393224 | tf_op jit(solution)/shard_map/ppermute | solution.py:230
  49.0 1.9 %collective-permute-start.18 = (bf16[4,8,2048]{2,1,0:T(8,128)(2,1)S(1)}, bf16[4,8,2048]{2,1,0:T(8,128)(2,1)S(1)}, u32[]{:S(2)}, u32[]{:S(2)}) collective-permute-start(bf16[4,8,2048]{2,1,0:T(8,128)(2,1)S(1)} %finish.3.refs_0_), channel_id=1, source_target_pairs={{0,2},{1,5},{2,0},{3,7},{4,6},{5,1},{6,4},{7,3},{8,10},{9,13},{10,... | collective-permute-start | bytes 393224 | tf_op jit(solution)/shard_map/ppermute | solution.py:230
  51.1 0.2 collective-permute-start.10
  51.3 0.8 %collective-permute-start.8 = (bf16[4,8,2048]{2,1,0:T(8,128)(2,1)S(1)}, bf16[4,8,2048]{2,1,0:T(8,128)(2,1)S(1)}, u32[]{:S(2)}, u32[]{:S(2)}) collective-permute-start(bf16[4,8,2048]{2,1,0:T(8,128)(2,1)S(1)} %finish.2.refs_0_), channel_id=1, source_target_pairs={{0,4},{1,3},{2,6},{3,1},{4,0},{5,7},{6,2},{7,5},{8,12},{9,11},{10,... | collective-permute-start | bytes 393224 | tf_op jit(solution)/shard_map/ppermute | solution.py:230
  52.1 2.5 %collective-permute-done.20.refs_3_ = bf16[4,8,2048]{2,1,0:T(8,128)(2,1)S(1)} collective-permute-done((bf16[4,8,2048]{2,1,0:T(8,128)(2,1)S(1)}, bf16[4,8,2048]{2,1,0:T(8,128)(2,1)S(1)}, u32[]{:S(2)}, u32[]{:S(2)}) %collective-permute-start.20) | collective-permute-done | bytes 131104 | tf_op jit(solution)/shard_map/ppermute | solution.py:230
  54.6 2.3 %collective-permute-done.19.refs_2_ = bf16[4,8,2048]{2,1,0:T(8,128)(2,1)S(1)} collective-permute-done((bf16[4,8,2048]{2,1,0:T(8,128)(2,1)S(1)}, bf16[4,8,2048]{2,1,0:T(8,128)(2,1)S(1)}, u32[]{:S(2)}, u32[]{:S(2)}) %collective-permute-start.19) | collective-permute-done | bytes 131104 | tf_op jit(solution)/shard_map/ppermute | solution.py:230
  56.9 0.5 collective-permute-start.23
  57.4 1.1 %collective-permute-done.10.refs_1_ = bf16[4,8,2048]{2,1,0:T(8,128)(2,1)S(1)} collective-permute-done((bf16[4,8,2048]{2,1,0:T(8,128)(2,1)S(1)}, bf16[4,8,2048]{2,1,0:T(8,128)(2,1)S(1)}, u32[]{:S(2)}, u32[]{:S(2)}) %collective-permute-start.10) | collective-permute-done | bytes 131104 | tf_op jit(solution)/shard_map/ppermute | solution.py:230
  58.6 1.3 %collective-permute-start.12 = (bf16[4,8,2048]{2,1,0:T(8,128)(2,1)S(1)}, bf16[4,8,2048]{2,1,0:T(8,128)(2,1)S(1)}, u32[]{:S(2)}, u32[]{:S(2)}) collective-permute-start(bf16[4,8,2048]{2,1,0:T(8,128)(2,1)S(1)} %finish.2.refs_0_), channel_id=1, source_target_pairs={{0,6},{1,7},{2,4},{3,5},{4,2},{5,3},{6,0},{7,1},{8,14},{9,15},{10,... | collective-permute-start | bytes 393224 | tf_op jit(solution)/shard_map/ppermute | solution.py:230
  59.9 0.5 collective-permute-start.11
  60.5 1.3 %project.3.refs_4_ = f32[128,512]{1,0:T(8,128)S(1)} custom-call(s32[18]{0:T(128)S(1)} %pad_add_fusion.meta, bf16[8192,512]{1,0:T(8,128)(2,1)S(1)} %bitcast.6, bf16[4,8,2048]{2,1,0:T(8,128)(2,1)S(1)} %finish.3.refs_0_, bf16[4,8,2048]{2,1,0:T(8,128)(2,1)S(1)} %collective-permute-done.18.refs_1_, bf16[4,8,2048]{2,1,0:T(8,128)(2,1)S(1)} %collective-permute-done.19.refs_2_, ...), custom_call_target="tpu_custom_call" | custom-call | flops 536870912 | bytes 4194304 | tf_op jit(solution)/shard_map/project/pallas_call | solution.py:342
  61.8 3.7 %collective-permute-done.12.refs_3_ = bf16[4,8,2048]{2,1,0:T(8,128)(2,1)S(1)} collective-permute-done((bf16[4,8,2048]{2,1,0:T(8,128)(2,1)S(1)}, bf16[4,8,2048]{2,1,0:T(8,128)(2,1)S(1)}, u32[]{:S(2)}, u32[]{:S(2)}) %collective-permute-start.12) | collective-permute-done | bytes 131104 | tf_op jit(solution)/shard_map/ppermute | solution.py:230
  65.6 1.0 %project.4.refs_4_ = f32[128,512]{1,0:T(8,128)S(1)} custom-call(s32[18]{0:T(128)S(1)} %pad_add_fusion.meta, bf16[8192,512]{1,0:T(8,128)(2,1)S(1)} %bitcast.6, bf16[4,8,2048]{2,1,0:T(8,128)(2,1)S(1)} %finish.2.refs_0_, bf16[4,8,2048]{2,1,0:T(8,128)(2,1)S(1)} %collective-permute-done.10.refs_1_, bf16[4,8,2048]{2,1,0:T(8,128)(2,1)S(1)} %collective-permute-done.8.refs_2_, ...), custom_call_target="tpu_custom_call" | custom-call | flops 268435456 | bytes 2097152 | tf_op jit(solution)/shard_map/project/pallas_call | solution.py:342
  66.9 1.7 %project.5 = f32[128,512]{1,0:T(8,128)} custom-call(s32[18]{0:T(128)S(1)} %pad_add_fusion.meta, bf16[8192,512]{1,0:T(8,128)(2,1)S(1)} %bitcast.6, bf16[4,8,2048]{2,1,0:T(8,128)(2,1)S(1)} %collective-permute-done.7.refs_0_, bf16[4,8,2048]{2,1,0:T(8,128)(2,1)S(1)} %collective-permute-done.9.refs_1_, bf16[4,8,2048]{2,1,0:T(8,128)(2,1)S(1)} %collective-permute-done.11.refs_2_, ...), custom_call_target="tpu_custom_call" | custom-call | flops 268435456 | bytes 2097152 | tf_op jit(solution)/shard_map/project/pallas_call | solution.py:342
  (42 shorter events, 1.7 us)
Async XLA Ops:
  0.7 3.4 %copy-start = (bf16[128,64,128]{2,1,0:T(8,128)(2,1)S(1)}, bf16[128,64,128]{2,1,0:T(8,128)(2,1)}, u32[]{:S(2)}) copy-start(bf16[128,64,128]{2,1,0:T(8,128)(2,1)} %q_ref.3) | copy-start | bytes 6291460
  4.0 2.5 %collective-permute-start = (bf16[16,144,128]{2,1,0:T(8,128)(2,1)S(1)}, bf16[16,144,128]{2,1,0:T(8,128)(2,1)S(1)}, u32[]{:S(2)}, u32[]{:S(2)}) collective-permute-start(bf16[16,144,128]{2,1,0:T(8,128)(2,1)S(1)} %get-tuple-element.28), channel_id=1, source_target_pairs={{0,1},{1,0},{2,3},{3,2},{4,5},{5,4},{6,7},{7,6},{8,9},{9,8},{10,11... | collective-permute-start | bytes 1769480 | tf_op jit(solution)/shard_map/ppermute | solution.py:224
  4.1 56.4 %slice-start = ((s8[8388608]{0:T(1024)(128)(4,1)}), s8[4194304]{0:T(1024)(128)(4,1)S(1)}, s32[]{:S(2)}) async-start(s8[8388608]{0:T(1024)(128)(4,1)} %bitcast.5), calls=%async_computation | async-start | bytes 8388608
  6.5 9.8 %collective-permute-start.1 = (bf16[16,144,128]{2,1,0:T(8,128)(2,1)S(1)}, bf16[16,144,128]{2,1,0:T(8,128)(2,1)S(1)}, u32[]{:S(2)}, u32[]{:S(2)}) collective-permute-start(bf16[16,144,128]{2,1,0:T(8,128)(2,1)S(1)} %get-tuple-element.34), channel_id=1, source_target_pairs={{0,1},{1,0},{2,3},{3,2},{4,5},{5,4},{6,7},{7,6},{8,9},{9,8},{10,11... | collective-permute-start | bytes 1769480 | tf_op jit(solution)/shard_map/ppermute | solution.py:224
  7.4 53.1 %slice-start.1 = ((s8[8388608]{0:T(1024)(128)(4,1)}), s8[4194304]{0:T(1024)(128)(4,1)S(1)}, s32[]{:S(2)}) async-start(s8[8388608]{0:T(1024)(128)(4,1)} %bitcast.5), calls=%async_computation.1 | async-start | bytes 8388608
  7.4 12.4 %collective-permute-start.13 = (bf16[4,144,128]{2,1,0:T(8,128)(2,1)S(1)}, bf16[4,144,128]{2,1,0:T(8,128)(2,1)S(1)}, u32[]{:S(2)}, u32[]{:S(2)}) collective-permute-start(bf16[4,144,128]{2,1,0:T(8,128)(2,1)S(1)} %get-tuple-element.40), channel_id=1, source_target_pairs={{0,2},{1,5},{2,0},{3,7},{4,6},{5,1},{6,4},{7,3},{8,10},{9,13},{10,... | collective-permute-start | bytes 442376 | tf_op jit(solution)/shard_map/ppermute | solution.py:230
  13.1 8.3 %collective-permute-start.14 = (bf16[4,144,128]{2,1,0:T(8,128)(2,1)S(1)}, bf16[4,144,128]{2,1,0:T(8,128)(2,1)S(1)}, u32[]{:S(2)}, u32[]{:S(2)}) collective-permute-start(bf16[4,144,128]{2,1,0:T(8,128)(2,1)S(1)} %get-tuple-element.41), channel_id=1, source_target_pairs={{0,4},{1,3},{2,6},{3,1},{4,0},{5,7},{6,2},{7,5},{8,12},{9,11},{10,... | collective-permute-start | bytes 442376 | tf_op jit(solution)/shard_map/ppermute | solution.py:230
  13.1 8.7 %collective-permute-start.15 = (bf16[4,144,128]{2,1,0:T(8,128)(2,1)S(1)}, bf16[4,144,128]{2,1,0:T(8,128)(2,1)S(1)}, u32[]{:S(2)}, u32[]{:S(2)}) collective-permute-start(bf16[4,144,128]{2,1,0:T(8,128)(2,1)S(1)} %get-tuple-element.42), channel_id=1, source_target_pairs={{0,6},{1,7},{2,4},{3,5},{4,2},{5,3},{6,0},{7,1},{8,14},{9,15},{10,... | collective-permute-start | bytes 442376 | tf_op jit(solution)/shard_map/ppermute | solution.py:230
  17.1 9.8 %collective-permute-start.2 = (bf16[4,144,128]{2,1,0:T(8,128)(2,1)S(1)}, bf16[4,144,128]{2,1,0:T(8,128)(2,1)S(1)}, u32[]{:S(2)}, u32[]{:S(2)}) collective-permute-start(bf16[4,144,128]{2,1,0:T(8,128)(2,1)S(1)} %get-tuple-element.36), channel_id=1, source_target_pairs={{0,2},{1,5},{2,0},{3,7},{4,6},{5,1},{6,4},{7,3},{8,10},{9,13},{10,... | collective-permute-start | bytes 442376 | tf_op jit(solution)/shard_map/ppermute | solution.py:230
  19.8 8.3 %collective-permute-start.3 = (bf16[4,144,128]{2,1,0:T(8,128)(2,1)S(1)}, bf16[4,144,128]{2,1,0:T(8,128)(2,1)S(1)}, u32[]{:S(2)}, u32[]{:S(2)}) collective-permute-start(bf16[4,144,128]{2,1,0:T(8,128)(2,1)S(1)} %get-tuple-element.37), channel_id=1, source_target_pairs={{0,4},{1,3},{2,6},{3,1},{4,0},{5,7},{6,2},{7,5},{8,12},{9,11},{10,... | collective-permute-start | bytes 442376 | tf_op jit(solution)/shard_map/ppermute | solution.py:230
  19.8 8.3 %collective-permute-start.4 = (bf16[4,144,128]{2,1,0:T(8,128)(2,1)S(1)}, bf16[4,144,128]{2,1,0:T(8,128)(2,1)S(1)}, u32[]{:S(2)}, u32[]{:S(2)}) collective-permute-start(bf16[4,144,128]{2,1,0:T(8,128)(2,1)S(1)} %get-tuple-element.38), channel_id=1, source_target_pairs={{0,6},{1,7},{2,4},{3,5},{4,2},{5,3},{6,0},{7,1},{8,14},{9,15},{10,... | collective-permute-start | bytes 442376 | tf_op jit(solution)/shard_map/ppermute | solution.py:230
  21.9 11.7 %collective-permute-start.16 = (bf16[4,144,128]{2,1,0:T(8,128)(2,1)S(1)}, bf16[4,144,128]{2,1,0:T(8,128)(2,1)S(1)}, u32[]{:S(2)}, u32[]{:S(2)}) collective-permute-start(bf16[4,144,128]{2,1,0:T(8,128)(2,1)S(1)} %merge_chips.6.refs_0_), channel_id=1, source_target_pairs={{0,8},{1,9},{2,10},{3,11},{4,12},{5,13},{6,14},{7,15},{8,0},{9,1},... | collective-permute-start | bytes 442376 | tf_op jit(solution)/shard_map/ppermute | solution.py:224
  28.3 10.1 %collective-permute-start.5 = (bf16[4,144,128]{2,1,0:T(8,128)(2,1)S(1)}, bf16[4,144,128]{2,1,0:T(8,128)(2,1)S(1)}, u32[]{:S(2)}, u32[]{:S(2)}) collective-permute-start(bf16[4,144,128]{2,1,0:T(8,128)(2,1)S(1)} %merge_chips.4.refs_0_), channel_id=1, source_target_pairs={{0,8},{1,9},{2,10},{3,11},{4,12},{5,13},{6,14},{7,15},{8,0},{9,1},... | collective-permute-start | bytes 442376 | tf_op jit(solution)/shard_map/ppermute | solution.py:224
  33.7 13.3 %collective-permute-start.17 = (bf16[4,144,128]{2,1,0:T(8,128)(2,1)S(1)}, bf16[4,144,128]{2,1,0:T(8,128)(2,1)S(1)}, u32[]{:S(2)}, u32[]{:S(2)}) collective-permute-start(bf16[4,144,128]{2,1,0:T(8,128)(2,1)S(1)} %merge_chips.7.refs_0_), channel_id=1, source_target_pairs={{0,16},{1,17},{2,18},{3,19},{4,20},{5,21},{6,22},{7,23},{8,24},{9,... | collective-permute-start | bytes 442376 | tf_op jit(solution)/shard_map/ppermute | solution.py:224
  38.4 12.4 %collective-permute-start.6 = (bf16[4,144,128]{2,1,0:T(8,128)(2,1)S(1)}, bf16[4,144,128]{2,1,0:T(8,128)(2,1)S(1)}, u32[]{:S(2)}, u32[]{:S(2)}) collective-permute-start(bf16[4,144,128]{2,1,0:T(8,128)(2,1)S(1)} %merge_chips.5.refs_0_), channel_id=1, source_target_pairs={{0,16},{1,17},{2,18},{3,19},{4,20},{5,21},{6,22},{7,23},{8,24},{9,... | collective-permute-start | bytes 442376 | tf_op jit(solution)/shard_map/ppermute | solution.py:224
  47.2 4.1 %collective-permute-start.21 = (bf16[4,8,2048]{2,1,0:T(8,128)(2,1)S(1)}, bf16[4,8,2048]{2,1,0:T(8,128)(2,1)S(1)}, u32[]{:S(2)}, u32[]{:S(2)}) collective-permute-start(bf16[4,8,2048]{2,1,0:T(8,128)(2,1)S(1)} %finish.3.refs_0_), channel_id=1, source_target_pairs={{0,1},{1,0},{2,3},{3,2},{4,5},{5,4},{6,7},{7,6},{8,9},{9,8},{10,11... | collective-permute-start | bytes 393224 | tf_op jit(solution)/shard_map/ppermute | solution.py:224
  47.3 7.3 %collective-permute-start.20 = (bf16[4,8,2048]{2,1,0:T(8,128)(2,1)S(1)}, bf16[4,8,2048]{2,1,0:T(8,128)(2,1)S(1)}, u32[]{:S(2)}, u32[]{:S(2)}) collective-permute-start(bf16[4,8,2048]{2,1,0:T(8,128)(2,1)S(1)} %finish.3.refs_0_), channel_id=1, source_target_pairs={{0,6},{1,7},{2,4},{3,5},{4,2},{5,3},{6,0},{7,1},{8,14},{9,15},{10,... | collective-permute-start | bytes 393224 | tf_op jit(solution)/shard_map/ppermute | solution.py:230
  47.8 9.1 %collective-permute-start.19 = (bf16[4,8,2048]{2,1,0:T(8,128)(2,1)S(1)}, bf16[4,8,2048]{2,1,0:T(8,128)(2,1)S(1)}, u32[]{:S(2)}, u32[]{:S(2)}) collective-permute-start(bf16[4,8,2048]{2,1,0:T(8,128)(2,1)S(1)} %finish.3.refs_0_), channel_id=1, source_target_pairs={{0,4},{1,3},{2,6},{3,1},{4,0},{5,7},{6,2},{7,5},{8,12},{9,11},{10,... | collective-permute-start | bytes 393224 | tf_op jit(solution)/shard_map/ppermute | solution.py:230
  49.0 7.9 %collective-permute-start.18 = (bf16[4,8,2048]{2,1,0:T(8,128)(2,1)S(1)}, bf16[4,8,2048]{2,1,0:T(8,128)(2,1)S(1)}, u32[]{:S(2)}, u32[]{:S(2)}) collective-permute-start(bf16[4,8,2048]{2,1,0:T(8,128)(2,1)S(1)} %finish.3.refs_0_), channel_id=1, source_target_pairs={{0,2},{1,5},{2,0},{3,7},{4,6},{5,1},{6,4},{7,3},{8,10},{9,13},{10,... | collective-permute-start | bytes 393224 | tf_op jit(solution)/shard_map/ppermute | solution.py:230
  51.1 7.5 %collective-permute-start.10 = (bf16[4,8,2048]{2,1,0:T(8,128)(2,1)S(1)}, bf16[4,8,2048]{2,1,0:T(8,128)(2,1)S(1)}, u32[]{:S(2)}, u32[]{:S(2)}) collective-permute-start(bf16[4,8,2048]{2,1,0:T(8,128)(2,1)S(1)} %finish.2.refs_0_), channel_id=1, source_target_pairs={{0,2},{1,5},{2,0},{3,7},{4,6},{5,1},{6,4},{7,3},{8,10},{9,13},{10,... | collective-permute-start | bytes 393224 | tf_op jit(solution)/shard_map/ppermute | solution.py:230
  51.3 8.6 %collective-permute-start.8 = (bf16[4,8,2048]{2,1,0:T(8,128)(2,1)S(1)}, bf16[4,8,2048]{2,1,0:T(8,128)(2,1)S(1)}, u32[]{:S(2)}, u32[]{:S(2)}) collective-permute-start(bf16[4,8,2048]{2,1,0:T(8,128)(2,1)S(1)} %finish.2.refs_0_), channel_id=1, source_target_pairs={{0,4},{1,3},{2,6},{3,1},{4,0},{5,7},{6,2},{7,5},{8,12},{9,11},{10,... | collective-permute-start | bytes 393224 | tf_op jit(solution)/shard_map/ppermute | solution.py:230
  54.6 5.3 %collective-permute-start.24 = (bf16[4,8,2048]{2,1,0:T(8,128)(2,1)S(1)}, bf16[4,8,2048]{2,1,0:T(8,128)(2,1)S(1)}, u32[]{:S(2)}, u32[]{:S(2)}) collective-permute-start(bf16[4,8,2048]{2,1,0:T(8,128)(2,1)S(1)} %collective-permute-done.20.refs_3_), channel_id=1, source_target_pairs={{0,1},{1,0},{2,3},{3,2},{4,5},{5,4},{6,7},{7,6},{8,9},{9,8},{10,11... | collective-permute-start | bytes 393224 | tf_op jit(solution)/shard_map/ppermute | solution.py:224
  56.9 3.5 %collective-permute-start.22 = (bf16[4,8,2048]{2,1,0:T(8,128)(2,1)S(1)}, bf16[4,8,2048]{2,1,0:T(8,128)(2,1)S(1)}, u32[]{:S(2)}, u32[]{:S(2)}) collective-permute-start(bf16[4,8,2048]{2,1,0:T(8,128)(2,1)S(1)} %collective-permute-done.19.refs_2_), channel_id=1, source_target_pairs={{0,1},{1,0},{2,3},{3,2},{4,5},{5,4},{6,7},{7,6},{8,9},{9,8},{10,11... | collective-permute-start | bytes 393224 | tf_op jit(solution)/shard_map/ppermute | solution.py:224
  56.9 3.6 %collective-permute-start.23 = (bf16[4,8,2048]{2,1,0:T(8,128)(2,1)S(1)}, bf16[4,8,2048]{2,1,0:T(8,128)(2,1)S(1)}, u32[]{:S(2)}, u32[]{:S(2)}) collective-permute-start(bf16[4,8,2048]{2,1,0:T(8,128)(2,1)S(1)} %collective-permute-done.18.refs_1_), channel_id=1, source_target_pairs={{0,1},{1,0},{2,3},{3,2},{4,5},{5,4},{6,7},{7,6},{8,9},{9,8},{10,11... | collective-permute-start | bytes 393224 | tf_op jit(solution)/shard_map/ppermute | solution.py:224
  58.6 7.0 %collective-permute-start.12 = (bf16[4,8,2048]{2,1,0:T(8,128)(2,1)S(1)}, bf16[4,8,2048]{2,1,0:T(8,128)(2,1)S(1)}, u32[]{:S(2)}, u32[]{:S(2)}) collective-permute-start(bf16[4,8,2048]{2,1,0:T(8,128)(2,1)S(1)} %finish.2.refs_0_), channel_id=1, source_target_pairs={{0,6},{1,7},{2,4},{3,5},{4,2},{5,3},{6,0},{7,1},{8,14},{9,15},{10,... | collective-permute-start | bytes 393224 | tf_op jit(solution)/shard_map/ppermute | solution.py:230
  59.9 6.7 %collective-permute-start.7 = (bf16[4,8,2048]{2,1,0:T(8,128)(2,1)S(1)}, bf16[4,8,2048]{2,1,0:T(8,128)(2,1)S(1)}, u32[]{:S(2)}, u32[]{:S(2)}) collective-permute-start(bf16[4,8,2048]{2,1,0:T(8,128)(2,1)S(1)} %finish.2.refs_0_), channel_id=1, source_target_pairs={{0,1},{1,0},{2,3},{3,2},{4,5},{5,4},{6,7},{7,6},{8,9},{9,8},{10,11... | collective-permute-start | bytes 393224 | tf_op jit(solution)/shard_map/ppermute | solution.py:224
  59.9 6.7 %collective-permute-start.11 = (bf16[4,8,2048]{2,1,0:T(8,128)(2,1)S(1)}, bf16[4,8,2048]{2,1,0:T(8,128)(2,1)S(1)}, u32[]{:S(2)}, u32[]{:S(2)}) collective-permute-start(bf16[4,8,2048]{2,1,0:T(8,128)(2,1)S(1)} %collective-permute-done.10.refs_1_), channel_id=1, source_target_pairs={{0,1},{1,0},{2,3},{3,2},{4,5},{5,4},{6,7},{7,6},{8,9},{9,8},{10,11... | collective-permute-start | bytes 393224 | tf_op jit(solution)/shard_map/ppermute | solution.py:224
  60.4 6.2 %collective-permute-start.9 = (bf16[4,8,2048]{2,1,0:T(8,128)(2,1)S(1)}, bf16[4,8,2048]{2,1,0:T(8,128)(2,1)S(1)}, u32[]{:S(2)}, u32[]{:S(2)}) collective-permute-start(bf16[4,8,2048]{2,1,0:T(8,128)(2,1)S(1)} %collective-permute-done.8.refs_2_), channel_id=1, source_target_pairs={{0,1},{1,0},{2,3},{3,2},{4,5},{5,4},{6,7},{7,6},{8,9},{9,8},{10,11... | collective-permute-start | bytes 393224 | tf_op jit(solution)/shard_map/ppermute | solution.py:224
  65.5 1.3 %collective-permute-start.25 = (bf16[4,8,2048]{2,1,0:T(8,128)(2,1)S(1)}, bf16[4,8,2048]{2,1,0:T(8,128)(2,1)S(1)}, u32[]{:S(2)}, u32[]{:S(2)}) collective-permute-start(bf16[4,8,2048]{2,1,0:T(8,128)(2,1)S(1)} %collective-permute-done.12.refs_3_), channel_id=1, source_target_pairs={{0,1},{1,0},{2,3},{3,2},{4,5},{5,4},{6,7},{7,6},{8,9},{9,8},{10,11... | collective-permute-start | bytes 393224 | tf_op jit(solution)/shard_map/ppermute | solution.py:224

commit v7 on v6

--- a/solution.py
+++ b/solution.py
@@ -10,7 +10,7 @@
 
 BLK = 128
 LANES = 128
-STAT = 16
+STAT = 8
 very_low = -1e30
 lowest_top = -(2.0**99)
 bf16 = jnp.bfloat16
@@ -226,6 +226,12 @@
 
 def plane_hop(value, number):
     masks = {1: (2, 4), 2: (4, 2), 3: (6, 6)}[number]
+    pairs = [(source, source ^ masks[source % 2]) for source in range(lax.axis_size("ctx"))]
+    return lax.ppermute(value, "ctx", pairs)
+
+
+def line_hop(value, reach, z_size):
+    masks = (8 * reach, 4 * z_size // reach)
     pairs = [(source, source ^ masks[source % 2]) for source in range(lax.axis_size("ctx"))]
     return lax.ppermute(value, "ctx", pairs)
 
@@ -361,9 +367,9 @@
         part = merge_chips(parts)
         reach = 1
         while 2 * reach < z_size:
-            part = merge_chips([part, hop(part, 8 * reach)])
+            part = merge_chips([part, line_hop(part, reach, z_size)])
             reach *= 2
-        return finish([part, hop(part, 8 * reach)])
+        return finish([part, line_hop(part, reach, z_size)])
 
     def gather_plane(attended):
         return [attended] + [plane_hop(attended, j) for j in (1, 2, 3)]

time: 67.7 us -> 61.6 us (0.910)
  the two profiles are of different devices: /device:TPU:0 before, /device:TPU:9 now
where the time goes in v7:
time: 61.6 us; the launch traced here: 61.2 us
  starting transfers between devices  36 us (58%)
  waiting for transfers between devices  13.5 us (22%)
  Pallas kernels  10.7 us (17%)
  other arithmetic  0.75 us (1%)
    ppermute x4, starting transfers between devices, line_hop(): return lax.ppermute(value, 'ctx', pairs)  13.3 us
    ppermute x10, starting transfers between devices, hop(): return lax.ppermute(value, 'ctx', pairs)  11.6 us
    ppermute x12, starting transfers between devices, plane_hop(): return lax.ppermute(value, 'ctx', pairs)  11.1 us
    ppermute x12, waiting for transfers between devices, plane_hop(): return lax.ppermute(value, 'ctx', pairs)  9.27 us
    ppermute x4, waiting for transfers between devices, line_hop(): return lax.ppermute(value, 'ctx', pairs)  4.23 us
    pallas_call x3, Pallas kernels, project(): pl.pallas_call(functools.partial(project_kernel, terms, bool(more), last)...  3.95 us
    pallas_call x1, Pallas kernels, split_and_attend(): pl.pallas_call(split_kernel, in_specs=[SMEM] + [HBM] * 3, out_specs=[VMEM...  2.4 us
    pallas_call x2, Pallas kernels, attend(): pl.pallas_call(functools.partial(attention_kernel, chunk_roles), in_specs...  1.77 us
  transfers between devices with their start and end apart: 26, of which 7 were waited for; matrix products, arithmetic and copies ran while one was open for 0% of the time, Pallas kernels for 11%

profile of v7, /device:TPU:9, one launch (start us, length us, event | category | flops | bytes accessed | tf_op | source)
XLA Modules:
  0.0 61.2 jit_solution(10756141470987370769)
XLA Ops:
  0.0 0.7 %pad_add_fusion.meta = s32[18]{0:T(128)S(1)} fusion(s32[8]{0:T(128)} %param.10, s32[8]{0:T(128)} %bitcast.9, s32[1]{0:T(128)} %bitcast.1, s32[1]{0:T(128)} %bitcast), kind=kLoop, calls=%fused_computation | loop fusion | flops 54 | bytes 144 | tf_op jit(solution)/shard_map/concatenate | solution.py:260
  0.8 2.4 %split_and_attend.1 = (bf16[4,1024,128]{2,1,0:T(8,128)(2,1)S(1)}, bf16[4,136,1024]{2,1,0:T(8,128)(2,1)S(1)}, bf16[16,136,128]{2,1,0:T(8,128)(2,1)S(1)}) custom-call(s32[18]{0:T(128)S(1)} %pad_add_fusion.meta, bf16[4096,128]{1,0:T(8,128)(2,1)} %bitcast.7, bf16[4096,128]{1,0:T(8,128)(2,1)} %bitcast.8, bf16[128,64,128]{2,1,0:T(8,128)(2,1)} %q_ref.3), custom_call_target="tpu_custom_call" | custom-call | flops 1073741824 | bytes 2097152 | tf_op jit(solution)/shard_map/split_and_attend/pallas_call | solution.py:270
  3.2 1.6 %collective-permute-start = (bf16[16,136,128]{2,1,0:T(8,128)(2,1)S(1)}, bf16[16,136,128]{2,1,0:T(8,128)(2,1)S(1)}, u32[]{:S(2)}, u32[]{:S(2)}) collective-permute-start(bf16[16,136,128]{2,1,0:T(8,128)(2,1)S(1)} %get-tuple-element.28), channel_id=1, source_target_pairs={{0,1},{1,0},{2,3},{3,2},{4,5},{5,4},{6,7},{7,6},{8,9},{9,8},{10,11... | collective-permute-start | bytes 1671176 | tf_op jit(solution)/shard_map/ppermute | solution.py:224
  4.8 0.9 %attend.2 = (bf16[16,136,128]{2,1,0:T(8,128)(2,1)S(1)}, bf16[16,136,128]{2,1,0:T(8,128)(2,1)S(1)}) custom-call(s32[18]{0:T(128)S(1)} %pad_add_fusion.meta, bf16[4,1024,128]{2,1,0:T(8,128)(2,1)S(1)} %get-tuple-element.33.kd, bf16[4,136,1024]{2,1,0:T(8,128)(2,1)S(1)} %get-tuple-element.26.vt, bf16[128,64,128]{2,1,0:T(8,128)(2,1)S(1)} %copy-done), custom_call_target="tpu_custom_call" | custom-call | flops 2147483648 | bytes 1048576 | tf_op jit(solution)/shard_map/attend/pallas_call | solution.py:299
  5.7 1.5 %collective-permute-start.1 = (bf16[16,136,128]{2,1,0:T(8,128)(2,1)S(1)}, bf16[16,136,128]{2,1,0:T(8,128)(2,1)S(1)}, u32[]{:S(2)}, u32[]{:S(2)}) collective-permute-start(bf16[16,136,128]{2,1,0:T(8,128)(2,1)S(1)} %get-tuple-element.34), channel_id=1, source_target_pairs={{0,1},{1,0},{2,3},{3,2},{4,5},{5,4},{6,7},{7,6},{8,9},{9,8},{10,11... | collective-permute-start | bytes 1671176 | tf_op jit(solution)/shard_map/ppermute | solution.py:224
  7.2 0.8 %merge_cores.2 = (bf16[4,136,128]{2,1,0:T(8,128)(2,1)S(1)}, bf16[4,136,128]{2,1,0:T(8,128)(2,1)S(1)}, bf16[4,136,128]{2,1,0:T(8,128)(2,1)S(1)}, bf16[4,136,128]{2,1,0:T(8,128)(2,1)S(1)}) custom-call(s32[18]{0:T(128)S(1)} %pad_add_fusion.meta, bf16[16,136,128]{2,1,0:T(8,128)(2,1)S(1)} %get-tuple-element.27.kept, ...), custom_call_target="tpu_custom_call" | custom-call | tf_op jit(solution)/shard_map/merge_cores/pallas_call | solution.py:314
  8.1 2.4 %collective-permute-start.14 = (bf16[4,136,128]{2,1,0:T(8,128)(2,1)S(1)}, bf16[4,136,128]{2,1,0:T(8,128)(2,1)S(1)}, u32[]{:S(2)}, u32[]{:S(2)}) collective-permute-start(bf16[4,136,128]{2,1,0:T(8,128)(2,1)S(1)} %get-tuple-element.41), channel_id=1, source_target_pairs={{0,4},{1,3},{2,6},{3,1},{4,0},{5,7},{6,2},{7,5},{8,12},{9,11},{10,... | collective-permute-start | bytes 417800 | tf_op jit(solution)/shard_map/ppermute | solution.py:230
  10.8 0.9 %attend.3.kept = bf16[16,136,128]{2,1,0:T(8,128)(2,1)S(1)} custom-call(s32[18]{0:T(128)S(1)} %pad_add_fusion.meta, bf16[4,1024,128]{2,1,0:T(8,128)(2,1)S(1)} %get-tuple-element.33.kd, bf16[4,136,1024]{2,1,0:T(8,128)(2,1)S(1)} %get-tuple-element.26.vt, bf16[128,64,128]{2,1,0:T(8,128)(2,1)S(1)} %copy-done), custom_call_target="tpu_custom_call" | custom-call | flops 1073741824 | bytes 524288 | tf_op jit(solution)/shard_map/attend/pallas_call | solution.py:299
  11.6 0.8 %merge_cores.3 = (bf16[4,136,128]{2,1,0:T(8,128)(2,1)S(1)}, bf16[4,136,128]{2,1,0:T(8,128)(2,1)S(1)}, bf16[4,136,128]{2,1,0:T(8,128)(2,1)S(1)}, bf16[4,136,128]{2,1,0:T(8,128)(2,1)S(1)}) custom-call(s32[18]{0:T(128)S(1)} %pad_add_fusion.meta, bf16[16,136,128]{2,1,0:T(8,128)(2,1)S(1)} %attend.3.kept, bf16[16,136,128]{2,1,0:T(8,128)(2,1)S(1)} %collective-permute-done.1.received), custom_call_target="tpu_custom_call" | custom-call | tf_op jit(solution)/shard_map/merge_cores/pallas_call | solution.py:314
  12.5 1.1 %collective-permute-start.2 = (bf16[4,136,128]{2,1,0:T(8,128)(2,1)S(1)}, bf16[4,136,128]{2,1,0:T(8,128)(2,1)S(1)}, u32[]{:S(2)}, u32[]{:S(2)}) collective-permute-start(bf16[4,136,128]{2,1,0:T(8,128)(2,1)S(1)} %get-tuple-element.36), channel_id=1, source_target_pairs={{0,2},{1,5},{2,0},{3,7},{4,6},{5,1},{6,4},{7,3},{8,10},{9,13},{10,... | collective-permute-start | bytes 417800 | tf_op jit(solution)/shard_map/ppermute | solution.py:230
  13.5 2.3 %collective-permute-start.3 = (bf16[4,136,128]{2,1,0:T(8,128)(2,1)S(1)}, bf16[4,136,128]{2,1,0:T(8,128)(2,1)S(1)}, u32[]{:S(2)}, u32[]{:S(2)}) collective-permute-start(bf16[4,136,128]{2,1,0:T(8,128)(2,1)S(1)} %get-tuple-element.37), channel_id=1, source_target_pairs={{0,4},{1,3},{2,6},{3,1},{4,0},{5,7},{6,2},{7,5},{8,12},{9,11},{10,... | collective-permute-start | bytes 417800 | tf_op jit(solution)/shard_map/ppermute | solution.py:230
  15.8 1.5 %collective-permute-done.15.refs_3_ = bf16[4,136,128]{2,1,0:T(8,128)(2,1)S(1)} collective-permute-done((bf16[4,136,128]{2,1,0:T(8,128)(2,1)S(1)}, bf16[4,136,128]{2,1,0:T(8,128)(2,1)S(1)}, u32[]{:S(2)}, u32[]{:S(2)}) %collective-permute-start.15) | collective-permute-done | bytes 139296 | tf_op jit(solution)/shard_map/ppermute | solution.py:230
  17.4 6.8 %collective-permute-start.16 = (bf16[4,136,128]{2,1,0:T(8,128)(2,1)S(1)}, bf16[4,136,128]{2,1,0:T(8,128)(2,1)S(1)}, u32[]{:S(2)}, u32[]{:S(2)}) collective-permute-start(bf16[4,136,128]{2,1,0:T(8,128)(2,1)S(1)} %merge_chips.6.refs_0_), channel_id=1, source_target_pairs={{0,8},{1,17},{2,10},{3,19},{4,12},{5,21},{6,14},{7,23},{8,0},{9,25... | collective-permute-start | bytes 417800 | tf_op jit(solution)/shard_map/ppermute | solution.py:236
  24.4 5.3 %collective-permute-start.5 = (bf16[4,136,128]{2,1,0:T(8,128)(2,1)S(1)}, bf16[4,136,128]{2,1,0:T(8,128)(2,1)S(1)}, u32[]{:S(2)}, u32[]{:S(2)}) collective-permute-start(bf16[4,136,128]{2,1,0:T(8,128)(2,1)S(1)} %merge_chips.4.refs_0_), channel_id=1, source_target_pairs={{0,8},{1,17},{2,10},{3,19},{4,12},{5,21},{6,14},{7,23},{8,0},{9,25... | collective-permute-start | bytes 417800 | tf_op jit(solution)/shard_map/ppermute | solution.py:236
  29.8 0.6 %collective-permute-start.17 = (bf16[4,136,128]{2,1,0:T(8,128)(2,1)S(1)}, bf16[4,136,128]{2,1,0:T(8,128)(2,1)S(1)}, u32[]{:S(2)}, u32[]{:S(2)}) collective-permute-start(bf16[4,136,128]{2,1,0:T(8,128)(2,1)S(1)} %merge_chips.7.refs_0_), channel_id=1, source_target_pairs={{0,16},{1,9},{2,18},{3,11},{4,20},{5,13},{6,22},{7,15},{8,24},{9,1... | collective-permute-start | bytes 417800 | tf_op jit(solution)/shard_map/ppermute | solution.py:236
  30.4 3.4 %collective-permute-done.5.refs_1_ = bf16[4,136,128]{2,1,0:T(8,128)(2,1)S(1)} collective-permute-done((bf16[4,136,128]{2,1,0:T(8,128)(2,1)S(1)}, bf16[4,136,128]{2,1,0:T(8,128)(2,1)S(1)}, u32[]{:S(2)}, u32[]{:S(2)}) %collective-permute-start.5) | collective-permute-done | bytes 139296 | tf_op jit(solution)/shard_map/ppermute | solution.py:236
  33.9 0.6 collective-permute-start.6
  34.5 0.8 %collective-permute-done.17.refs_1_ = bf16[4,136,128]{2,1,0:T(8,128)(2,1)S(1)} collective-permute-done((bf16[4,136,128]{2,1,0:T(8,128)(2,1)S(1)}, bf16[4,136,128]{2,1,0:T(8,128)(2,1)S(1)}, u32[]{:S(2)}, u32[]{:S(2)}) %collective-permute-start.17) | collective-permute-done | bytes 139296 | tf_op jit(solution)/shard_map/ppermute | solution.py:236
  35.5 4.0 %collective-permute-start.21 = (bf16[4,8,2048]{2,1,0:T(8,128)(2,1)S(1)}, bf16[4,8,2048]{2,1,0:T(8,128)(2,1)S(1)}, u32[]{:S(2)}, u32[]{:S(2)}) collective-permute-start(bf16[4,8,2048]{2,1,0:T(8,128)(2,1)S(1)} %finish.3.refs_0_), channel_id=1, source_target_pairs={{0,1},{1,0},{2,3},{3,2},{4,5},{5,4},{6,7},{7,6},{8,9},{9,8},{10,11... | collective-permute-start | bytes 393224 | tf_op jit(solution)/shard_map/ppermute | solution.py:224
  39.6 1.1 %collective-permute-start.20 = (bf16[4,8,2048]{2,1,0:T(8,128)(2,1)S(1)}, bf16[4,8,2048]{2,1,0:T(8,128)(2,1)S(1)}, u32[]{:S(2)}, u32[]{:S(2)}) collective-permute-start(bf16[4,8,2048]{2,1,0:T(8,128)(2,1)S(1)} %finish.3.refs_0_), channel_id=1, source_target_pairs={{0,6},{1,7},{2,4},{3,5},{4,2},{5,3},{6,0},{7,1},{8,14},{9,15},{10,... | collective-permute-start | bytes 393224 | tf_op jit(solution)/shard_map/ppermute | solution.py:230
  41.2 1.1 %collective-permute-start.18 = (bf16[4,8,2048]{2,1,0:T(8,128)(2,1)S(1)}, bf16[4,8,2048]{2,1,0:T(8,128)(2,1)S(1)}, u32[]{:S(2)}, u32[]{:S(2)}) collective-permute-start(bf16[4,8,2048]{2,1,0:T(8,128)(2,1)S(1)} %finish.3.refs_0_), channel_id=1, source_target_pairs={{0,2},{1,5},{2,0},{3,7},{4,6},{5,1},{6,4},{7,3},{8,10},{9,13},{10,... | collective-permute-start | bytes 393224 | tf_op jit(solution)/shard_map/ppermute | solution.py:230
  42.9 0.9 %collective-permute-start.8 = (bf16[4,8,2048]{2,1,0:T(8,128)(2,1)S(1)}, bf16[4,8,2048]{2,1,0:T(8,128)(2,1)S(1)}, u32[]{:S(2)}, u32[]{:S(2)}) collective-permute-start(bf16[4,8,2048]{2,1,0:T(8,128)(2,1)S(1)} %finish.2.refs_0_), channel_id=1, source_target_pairs={{0,4},{1,3},{2,6},{3,1},{4,0},{5,7},{6,2},{7,5},{8,12},{9,11},{10,... | collective-permute-start | bytes 393224 | tf_op jit(solution)/shard_map/ppermute | solution.py:230
  43.9 1.7 %collective-permute-done.20.refs_3_ = bf16[4,8,2048]{2,1,0:T(8,128)(2,1)S(1)} collective-permute-done((bf16[4,8,2048]{2,1,0:T(8,128)(2,1)S(1)}, bf16[4,8,2048]{2,1,0:T(8,128)(2,1)S(1)}, u32[]{:S(2)}, u32[]{:S(2)}) %collective-permute-start.20) | collective-permute-done | bytes 131104 | tf_op jit(solution)/shard_map/ppermute | solution.py:230
  45.6 1.3 %collective-permute-start.24 = (bf16[4,8,2048]{2,1,0:T(8,128)(2,1)S(1)}, bf16[4,8,2048]{2,1,0:T(8,128)(2,1)S(1)}, u32[]{:S(2)}, u32[]{:S(2)}) collective-permute-start(bf16[4,8,2048]{2,1,0:T(8,128)(2,1)S(1)} %collective-permute-done.20.refs_3_), channel_id=1, source_target_pairs={{0,1},{1,0},{2,3},{3,2},{4,5},{5,4},{6,7},{7,6},{8,9},{9,8},{10,11... | collective-permute-start | bytes 393224 | tf_op jit(solution)/shard_map/ppermute | solution.py:224
  46.9 0.7 %collective-permute-done.19.refs_2_ = bf16[4,8,2048]{2,1,0:T(8,128)(2,1)S(1)} collective-permute-done((bf16[4,8,2048]{2,1,0:T(8,128)(2,1)S(1)}, bf16[4,8,2048]{2,1,0:T(8,128)(2,1)S(1)}, u32[]{:S(2)}, u32[]{:S(2)}) %collective-permute-start.19) | collective-permute-done | bytes 131104 | tf_op jit(solution)/shard_map/ppermute | solution.py:230
  47.6 1.7 %collective-permute-start.22 = (bf16[4,8,2048]{2,1,0:T(8,128)(2,1)S(1)}, bf16[4,8,2048]{2,1,0:T(8,128)(2,1)S(1)}, u32[]{:S(2)}, u32[]{:S(2)}) collective-permute-start(bf16[4,8,2048]{2,1,0:T(8,128)(2,1)S(1)} %collective-permute-done.19.refs_2_), channel_id=1, source_target_pairs={{0,1},{1,0},{2,3},{3,2},{4,5},{5,4},{6,7},{7,6},{8,9},{9,8},{10,11... | collective-permute-start | bytes 393224 | tf_op jit(solution)/shard_map/ppermute | solution.py:224
  49.2 2.4 %collective-permute-done.10.refs_1_ = bf16[4,8,2048]{2,1,0:T(8,128)(2,1)S(1)} collective-permute-done((bf16[4,8,2048]{2,1,0:T(8,128)(2,1)S(1)}, bf16[4,8,2048]{2,1,0:T(8,128)(2,1)S(1)}, u32[]{:S(2)}, u32[]{:S(2)}) %collective-permute-start.10) | collective-permute-done | bytes 131104 | tf_op jit(solution)/shard_map/ppermute | solution.py:230
  51.6 1.1 %collective-permute-start.12 = (bf16[4,8,2048]{2,1,0:T(8,128)(2,1)S(1)}, bf16[4,8,2048]{2,1,0:T(8,128)(2,1)S(1)}, u32[]{:S(2)}, u32[]{:S(2)}) collective-permute-start(bf16[4,8,2048]{2,1,0:T(8,128)(2,1)S(1)} %finish.2.refs_0_), channel_id=1, source_target_pairs={{0,6},{1,7},{2,4},{3,5},{4,2},{5,3},{6,0},{7,1},{8,14},{9,15},{10,... | collective-permute-start | bytes 393224 | tf_op jit(solution)/shard_map/ppermute | solution.py:230
  53.6 1.3 %project.3.refs_4_ = f32[128,512]{1,0:T(8,128)S(1)} custom-call(s32[18]{0:T(128)S(1)} %pad_add_fusion.meta, bf16[8192,512]{1,0:T(8,128)(2,1)S(1)} %bitcast.6, bf16[4,8,2048]{2,1,0:T(8,128)(2,1)S(1)} %finish.3.refs_0_, bf16[4,8,2048]{2,1,0:T(8,128)(2,1)S(1)} %collective-permute-done.18.refs_1_, bf16[4,8,2048]{2,1,0:T(8,128)(2,1)S(1)} %collective-permute-done.19.refs_2_, ...), custom_call_target="tpu_custom_call" | custom-call | flops 536870912 | bytes 4194304 | tf_op jit(solution)/shard_map/project/pallas_call | solution.py:348
  54.9 3.0 %collective-permute-done.12.refs_3_ = bf16[4,8,2048]{2,1,0:T(8,128)(2,1)S(1)} collective-permute-done((bf16[4,8,2048]{2,1,0:T(8,128)(2,1)S(1)}, bf16[4,8,2048]{2,1,0:T(8,128)(2,1)S(1)}, u32[]{:S(2)}, u32[]{:S(2)}) %collective-permute-start.12) | collective-permute-done | bytes 131104 | tf_op jit(solution)/shard_map/ppermute | solution.py:230
  58.4 1.0 %project.4.refs_4_ = f32[128,512]{1,0:T(8,128)S(1)} custom-call(s32[18]{0:T(128)S(1)} %pad_add_fusion.meta, bf16[8192,512]{1,0:T(8,128)(2,1)S(1)} %bitcast.6, bf16[4,8,2048]{2,1,0:T(8,128)(2,1)S(1)} %finish.2.refs_0_, bf16[4,8,2048]{2,1,0:T(8,128)(2,1)S(1)} %collective-permute-done.10.refs_1_, bf16[4,8,2048]{2,1,0:T(8,128)(2,1)S(1)} %collective-permute-done.8.refs_2_, ...), custom_call_target="tpu_custom_call" | custom-call | flops 268435456 | bytes 2097152 | tf_op jit(solution)/shard_map/project/pallas_call | solution.py:348
  59.5 1.7 %project.5 = f32[128,512]{1,0:T(8,128)} custom-call(s32[18]{0:T(128)S(1)} %pad_add_fusion.meta, bf16[8192,512]{1,0:T(8,128)(2,1)S(1)} %bitcast.6, bf16[4,8,2048]{2,1,0:T(8,128)(2,1)S(1)} %collective-permute-done.7.refs_0_, bf16[4,8,2048]{2,1,0:T(8,128)(2,1)S(1)} %collective-permute-done.9.refs_1_, bf16[4,8,2048]{2,1,0:T(8,128)(2,1)S(1)} %collective-permute-done.11.refs_2_, ...), custom_call_target="tpu_custom_call" | custom-call | flops 268435456 | bytes 2097152 | tf_op jit(solution)/shard_map/project/pallas_call | solution.py:348
  (42 shorter events, 3.6 us)
Async XLA Ops:
  0.7 4.0 %copy-start = (bf16[128,64,128]{2,1,0:T(8,128)(2,1)S(1)}, bf16[128,64,128]{2,1,0:T(8,128)(2,1)}, u32[]{:S(2)}) copy-start(bf16[128,64,128]{2,1,0:T(8,128)(2,1)} %q_ref.3) | copy-start | bytes 6291460
  3.2 4.0 %collective-permute-start = (bf16[16,136,128]{2,1,0:T(8,128)(2,1)S(1)}, bf16[16,136,128]{2,1,0:T(8,128)(2,1)S(1)}, u32[]{:S(2)}, u32[]{:S(2)}) collective-permute-start(bf16[16,136,128]{2,1,0:T(8,128)(2,1)S(1)} %get-tuple-element.28), channel_id=1, source_target_pairs={{0,1},{1,0},{2,3},{3,2},{4,5},{5,4},{6,7},{7,6},{8,9},{9,8},{10,11... | collective-permute-start | bytes 1671176 | tf_op jit(solution)/shard_map/ppermute | solution.py:224
  4.8 48.9 %slice-start = ((s8[8388608]{0:T(1024)(128)(4,1)}), s8[4194304]{0:T(1024)(128)(4,1)S(1)}, s32[]{:S(2)}) async-start(s8[8388608]{0:T(1024)(128)(4,1)} %bitcast.5), calls=%async_computation | async-start | bytes 8388608
  5.7 6.0 %collective-permute-start.1 = (bf16[16,136,128]{2,1,0:T(8,128)(2,1)S(1)}, bf16[16,136,128]{2,1,0:T(8,128)(2,1)S(1)}, u32[]{:S(2)}, u32[]{:S(2)}) collective-permute-start(bf16[16,136,128]{2,1,0:T(8,128)(2,1)S(1)} %get-tuple-element.34), channel_id=1, source_target_pairs={{0,1},{1,0},{2,3},{3,2},{4,5},{5,4},{6,7},{7,6},{8,9},{9,8},{10,11... | collective-permute-start | bytes 1671176 | tf_op jit(solution)/shard_map/ppermute | solution.py:224
  7.2 46.4 %slice-start.1 = ((s8[8388608]{0:T(1024)(128)(4,1)}), s8[4194304]{0:T(1024)(128)(4,1)S(1)}, s32[]{:S(2)}) async-start(s8[8388608]{0:T(1024)(128)(4,1)} %bitcast.5), calls=%async_computation.1 | async-start | bytes 8388608
  8.0 7.8 %collective-permute-start.13 = (bf16[4,136,128]{2,1,0:T(8,128)(2,1)S(1)}, bf16[4,136,128]{2,1,0:T(8,128)(2,1)S(1)}, u32[]{:S(2)}, u32[]{:S(2)}) collective-permute-start(bf16[4,136,128]{2,1,0:T(8,128)(2,1)S(1)} %get-tuple-element.40), channel_id=1, source_target_pairs={{0,2},{1,5},{2,0},{3,7},{4,6},{5,1},{6,4},{7,3},{8,10},{9,13},{10,... | collective-permute-start | bytes 417800 | tf_op jit(solution)/shard_map/ppermute | solution.py:230
  8.1 7.7 %collective-permute-start.14 = (bf16[4,136,128]{2,1,0:T(8,128)(2,1)S(1)}, bf16[4,136,128]{2,1,0:T(8,128)(2,1)S(1)}, u32[]{:S(2)}, u32[]{:S(2)}) collective-permute-start(bf16[4,136,128]{2,1,0:T(8,128)(2,1)S(1)} %get-tuple-element.41), channel_id=1, source_target_pairs={{0,4},{1,3},{2,6},{3,1},{4,0},{5,7},{6,2},{7,5},{8,12},{9,11},{10,... | collective-permute-start | bytes 417800 | tf_op jit(solution)/shard_map/ppermute | solution.py:230
  10.6 6.7 %collective-permute-start.15 = (bf16[4,136,128]{2,1,0:T(8,128)(2,1)S(1)}, bf16[4,136,128]{2,1,0:T(8,128)(2,1)S(1)}, u32[]{:S(2)}, u32[]{:S(2)}) collective-permute-start(bf16[4,136,128]{2,1,0:T(8,128)(2,1)S(1)} %get-tuple-element.42), channel_id=1, source_target_pairs={{0,6},{1,7},{2,4},{3,5},{4,2},{5,3},{6,0},{7,1},{8,14},{9,15},{10,... | collective-permute-start | bytes 417800 | tf_op jit(solution)/shard_map/ppermute | solution.py:230
  12.5 11.7 %collective-permute-start.2 = (bf16[4,136,128]{2,1,0:T(8,128)(2,1)S(1)}, bf16[4,136,128]{2,1,0:T(8,128)(2,1)S(1)}, u32[]{:S(2)}, u32[]{:S(2)}) collective-permute-start(bf16[4,136,128]{2,1,0:T(8,128)(2,1)S(1)} %get-tuple-element.36), channel_id=1, source_target_pairs={{0,2},{1,5},{2,0},{3,7},{4,6},{5,1},{6,4},{7,3},{8,10},{9,13},{10,... | collective-permute-start | bytes 417800 | tf_op jit(solution)/shard_map/ppermute | solution.py:230
  13.5 10.7 %collective-permute-start.3 = (bf16[4,136,128]{2,1,0:T(8,128)(2,1)S(1)}, bf16[4,136,128]{2,1,0:T(8,128)(2,1)S(1)}, u32[]{:S(2)}, u32[]{:S(2)}) collective-permute-start(bf16[4,136,128]{2,1,0:T(8,128)(2,1)S(1)} %get-tuple-element.37), channel_id=1, source_target_pairs={{0,4},{1,3},{2,6},{3,1},{4,0},{5,7},{6,2},{7,5},{8,12},{9,11},{10,... | collective-permute-start | bytes 417800 | tf_op jit(solution)/shard_map/ppermute | solution.py:230
  15.8 8.4 %collective-permute-start.4 = (bf16[4,136,128]{2,1,0:T(8,128)(2,1)S(1)}, bf16[4,136,128]{2,1,0:T(8,128)(2,1)S(1)}, u32[]{:S(2)}, u32[]{:S(2)}) collective-permute-start(bf16[4,136,128]{2,1,0:T(8,128)(2,1)S(1)} %get-tuple-element.38), channel_id=1, source_target_pairs={{0,6},{1,7},{2,4},{3,5},{4,2},{5,3},{6,0},{7,1},{8,14},{9,15},{10,... | collective-permute-start | bytes 417800 | tf_op jit(solution)/shard_map/ppermute | solution.py:230
  17.4 12.3 %collective-permute-start.16 = (bf16[4,136,128]{2,1,0:T(8,128)(2,1)S(1)}, bf16[4,136,128]{2,1,0:T(8,128)(2,1)S(1)}, u32[]{:S(2)}, u32[]{:S(2)}) collective-permute-start(bf16[4,136,128]{2,1,0:T(8,128)(2,1)S(1)} %merge_chips.6.refs_0_), channel_id=1, source_target_pairs={{0,8},{1,17},{2,10},{3,19},{4,12},{5,21},{6,14},{7,23},{8,0},{9,25... | collective-permute-start | bytes 417800 | tf_op jit(solution)/shard_map/ppermute | solution.py:236
  24.4 9.4 %collective-permute-start.5 = (bf16[4,136,128]{2,1,0:T(8,128)(2,1)S(1)}, bf16[4,136,128]{2,1,0:T(8,128)(2,1)S(1)}, u32[]{:S(2)}, u32[]{:S(2)}) collective-permute-start(bf16[4,136,128]{2,1,0:T(8,128)(2,1)S(1)} %merge_chips.4.refs_0_), channel_id=1, source_target_pairs={{0,8},{1,17},{2,10},{3,19},{4,12},{5,21},{6,14},{7,23},{8,0},{9,25... | collective-permute-start | bytes 417800 | tf_op jit(solution)/shard_map/ppermute | solution.py:236
  29.8 5.5 %collective-permute-start.17 = (bf16[4,136,128]{2,1,0:T(8,128)(2,1)S(1)}, bf16[4,136,128]{2,1,0:T(8,128)(2,1)S(1)}, u32[]{:S(2)}, u32[]{:S(2)}) collective-permute-start(bf16[4,136,128]{2,1,0:T(8,128)(2,1)S(1)} %merge_chips.7.refs_0_), channel_id=1, source_target_pairs={{0,16},{1,9},{2,18},{3,11},{4,20},{5,13},{6,22},{7,15},{8,24},{9,1... | collective-permute-start | bytes 417800 | tf_op jit(solution)/shard_map/ppermute | solution.py:236
  33.9 8.3 %collective-permute-start.6 = (bf16[4,136,128]{2,1,0:T(8,128)(2,1)S(1)}, bf16[4,136,128]{2,1,0:T(8,128)(2,1)S(1)}, u32[]{:S(2)}, u32[]{:S(2)}) collective-permute-start(bf16[4,136,128]{2,1,0:T(8,128)(2,1)S(1)} %merge_chips.5.refs_0_), channel_id=1, source_target_pairs={{0,16},{1,9},{2,18},{3,11},{4,20},{5,13},{6,22},{7,15},{8,24},{9,1... | collective-permute-start | bytes 417800 | tf_op jit(solution)/shard_map/ppermute | solution.py:236
  35.5 7.4 %collective-permute-start.21 = (bf16[4,8,2048]{2,1,0:T(8,128)(2,1)S(1)}, bf16[4,8,2048]{2,1,0:T(8,128)(2,1)S(1)}, u32[]{:S(2)}, u32[]{:S(2)}) collective-permute-start(bf16[4,8,2048]{2,1,0:T(8,128)(2,1)S(1)} %finish.3.refs_0_), channel_id=1, source_target_pairs={{0,1},{1,0},{2,3},{3,2},{4,5},{5,4},{6,7},{7,6},{8,9},{9,8},{10,11... | collective-permute-start | bytes 393224 | tf_op jit(solution)/shard_map/ppermute | solution.py:224
  39.6 6.0 %collective-permute-start.20 = (bf16[4,8,2048]{2,1,0:T(8,128)(2,1)S(1)}, bf16[4,8,2048]{2,1,0:T(8,128)(2,1)S(1)}, u32[]{:S(2)}, u32[]{:S(2)}) collective-permute-start(bf16[4,8,2048]{2,1,0:T(8,128)(2,1)S(1)} %finish.3.refs_0_), channel_id=1, source_target_pairs={{0,6},{1,7},{2,4},{3,5},{4,2},{5,3},{6,0},{7,1},{8,14},{9,15},{10,... | collective-permute-start | bytes 393224 | tf_op jit(solution)/shard_map/ppermute | solution.py:230
  40.6 6.9 %collective-permute-start.19 = (bf16[4,8,2048]{2,1,0:T(8,128)(2,1)S(1)}, bf16[4,8,2048]{2,1,0:T(8,128)(2,1)S(1)}, u32[]{:S(2)}, u32[]{:S(2)}) collective-permute-start(bf16[4,8,2048]{2,1,0:T(8,128)(2,1)S(1)} %finish.3.refs_0_), channel_id=1, source_target_pairs={{0,4},{1,3},{2,6},{3,1},{4,0},{5,7},{6,2},{7,5},{8,12},{9,11},{10,... | collective-permute-start | bytes 393224 | tf_op jit(solution)/shard_map/ppermute | solution.py:230
  41.2 8.1 %collective-permute-start.18 = (bf16[4,8,2048]{2,1,0:T(8,128)(2,1)S(1)}, bf16[4,8,2048]{2,1,0:T(8,128)(2,1)S(1)}, u32[]{:S(2)}, u32[]{:S(2)}) collective-permute-start(bf16[4,8,2048]{2,1,0:T(8,128)(2,1)S(1)} %finish.3.refs_0_), channel_id=1, source_target_pairs={{0,2},{1,5},{2,0},{3,7},{4,6},{5,1},{6,4},{7,3},{8,10},{9,13},{10,... | collective-permute-start | bytes 393224 | tf_op jit(solution)/shard_map/ppermute | solution.py:230
  42.5 9.1 %collective-permute-start.10 = (bf16[4,8,2048]{2,1,0:T(8,128)(2,1)S(1)}, bf16[4,8,2048]{2,1,0:T(8,128)(2,1)S(1)}, u32[]{:S(2)}, u32[]{:S(2)}) collective-permute-start(bf16[4,8,2048]{2,1,0:T(8,128)(2,1)S(1)} %finish.2.refs_0_), channel_id=1, source_target_pairs={{0,2},{1,5},{2,0},{3,7},{4,6},{5,1},{6,4},{7,3},{8,10},{9,13},{10,... | collective-permute-start | bytes 393224 | tf_op jit(solution)/shard_map/ppermute | solution.py:230
  42.9 9.8 %collective-permute-start.8 = (bf16[4,8,2048]{2,1,0:T(8,128)(2,1)S(1)}, bf16[4,8,2048]{2,1,0:T(8,128)(2,1)S(1)}, u32[]{:S(2)}, u32[]{:S(2)}) collective-permute-start(bf16[4,8,2048]{2,1,0:T(8,128)(2,1)S(1)} %finish.2.refs_0_), channel_id=1, source_target_pairs={{0,4},{1,3},{2,6},{3,1},{4,0},{5,7},{6,2},{7,5},{8,12},{9,11},{10,... | collective-permute-start | bytes 393224 | tf_op jit(solution)/shard_map/ppermute | solution.py:230
  45.6 7.5 %collective-permute-start.24 = (bf16[4,8,2048]{2,1,0:T(8,128)(2,1)S(1)}, bf16[4,8,2048]{2,1,0:T(8,128)(2,1)S(1)}, u32[]{:S(2)}, u32[]{:S(2)}) collective-permute-start(bf16[4,8,2048]{2,1,0:T(8,128)(2,1)S(1)} %collective-permute-done.20.refs_3_), channel_id=1, source_target_pairs={{0,1},{1,0},{2,3},{3,2},{4,5},{5,4},{6,7},{7,6},{8,9},{9,8},{10,11... | collective-permute-start | bytes 393224 | tf_op jit(solution)/shard_map/ppermute | solution.py:224
  47.6 5.6 %collective-permute-start.22 = (bf16[4,8,2048]{2,1,0:T(8,128)(2,1)S(1)}, bf16[4,8,2048]{2,1,0:T(8,128)(2,1)S(1)}, u32[]{:S(2)}, u32[]{:S(2)}) collective-permute-start(bf16[4,8,2048]{2,1,0:T(8,128)(2,1)S(1)} %collective-permute-done.19.refs_2_), channel_id=1, source_target_pairs={{0,1},{1,0},{2,3},{3,2},{4,5},{5,4},{6,7},{7,6},{8,9},{9,8},{10,11... | collective-permute-start | bytes 393224 | tf_op jit(solution)/shard_map/ppermute | solution.py:224
  49.2 4.4 %collective-permute-start.23 = (bf16[4,8,2048]{2,1,0:T(8,128)(2,1)S(1)}, bf16[4,8,2048]{2,1,0:T(8,128)(2,1)S(1)}, u32[]{:S(2)}, u32[]{:S(2)}) collective-permute-start(bf16[4,8,2048]{2,1,0:T(8,128)(2,1)S(1)} %collective-permute-done.18.refs_1_), channel_id=1, source_target_pairs={{0,1},{1,0},{2,3},{3,2},{4,5},{5,4},{6,7},{7,6},{8,9},{9,8},{10,11... | collective-permute-start | bytes 393224 | tf_op jit(solution)/shard_map/ppermute | solution.py:224
  51.6 6.3 %collective-permute-start.12 = (bf16[4,8,2048]{2,1,0:T(8,128)(2,1)S(1)}, bf16[4,8,2048]{2,1,0:T(8,128)(2,1)S(1)}, u32[]{:S(2)}, u32[]{:S(2)}) collective-permute-start(bf16[4,8,2048]{2,1,0:T(8,128)(2,1)S(1)} %finish.2.refs_0_), channel_id=1, source_target_pairs={{0,6},{1,7},{2,4},{3,5},{4,2},{5,3},{6,0},{7,1},{8,14},{9,15},{10,... | collective-permute-start | bytes 393224 | tf_op jit(solution)/shard_map/ppermute | solution.py:230
  52.7 6.7 %collective-permute-start.7 = (bf16[4,8,2048]{2,1,0:T(8,128)(2,1)S(1)}, bf16[4,8,2048]{2,1,0:T(8,128)(2,1)S(1)}, u32[]{:S(2)}, u32[]{:S(2)}) collective-permute-start(bf16[4,8,2048]{2,1,0:T(8,128)(2,1)S(1)} %finish.2.refs_0_), channel_id=1, source_target_pairs={{0,1},{1,0},{2,3},{3,2},{4,5},{5,4},{6,7},{7,6},{8,9},{9,8},{10,11... | collective-permute-start | bytes 393224 | tf_op jit(solution)/shard_map/ppermute | solution.py:224
  53.1 6.3 %collective-permute-start.11 = (bf16[4,8,2048]{2,1,0:T(8,128)(2,1)S(1)}, bf16[4,8,2048]{2,1,0:T(8,128)(2,1)S(1)}, u32[]{:S(2)}, u32[]{:S(2)}) collective-permute-start(bf16[4,8,2048]{2,1,0:T(8,128)(2,1)S(1)} %collective-permute-done.10.refs_1_), channel_id=1, source_target_pairs={{0,1},{1,0},{2,3},{3,2},{4,5},{5,4},{6,7},{7,6},{8,9},{9,8},{10,11... | collective-permute-start | bytes 393224 | tf_op jit(solution)/shard_map/ppermute | solution.py:224
  53.2 6.2 %collective-permute-start.9 = (bf16[4,8,2048]{2,1,0:T(8,128)(2,1)S(1)}, bf16[4,8,2048]{2,1,0:T(8,128)(2,1)S(1)}, u32[]{:S(2)}, u32[]{:S(2)}) collective-permute-start(bf16[4,8,2048]{2,1,0:T(8,128)(2,1)S(1)} %collective-permute-done.8.refs_2_), channel_id=1, source_target_pairs={{0,1},{1,0},{2,3},{3,2},{4,5},{5,4},{6,7},{7,6},{8,9},{9,8},{10,11... | collective-permute-start | bytes 393224 | tf_op jit(solution)/shard_map/ppermute | solution.py:224
  57.9 1.5 %collective-permute-start.25 = (bf16[4,8,2048]{2,1,0:T(8,128)(2,1)S(1)}, bf16[4,8,2048]{2,1,0:T(8,128)(2,1)S(1)}, u32[]{:S(2)}, u32[]{:S(2)}) collective-permute-start(bf16[4,8,2048]{2,1,0:T(8,128)(2,1)S(1)} %collective-permute-done.12.refs_3_), channel_id=1, source_target_pairs={{0,1},{1,0},{2,3},{3,2},{4,5},{5,4},{6,7},{7,6},{8,9},{9,8},{10,11... | collective-permute-start | bytes 393224 | tf_op jit(solution)/shard_map/ppermute | solution.py:224

commit v8 on v7

--- a/solution.py
+++ b/solution.py
@@ -372,7 +372,8 @@
         return finish([part, line_hop(part, reach, z_size)])
 
     def gather_plane(attended):
-        return [attended] + [plane_hop(attended, j) for j in (1, 2, 3)]
+        first, second = plane_hop(attended, 1), plane_hop(attended, 2)
+        return [attended, first, second, plane_hop(first, 2)]
 
     kd, vt, sent = split_and_attend()
     received = hop(sent, 1)

time: 61.6 us -> 62.3 us (1.011)
  the two profiles are of different devices: /device:TPU:9 before, /device:TPU:0 now
where the time goes in v8:
time: 62.3 us; the launch traced here: 61.3 us
  starting transfers between devices  29.4 us (47%)
  waiting for transfers between devices  17.2 us (28%)
  Pallas kernels  13.8 us (22%)
  other arithmetic  0.75 us (1%)
    ppermute x12, starting transfers between devices, plane_hop(): return lax.ppermute(value, 'ctx', pairs)  16.3 us
    ppermute x12, waiting for transfers between devices, plane_hop(): return lax.ppermute(value, 'ctx', pairs)  12.9 us
    ppermute x4, starting transfers between devices, line_hop(): return lax.ppermute(value, 'ctx', pairs)  11.8 us
    ppermute x4, waiting for transfers between devices, line_hop(): return lax.ppermute(value, 'ctx', pairs)  4 us
    pallas_call x2, Pallas kernels, attend(): pl.pallas_call(functools.partial(attention_kernel, chunk_roles), in_specs...  3.99 us
    pallas_call x3, Pallas kernels, project(): pl.pallas_call(functools.partial(project_kernel, terms, bool(more), last)...  3.95 us
    pallas_call x1, Pallas kernels, split_and_attend(): pl.pallas_call(split_kernel, in_specs=[SMEM] + [HBM] * 3, out_specs=[VMEM...  3.27 us
    pallas_call x2, Pallas kernels, merge_cores(): pl.pallas_call(core_kernel, in_specs=[SMEM] + [VMEM] * 2, out_specs=[VMEM...  1.69 us
  transfers between devices with their start and end apart: 26, of which 11 were waited for; matrix products, arithmetic and copies ran while one was open for 0% of the time, Pallas kernels for 14%

profile of v8, /device:TPU:0, one launch (start us, length us, event | category | flops | bytes accessed | tf_op | source)
XLA Modules:
  0.0 61.3 jit_solution(4542804998557467820)
XLA Ops:
  0.8 3.3 %split_and_attend.1 = (bf16[4,1024,128]{2,1,0:T(8,128)(2,1)S(1)}, bf16[4,136,1024]{2,1,0:T(8,128)(2,1)S(1)}, bf16[16,136,128]{2,1,0:T(8,128)(2,1)S(1)}) custom-call(s32[18]{0:T(128)S(1)} %pad_add_fusion.meta, bf16[4096,128]{1,0:T(8,128)(2,1)} %bitcast.7, bf16[4096,128]{1,0:T(8,128)(2,1)} %bitcast.8, bf16[128,64,128]{2,1,0:T(8,128)(2,1)} %q_ref.3), custom_call_target="tpu_custom_call" | custom-call | flops 1073741824 | bytes 2097152 | tf_op jit(solution)/shard_map/split_and_attend/pallas_call | solution.py:270
  4.1 2.3 %attend.2 = (bf16[16,136,128]{2,1,0:T(8,128)(2,1)S(1)}, bf16[16,136,128]{2,1,0:T(8,128)(2,1)S(1)}) custom-call(s32[18]{0:T(128)S(1)} %pad_add_fusion.meta, bf16[4,1024,128]{2,1,0:T(8,128)(2,1)S(1)} %get-tuple-element.33.kd, bf16[4,136,1024]{2,1,0:T(8,128)(2,1)S(1)} %get-tuple-element.26.vt, bf16[128,64,128]{2,1,0:T(8,128)(2,1)S(1)} %copy-done), custom_call_target="tpu_custom_call" | custom-call | flops 2147483648 | bytes 1048576 | tf_op jit(solution)/shard_map/attend/pallas_call | solution.py:299
  6.6 0.8 %merge_cores.2 = (bf16[4,136,128]{2,1,0:T(8,128)(2,1)S(1)}, bf16[4,136,128]{2,1,0:T(8,128)(2,1)S(1)}, bf16[4,136,128]{2,1,0:T(8,128)(2,1)S(1)}, bf16[4,136,128]{2,1,0:T(8,128)(2,1)S(1)}) custom-call(s32[18]{0:T(128)S(1)} %pad_add_fusion.meta, bf16[16,136,128]{2,1,0:T(8,128)(2,1)S(1)} %get-tuple-element.27.kept, ...), custom_call_target="tpu_custom_call" | custom-call | tf_op jit(solution)/shard_map/merge_cores/pallas_call | solution.py:314
  7.4 2.9 %collective-permute-start.13 = (bf16[4,136,128]{2,1,0:T(8,128)(2,1)S(1)}, bf16[4,136,128]{2,1,0:T(8,128)(2,1)S(1)}, u32[]{:S(2)}, u32[]{:S(2)}) collective-permute-start(bf16[4,136,128]{2,1,0:T(8,128)(2,1)S(1)} %get-tuple-element.40), channel_id=1, source_target_pairs={{0,2},{1,5},{2,0},{3,7},{4,6},{5,1},{6,4},{7,3},{8,10},{9,13},{10,... | collective-permute-start | bytes 417800 | tf_op jit(solution)/shard_map/ppermute | solution.py:230
  10.3 2.2 %collective-permute-start.14 = (bf16[4,136,128]{2,1,0:T(8,128)(2,1)S(1)}, bf16[4,136,128]{2,1,0:T(8,128)(2,1)S(1)}, u32[]{:S(2)}, u32[]{:S(2)}) collective-permute-start(bf16[4,136,128]{2,1,0:T(8,128)(2,1)S(1)} %get-tuple-element.41), channel_id=1, source_target_pairs={{0,4},{1,3},{2,6},{3,1},{4,0},{5,7},{6,2},{7,5},{8,12},{9,11},{10,... | collective-permute-start | bytes 417800 | tf_op jit(solution)/shard_map/ppermute | solution.py:230
  12.4 0.9 %collective-permute-done.13.refs_1_ = bf16[4,136,128]{2,1,0:T(8,128)(2,1)S(1)} collective-permute-done((bf16[4,136,128]{2,1,0:T(8,128)(2,1)S(1)}, bf16[4,136,128]{2,1,0:T(8,128)(2,1)S(1)}, u32[]{:S(2)}, u32[]{:S(2)}) %collective-permute-start.13) | collective-permute-done | bytes 139296 | tf_op jit(solution)/shard_map/ppermute | solution.py:230
  13.4 4.6 %collective-permute-done.14.refs_2_ = bf16[4,136,128]{2,1,0:T(8,128)(2,1)S(1)} collective-permute-done((bf16[4,136,128]{2,1,0:T(8,128)(2,1)S(1)}, bf16[4,136,128]{2,1,0:T(8,128)(2,1)S(1)}, u32[]{:S(2)}, u32[]{:S(2)}) %collective-permute-start.14) | collective-permute-done | bytes 139296 | tf_op jit(solution)/shard_map/ppermute | solution.py:230
  18.0 1.0 %collective-permute-done.15.refs_3_ = bf16[4,136,128]{2,1,0:T(8,128)(2,1)S(1)} collective-permute-done((bf16[4,136,128]{2,1,0:T(8,128)(2,1)S(1)}, bf16[4,136,128]{2,1,0:T(8,128)(2,1)S(1)}, u32[]{:S(2)}, u32[]{:S(2)}) %collective-permute-start.15) | collective-permute-done | bytes 139296 | tf_op jit(solution)/shard_map/ppermute | solution.py:230
  19.2 3.9 %collective-permute-start.16 = (bf16[4,136,128]{2,1,0:T(8,128)(2,1)S(1)}, bf16[4,136,128]{2,1,0:T(8,128)(2,1)S(1)}, u32[]{:S(2)}, u32[]{:S(2)}) collective-permute-start(bf16[4,136,128]{2,1,0:T(8,128)(2,1)S(1)} %merge_chips.6.refs_0_), channel_id=1, source_target_pairs={{0,8},{1,17},{2,10},{3,19},{4,12},{5,21},{6,14},{7,23},{8,0},{9,25... | collective-permute-start | bytes 417800 | tf_op jit(solution)/shard_map/ppermute | solution.py:236
  23.0 1.7 %attend.3.kept = bf16[16,136,128]{2,1,0:T(8,128)(2,1)S(1)} custom-call(s32[18]{0:T(128)S(1)} %pad_add_fusion.meta, bf16[4,1024,128]{2,1,0:T(8,128)(2,1)S(1)} %get-tuple-element.33.kd, bf16[4,136,1024]{2,1,0:T(8,128)(2,1)S(1)} %get-tuple-element.26.vt, bf16[128,64,128]{2,1,0:T(8,128)(2,1)S(1)} %copy-done), custom_call_target="tpu_custom_call" | custom-call | flops 1073741824 | bytes 524288 | tf_op jit(solution)/shard_map/attend/pallas_call | solution.py:299
  24.7 0.8 %merge_cores.3 = (bf16[4,136,128]{2,1,0:T(8,128)(2,1)S(1)}, bf16[4,136,128]{2,1,0:T(8,128)(2,1)S(1)}, bf16[4,136,128]{2,1,0:T(8,128)(2,1)S(1)}, bf16[4,136,128]{2,1,0:T(8,128)(2,1)S(1)}) custom-call(s32[18]{0:T(128)S(1)} %pad_add_fusion.meta, bf16[16,136,128]{2,1,0:T(8,128)(2,1)S(1)} %attend.3.kept, bf16[16,136,128]{2,1,0:T(8,128)(2,1)S(1)} %collective-permute-done.1.received), custom_call_target="tpu_custom_call" | custom-call | tf_op jit(solution)/shard_map/merge_cores/pallas_call | solution.py:314
  25.5 0.9 %collective-permute-start.2 = (bf16[4,136,128]{2,1,0:T(8,128)(2,1)S(1)}, bf16[4,136,128]{2,1,0:T(8,128)(2,1)S(1)}, u32[]{:S(2)}, u32[]{:S(2)}) collective-permute-start(bf16[4,136,128]{2,1,0:T(8,128)(2,1)S(1)} %get-tuple-element.36), channel_id=1, source_target_pairs={{0,2},{1,5},{2,0},{3,7},{4,6},{5,1},{6,4},{7,3},{8,10},{9,13},{10,... | collective-permute-start | bytes 417800 | tf_op jit(solution)/shard_map/ppermute | solution.py:230
  26.5 0.8 %collective-permute-start.3 = (bf16[4,136,128]{2,1,0:T(8,128)(2,1)S(1)}, bf16[4,136,128]{2,1,0:T(8,128)(2,1)S(1)}, u32[]{:S(2)}, u32[]{:S(2)}) collective-permute-start(bf16[4,136,128]{2,1,0:T(8,128)(2,1)S(1)} %get-tuple-element.37), channel_id=1, source_target_pairs={{0,4},{1,3},{2,6},{3,1},{4,0},{5,7},{6,2},{7,5},{8,12},{9,11},{10,... | collective-permute-start | bytes 417800 | tf_op jit(solution)/shard_map/ppermute | solution.py:230
  27.3 1.8 %collective-permute-start.4 = (bf16[4,136,128]{2,1,0:T(8,128)(2,1)S(1)}, bf16[4,136,128]{2,1,0:T(8,128)(2,1)S(1)}, u32[]{:S(2)}, u32[]{:S(2)}) collective-permute-start(bf16[4,136,128]{2,1,0:T(8,128)(2,1)S(1)} %get-tuple-element.38), channel_id=1, source_target_pairs={{0,6},{1,7},{2,4},{3,5},{4,2},{5,3},{6,0},{7,1},{8,14},{9,15},{10,... | collective-permute-start | bytes 417800 | tf_op jit(solution)/shard_map/ppermute | solution.py:230
  29.2 3.6 %collective-permute-start.17 = (bf16[4,136,128]{2,1,0:T(8,128)(2,1)S(1)}, bf16[4,136,128]{2,1,0:T(8,128)(2,1)S(1)}, u32[]{:S(2)}, u32[]{:S(2)}) collective-permute-start(bf16[4,136,128]{2,1,0:T(8,128)(2,1)S(1)} %merge_chips.7.refs_0_), channel_id=1, source_target_pairs={{0,16},{1,9},{2,18},{3,11},{4,20},{5,13},{6,22},{7,15},{8,24},{9,1... | collective-permute-start | bytes 417800 | tf_op jit(solution)/shard_map/ppermute | solution.py:236
  32.8 1.7 %collective-permute-done.3.refs_2_ = bf16[4,136,128]{2,1,0:T(8,128)(2,1)S(1)} collective-permute-done((bf16[4,136,128]{2,1,0:T(8,128)(2,1)S(1)}, bf16[4,136,128]{2,1,0:T(8,128)(2,1)S(1)}, u32[]{:S(2)}, u32[]{:S(2)}) %collective-permute-start.3) | collective-permute-done | bytes 139296 | tf_op jit(solution)/shard_map/ppermute | solution.py:230
  34.7 1.0 %collective-permute-start.5 = (bf16[4,136,128]{2,1,0:T(8,128)(2,1)S(1)}, bf16[4,136,128]{2,1,0:T(8,128)(2,1)S(1)}, u32[]{:S(2)}, u32[]{:S(2)}) collective-permute-start(bf16[4,136,128]{2,1,0:T(8,128)(2,1)S(1)} %merge_chips.4.refs_0_), channel_id=1, source_target_pairs={{0,8},{1,17},{2,10},{3,19},{4,12},{5,21},{6,14},{7,23},{8,0},{9,25... | collective-permute-start | bytes 417800 | tf_op jit(solution)/shard_map/ppermute | solution.py:236
  35.6 1.1 %collective-permute-done.17.refs_1_ = bf16[4,136,128]{2,1,0:T(8,128)(2,1)S(1)} collective-permute-done((bf16[4,136,128]{2,1,0:T(8,128)(2,1)S(1)}, bf16[4,136,128]{2,1,0:T(8,128)(2,1)S(1)}, u32[]{:S(2)}, u32[]{:S(2)}) %collective-permute-start.17) | collective-permute-done | bytes 139296 | tf_op jit(solution)/shard_map/ppermute | solution.py:236
  37.0 1.0 %collective-permute-start.18 = (bf16[4,8,2048]{2,1,0:T(8,128)(2,1)S(1)}, bf16[4,8,2048]{2,1,0:T(8,128)(2,1)S(1)}, u32[]{:S(2)}, u32[]{:S(2)}) collective-permute-start(bf16[4,8,2048]{2,1,0:T(8,128)(2,1)S(1)} %finish.3.refs_0_), channel_id=1, source_target_pairs={{0,2},{1,5},{2,0},{3,7},{4,6},{5,1},{6,4},{7,3},{8,10},{9,13},{10,... | collective-permute-start | bytes 393224 | tf_op jit(solution)/shard_map/ppermute | solution.py:230
  38.0 1.9 %collective-permute-done.5.refs_1_ = bf16[4,136,128]{2,1,0:T(8,128)(2,1)S(1)} collective-permute-done((bf16[4,136,128]{2,1,0:T(8,128)(2,1)S(1)}, bf16[4,136,128]{2,1,0:T(8,128)(2,1)S(1)}, u32[]{:S(2)}, u32[]{:S(2)}) %collective-permute-start.5) | collective-permute-done | bytes 139296 | tf_op jit(solution)/shard_map/ppermute | solution.py:236
  39.9 3.4 %collective-permute-start.6 = (bf16[4,136,128]{2,1,0:T(8,128)(2,1)S(1)}, bf16[4,136,128]{2,1,0:T(8,128)(2,1)S(1)}, u32[]{:S(2)}, u32[]{:S(2)}) collective-permute-start(bf16[4,136,128]{2,1,0:T(8,128)(2,1)S(1)} %merge_chips.5.refs_0_), channel_id=1, source_target_pairs={{0,16},{1,9},{2,18},{3,11},{4,20},{5,13},{6,22},{7,15},{8,24},{9,1... | collective-permute-start | bytes 417800 | tf_op jit(solution)/shard_map/ppermute | solution.py:236
  43.3 1.0 %collective-permute-start.19 = (bf16[4,8,2048]{2,1,0:T(8,128)(2,1)S(1)}, bf16[4,8,2048]{2,1,0:T(8,128)(2,1)S(1)}, u32[]{:S(2)}, u32[]{:S(2)}) collective-permute-start(bf16[4,8,2048]{2,1,0:T(8,128)(2,1)S(1)} %finish.3.refs_0_), channel_id=1, source_target_pairs={{0,4},{1,3},{2,6},{3,1},{4,0},{5,7},{6,2},{7,5},{8,12},{9,11},{10,... | collective-permute-start | bytes 393224 | tf_op jit(solution)/shard_map/ppermute | solution.py:230
  44.3 1.0 %collective-permute-start.20 = (bf16[4,8,2048]{2,1,0:T(8,128)(2,1)S(1)}, bf16[4,8,2048]{2,1,0:T(8,128)(2,1)S(1)}, u32[]{:S(2)}, u32[]{:S(2)}) collective-permute-start(bf16[4,8,2048]{2,1,0:T(8,128)(2,1)S(1)} %collective-permute-done.18.refs_1_), channel_id=1, source_target_pairs={{0,4},{1,3},{2,6},{3,1},{4,0},{5,7},{6,2},{7,5},{8,12},{9,11},{10,... | collective-permute-start | bytes 393224 | tf_op jit(solution)/shard_map/ppermute | solution.py:230
  45.4 1.0 %collective-permute-done.6.refs_1_ = bf16[4,136,128]{2,1,0:T(8,128)(2,1)S(1)} collective-permute-done((bf16[4,136,128]{2,1,0:T(8,128)(2,1)S(1)}, bf16[4,136,128]{2,1,0:T(8,128)(2,1)S(1)}, u32[]{:S(2)}, u32[]{:S(2)}) %collective-permute-start.6) | collective-permute-done | bytes 139296 | tf_op jit(solution)/shard_map/ppermute | solution.py:236
  46.6 3.7 %collective-permute-start.10 = (bf16[4,8,2048]{2,1,0:T(8,128)(2,1)S(1)}, bf16[4,8,2048]{2,1,0:T(8,128)(2,1)S(1)}, u32[]{:S(2)}, u32[]{:S(2)}) collective-permute-start(bf16[4,8,2048]{2,1,0:T(8,128)(2,1)S(1)} %finish.2.refs_0_), channel_id=1, source_target_pairs={{0,2},{1,5},{2,0},{3,7},{4,6},{5,1},{6,4},{7,3},{8,10},{9,13},{10,... | collective-permute-start | bytes 393224 | tf_op jit(solution)/shard_map/ppermute | solution.py:230
  51.1 2.3 %collective-permute-done.10.refs_1_ = bf16[4,8,2048]{2,1,0:T(8,128)(2,1)S(1)} collective-permute-done((bf16[4,8,2048]{2,1,0:T(8,128)(2,1)S(1)}, bf16[4,8,2048]{2,1,0:T(8,128)(2,1)S(1)}, u32[]{:S(2)}, u32[]{:S(2)}) %collective-permute-start.10) | collective-permute-done | bytes 131104 | tf_op jit(solution)/shard_map/ppermute | solution.py:230
  53.3 0.8 %collective-permute-start.12 = (bf16[4,8,2048]{2,1,0:T(8,128)(2,1)S(1)}, bf16[4,8,2048]{2,1,0:T(8,128)(2,1)S(1)}, u32[]{:S(2)}, u32[]{:S(2)}) collective-permute-start(bf16[4,8,2048]{2,1,0:T(8,128)(2,1)S(1)} %collective-permute-done.10.refs_1_), channel_id=1, source_target_pairs={{0,4},{1,3},{2,6},{3,1},{4,0},{5,7},{6,2},{7,5},{8,12},{9,11},{10,... | collective-permute-start | bytes 393224 | tf_op jit(solution)/shard_map/ppermute | solution.py:230
  54.1 1.2 %collective-permute-done.8.refs_2_ = bf16[4,8,2048]{2,1,0:T(8,128)(2,1)S(1)} collective-permute-done((bf16[4,8,2048]{2,1,0:T(8,128)(2,1)S(1)}, bf16[4,8,2048]{2,1,0:T(8,128)(2,1)S(1)}, u32[]{:S(2)}, u32[]{:S(2)}) %collective-permute-start.8) | collective-permute-done | bytes 131104 | tf_op jit(solution)/shard_map/ppermute | solution.py:230
  55.9 1.3 %project.3.refs_4_ = f32[128,512]{1,0:T(8,128)S(1)} custom-call(s32[18]{0:T(128)S(1)} %pad_add_fusion.meta, bf16[8192,512]{1,0:T(8,128)(2,1)S(1)} %bitcast.6, bf16[4,8,2048]{2,1,0:T(8,128)(2,1)S(1)} %finish.3.refs_0_, bf16[4,8,2048]{2,1,0:T(8,128)(2,1)S(1)} %collective-permute-done.18.refs_1_, bf16[4,8,2048]{2,1,0:T(8,128)(2,1)S(1)} %collective-permute-done.19.refs_2_, ...), custom_call_target="tpu_custom_call" | custom-call | flops 536870912 | bytes 4194304 | tf_op jit(solution)/shard_map/project/pallas_call | solution.py:348
  57.2 1.1 %collective-permute-done.12.refs_3_ = bf16[4,8,2048]{2,1,0:T(8,128)(2,1)S(1)} collective-permute-done((bf16[4,8,2048]{2,1,0:T(8,128)(2,1)S(1)}, bf16[4,8,2048]{2,1,0:T(8,128)(2,1)S(1)}, u32[]{:S(2)}, u32[]{:S(2)}) %collective-permute-start.12) | collective-permute-done | bytes 131104 | tf_op jit(solution)/shard_map/ppermute | solution.py:230
  58.3 1.0 %project.4.refs_4_ = f32[128,512]{1,0:T(8,128)S(1)} custom-call(s32[18]{0:T(128)S(1)} %pad_add_fusion.meta, bf16[8192,512]{1,0:T(8,128)(2,1)S(1)} %bitcast.6, bf16[4,8,2048]{2,1,0:T(8,128)(2,1)S(1)} %finish.2.refs_0_, bf16[4,8,2048]{2,1,0:T(8,128)(2,1)S(1)} %collective-permute-done.10.refs_1_, bf16[4,8,2048]{2,1,0:T(8,128)(2,1)S(1)} %collective-permute-done.8.refs_2_, ...), custom_call_target="tpu_custom_call" | custom-call | flops 268435456 | bytes 2097152 | tf_op jit(solution)/shard_map/project/pallas_call | solution.py:348
  59.6 1.7 %project.5 = f32[128,512]{1,0:T(8,128)} custom-call(s32[18]{0:T(128)S(1)} %pad_add_fusion.meta, bf16[8192,512]{1,0:T(8,128)(2,1)S(1)} %bitcast.6, bf16[4,8,2048]{2,1,0:T(8,128)(2,1)S(1)} %collective-permute-done.7.refs_0_, bf16[4,8,2048]{2,1,0:T(8,128)(2,1)S(1)} %collective-permute-done.9.refs_1_, bf16[4,8,2048]{2,1,0:T(8,128)(2,1)S(1)} %collective-permute-done.11.refs_2_, ...), custom_call_target="tpu_custom_call" | custom-call | flops 268435456 | bytes 2097152 | tf_op jit(solution)/shard_map/project/pallas_call | solution.py:348
  (42 shorter events, 3.5 us)
Async XLA Ops:
  0.7 3.4 %copy-start = (bf16[128,64,128]{2,1,0:T(8,128)(2,1)S(1)}, bf16[128,64,128]{2,1,0:T(8,128)(2,1)}, u32[]{:S(2)}) copy-start(bf16[128,64,128]{2,1,0:T(8,128)(2,1)} %q_ref.3) | copy-start | bytes 6291460
  4.0 2.5 %collective-permute-start = (bf16[16,136,128]{2,1,0:T(8,128)(2,1)S(1)}, bf16[16,136,128]{2,1,0:T(8,128)(2,1)S(1)}, u32[]{:S(2)}, u32[]{:S(2)}) collective-permute-start(bf16[16,136,128]{2,1,0:T(8,128)(2,1)S(1)} %get-tuple-element.28), channel_id=1, source_target_pairs={{0,1},{1,0},{2,3},{3,2},{4,5},{5,4},{6,7},{7,6},{8,9},{9,8},{10,11... | collective-permute-start | bytes 1671176 | tf_op jit(solution)/shard_map/ppermute | solution.py:224
  4.1 51.8 %slice-start = ((s8[8388608]{0:T(1024)(128)(4,1)}), s8[4194304]{0:T(1024)(128)(4,1)S(1)}, s32[]{:S(2)}) async-start(s8[8388608]{0:T(1024)(128)(4,1)} %bitcast.5), calls=%async_computation | async-start | bytes 8388608
  6.5 18.2 %collective-permute-start.1 = (bf16[16,136,128]{2,1,0:T(8,128)(2,1)S(1)}, bf16[16,136,128]{2,1,0:T(8,128)(2,1)S(1)}, u32[]{:S(2)}, u32[]{:S(2)}) collective-permute-start(bf16[16,136,128]{2,1,0:T(8,128)(2,1)S(1)} %get-tuple-element.34), channel_id=1, source_target_pairs={{0,1},{1,0},{2,3},{3,2},{4,5},{5,4},{6,7},{7,6},{8,9},{9,8},{10,11... | collective-permute-start | bytes 1671176 | tf_op jit(solution)/shard_map/ppermute | solution.py:224
  6.6 49.3 %slice-start.1 = ((s8[8388608]{0:T(1024)(128)(4,1)}), s8[4194304]{0:T(1024)(128)(4,1)S(1)}, s32[]{:S(2)}) async-start(s8[8388608]{0:T(1024)(128)(4,1)} %bitcast.5), calls=%async_computation.1 | async-start | bytes 8388608
  7.4 6.0 %collective-permute-start.13 = (bf16[4,136,128]{2,1,0:T(8,128)(2,1)S(1)}, bf16[4,136,128]{2,1,0:T(8,128)(2,1)S(1)}, u32[]{:S(2)}, u32[]{:S(2)}) collective-permute-start(bf16[4,136,128]{2,1,0:T(8,128)(2,1)S(1)} %get-tuple-element.40), channel_id=1, source_target_pairs={{0,2},{1,5},{2,0},{3,7},{4,6},{5,1},{6,4},{7,3},{8,10},{9,13},{10,... | collective-permute-start | bytes 417800 | tf_op jit(solution)/shard_map/ppermute | solution.py:230
  10.3 7.7 %collective-permute-start.14 = (bf16[4,136,128]{2,1,0:T(8,128)(2,1)S(1)}, bf16[4,136,128]{2,1,0:T(8,128)(2,1)S(1)}, u32[]{:S(2)}, u32[]{:S(2)}) collective-permute-start(bf16[4,136,128]{2,1,0:T(8,128)(2,1)S(1)} %get-tuple-element.41), channel_id=1, source_target_pairs={{0,4},{1,3},{2,6},{3,1},{4,0},{5,7},{6,2},{7,5},{8,12},{9,11},{10,... | collective-permute-start | bytes 417800 | tf_op jit(solution)/shard_map/ppermute | solution.py:230
  12.4 6.6 %collective-permute-start.15 = (bf16[4,136,128]{2,1,0:T(8,128)(2,1)S(1)}, bf16[4,136,128]{2,1,0:T(8,128)(2,1)S(1)}, u32[]{:S(2)}, u32[]{:S(2)}) collective-permute-start(bf16[4,136,128]{2,1,0:T(8,128)(2,1)S(1)} %get-tuple-element.42), channel_id=1, source_target_pairs={{0,6},{1,7},{2,4},{3,5},{4,2},{5,3},{6,0},{7,1},{8,14},{9,15},{10,... | collective-permute-start | bytes 417800 | tf_op jit(solution)/shard_map/ppermute | solution.py:230
  19.2 9.9 %collective-permute-start.16 = (bf16[4,136,128]{2,1,0:T(8,128)(2,1)S(1)}, bf16[4,136,128]{2,1,0:T(8,128)(2,1)S(1)}, u32[]{:S(2)}, u32[]{:S(2)}) collective-permute-start(bf16[4,136,128]{2,1,0:T(8,128)(2,1)S(1)} %merge_chips.6.refs_0_), channel_id=1, source_target_pairs={{0,8},{1,17},{2,10},{3,19},{4,12},{5,21},{6,14},{7,23},{8,0},{9,25... | collective-permute-start | bytes 417800 | tf_op jit(solution)/shard_map/ppermute | solution.py:236
  25.5 7.3 %collective-permute-start.2 = (bf16[4,136,128]{2,1,0:T(8,128)(2,1)S(1)}, bf16[4,136,128]{2,1,0:T(8,128)(2,1)S(1)}, u32[]{:S(2)}, u32[]{:S(2)}) collective-permute-start(bf16[4,136,128]{2,1,0:T(8,128)(2,1)S(1)} %get-tuple-element.36), channel_id=1, source_target_pairs={{0,2},{1,5},{2,0},{3,7},{4,6},{5,1},{6,4},{7,3},{8,10},{9,13},{10,... | collective-permute-start | bytes 417800 | tf_op jit(solution)/shard_map/ppermute | solution.py:230
  26.5 8.0 %collective-permute-start.3 = (bf16[4,136,128]{2,1,0:T(8,128)(2,1)S(1)}, bf16[4,136,128]{2,1,0:T(8,128)(2,1)S(1)}, u32[]{:S(2)}, u32[]{:S(2)}) collective-permute-start(bf16[4,136,128]{2,1,0:T(8,128)(2,1)S(1)} %get-tuple-element.37), channel_id=1, source_target_pairs={{0,4},{1,3},{2,6},{3,1},{4,0},{5,7},{6,2},{7,5},{8,12},{9,11},{10,... | collective-permute-start | bytes 417800 | tf_op jit(solution)/shard_map/ppermute | solution.py:230
  27.3 7.2 %collective-permute-start.4 = (bf16[4,136,128]{2,1,0:T(8,128)(2,1)S(1)}, bf16[4,136,128]{2,1,0:T(8,128)(2,1)S(1)}, u32[]{:S(2)}, u32[]{:S(2)}) collective-permute-start(bf16[4,136,128]{2,1,0:T(8,128)(2,1)S(1)} %get-tuple-element.38), channel_id=1, source_target_pairs={{0,6},{1,7},{2,4},{3,5},{4,2},{5,3},{6,0},{7,1},{8,14},{9,15},{10,... | collective-permute-start | bytes 417800 | tf_op jit(solution)/shard_map/ppermute | solution.py:230
  29.2 7.6 %collective-permute-start.17 = (bf16[4,136,128]{2,1,0:T(8,128)(2,1)S(1)}, bf16[4,136,128]{2,1,0:T(8,128)(2,1)S(1)}, u32[]{:S(2)}, u32[]{:S(2)}) collective-permute-start(bf16[4,136,128]{2,1,0:T(8,128)(2,1)S(1)} %merge_chips.7.refs_0_), channel_id=1, source_target_pairs={{0,16},{1,9},{2,18},{3,11},{4,20},{5,13},{6,22},{7,15},{8,24},{9,1... | collective-permute-start | bytes 417800 | tf_op jit(solution)/shard_map/ppermute | solution.py:236
  34.7 5.2 %collective-permute-start.5 = (bf16[4,136,128]{2,1,0:T(8,128)(2,1)S(1)}, bf16[4,136,128]{2,1,0:T(8,128)(2,1)S(1)}, u32[]{:S(2)}, u32[]{:S(2)}) collective-permute-start(bf16[4,136,128]{2,1,0:T(8,128)(2,1)S(1)} %merge_chips.4.refs_0_), channel_id=1, source_target_pairs={{0,8},{1,17},{2,10},{3,19},{4,12},{5,21},{6,14},{7,23},{8,0},{9,25... | collective-permute-start | bytes 417800 | tf_op jit(solution)/shard_map/ppermute | solution.py:236
  37.0 7.3 %collective-permute-start.18 = (bf16[4,8,2048]{2,1,0:T(8,128)(2,1)S(1)}, bf16[4,8,2048]{2,1,0:T(8,128)(2,1)S(1)}, u32[]{:S(2)}, u32[]{:S(2)}) collective-permute-start(bf16[4,8,2048]{2,1,0:T(8,128)(2,1)S(1)} %finish.3.refs_0_), channel_id=1, source_target_pairs={{0,2},{1,5},{2,0},{3,7},{4,6},{5,1},{6,4},{7,3},{8,10},{9,13},{10,... | collective-permute-start | bytes 393224 | tf_op jit(solution)/shard_map/ppermute | solution.py:230
  39.9 6.4 %collective-permute-start.6 = (bf16[4,136,128]{2,1,0:T(8,128)(2,1)S(1)}, bf16[4,136,128]{2,1,0:T(8,128)(2,1)S(1)}, u32[]{:S(2)}, u32[]{:S(2)}) collective-permute-start(bf16[4,136,128]{2,1,0:T(8,128)(2,1)S(1)} %merge_chips.5.refs_0_), channel_id=1, source_target_pairs={{0,16},{1,9},{2,18},{3,11},{4,20},{5,13},{6,22},{7,15},{8,24},{9,1... | collective-permute-start | bytes 417800 | tf_op jit(solution)/shard_map/ppermute | solution.py:236
  43.3 7.1 %collective-permute-start.19 = (bf16[4,8,2048]{2,1,0:T(8,128)(2,1)S(1)}, bf16[4,8,2048]{2,1,0:T(8,128)(2,1)S(1)}, u32[]{:S(2)}, u32[]{:S(2)}) collective-permute-start(bf16[4,8,2048]{2,1,0:T(8,128)(2,1)S(1)} %finish.3.refs_0_), channel_id=1, source_target_pairs={{0,4},{1,3},{2,6},{3,1},{4,0},{5,7},{6,2},{7,5},{8,12},{9,11},{10,... | collective-permute-start | bytes 393224 | tf_op jit(solution)/shard_map/ppermute | solution.py:230
  44.3 6.1 %collective-permute-start.21 = (bf16[4,8,2048]{2,1,0:T(8,128)(2,1)S(1)}, bf16[4,8,2048]{2,1,0:T(8,128)(2,1)S(1)}, u32[]{:S(2)}, u32[]{:S(2)}) collective-permute-start(bf16[4,8,2048]{2,1,0:T(8,128)(2,1)S(1)} %finish.3.refs_0_), channel_id=1, source_target_pairs={{0,1},{1,0},{2,3},{3,2},{4,5},{5,4},{6,7},{7,6},{8,9},{9,8},{10,11... | collective-permute-start | bytes 393224 | tf_op jit(solution)/shard_map/ppermute | solution.py:224
  44.3 6.7 %collective-permute-start.20 = (bf16[4,8,2048]{2,1,0:T(8,128)(2,1)S(1)}, bf16[4,8,2048]{2,1,0:T(8,128)(2,1)S(1)}, u32[]{:S(2)}, u32[]{:S(2)}) collective-permute-start(bf16[4,8,2048]{2,1,0:T(8,128)(2,1)S(1)} %collective-permute-done.18.refs_1_), channel_id=1, source_target_pairs={{0,4},{1,3},{2,6},{3,1},{4,0},{5,7},{6,2},{7,5},{8,12},{9,11},{10,... | collective-permute-start | bytes 393224 | tf_op jit(solution)/shard_map/ppermute | solution.py:230
  46.6 6.7 %collective-permute-start.10 = (bf16[4,8,2048]{2,1,0:T(8,128)(2,1)S(1)}, bf16[4,8,2048]{2,1,0:T(8,128)(2,1)S(1)}, u32[]{:S(2)}, u32[]{:S(2)}) collective-permute-start(bf16[4,8,2048]{2,1,0:T(8,128)(2,1)S(1)} %finish.2.refs_0_), channel_id=1, source_target_pairs={{0,2},{1,5},{2,0},{3,7},{4,6},{5,1},{6,4},{7,3},{8,10},{9,13},{10,... | collective-permute-start | bytes 393224 | tf_op jit(solution)/shard_map/ppermute | solution.py:230
  50.3 5.0 %collective-permute-start.8 = (bf16[4,8,2048]{2,1,0:T(8,128)(2,1)S(1)}, bf16[4,8,2048]{2,1,0:T(8,128)(2,1)S(1)}, u32[]{:S(2)}, u32[]{:S(2)}) collective-permute-start(bf16[4,8,2048]{2,1,0:T(8,128)(2,1)S(1)} %finish.2.refs_0_), channel_id=1, source_target_pairs={{0,4},{1,3},{2,6},{3,1},{4,0},{5,7},{6,2},{7,5},{8,12},{9,11},{10,... | collective-permute-start | bytes 393224 | tf_op jit(solution)/shard_map/ppermute | solution.py:230
  50.5 4.8 %collective-permute-start.22 = (bf16[4,8,2048]{2,1,0:T(8,128)(2,1)S(1)}, bf16[4,8,2048]{2,1,0:T(8,128)(2,1)S(1)}, u32[]{:S(2)}, u32[]{:S(2)}) collective-permute-start(bf16[4,8,2048]{2,1,0:T(8,128)(2,1)S(1)} %collective-permute-done.19.refs_2_), channel_id=1, source_target_pairs={{0,1},{1,0},{2,3},{3,2},{4,5},{5,4},{6,7},{7,6},{8,9},{9,8},{10,11... | collective-permute-start | bytes 393224 | tf_op jit(solution)/shard_map/ppermute | solution.py:224
  50.5 5.3 %collective-permute-start.23 = (bf16[4,8,2048]{2,1,0:T(8,128)(2,1)S(1)}, bf16[4,8,2048]{2,1,0:T(8,128)(2,1)S(1)}, u32[]{:S(2)}, u32[]{:S(2)}) collective-permute-start(bf16[4,8,2048]{2,1,0:T(8,128)(2,1)S(1)} %collective-permute-done.18.refs_1_), channel_id=1, source_target_pairs={{0,1},{1,0},{2,3},{3,2},{4,5},{5,4},{6,7},{7,6},{8,9},{9,8},{10,11... | collective-permute-start | bytes 393224 | tf_op jit(solution)/shard_map/ppermute | solution.py:224
  51.0 4.9 %collective-permute-start.24 = (bf16[4,8,2048]{2,1,0:T(8,128)(2,1)S(1)}, bf16[4,8,2048]{2,1,0:T(8,128)(2,1)S(1)}, u32[]{:S(2)}, u32[]{:S(2)}) collective-permute-start(bf16[4,8,2048]{2,1,0:T(8,128)(2,1)S(1)} %collective-permute-done.20.refs_3_), channel_id=1, source_target_pairs={{0,1},{1,0},{2,3},{3,2},{4,5},{5,4},{6,7},{7,6},{8,9},{9,8},{10,11... | collective-permute-start | bytes 393224 | tf_op jit(solution)/shard_map/ppermute | solution.py:224
  53.3 5.0 %collective-permute-start.12 = (bf16[4,8,2048]{2,1,0:T(8,128)(2,1)S(1)}, bf16[4,8,2048]{2,1,0:T(8,128)(2,1)S(1)}, u32[]{:S(2)}, u32[]{:S(2)}) collective-permute-start(bf16[4,8,2048]{2,1,0:T(8,128)(2,1)S(1)} %collective-permute-done.10.refs_1_), channel_id=1, source_target_pairs={{0,4},{1,3},{2,6},{3,1},{4,0},{5,7},{6,2},{7,5},{8,12},{9,11},{10,... | collective-permute-start | bytes 393224 | tf_op jit(solution)/shard_map/ppermute | solution.py:230
  55.3 4.0 %collective-permute-start.7 = (bf16[4,8,2048]{2,1,0:T(8,128)(2,1)S(1)}, bf16[4,8,2048]{2,1,0:T(8,128)(2,1)S(1)}, u32[]{:S(2)}, u32[]{:S(2)}) collective-permute-start(bf16[4,8,2048]{2,1,0:T(8,128)(2,1)S(1)} %finish.2.refs_0_), channel_id=1, source_target_pairs={{0,1},{1,0},{2,3},{3,2},{4,5},{5,4},{6,7},{7,6},{8,9},{9,8},{10,11... | collective-permute-start | bytes 393224 | tf_op jit(solution)/shard_map/ppermute | solution.py:224
  55.3 4.0 %collective-permute-start.11 = (bf16[4,8,2048]{2,1,0:T(8,128)(2,1)S(1)}, bf16[4,8,2048]{2,1,0:T(8,128)(2,1)S(1)}, u32[]{:S(2)}, u32[]{:S(2)}) collective-permute-start(bf16[4,8,2048]{2,1,0:T(8,128)(2,1)S(1)} %collective-permute-done.10.refs_1_), channel_id=1, source_target_pairs={{0,1},{1,0},{2,3},{3,2},{4,5},{5,4},{6,7},{7,6},{8,9},{9,8},{10,11... | collective-permute-start | bytes 393224 | tf_op jit(solution)/shard_map/ppermute | solution.py:224
  55.8 3.5 %collective-permute-start.9 = (bf16[4,8,2048]{2,1,0:T(8,128)(2,1)S(1)}, bf16[4,8,2048]{2,1,0:T(8,128)(2,1)S(1)}, u32[]{:S(2)}, u32[]{:S(2)}) collective-permute-start(bf16[4,8,2048]{2,1,0:T(8,128)(2,1)S(1)} %collective-permute-done.8.refs_2_), channel_id=1, source_target_pairs={{0,1},{1,0},{2,3},{3,2},{4,5},{5,4},{6,7},{7,6},{8,9},{9,8},{10,11... | collective-permute-start | bytes 393224 | tf_op jit(solution)/shard_map/ppermute | solution.py:224
  58.3 1.3 %collective-permute-start.25 = (bf16[4,8,2048]{2,1,0:T(8,128)(2,1)S(1)}, bf16[4,8,2048]{2,1,0:T(8,128)(2,1)S(1)}, u32[]{:S(2)}, u32[]{:S(2)}) collective-permute-start(bf16[4,8,2048]{2,1,0:T(8,128)(2,1)S(1)} %collective-permute-done.12.refs_3_), channel_id=1, source_target_pairs={{0,1},{1,0},{2,3},{3,2},{4,5},{5,4},{6,7},{7,6},{8,9},{9,8},{10,11... | collective-permute-start | bytes 393224 | tf_op jit(solution)/shard_map/ppermute | solution.py:224
